TPU v7x, 32 devices: a whole 2x2x4 slice. The times are simulated.
32 devices in a mesh: win: 2 (over x), fib: 16 (over z, y, core).
Axes of the slice: x: 2, y: 2, z: 4, core: 2. Of those that a mesh axis runs over, the one named last changes fastest.
Arguments:
- strain: bfloat16 [8192, 4096], P(('win', 'fib')), parts along dimension 0, may hold values from -6 to 6
- steering: bfloat16 [9, 128, 256], replicated, may hold values from -0.375 to 0.375
- lag_range: bfloat16 [9, 512, 384], replicated, may hold values from -0.25 to 0.25
- pair_listed: int32 [32, 8], P(('win', 'fib')), parts along dimension 0, may hold values 0 or 1
- band_used: int32 [32, 8, 4], P(('win', 'fib')), parts along dimension 0, may hold values 0 or 1
Outputs:
- image: float32 [128, 4096], P(None, ('win', 'fib')), parts along dimension 1
There are 2 independent parts, one for each index of `win`. A program takes and returns all parts, laid end to end along the dimension named above; an argument that names none is the same for every part. Nothing has to cross between parts.
All inputs are finite; a program needn't handle non-finite values. No bound on the sum of `pair_listed` or of `band_used` on one device may be relied on, other than what follows from the above.
Results may differ from a plain program's by a relative error of at most 0.012.
Values may be sent and summed in bfloat16 or wider, within the bound.
No kernel may reach another device: no remote copies, remote signals or barrier semaphores. Data moves between devices by JAX's collectives and lax.ppermute only.
A program may use at most 64 MiB of HBM per device.

v0:
```python
import math

import jax
import jax.numpy as jnp
from jax import lax
from jax.sharding import PartitionSpec as P

F = 512
L = 512


def shifted(shard, axis, by):
    devices = lax.axis_size(axis)
    pairs = [(i, i + by) for i in range(devices) if 0 <= i + by < devices]
    return lax.ppermute(shard, axis, pairs)


def make_tables(samples):
    steps_t = jnp.arange(samples, dtype=jnp.int32)[:, None]
    freq = jnp.arange(1, F + 1, dtype=jnp.int32)[None, :]
    phase = (steps_t * freq % samples).astype(jnp.float32) * (2.0 * math.pi / samples)
    forward = (
        jnp.concatenate([jnp.cos(phase), -jnp.sin(phase)], axis=1) * samples ** (-0.5)
    ).astype(jnp.bfloat16)
    lag_index = (jnp.arange(L, dtype=jnp.int32) - L // 2)[None, :]
    theta = (freq.reshape(F, 1) * lag_index % samples).astype(jnp.float32) * (
        2.0 * math.pi / samples
    )
    inverse = (
        jnp.concatenate([jnp.cos(theta), -jnp.sin(theta)], axis=0) * (2 * F) ** (-0.5)
    ).astype(jnp.bfloat16)
    return (forward, inverse)


def pair_window(near, far_spec, listed, bands, dist, inverse, steering, lag_range):
    near_float = near.astype(jnp.float32)
    far = far_spec.astype(jnp.float32)
    real_own = near_float[:, :F]
    imag_own = near_float[:, F:]
    real_far = far[:, :F]
    imag_far = far[:, F:]
    real_part = real_own * real_far + imag_own * imag_far
    imag_part = imag_own * real_far - real_own * imag_far
    cross = jnp.concatenate([real_part, imag_part], axis=1).astype(jnp.bfloat16)
    lags = jnp.dot(cross, inverse, preferred_element_type=jnp.float32)
    channels = near.shape[0]
    nbands = bands.shape[0]
    weight = (listed * bands).astype(jnp.float32)
    lags = (
        (lags.reshape(channels, nbands, -1) * weight[None, :, None])
        .reshape(channels, -1)
        .astype(jnp.bfloat16)
    )
    beams = jnp.dot(steering[dist], lags, preferred_element_type=jnp.float32).astype(jnp.bfloat16)
    return jnp.dot(beams, lag_range[dist], preferred_element_type=jnp.float32)


def per_device(strain, steering, lag_range, pair_listed, band_used):
    forward, inverse = make_tables(strain.shape[1])
    spectrum = jnp.dot(strain, forward, preferred_element_type=jnp.float32).astype(jnp.bfloat16)
    rounds = steering.shape[0] - 1
    width = lag_range.shape[2] // 3
    all_bands = jnp.ones((band_used.shape[2],), jnp.int32)
    window = pair_window(
        spectrum, spectrum, jnp.int32(1), all_bands, 0, inverse, steering, lag_range
    )
    stacked = spectrum[None]
    held = 1
    while held < rounds + 1:
        taken = min(held, rounds + 1 - held)
        received = shifted(stacked[:taken], "fib", held)
        stacked = jnp.concatenate([stacked, received], axis=0)
        held = held + taken
    partners = [stacked[dist] for dist in range(1, rounds + 1)]
    for dist in range(1, rounds + 1):
        window = window + pair_window(
            spectrum,
            partners[dist - 1],
            pair_listed[0, dist - 1],
            band_used[0, dist - 1, :],
            dist,
            inverse,
            steering,
            lag_range,
        )
    from_below = shifted(window[:, 2 * width :].astype(jnp.bfloat16), "fib", 1).astype(jnp.float32)
    from_above = shifted(window[:, :width].astype(jnp.bfloat16), "fib", -1).astype(jnp.float32)
    image = window[:, width : 2 * width] + from_below + from_above
    return image


def solution(mesh):
    return jax.shard_map(
        per_device,
        mesh=mesh,
        in_specs=(
            P(("win", "fib"), None),
            P(),
            P(),
            P(("win", "fib"), None),
            P(("win", "fib"), None, None),
        ),
        out_specs=P(None, ("win", "fib")),
        check_vma=False,
    )
```

profile of v0, /device:TPU:17, one launch (start us, length us, event | category | flops | bytes accessed | tf_op | source)
XLA Modules:
  0.0 188.2 jit_solution(6910317218147580989)
XLA Ops:
  0.0 34.4 %fusion.9 = (f32[4096,512]{1,0:T(8,128)S(1)}, f32[4096,512]{1,0:T(8,128)}) fusion(s32[512]{0:T(512)S(1)} %get-tuple-element.64), kind=kLoop, calls=%fused_computation.13 | loop fusion | flops 31457280 | bytes 16779264 | tf_op jit(solution)/shard_map/cos | solution.py:23
  34.5 5.7 %bitcast_convert_fusion.2 = (f32[256,1024]{0,1:T(8,128)S(1)}, bf16[1024,256]{1,0:T(8,128)(2,1)S(1)}) fusion(bf16[256,4096]{1,0:T(8,128)(2,1)S(1)} %copy-done, f32[4096,512]{1,0:T(8,128)} %get-tuple-element.50, f32[4096,512]{1,0:T(8,128)S(1)} %get-tuple-element.49), kind=kOutput, calls=%fused_computation.112 | convolution fusion | flops 2160590848 | bytes 20447232 | tf_op jit(solution)/shard_map/dot_general | solution.py:60
  40.2 3.7 %collective-permute-start = (bf16[1,256,1024]{1,2,0:T(8,128)(2,1)S(1)}, bf16[1,256,1024]{1,2,0:T(8,128)(2,1)S(1)}, u32[]{:S(2)}, u32[]{:S(2)}) collective-permute-start(bf16[1,256,1024]{1,2,0:T(8,128)(2,1)S(1)} %bitcast.139), channel_id=1, source_target_pairs={{0,1},{1,2},{2,3},{3,4},{4,5},{5,6},{6,7},{7,8},{8,9},{9,10},{10,1... | collective-permute-start | bytes 1572872 | tf_op jit(solution)/shard_map/ppermute | solution.py:15
  43.9 6.1 %collective-permute-done = bf16[1,256,1024]{1,2,0:T(8,128)(2,1)S(1)} collective-permute-done((bf16[1,256,1024]{1,2,0:T(8,128)(2,1)S(1)}, bf16[1,256,1024]{1,2,0:T(8,128)(2,1)S(1)}, u32[]{:S(2)}, u32[]{:S(2)}) %collective-permute-start) | collective-permute-done | bytes 524320 | tf_op jit(solution)/shard_map/ppermute | solution.py:15
  50.1 3.1 %collective-permute-start.1 = (bf16[2,256,1024]{1,2,0:T(8,128)(2,1)S(1)}, bf16[2,256,1024]{1,2,0:T(8,128)(2,1)S(1)}, u32[]{:S(2)}, u32[]{:S(2)}) collective-permute-start(bf16[2,256,1024]{1,2,0:T(8,128)(2,1)S(1)} %pad_maximum_fusion.1), channel_id=1, source_target_pairs={{0,2},{1,3},{2,4},{3,5},{4,6},{5,7},{6,8},{7,9},{8,10},{9,11},{10,... | collective-permute-start | bytes 3145736 | tf_op jit(solution)/shard_map/ppermute | solution.py:15
  55.2 5.3 %convert_reduce_fusion = (f32[4]{0:T(128)S(1)}, f32[4]{0:T(128)S(1)}, f32[4]{0:T(128)S(1)}, f32[4]{0:T(128)S(1)}, f32[4]{0:T(128)S(1)}, /*index=5*/f32[4]{0:T(128)S(1)}, f32[4]{0:T(128)S(1)}, f32[4]{0:T(128)S(1)}) fusion(s32[1,8,4]{1,2,0:T(4,128)S(1)} %copy-done.3, s32[]{:T(128)} %bitcast.49, s32[]{:T(128)} %bitcast.37, s32[]{:T(128)} %bitcast.31, ...), kind=kLoop, calls=%fused_computation.179 | loop fusion | flops 64 | bytes 288 | tf_op jit(solution)/shard_map/convert_element_type | solution.py:48
  60.7 4.2 %fusion.103 = (f32[512,512]{1,0:T(8,128)S(1)}, f32[512,512]{1,0:T(8,128)S(1)}) fusion(s32[512]{0:T(512)S(1)} %get-tuple-element.63, s32[512]{0:T(512)S(1)} %get-tuple-element.64), kind=kLoop, calls=%fused_computation.129 | loop fusion | flops 3932160 | bytes 2101248 | tf_op jit(solution)/shard_map/cos | solution.py:30
  64.9 10.6 %collective-permute-done.1 = bf16[2,256,1024]{1,2,0:T(8,128)(2,1)S(1)} collective-permute-done((bf16[2,256,1024]{1,2,0:T(8,128)(2,1)S(1)}, bf16[2,256,1024]{1,2,0:T(8,128)(2,1)S(1)}, u32[]{:S(2)}, u32[]{:S(2)}) %collective-permute-start.1) | collective-permute-done | bytes 1048608 | tf_op jit(solution)/shard_map/ppermute | solution.py:15
  75.5 1.7 pad_maximum_fusion
  77.1 3.3 %collective-permute-start.2 = (bf16[4,256,1024]{1,2,0:T(8,128)(2,1)}, bf16[4,256,1024]{1,2,0:T(8,128)(2,1)}, u32[]{:S(2)}, u32[]{:S(2)}) collective-permute-start(bf16[4,256,1024]{1,2,0:T(8,128)(2,1)} %pad_maximum_fusion), channel_id=1, source_target_pairs={{0,4},{1,5},{2,6},{3,7},{4,8},{5,9},{6,10},{7,11},{8,12},{9,13},{1... | collective-permute-start | bytes 6291464 | tf_op jit(solution)/shard_map/ppermute | solution.py:15
  83.1 1.4 add_convert_fusion
  84.5 2.8 %fusion.38 = bf16[512,128]{1,0:T(8,128)(2,1)} fusion(bf16[1024,512]{1,0:T(8,128)(2,1)} %fusion.10, bf16[256,512]{0,1:T(8,128)(2,1)} %get-tuple-element.14, bf16[256,512]{0,1:T(8,128)(2,1)} %get-tuple-element.13, f32[512]{0:T(512)S(1)} %get-tuple-element.65, bf16[9,128,256]{2,1,0:T(8,128)(2,1)} %param.6), kind=kOutput, calls=%fused_computation.64 | convolution fusion | flops 303366144 | bytes 1771520 | tf_op jit(solution)/shard_map/dot_general | solution.py:54
  87.3 2.1 %fusion.31 = bf16[512,128]{1,0:T(8,128)(2,1)S(1)} fusion(bf16[1024,512]{1,0:T(8,128)(2,1)} %fusion.10, bf16[256,512]{0,1:T(8,128)(2,1)} %get-tuple-element.33, bf16[256,512]{0,1:T(8,128)(2,1)} %get-tuple-element.34, f32[512]{0:T(512)} %get-tuple-element.72, bf16[9,128,256]{2,1,0:T(8,128)(2,1)} %param.6), kind=kOutput, calls=%fused_computation.57 | convolution fusion | flops 303366144 | bytes 1771520 | tf_op jit(solution)/shard_map/dot_general | solution.py:54
  89.5 1.4 fusion.47
  90.8 19.2 %collective-permute-done.2 = bf16[4,256,1024]{1,2,0:T(8,128)(2,1)} collective-permute-done((bf16[4,256,1024]{1,2,0:T(8,128)(2,1)}, bf16[4,256,1024]{1,2,0:T(8,128)(2,1)}, u32[]{:S(2)}, u32[]{:S(2)}) %collective-permute-start.2) | collective-permute-done | bytes 2097184 | tf_op jit(solution)/shard_map/ppermute | solution.py:15
  110.0 1.9 fusion.43
  111.9 1.6 add_convert_fusion.1
  113.5 1.4 add_convert_fusion.2
  115.0 1.4 add_convert_fusion.3
  116.4 2.7 %fusion.39 = bf16[512,128]{1,0:T(8,128)(2,1)} fusion(bf16[1024,512]{1,0:T(8,128)(2,1)} %fusion.10, bf16[256,512]{0,1:T(8,128)(2,1)} %get-tuple-element.38, bf16[256,512]{0,1:T(8,128)(2,1)S(1)} %get-tuple-element.35, bf16[9,128,256]{2,1,0:T(8,128)(2,1)} %param.6), kind=kOutput, calls=%fused_computation.65 | convolution fusion | flops 303235072 | bytes 1769472 | tf_op jit(solution)/shard_map/dot_general | solution.py:54
  121.7 2.4 %fusion.32 = bf16[512,128]{1,0:T(8,128)(2,1)} fusion(bf16[1024,512]{1,0:T(8,128)(2,1)S(1)} %copy-done.2, bf16[256,512]{0,1:T(8,128)(2,1)} %get-tuple-element.36, bf16[256,512]{0,1:T(8,128)(2,1)} %get-tuple-element.37, f32[512]{0:T(512)} %get-tuple-element.71, bf16[9,128,256]{2,1,0:T(8,128)(2,1)} %param.6), kind=kOutput, calls=%fused_computation.58 | convolution fusion | flops 303366144 | bytes 1771520 | tf_op jit(solution)/shard_map/dot_general | solution.py:54
  125.5 2.4 %fusion.33 = bf16[512,128]{1,0:T(8,128)(2,1)} fusion(bf16[1024,512]{1,0:T(8,128)(2,1)S(1)} %copy-done.2, bf16[256,512]{0,1:T(8,128)(2,1)} %get-tuple-element.39, bf16[256,512]{0,1:T(8,128)(2,1)} %get-tuple-element.40, f32[512]{0:T(512)} %get-tuple-element.70, bf16[9,128,256]{2,1,0:T(8,128)(2,1)} %param.6), kind=kOutput, calls=%fused_computation.59 | convolution fusion | flops 303366144 | bytes 1771520 | tf_op jit(solution)/shard_map/dot_general | solution.py:54
  129.3 1.8 fusion.34
  131.0 1.9 %convolution_add_fusion.4 = f32[128,384]{1,0:T(8,128)} fusion(f32[128,384]{1,0:T(8,128)S(1)} %convolution_add_fusion.5, bf16[512,128]{1,0:T(8,128)(2,1)S(1)} %fusion.34, bf16[9,512,384]{2,1,0:T(8,128)(2,1)} %param.7), kind=kOutput, calls=%fused_computation.53 | convolution fusion | flops 50380800 | bytes 917504 | tf_op jit(solution)/shard_map/dot_general | solution.py:55
  133.0 1.8 fusion.35
  136.1 2.4 %fusion.36 = bf16[512,128]{1,0:T(8,128)(2,1)} fusion(bf16[1024,512]{1,0:T(8,128)(2,1)S(1)} %copy-done.2, bf16[256,512]{0,1:T(8,128)(2,1)} %get-tuple-element.22, bf16[256,512]{0,1:T(8,128)(2,1)} %get-tuple-element.21, f32[512]{0:T(512)S(1)} %get-tuple-element.67, bf16[9,128,256]{2,1,0:T(8,128)(2,1)} %param.6), kind=kOutput, calls=%fused_computation.62 | convolution fusion | flops 303366144 | bytes 1771520 | tf_op jit(solution)/shard_map/dot_general | solution.py:54
  138.5 1.3 convolution_add_fusion.2
  139.8 1.8 fusion.37
  142.9 1.3 fusion.172
  144.2 38.1 %collective-permute-start.4 = (bf16[128,128]{1,0:T(8,128)(2,1)S(1)}, bf16[128,128]{1,0:T(8,128)(2,1)S(1)}, u32[]{:S(2)}, u32[]{:S(2)}) collective-permute-start(bf16[128,128]{1,0:T(8,128)(2,1)S(1)} %get-tuple-element.45), channel_id=1, source_target_pairs={{0,1},{1,2},{2,3},{3,4},{4,5},{5,6},{6,7},{7,8},{8,9},{9,10},{10,1... | collective-permute-start | bytes 98312 | tf_op jit(solution)/shard_map/ppermute | solution.py:15
  182.3 1.9 %collective-permute-start.5 = (bf16[128,128]{1,0:T(8,128)(2,1)S(1)}, bf16[128,128]{1,0:T(8,128)(2,1)S(1)}, u32[]{:S(2)}, u32[]{:S(2)}) collective-permute-start(bf16[128,128]{1,0:T(8,128)(2,1)S(1)} %get-tuple-element.46), channel_id=1, source_target_pairs={{1,0},{2,1},{3,2},{4,3},{5,4},{6,5},{7,6},{8,7},{9,8},{10,9},{11,1... | collective-permute-start | bytes 98312 | tf_op jit(solution)/shard_map/ppermute | solution.py:15
  184.3 3.3 %collective-permute-done.5 = bf16[128,128]{1,0:T(8,128)(2,1)S(1)} collective-permute-done((bf16[128,128]{1,0:T(8,128)(2,1)S(1)}, bf16[128,128]{1,0:T(8,128)(2,1)S(1)}, u32[]{:S(2)}, u32[]{:S(2)}) %collective-permute-start.5) | collective-permute-done | bytes 32800 | tf_op jit(solution)/shard_map/ppermute | solution.py:15
  (31 shorter events, 13.4 us)
Async XLA Ops:
  0.0 34.4 %copy-start = (bf16[256,4096]{1,0:T(8,128)(2,1)S(1)}, bf16[256,4096]{1,0:T(8,128)(2,1)}, u32[]{:S(2)}) copy-start(bf16[256,4096]{1,0:T(8,128)(2,1)} %param.5) | copy-start | bytes 6291460
  34.4 20.1 %copy-start.4 = (s32[1,8]{1,0:T(1,128)S(1)}, s32[1,8]{1,0:T(1,128)}, u32[]{:S(2)}) copy-start(s32[1,8]{1,0:T(1,128)} %param.8) | copy-start | bytes 100
  34.5 20.8 %copy-start.3 = (s32[1,8,4]{1,2,0:T(4,128)S(1)}, s32[1,8,4]{1,2,0:T(4,128)}, u32[]{:S(2)}) copy-start(s32[1,8,4]{1,2,0:T(4,128)} %param.9) | copy-start | bytes 388
  40.2 9.8 %collective-permute-start = (bf16[1,256,1024]{1,2,0:T(8,128)(2,1)S(1)}, bf16[1,256,1024]{1,2,0:T(8,128)(2,1)S(1)}, u32[]{:S(2)}, u32[]{:S(2)}) collective-permute-start(bf16[1,256,1024]{1,2,0:T(8,128)(2,1)S(1)} %bitcast.139), channel_id=1, source_target_pairs={{0,1},{1,2},{2,3},{3,4},{4,5},{5,6},{6,7},{7,8},{8,9},{9,10},{10,1... | collective-permute-start | bytes 1572872 | tf_op jit(solution)/shard_map/ppermute | solution.py:15
  50.1 25.4 %collective-permute-start.1 = (bf16[2,256,1024]{1,2,0:T(8,128)(2,1)S(1)}, bf16[2,256,1024]{1,2,0:T(8,128)(2,1)S(1)}, u32[]{:S(2)}, u32[]{:S(2)}) collective-permute-start(bf16[2,256,1024]{1,2,0:T(8,128)(2,1)S(1)} %pad_maximum_fusion.1), channel_id=1, source_target_pairs={{0,2},{1,3},{2,4},{3,5},{4,6},{5,7},{6,8},{7,9},{8,10},{9,11},{10,... | collective-permute-start | bytes 3145736 | tf_op jit(solution)/shard_map/ppermute | solution.py:15
  53.2 29.8 %collective-permute-start.3 = (bf16[1,256,1024]{1,2,0:T(8,128)(2,1)S(1)}, bf16[1,256,1024]{1,2,0:T(8,128)(2,1)S(1)}, u32[]{:S(2)}, u32[]{:S(2)}) collective-permute-start(bf16[1,256,1024]{1,2,0:T(8,128)(2,1)S(1)} %bitcast.141), channel_id=1, source_target_pairs={{0,8},{1,9},{2,10},{3,11},{4,12},{5,13},{6,14},{7,15},{16,24},{17,... | collective-permute-start | bytes 1572872 | tf_op jit(solution)/shard_map/ppermute | solution.py:15
  75.5 9.1 %copy-start.1 = (bf16[2,256,1024]{1,2,0:T(8,128)(2,1)}, bf16[2,256,1024]{1,2,0:T(8,128)(2,1)S(1)}, u32[]{:S(2)}) copy-start(bf16[2,256,1024]{1,2,0:T(8,128)(2,1)S(1)} %collective-permute-done.1) | copy-start | bytes 3145732
  77.1 32.9 %collective-permute-start.2 = (bf16[4,256,1024]{1,2,0:T(8,128)(2,1)}, bf16[4,256,1024]{1,2,0:T(8,128)(2,1)}, u32[]{:S(2)}, u32[]{:S(2)}) collective-permute-start(bf16[4,256,1024]{1,2,0:T(8,128)(2,1)} %pad_maximum_fusion), channel_id=1, source_target_pairs={{0,4},{1,5},{2,6},{3,7},{4,8},{5,9},{6,10},{7,11},{8,12},{9,13},{1... | collective-permute-start | bytes 6291464 | tf_op jit(solution)/shard_map/ppermute | solution.py:15
  116.4 5.3 %copy-start.2 = (bf16[1024,512]{1,0:T(8,128)(2,1)S(1)}, bf16[1024,512]{1,0:T(8,128)(2,1)}, u32[]{:S(2)}) copy-start(bf16[1024,512]{1,0:T(8,128)(2,1)} %fusion.10) | copy-start | bytes 3145732
  144.2 40.1 %collective-permute-start.4 = (bf16[128,128]{1,0:T(8,128)(2,1)S(1)}, bf16[128,128]{1,0:T(8,128)(2,1)S(1)}, u32[]{:S(2)}, u32[]{:S(2)}) collective-permute-start(bf16[128,128]{1,0:T(8,128)(2,1)S(1)} %get-tuple-element.45), channel_id=1, source_target_pairs={{0,1},{1,2},{2,3},{3,4},{4,5},{5,6},{6,7},{7,8},{8,9},{9,10},{10,1... | collective-permute-start | bytes 98312 | tf_op jit(solution)/shard_map/ppermute | solution.py:15
  182.3 5.2 %collective-permute-start.5 = (bf16[128,128]{1,0:T(8,128)(2,1)S(1)}, bf16[128,128]{1,0:T(8,128)(2,1)S(1)}, u32[]{:S(2)}, u32[]{:S(2)}) collective-permute-start(bf16[128,128]{1,0:T(8,128)(2,1)S(1)} %get-tuple-element.46), channel_id=1, source_target_pairs={{1,0},{2,1},{3,2},{4,3},{5,4},{6,5},{7,6},{8,7},{9,8},{10,9},{11,1... | collective-permute-start | bytes 98312 | tf_op jit(solution)/shard_map/ppermute | solution.py:15
where the time goes:
time: 189 us; the launch traced here: 188 us
  other arithmetic  56.8 us (30%)
  starting transfers between devices  51.4 us (27%)
  waiting for transfers between devices  39.1 us (21%)
  matrix products  38.4 us (20%)
  local copies, waits for them, and re-layouts  2.17 us (1%)
    ppermute x6, starting transfers between devices, shifted(): return lax.ppermute(shard, axis, pairs)  51.4 us
    ppermute x6, waiting for transfers between devices, shifted(): return lax.ppermute(shard, axis, pairs)  39.1 us
    cos x1, other arithmetic, make_tables(): jnp.cos(phase)  34.4 us
    dot_general x9, matrix products, pair_window(): jnp.dot(steering[dist], lags, preferred_element_type=jnp.float32)  20.3 us
    dot_general x9, matrix products, pair_window(): return jnp.dot(beams, lag_range[dist], preferred_element_type=jnp.float32)  12.3 us
    another operation x4, other arithmetic  5.88 us
    dot_general x1, matrix products, per_device(): jnp.dot(strain, forward, preferred_element_type=jnp.float32)  5.7 us
    convert_element_type x1, other arithmetic, pair_window(): weight = (listed * bands).astype(jnp.float32)  5.3 us
  transfers between devices with their start and end apart: 6, of which 4 were waited for; matrix products, arithmetic and copies ran while one was open for 12% of the time, Pallas kernels for 0%

commit v1 on v0

v1 whole, which is shorter than its diff:
```python
import functools

import jax
import jax.numpy as jnp
import numpy as np
from jax import lax
from jax.experimental import pallas as pl
from jax.experimental.pallas import tpu as pltpu
from jax.sharding import PartitionSpec as P

AXIS = "fib"
F = 512
L = 512
Q = 4


def forward_table(samples):
    freqs = F // Q
    t = np.arange(samples // Q, dtype=np.int64)[None, :, None]
    k = Q * np.arange(freqs, dtype=np.int64)[None, None, :] + np.arange(Q)[:, None, None] + 1
    phase = (t * k % samples) * (2.0 * np.pi / samples)
    table = np.concatenate([np.cos(phase), -np.sin(phase)], axis=2) * samples ** (-0.5)
    return table.astype(jnp.bfloat16)


def inverse_table(samples):
    freqs = F // Q
    k = Q * np.arange(freqs, dtype=np.int64)[None, :, None] + np.arange(Q)[:, None, None] + 1
    lag = np.arange(L, dtype=np.int64)[None, None, :] - L // 2
    theta = (k * lag % samples) * (2.0 * np.pi / samples)
    table = np.concatenate([np.cos(theta), -np.sin(theta)], axis=1) * (2 * F) ** (-0.5)
    return table.astype(jnp.bfloat16)


def dot(a, b):
    return jnp.dot(a, b, preferred_element_type=jnp.float32)


def spectrum_kernel(listed, bands, x0, x1, x2, x3, table, *refs):
    outs, acc = refs[:Q], refs[Q]
    step, steps = pl.program_id(0), pl.num_programs(0)
    half = table.shape[2] // 2
    channels = x0.shape[0]
    me = lax.rem(lax.axis_index(AXIS), Q)

    q0, q1, q2, q3 = (x[...].astype(jnp.float32) for x in (x0, x1, x2, x3))
    even, odd = q0 + q2, q1 + q3
    fold0 = (even + odd).astype(jnp.bfloat16)
    fold2 = (even - odd).astype(jnp.bfloat16)
    a = (q0 - q2).astype(jnp.bfloat16)
    b = (q1 - q3).astype(jnp.bfloat16)
    parts = [
        dot(a, table[0]),
        dot(b, table[0]),
        dot(fold2, table[1]),
        dot(a, table[2]),
        dot(b, table[2]),
        dot(fold0, table[3]),
    ]

    @pl.when(step == 0)
    def _():
        for n, part in enumerate(parts):
            acc[n] = part

    @pl.when((step > 0) & (step < steps - 1))
    def _():
        for n, part in enumerate(parts):
            acc[n] += part

    @pl.when(step == steps - 1)
    def _():
        p1, b1, s2, p3, b3, s0 = (acc[n] + part for n, part in enumerate(parts))
        s1 = jnp.concatenate([p1[:, :half] + b1[:, half:], p1[:, half:] - b1[:, :half]], axis=1)
        s3 = jnp.concatenate([p3[:, :half] - b3[:, half:], p3[:, half:] + b3[:, :half]], axis=1)
        for s, value in enumerate((s1, s2, s3, s0)):
            value = value.astype(jnp.bfloat16)
            for p in range(Q):

                @pl.when(lax.bitwise_xor(me, s) == p)
                def _():
                    outs[p][:channels, :] = value

        rows, cols = outs[0].shape[0] - channels, outs[0].shape[1]
        rounds, nbands = bands.shape[1], bands.shape[2]
        place = (
            lax.broadcasted_iota(jnp.int32, (rows, cols), 0) * cols
            + lax.broadcasted_iota(jnp.int32, (rows, cols), 1)
        ) // (L // nbands)
        weight = jnp.zeros((rows, cols), jnp.float32)
        for d in range(rounds):
            for j in range(nbands):
                value = (listed[0, d] * bands[0, d, j]).astype(jnp.float32)
                weight = jnp.where(place == d * nbands + j, value, weight)
        weight = weight.astype(jnp.bfloat16)
        for p in range(Q):
            outs[p][channels:, :] = weight


def spectrum_call(strain, listed, bands, steps=2):
    channels, samples = strain.shape
    table = forward_table(samples)
    cols = table.shape[2]
    depth = samples // Q // steps
    rows = channels + bands.shape[1] * L // cols
    quarter = [
        pl.BlockSpec((channels, depth), lambda k, q=q: (0, q * steps + k)) for q in range(Q)
    ]
    return pl.pallas_call(
        spectrum_kernel,
        grid=(steps,),
        in_specs=[
            pl.BlockSpec(memory_space=pltpu.SMEM),
            pl.BlockSpec(memory_space=pltpu.SMEM),
            *quarter,
            pl.BlockSpec((Q, depth, cols), lambda k: (0, k, 0)),
        ],
        out_specs=[pl.BlockSpec((rows, cols), lambda k: (0, 0))] * Q,
        out_shape=[jax.ShapeDtypeStruct((rows, cols), jnp.bfloat16)] * Q,
        scratch_shapes=[pltpu.VMEM((6, channels, cols), jnp.float32)],
        compiler_params=pltpu.CompilerParams(dimension_semantics=("arbitrary",)),
        name="spectrum",
    )(listed, bands, strain, strain, strain, strain, jnp.asarray(table))


def pair_kernel(*refs):
    spec_in = refs[: 3 * Q]
    inv_in, steering, lag_range = refs[3 * Q : 3 * Q + 3]
    own, *outs = refs[3 * Q + 3 : 3 * Q + 3 + Q]
    spec, inv, grouped, window, segs, sems, inv_sem = refs[3 * Q + 3 + Q :]
    me = lax.rem(lax.axis_index(AXIS), Q)
    copies = []
    for plane in range(3):
        for p in range(Q):
            copies.append(
                pltpu.make_async_copy(
                    spec_in[plane * Q + p],
                    spec.at[plane * Q + lax.bitwise_xor(me, p)],
                    sems.at[plane * Q + p],
                )
            )
    inv_copy = pltpu.make_async_copy(inv_in.at[me], inv, inv_sem)
    for copy in copies:
        copy.start()
    inv_copy.start()
    for copy in copies:
        copy.wait()
    inv_copy.wait()

    rounds = steering.shape[0] - 1
    angles, channels = steering.shape[1], steering.shape[2]
    cols = spec.shape[2]
    half = cols // 2
    per = L // cols
    first = {}
    for d in range(rounds + 1):
        units = []
        for i in range(2 * Q):
            j = i - d
            if i < Q and -Q <= j:
                units.append((i, i, j if j >= 0 else 2 * Q + j))
            elif i >= Q and -Q <= j < 0:
                units.append((i, Q + i, 2 * Q + j))
        for n, (_, target, source) in enumerate(units):
            near_re = spec[target, :channels, :half].astype(jnp.float32)
            near_im = spec[target, :channels, half:].astype(jnp.float32)
            far_re = spec[source, :channels, :half].astype(jnp.float32)
            far_im = spec[source, :channels, half:].astype(jnp.float32)
            real = near_re * far_re + near_im * far_im
            imag = near_im * far_re - near_re * far_im
            cross = jnp.concatenate([real, imag], axis=1).astype(jnp.bfloat16)
            grouped[n * angles : (n + 1) * angles, :] = dot(steering[d], cross).astype(
                jnp.bfloat16
            )
        count = len(units)
        beams = dot(grouped[: count * angles, :], inv[...])
        if d > 0:
            masked = []
            for n, (_, target, _) in enumerate(units):
                row = channels + (d - 1) * per
                weight = jnp.concatenate(
                    [spec[target, row + h : row + h + 1, :] for h in range(per)], axis=1
                ).astype(jnp.float32)
                masked.append(beams[n * angles : (n + 1) * angles, :] * weight)
            beams = jnp.concatenate(masked, axis=0)
        part = dot(beams.astype(jnp.bfloat16), lag_range[d])
        for n, (slot, _, _) in enumerate(units):
            value = part[n * angles : (n + 1) * angles, :]
            if slot in first:
                window[slot] += value
            else:
                window[slot] = value
                first[slot] = True

    width = window.shape[2] // 3

    def third(slot, part):
        return window[slot, :, part * width : (part + 1) * width]

    def segment(s):
        total = None
        for slot, part in ((s, 1), (s - 1, 2), (s + 1, 0)):
            if 0 <= slot < 2 * Q:
                value = third(slot, part)
                total = value if total is None else total + value
        return total

    for p in range(Q):
        segs[p, 0] = segment(p)
        segs[p, 1] = segment(Q + p)
        if p == 0:
            segs[p, 2] = segment(2 * Q)
        elif p == Q - 1:
            segs[p, 2] = segment(-1)
        else:
            segs[p, 2] = jnp.zeros((angles, width), jnp.float32)
    own[...] = segs[me]
    for p in range(1, Q):
        outs[p - 1][...] = segs[lax.bitwise_xor(me, p)].astype(jnp.bfloat16)


def pair_call(spectra, samples, steering, lag_range):
    rows, cols = spectra[0].shape
    angles = steering.shape[1]
    width = lag_range.shape[2] // 3
    inv = inverse_table(samples)
    hbm = pl.BlockSpec(memory_space=pl.ANY)
    vmem = pl.BlockSpec(memory_space=pltpu.VMEM)
    return pl.pallas_call(
        pair_kernel,
        in_specs=[hbm] * (3 * Q + 1) + [vmem, vmem],
        out_specs=[vmem] * Q,
        out_shape=[jax.ShapeDtypeStruct((3, angles, width), jnp.float32)]
        + [jax.ShapeDtypeStruct((3, angles, width), jnp.bfloat16)] * (Q - 1),
        scratch_shapes=[
            pltpu.VMEM((3 * Q, rows, cols), jnp.bfloat16),
            pltpu.VMEM((cols, L), jnp.bfloat16),
            pltpu.VMEM((Q * angles, cols), jnp.bfloat16),
            pltpu.VMEM((2 * Q, angles, 3 * width), jnp.float32),
            pltpu.VMEM((Q, 3, angles, width), jnp.float32),
            pltpu.SemaphoreType.DMA((3 * Q,)),
            pltpu.SemaphoreType.DMA(()),
        ],
        name="pairs",
    )(*spectra, jnp.asarray(inv), steering, lag_range)


def exchange(value, devices, target):
    pairs = [(i, target(i)) for i in range(devices) if target(i) is not None]
    pairs = [(i, j) for i, j in pairs if 0 <= j < devices]
    return lax.ppermute(value, AXIS, pairs)


def per_device(devices, strain, steering, lag_range, pair_listed, band_used):
    slices = spectrum_call(strain, pair_listed, band_used)
    own = [slices[0]] + [
        exchange(slices[p], devices, lambda i: i ^ p) for p in range(1, Q)
    ]
    below = [exchange(slices[p], devices, lambda i: (i ^ p) + Q) for p in range(Q)]
    above = [exchange(slices[p], devices, lambda i: (i ^ p) - Q) for p in range(Q)]
    mine, *sends = pair_call(own + below + above, strain.shape[1], steering, lag_range)
    for p in range(1, Q):
        mine = mine + exchange(sends[p - 1], devices, lambda i: i ^ p).astype(jnp.float32)
    up = exchange(mine[1].astype(jnp.bfloat16), devices, lambda i: i + Q)

    def ends(i):
        if i % Q == 0:
            return i + 2 * Q
        if i % Q == Q - 1:
            return i - Q
        return None

    extra = exchange(mine[2].astype(jnp.bfloat16), devices, ends)
    return mine[0] + up.astype(jnp.float32) + extra.astype(jnp.float32)


def solution(mesh):
    return jax.shard_map(
        functools.partial(per_device, mesh.shape[AXIS]),
        mesh=mesh,
        in_specs=(
            P(("win", AXIS), None),
            P(),
            P(),
            P(("win", AXIS), None),
            P(("win", AXIS), None, None),
        ),
        out_specs=P(None, ("win", AXIS)),
        check_vma=False,
    )
```

time: 189 us -> 70 us (0.37)
  the two profiles are of different devices: /device:TPU:17 before, /device:TPU:0 now
where the time goes in v1:
time: 70 us; the launch traced here: 69.6 us
  starting transfers between devices  39.2 us (56%)
  Pallas kernels  13.9 us (20%)
  waiting for transfers between devices  12.6 us (18%)
  local copies, waits for them, and re-layouts  2.03 us (3%)
  other arithmetic  1.62 us (2%)
    ppermute x16, starting transfers between devices, exchange(): return lax.ppermute(value, AXIS, pairs)  39.2 us
    ppermute x16, waiting for transfers between devices, exchange(): return lax.ppermute(value, AXIS, pairs)  12.6 us
    pallas_call x1, Pallas kernels, pair_call(): pl.pallas_call(pair_kernel, in_specs=[hbm] * (3 * Q + 1) + [vmem, vmem],...  9.83 us
    pallas_call x1, Pallas kernels, spectrum_call(): pl.pallas_call(spectrum_kernel, grid=(steps,), in_specs=[pl.BlockSpec(mem...  4.05 us
    unnamed x23, local copies, waits for them, and re-layouts  2.03 us
  transfers between devices with their start and end apart: 16, of which 6 were waited for; matrix products, arithmetic and copies ran while one was open for 0% of the time, Pallas kernels for 0%

profile of v1, /device:TPU:0, one launch (start us, length us, event | category | flops | bytes accessed | tf_op | source)
XLA Modules:
  0.0 69.6 jit_solution(801268706848502860)
XLA Ops:
  0.0 1.3 %copy.8.bands = s32[1,8,4]{2,1,0:T(8,128)} copy(s32[1,8,4]{1,2,0:T(4,128)} %param.11) | data formatting | bytes 256 | tf_op args[4]
  1.3 4.1 %spectrum.1 = (bf16[272,256]{1,0:T(8,128)(2,1)}, bf16[272,256]{1,0:T(8,128)(2,1)}, bf16[272,256]{1,0:T(8,128)(2,1)}, bf16[272,256]{1,0:T(8,128)(2,1)}) custom-call(s32[1,8]{1,0:T(1,128)} %listed.1, s32[1,8,4]{2,1,0:T(8,128)} %copy.8.bands, bf16[256,4096]{1,0:T(8,128)(2,1)} %x3.1, bf16[256,4096]{1,0:T(8,128)(2,1)} %x3.1, bf16[256,4096]{1,0:T(8,128)(2,1)} %x3.1, ...), custom_call_target="tpu_custom_call" | custom-call | tf_op jit(solution)/shard_map/spectrum/pallas_call | solution.py:109
  5.4 1.3 %collective-permute-start.7 = (bf16[272,256]{1,0:T(8,128)(2,1)}, bf16[272,256]{1,0:T(8,128)(2,1)S(1)}, u32[]{:S(2)}, u32[]{:S(2)}) collective-permute-start(bf16[272,256]{1,0:T(8,128)(2,1)} %get-tuple-element.13.refs_0_), channel_id=1, source_target_pairs={{4,0},{5,1},{6,2},{7,3},{8,4},{9,5},{10,6},{11,7},{12,8},{13,9},{1... | collective-permute-start | bytes 417800 | tf_op jit(solution)/shard_map/ppermute | solution.py:251
  6.7 5.6 %collective-permute-start.3 = (bf16[272,256]{1,0:T(8,128)(2,1)}, bf16[272,256]{1,0:T(8,128)(2,1)S(1)}, u32[]{:S(2)}, u32[]{:S(2)}) collective-permute-start(bf16[272,256]{1,0:T(8,128)(2,1)} %get-tuple-element.13.refs_0_), channel_id=1, source_target_pairs={{0,4},{1,5},{2,6},{3,7},{4,8},{5,9},{6,10},{7,11},{8,12},{9,13},{1... | collective-permute-start | bytes 417800 | tf_op jit(solution)/shard_map/ppermute | solution.py:251
  12.3 1.3 %collective-permute-start.8 = (bf16[272,256]{1,0:T(8,128)(2,1)}, bf16[272,256]{1,0:T(8,128)(2,1)S(1)}, u32[]{:S(2)}, u32[]{:S(2)}) collective-permute-start(bf16[272,256]{1,0:T(8,128)(2,1)} %get-tuple-element.14), channel_id=1, source_target_pairs={{4,1},{5,0},{6,3},{7,2},{8,5},{9,4},{10,7},{11,6},{12,9},{13,8},{1... | collective-permute-start | bytes 417800 | tf_op jit(solution)/shard_map/ppermute | solution.py:251
  13.6 4.3 %collective-permute-start.4 = (bf16[272,256]{1,0:T(8,128)(2,1)}, bf16[272,256]{1,0:T(8,128)(2,1)S(1)}, u32[]{:S(2)}, u32[]{:S(2)}) collective-permute-start(bf16[272,256]{1,0:T(8,128)(2,1)} %get-tuple-element.14), channel_id=1, source_target_pairs={{0,5},{1,4},{2,7},{3,6},{4,9},{5,8},{6,11},{7,10},{8,13},{9,12},{1... | collective-permute-start | bytes 417800 | tf_op jit(solution)/shard_map/ppermute | solution.py:251
  17.9 0.5 collective-permute-start
  18.3 1.3 %collective-permute-start.9 = (bf16[272,256]{1,0:T(8,128)(2,1)}, bf16[272,256]{1,0:T(8,128)(2,1)S(1)}, u32[]{:S(2)}, u32[]{:S(2)}) collective-permute-start(bf16[272,256]{1,0:T(8,128)(2,1)} %get-tuple-element.15), channel_id=1, source_target_pairs={{4,2},{5,3},{6,0},{7,1},{8,6},{9,7},{10,4},{11,5},{12,10},{13,11},... | collective-permute-start | bytes 417800 | tf_op jit(solution)/shard_map/ppermute | solution.py:251
  19.6 0.0 collective-permute-done.3.refs_4_
  19.6 5.5 %collective-permute-start.5 = (bf16[272,256]{1,0:T(8,128)(2,1)}, bf16[272,256]{1,0:T(8,128)(2,1)S(1)}, u32[]{:S(2)}, u32[]{:S(2)}) collective-permute-start(bf16[272,256]{1,0:T(8,128)(2,1)} %get-tuple-element.15), channel_id=1, source_target_pairs={{0,6},{1,7},{2,4},{3,5},{4,10},{5,11},{6,8},{7,9},{8,14},{9,15},{1... | collective-permute-start | bytes 417800 | tf_op jit(solution)/shard_map/ppermute | solution.py:251
  25.1 1.7 %collective-permute-start.1 = (bf16[272,256]{1,0:T(8,128)(2,1)}, bf16[272,256]{1,0:T(8,128)(2,1)S(1)}, u32[]{:S(2)}, u32[]{:S(2)}) collective-permute-start(bf16[272,256]{1,0:T(8,128)(2,1)} %get-tuple-element.15), channel_id=1, source_target_pairs={{0,2},{1,3},{2,0},{3,1},{4,6},{5,7},{6,4},{7,5},{8,10},{9,11},{10,... | collective-permute-start | bytes 417800 | tf_op jit(solution)/shard_map/ppermute | solution.py:251
  26.8 1.3 %collective-permute-start.10 = (bf16[272,256]{1,0:T(8,128)(2,1)}, bf16[272,256]{1,0:T(8,128)(2,1)S(1)}, u32[]{:S(2)}, u32[]{:S(2)}) collective-permute-start(bf16[272,256]{1,0:T(8,128)(2,1)} %get-tuple-element.16), channel_id=1, source_target_pairs={{4,3},{5,2},{6,1},{7,0},{8,7},{9,6},{10,5},{11,4},{12,11},{13,10},... | collective-permute-start | bytes 417800 | tf_op jit(solution)/shard_map/ppermute | solution.py:251
  28.1 0.0 collective-permute-done.refs_1_
  28.1 5.2 %collective-permute-start.6 = (bf16[272,256]{1,0:T(8,128)(2,1)}, bf16[272,256]{1,0:T(8,128)(2,1)S(1)}, u32[]{:S(2)}, u32[]{:S(2)}) collective-permute-start(bf16[272,256]{1,0:T(8,128)(2,1)} %get-tuple-element.16), channel_id=1, source_target_pairs={{0,7},{1,6},{2,5},{3,4},{4,11},{5,10},{6,9},{7,8},{8,15},{9,14},{1... | collective-permute-start | bytes 417800 | tf_op jit(solution)/shard_map/ppermute | solution.py:251
  33.3 0.0 collective-permute-done.9.refs_10_
  33.3 0.2 collective-permute-start.2
  33.5 0.0 collective-permute-done.5.refs_6_
  33.5 2.1 %collective-permute-done.10.refs_11_ = bf16[272,256]{1,0:T(8,128)(2,1)S(1)} collective-permute-done((bf16[272,256]{1,0:T(8,128)(2,1)}, bf16[272,256]{1,0:T(8,128)(2,1)S(1)}, u32[]{:S(2)}, u32[]{:S(2)}) %collective-permute-start.10) | collective-permute-done | bytes 139296 | tf_op jit(solution)/shard_map/ppermute | solution.py:251
  35.6 1.4 %collective-permute-done.6.refs_7_ = bf16[272,256]{1,0:T(8,128)(2,1)S(1)} collective-permute-done((bf16[272,256]{1,0:T(8,128)(2,1)}, bf16[272,256]{1,0:T(8,128)(2,1)S(1)}, u32[]{:S(2)}, u32[]{:S(2)}) %collective-permute-start.6) | collective-permute-done | bytes 139296 | tf_op jit(solution)/shard_map/ppermute | solution.py:251
  37.0 2.3 %collective-permute-done.2.refs_3_ = bf16[272,256]{1,0:T(8,128)(2,1)S(1)} collective-permute-done((bf16[272,256]{1,0:T(8,128)(2,1)}, bf16[272,256]{1,0:T(8,128)(2,1)S(1)}, u32[]{:S(2)}, u32[]{:S(2)}) %collective-permute-start.2) | collective-permute-done | bytes 139296 | tf_op jit(solution)/shard_map/ppermute | solution.py:251
  39.5 0.6 copy-done.10
  40.1 9.8 %pairs.1 = (f32[3,128,128]{2,1,0:T(8,128)}, bf16[3,128,128]{2,1,0:T(8,128)(2,1)}, bf16[3,128,128]{2,1,0:T(8,128)(2,1)}, bf16[3,128,128]{2,1,0:T(8,128)(2,1)}) custom-call(bf16[272,256]{1,0:T(8,128)(2,1)} %get-tuple-element.13.refs_0_, bf16[272,256]{1,0:T(8,128)(2,1)} %copy-done.4, bf16[272,256]{1,0:T(8,128)(2,1)} %copy-done.7, bf16[272,256]{1,0:T(8,128)(2,1)} %copy-done.10, ...), custom_call_target="tpu_custom_call" | custom-call | tf_op jit(solution)/shard_map/pairs/pallas_call | solution.py:229
  49.9 0.1 collective-permute-start.11
  50.0 0.5 collective-permute-start.12
  50.5 1.4 %collective-permute-start.13 = (bf16[3,128,128]{2,1,0:T(8,128)(2,1)}, bf16[3,128,128]{2,1,0:T(8,128)(2,1)S(1)}, u32[]{:S(2)}, u32[]{:S(2)}) collective-permute-start(bf16[3,128,128]{2,1,0:T(8,128)(2,1)} %get-tuple-element.20), channel_id=1, source_target_pairs={{0,3},{1,2},{2,1},{3,0},{4,7},{5,6},{6,5},{7,4},{8,11},{9,10},{10,... | collective-permute-start | bytes 294920 | tf_op jit(solution)/shard_map/ppermute | solution.py:251
  51.9 4.1 %collective-permute-done.12 = bf16[3,128,128]{2,1,0:T(8,128)(2,1)S(1)} collective-permute-done((bf16[3,128,128]{2,1,0:T(8,128)(2,1)}, bf16[3,128,128]{2,1,0:T(8,128)(2,1)S(1)}, u32[]{:S(2)}, u32[]{:S(2)}) %collective-permute-start.12) | collective-permute-done | bytes 98336 | tf_op jit(solution)/shard_map/ppermute | solution.py:251
  56.0 1.0 %collective-permute-done.13 = bf16[3,128,128]{2,1,0:T(8,128)(2,1)S(1)} collective-permute-done((bf16[3,128,128]{2,1,0:T(8,128)(2,1)}, bf16[3,128,128]{2,1,0:T(8,128)(2,1)S(1)}, u32[]{:S(2)}, u32[]{:S(2)}) %collective-permute-start.13) | collective-permute-done | bytes 98336 | tf_op jit(solution)/shard_map/ppermute | solution.py:251
  57.0 1.0 %fusion.2 = (bf16[3,128,128]{2,1,0:T(8,128)(2,1)S(1)}, f32[3,128,128]{2,1,0:T(8,128)S(1)}) fusion(bf16[3,128,128]{2,1,0:T(8,128)(2,1)S(1)} %collective-permute-done.13, bf16[3,128,128]{2,1,0:T(8,128)(2,1)S(1)} %collective-permute-done.12, f32[3,128,128]{2,1,0:T(8,128)} %get-tuple-element.17, bf16[3,128,128]{2,1,0:T(8,128)(2,1)S(1)} %collective-permute-done.11), kind=kLoop, calls=%fused_computation.6 | loop fusion | flops 344064 | bytes 786432 | tf_op jit(solution)/shard_map/convert.1
  58.0 6.5 %collective-permute-start.14 = (bf16[128,128]{1,0:T(8,128)(2,1)S(1)}, bf16[128,128]{1,0:T(8,128)(2,1)S(1)}, u32[]{:S(2)}, u32[]{:S(2)}) collective-permute-start(bf16[128,128]{1,0:T(8,128)(2,1)S(1)} %get-tuple-element.23), channel_id=1, source_target_pairs={{0,4},{1,5},{2,6},{3,7},{4,8},{5,9},{6,10},{7,11},{8,12},{9,13},{1... | collective-permute-start | bytes 98312 | tf_op jit(solution)/shard_map/ppermute | solution.py:251
  64.4 2.9 %collective-permute-start.15 = (bf16[128,128]{1,0:T(8,128)(2,1)S(1)}, bf16[128,128]{1,0:T(8,128)(2,1)S(1)}, u32[]{:S(2)}, u32[]{:S(2)}) collective-permute-start(bf16[128,128]{1,0:T(8,128)(2,1)S(1)} %get-tuple-element.24), channel_id=1, source_target_pairs={{0,8},{4,12},{7,3},{11,7},{15,11},{16,24},{20,28},{23,19},{27,23},... | collective-permute-start | bytes 98312 | tf_op jit(solution)/shard_map/ppermute | solution.py:251
  67.4 1.6 %collective-permute-done.15 = bf16[128,128]{1,0:T(8,128)(2,1)S(1)} collective-permute-done((bf16[128,128]{1,0:T(8,128)(2,1)S(1)}, bf16[128,128]{1,0:T(8,128)(2,1)S(1)}, u32[]{:S(2)}, u32[]{:S(2)}) %collective-permute-start.15) | collective-permute-done | bytes 32800 | tf_op jit(solution)/shard_map/ppermute | solution.py:251
  69.0 0.6 fusion.1
  (28 shorter events, 0.1 us)
Async XLA Ops:
  5.4 12.9 %collective-permute-start.7 = (bf16[272,256]{1,0:T(8,128)(2,1)}, bf16[272,256]{1,0:T(8,128)(2,1)S(1)}, u32[]{:S(2)}, u32[]{:S(2)}) collective-permute-start(bf16[272,256]{1,0:T(8,128)(2,1)} %get-tuple-element.13.refs_0_), channel_id=1, source_target_pairs={{4,0},{5,1},{6,2},{7,3},{8,4},{9,5},{10,6},{11,7},{12,8},{13,9},{1... | collective-permute-start | bytes 417800 | tf_op jit(solution)/shard_map/ppermute | solution.py:251
  6.7 12.9 %collective-permute-start.3 = (bf16[272,256]{1,0:T(8,128)(2,1)}, bf16[272,256]{1,0:T(8,128)(2,1)S(1)}, u32[]{:S(2)}, u32[]{:S(2)}) collective-permute-start(bf16[272,256]{1,0:T(8,128)(2,1)} %get-tuple-element.13.refs_0_), channel_id=1, source_target_pairs={{0,4},{1,5},{2,6},{3,7},{4,8},{5,9},{6,10},{7,11},{8,12},{9,13},{1... | collective-permute-start | bytes 417800 | tf_op jit(solution)/shard_map/ppermute | solution.py:251
  12.3 12.8 %collective-permute-start.8 = (bf16[272,256]{1,0:T(8,128)(2,1)}, bf16[272,256]{1,0:T(8,128)(2,1)S(1)}, u32[]{:S(2)}, u32[]{:S(2)}) collective-permute-start(bf16[272,256]{1,0:T(8,128)(2,1)} %get-tuple-element.14), channel_id=1, source_target_pairs={{4,1},{5,0},{6,3},{7,2},{8,5},{9,4},{10,7},{11,6},{12,9},{13,8},{1... | collective-permute-start | bytes 417800 | tf_op jit(solution)/shard_map/ppermute | solution.py:251
  13.6 13.2 %collective-permute-start.4 = (bf16[272,256]{1,0:T(8,128)(2,1)}, bf16[272,256]{1,0:T(8,128)(2,1)S(1)}, u32[]{:S(2)}, u32[]{:S(2)}) collective-permute-start(bf16[272,256]{1,0:T(8,128)(2,1)} %get-tuple-element.14), channel_id=1, source_target_pairs={{0,5},{1,4},{2,7},{3,6},{4,9},{5,8},{6,11},{7,10},{8,13},{9,12},{1... | collective-permute-start | bytes 417800 | tf_op jit(solution)/shard_map/ppermute | solution.py:251
  17.9 10.2 %collective-permute-start = (bf16[272,256]{1,0:T(8,128)(2,1)}, bf16[272,256]{1,0:T(8,128)(2,1)S(1)}, u32[]{:S(2)}, u32[]{:S(2)}) collective-permute-start(bf16[272,256]{1,0:T(8,128)(2,1)} %get-tuple-element.14), channel_id=1, source_target_pairs={{0,1},{1,0},{2,3},{3,2},{4,5},{5,4},{6,7},{7,6},{8,9},{9,8},{10,11... | collective-permute-start | bytes 417800 | tf_op jit(solution)/shard_map/ppermute | solution.py:251
  18.3 21.0 %copy-start = (bf16[272,256]{1,0:T(8,128)(2,1)}, bf16[272,256]{1,0:T(8,128)(2,1)S(1)}, u32[]{:S(2)}) copy-start(bf16[272,256]{1,0:T(8,128)(2,1)S(1)} %collective-permute-done.7.refs_8_) | copy-start | bytes 417796
  18.3 15.0 %collective-permute-start.9 = (bf16[272,256]{1,0:T(8,128)(2,1)}, bf16[272,256]{1,0:T(8,128)(2,1)S(1)}, u32[]{:S(2)}, u32[]{:S(2)}) collective-permute-start(bf16[272,256]{1,0:T(8,128)(2,1)} %get-tuple-element.15), channel_id=1, source_target_pairs={{4,2},{5,3},{6,0},{7,1},{8,6},{9,7},{10,4},{11,5},{12,10},{13,11},... | collective-permute-start | bytes 417800 | tf_op jit(solution)/shard_map/ppermute | solution.py:251
  19.6 19.7 %copy-start.1 = (bf16[272,256]{1,0:T(8,128)(2,1)}, bf16[272,256]{1,0:T(8,128)(2,1)S(1)}, u32[]{:S(2)}) copy-start(bf16[272,256]{1,0:T(8,128)(2,1)S(1)} %collective-permute-done.3.refs_4_) | copy-start | bytes 417796
  19.6 13.8 %collective-permute-start.5 = (bf16[272,256]{1,0:T(8,128)(2,1)}, bf16[272,256]{1,0:T(8,128)(2,1)S(1)}, u32[]{:S(2)}, u32[]{:S(2)}) collective-permute-start(bf16[272,256]{1,0:T(8,128)(2,1)} %get-tuple-element.15), channel_id=1, source_target_pairs={{0,6},{1,7},{2,4},{3,5},{4,10},{5,11},{6,8},{7,9},{8,14},{9,15},{1... | collective-permute-start | bytes 417800 | tf_op jit(solution)/shard_map/ppermute | solution.py:251
  25.1 14.3 %copy-start.2 = (bf16[272,256]{1,0:T(8,128)(2,1)}, bf16[272,256]{1,0:T(8,128)(2,1)S(1)}, u32[]{:S(2)}) copy-start(bf16[272,256]{1,0:T(8,128)(2,1)S(1)} %collective-permute-done.8.refs_9_) | copy-start | bytes 417796
  25.1 8.4 %collective-permute-start.1 = (bf16[272,256]{1,0:T(8,128)(2,1)}, bf16[272,256]{1,0:T(8,128)(2,1)S(1)}, u32[]{:S(2)}, u32[]{:S(2)}) collective-permute-start(bf16[272,256]{1,0:T(8,128)(2,1)} %get-tuple-element.15), channel_id=1, source_target_pairs={{0,2},{1,3},{2,0},{3,1},{4,6},{5,7},{6,4},{7,5},{8,10},{9,11},{10,... | collective-permute-start | bytes 417800 | tf_op jit(solution)/shard_map/ppermute | solution.py:251
  26.8 12.6 %copy-start.3 = (bf16[272,256]{1,0:T(8,128)(2,1)}, bf16[272,256]{1,0:T(8,128)(2,1)S(1)}, u32[]{:S(2)}) copy-start(bf16[272,256]{1,0:T(8,128)(2,1)S(1)} %collective-permute-done.4.refs_5_) | copy-start | bytes 417796
  26.8 8.8 %collective-permute-start.10 = (bf16[272,256]{1,0:T(8,128)(2,1)}, bf16[272,256]{1,0:T(8,128)(2,1)S(1)}, u32[]{:S(2)}, u32[]{:S(2)}) collective-permute-start(bf16[272,256]{1,0:T(8,128)(2,1)} %get-tuple-element.16), channel_id=1, source_target_pairs={{4,3},{5,2},{6,1},{7,0},{8,7},{9,6},{10,5},{11,4},{12,11},{13,10},... | collective-permute-start | bytes 417800 | tf_op jit(solution)/shard_map/ppermute | solution.py:251
  28.1 11.3 %copy-start.4 = (bf16[272,256]{1,0:T(8,128)(2,1)}, bf16[272,256]{1,0:T(8,128)(2,1)S(1)}, u32[]{:S(2)}) copy-start(bf16[272,256]{1,0:T(8,128)(2,1)S(1)} %collective-permute-done.refs_1_) | copy-start | bytes 417796
  28.1 8.9 %collective-permute-start.6 = (bf16[272,256]{1,0:T(8,128)(2,1)}, bf16[272,256]{1,0:T(8,128)(2,1)S(1)}, u32[]{:S(2)}, u32[]{:S(2)}) collective-permute-start(bf16[272,256]{1,0:T(8,128)(2,1)} %get-tuple-element.16), channel_id=1, source_target_pairs={{0,7},{1,6},{2,5},{3,4},{4,11},{5,10},{6,9},{7,8},{8,15},{9,14},{1... | collective-permute-start | bytes 417800 | tf_op jit(solution)/shard_map/ppermute | solution.py:251
  33.3 6.1 %copy-start.5 = (bf16[272,256]{1,0:T(8,128)(2,1)}, bf16[272,256]{1,0:T(8,128)(2,1)S(1)}, u32[]{:S(2)}) copy-start(bf16[272,256]{1,0:T(8,128)(2,1)S(1)} %collective-permute-done.9.refs_10_) | copy-start | bytes 417796
  33.3 6.1 %collective-permute-start.2 = (bf16[272,256]{1,0:T(8,128)(2,1)}, bf16[272,256]{1,0:T(8,128)(2,1)S(1)}, u32[]{:S(2)}, u32[]{:S(2)}) collective-permute-start(bf16[272,256]{1,0:T(8,128)(2,1)} %get-tuple-element.16), channel_id=1, source_target_pairs={{0,3},{1,2},{2,1},{3,0},{4,7},{5,6},{6,5},{7,4},{8,11},{9,10},{10,... | collective-permute-start | bytes 417800 | tf_op jit(solution)/shard_map/ppermute | solution.py:251
  33.5 5.9 %copy-start.6 = (bf16[272,256]{1,0:T(8,128)(2,1)}, bf16[272,256]{1,0:T(8,128)(2,1)S(1)}, u32[]{:S(2)}) copy-start(bf16[272,256]{1,0:T(8,128)(2,1)S(1)} %collective-permute-done.5.refs_6_) | copy-start | bytes 417796
  33.5 5.9 %copy-start.7 = (bf16[272,256]{1,0:T(8,128)(2,1)}, bf16[272,256]{1,0:T(8,128)(2,1)S(1)}, u32[]{:S(2)}) copy-start(bf16[272,256]{1,0:T(8,128)(2,1)S(1)} %collective-permute-done.1.refs_2_) | copy-start | bytes 417796
  35.6 3.9 %copy-start.8 = (bf16[272,256]{1,0:T(8,128)(2,1)}, bf16[272,256]{1,0:T(8,128)(2,1)S(1)}, u32[]{:S(2)}) copy-start(bf16[272,256]{1,0:T(8,128)(2,1)S(1)} %collective-permute-done.10.refs_11_) | copy-start | bytes 417796
  37.0 2.4 %copy-start.9 = (bf16[272,256]{1,0:T(8,128)(2,1)}, bf16[272,256]{1,0:T(8,128)(2,1)S(1)}, u32[]{:S(2)}) copy-start(bf16[272,256]{1,0:T(8,128)(2,1)S(1)} %collective-permute-done.6.refs_7_) | copy-start | bytes 417796
  39.4 0.6 copy-start.10
  49.9 1.9 %collective-permute-start.11 = (bf16[3,128,128]{2,1,0:T(8,128)(2,1)}, bf16[3,128,128]{2,1,0:T(8,128)(2,1)S(1)}, u32[]{:S(2)}, u32[]{:S(2)}) collective-permute-start(bf16[3,128,128]{2,1,0:T(8,128)(2,1)} %get-tuple-element.18), channel_id=1, source_target_pairs={{0,1},{1,0},{2,3},{3,2},{4,5},{5,4},{6,7},{7,6},{8,9},{9,8},{10,11... | collective-permute-start | bytes 294920 | tf_op jit(solution)/shard_map/ppermute | solution.py:251
  50.0 5.9 %collective-permute-start.12 = (bf16[3,128,128]{2,1,0:T(8,128)(2,1)}, bf16[3,128,128]{2,1,0:T(8,128)(2,1)S(1)}, u32[]{:S(2)}, u32[]{:S(2)}) collective-permute-start(bf16[3,128,128]{2,1,0:T(8,128)(2,1)} %get-tuple-element.19), channel_id=1, source_target_pairs={{0,2},{1,3},{2,0},{3,1},{4,6},{5,7},{6,4},{7,5},{8,10},{9,11},{10,... | collective-permute-start | bytes 294920 | tf_op jit(solution)/shard_map/ppermute | solution.py:251
  50.5 6.5 %collective-permute-start.13 = (bf16[3,128,128]{2,1,0:T(8,128)(2,1)}, bf16[3,128,128]{2,1,0:T(8,128)(2,1)S(1)}, u32[]{:S(2)}, u32[]{:S(2)}) collective-permute-start(bf16[3,128,128]{2,1,0:T(8,128)(2,1)} %get-tuple-element.20), channel_id=1, source_target_pairs={{0,3},{1,2},{2,1},{3,0},{4,7},{5,6},{6,5},{7,4},{8,11},{9,10},{10,... | collective-permute-start | bytes 294920 | tf_op jit(solution)/shard_map/ppermute | solution.py:251
  58.0 9.4 %collective-permute-start.14 = (bf16[128,128]{1,0:T(8,128)(2,1)S(1)}, bf16[128,128]{1,0:T(8,128)(2,1)S(1)}, u32[]{:S(2)}, u32[]{:S(2)}) collective-permute-start(bf16[128,128]{1,0:T(8,128)(2,1)S(1)} %get-tuple-element.23), channel_id=1, source_target_pairs={{0,4},{1,5},{2,6},{3,7},{4,8},{5,9},{6,10},{7,11},{8,12},{9,13},{1... | collective-permute-start | bytes 98312 | tf_op jit(solution)/shard_map/ppermute | solution.py:251
  64.4 4.5 %collective-permute-start.15 = (bf16[128,128]{1,0:T(8,128)(2,1)S(1)}, bf16[128,128]{1,0:T(8,128)(2,1)S(1)}, u32[]{:S(2)}, u32[]{:S(2)}) collective-permute-start(bf16[128,128]{1,0:T(8,128)(2,1)S(1)} %get-tuple-element.24), channel_id=1, source_target_pairs={{0,8},{4,12},{7,3},{11,7},{15,11},{16,24},{20,28},{23,19},{27,23},... | collective-permute-start | bytes 98312 | tf_op jit(solution)/shard_map/ppermute | solution.py:251

commit v2 on v1

--- a/solution.py
+++ b/solution.py
@@ -36,8 +36,7 @@
     return jnp.dot(a, b, preferred_element_type=jnp.float32)
 
 
-def spectrum_kernel(listed, bands, x0, x1, x2, x3, table, *refs):
-    outs, acc = refs[:Q], refs[Q]
+def spectrum_kernel(listed, bands, x0, x1, x2, x3, table, keep, mate, swap, acc, weight):
     step, steps = pl.program_id(0), pl.num_programs(0)
     half = table.shape[2] // 2
     channels = x0.shape[0]
@@ -73,28 +72,36 @@
         p1, b1, s2, p3, b3, s0 = (acc[n] + part for n, part in enumerate(parts))
         s1 = jnp.concatenate([p1[:, :half] + b1[:, half:], p1[:, half:] - b1[:, :half]], axis=1)
         s3 = jnp.concatenate([p3[:, :half] - b3[:, half:], p3[:, half:] + b3[:, :half]], axis=1)
+        outs = (keep, swap.at[0], mate, swap.at[1])
         for s, value in enumerate((s1, s2, s3, s0)):
             value = value.astype(jnp.bfloat16)
-            for p in range(Q):
+            for p, out in enumerate(outs):
 
                 @pl.when(lax.bitwise_xor(me, s) == p)
                 def _():
-                    outs[p][:channels, :] = value
-
-        rows, cols = outs[0].shape[0] - channels, outs[0].shape[1]
+                    out[:channels, :] = value
+
+        cols = keep.shape[1]
         rounds, nbands = bands.shape[1], bands.shape[2]
-        place = (
-            lax.broadcasted_iota(jnp.int32, (rows, cols), 0) * cols
-            + lax.broadcasted_iota(jnp.int32, (rows, cols), 1)
-        ) // (L // nbands)
-        weight = jnp.zeros((rows, cols), jnp.float32)
+        width = L // nbands
+        square = (rounds, rounds)
+        diagonal = lax.broadcasted_iota(jnp.int32, square, 0) == lax.broadcasted_iota(
+            jnp.int32, square, 1
+        )
+        column = jnp.sum(
+            jnp.where(diagonal, jnp.broadcast_to(listed[...], square), 0).astype(jnp.float32),
+            axis=1,
+            keepdims=True,
+        )
+        used = column * bands[0].astype(jnp.float32)
         for d in range(rounds):
             for j in range(nbands):
-                value = (listed[0, d] * bands[0, d, j]).astype(jnp.float32)
-                weight = jnp.where(place == d * nbands + j, value, weight)
-        weight = weight.astype(jnp.bfloat16)
-        for p in range(Q):
-            outs[p][channels:, :] = weight
+                row, lane = divmod((d * nbands + j) * width, cols)
+                weight[row : row + 1, lane : lane + width] = jnp.broadcast_to(
+                    used[d : d + 1, j : j + 1], (1, width)
+                )
+        for out in outs:
+            out[channels:, :] = weight[...].astype(jnp.bfloat16)
 
 
 def spectrum_call(strain, listed, bands, steps=2):
@@ -110,35 +117,42 @@
         spectrum_kernel,
         grid=(steps,),
         in_specs=[
-            pl.BlockSpec(memory_space=pltpu.SMEM),
-            pl.BlockSpec(memory_space=pltpu.SMEM),
+            pl.BlockSpec(listed.shape, lambda k: (0, 0)),
+            pl.BlockSpec(bands.shape, lambda k: (0, 0, 0)),
             *quarter,
             pl.BlockSpec((Q, depth, cols), lambda k: (0, k, 0)),
         ],
-        out_specs=[pl.BlockSpec((rows, cols), lambda k: (0, 0))] * Q,
-        out_shape=[jax.ShapeDtypeStruct((rows, cols), jnp.bfloat16)] * Q,
-        scratch_shapes=[pltpu.VMEM((6, channels, cols), jnp.float32)],
+        out_specs=[
+            pl.BlockSpec((rows, cols), lambda k: (0, 0)),
+            pl.BlockSpec((rows, cols), lambda k: (0, 0)),
+            pl.BlockSpec((2, rows, cols), lambda k: (0, 0, 0)),
+        ],
+        out_shape=[
+            jax.ShapeDtypeStruct((rows, cols), jnp.bfloat16),
+            jax.ShapeDtypeStruct((rows, cols), jnp.bfloat16),
+            jax.ShapeDtypeStruct((2, rows, cols), jnp.bfloat16),
+        ],
+        scratch_shapes=[
+            pltpu.VMEM((6, channels, cols), jnp.float32),
+            pltpu.VMEM((rows - channels, cols), jnp.float32),
+        ],
         compiler_params=pltpu.CompilerParams(dimension_semantics=("arbitrary",)),
         name="spectrum",
     )(listed, bands, strain, strain, strain, strain, jnp.asarray(table))
 
 
-def pair_kernel(*refs):
-    spec_in = refs[: 3 * Q]
-    inv_in, steering, lag_range = refs[3 * Q : 3 * Q + 3]
-    own, *outs = refs[3 * Q + 3 : 3 * Q + 3 + Q]
-    spec, inv, grouped, window, segs, sems, inv_sem = refs[3 * Q + 3 + Q :]
+def pair_kernel(keep, swap, mate, near_b, far_b, near_a, far_a, inv_in, steering, lag_range, *refs):
+    own, send, spec, inv, grouped, window, segs, sems, inv_sem = refs
     me = lax.rem(lax.axis_index(AXIS), Q)
+    sources = [
+        keep, swap.at[0], mate.at[0], mate.at[1],
+        near_b.at[0], near_b.at[1], far_b.at[0], far_b.at[1],
+        near_a.at[0], near_a.at[1], far_a.at[0], far_a.at[1],
+    ]
     copies = []
-    for plane in range(3):
-        for p in range(Q):
-            copies.append(
-                pltpu.make_async_copy(
-                    spec_in[plane * Q + p],
-                    spec.at[plane * Q + lax.bitwise_xor(me, p)],
-                    sems.at[plane * Q + p],
-                )
-            )
+    for n, source in enumerate(sources):
+        slot = n // Q * Q + lax.bitwise_xor(me, n % Q)
+        copies.append(pltpu.make_async_copy(source, spec.at[slot], sems.at[n]))
     inv_copy = pltpu.make_async_copy(inv_in.at[me], inv, inv_sem)
     for copy in copies:
         copy.start()
@@ -214,9 +228,10 @@
             segs[p, 2] = segment(-1)
         else:
             segs[p, 2] = jnp.zeros((angles, width), jnp.float32)
-    own[...] = segs[me]
-    for p in range(1, Q):
-        outs[p - 1][...] = segs[lax.bitwise_xor(me, p)].astype(jnp.bfloat16)
+    own[0] = segs[me]
+    own[1] = segs[lax.bitwise_xor(me, 2)]
+    send[0] = segs[lax.bitwise_xor(me, 1)].astype(jnp.bfloat16)
+    send[1] = segs[lax.bitwise_xor(me, 3)].astype(jnp.bfloat16)
 
 
 def pair_call(spectra, samples, steering, lag_range):
@@ -228,10 +243,12 @@
     vmem = pl.BlockSpec(memory_space=pltpu.VMEM)
     return pl.pallas_call(
         pair_kernel,
-        in_specs=[hbm] * (3 * Q + 1) + [vmem, vmem],
-        out_specs=[vmem] * Q,
-        out_shape=[jax.ShapeDtypeStruct((3, angles, width), jnp.float32)]
-        + [jax.ShapeDtypeStruct((3, angles, width), jnp.bfloat16)] * (Q - 1),
+        in_specs=[vmem] * len(spectra) + [hbm, vmem, vmem],
+        out_specs=[vmem, vmem],
+        out_shape=[
+            jax.ShapeDtypeStruct((2, 3, angles, width), jnp.float32),
+            jax.ShapeDtypeStruct((2, 3, angles, width), jnp.bfloat16),
+        ],
         scratch_shapes=[
             pltpu.VMEM((3 * Q, rows, cols), jnp.bfloat16),
             pltpu.VMEM((cols, L), jnp.bfloat16),
@@ -252,16 +269,23 @@
 
 
 def per_device(devices, strain, steering, lag_range, pair_listed, band_used):
-    slices = spectrum_call(strain, pair_listed, band_used)
-    own = [slices[0]] + [
-        exchange(slices[p], devices, lambda i: i ^ p) for p in range(1, Q)
-    ]
-    below = [exchange(slices[p], devices, lambda i: (i ^ p) + Q) for p in range(Q)]
-    above = [exchange(slices[p], devices, lambda i: (i ^ p) - Q) for p in range(Q)]
-    mine, *sends = pair_call(own + below + above, strain.shape[1], steering, lag_range)
-    for p in range(1, Q):
-        mine = mine + exchange(sends[p - 1], devices, lambda i: i ^ p).astype(jnp.float32)
-    up = exchange(mine[1].astype(jnp.bfloat16), devices, lambda i: i + Q)
+    def shift(value, by):
+        return exchange(value, devices, lambda i: i + by)
+
+    def flip(value, by):
+        return exchange(value, devices, lambda i: i ^ by)
+
+    keep, mate, swap = spectrum_call(strain, pair_listed, band_used)
+    swap = flip(swap, 1)
+    mates = flip(jnp.stack([mate, swap[1]]), 2)
+    near = jnp.stack([keep, swap[0]])
+    spectra = [keep, swap, mates]
+    for by in (Q, -Q):
+        spectra += [shift(near, by), shift(mates, by)]
+    mine, send = pair_call(spectra, strain.shape[1], steering, lag_range)
+    mine = mine + flip(send, 1).astype(jnp.float32)
+    mine = mine[0] + flip(mine[1].astype(jnp.bfloat16), 2).astype(jnp.float32)
+    up = shift(mine[1].astype(jnp.bfloat16), Q)
 
     def ends(i):
         if i % Q == 0:

time: 70 us -> 61.7 us (0.88)
  starting transfers between devices: 39.2 us -> 25.4 us
  Pallas kernels: 13.9 us -> 16.1 us
  other arithmetic: 1.62 us -> 3.68 us
  waiting for transfers between devices: 12.6 us -> 13.9 us
    ppermute x16 -> x10, starting transfers between devices: 39.2 us -> 25.4 us  [exchange(): return lax.ppermute(value, AXIS, pairs)]
    pallas_call x2, Pallas kernels: 13.9 us -> 16.1 us  [the longest x1 11.9 us: pair_call(): pl.pallas_call(pair_kernel, in_specs=[vmem] * len(spectra) + [hbm, vmem,...]
    ppermute x16 -> x10, waiting for transfers between devices: 12.6 us -> 13.9 us  [exchange(): return lax.ppermute(value, AXIS, pairs)]
    add x0 -> x1, other arithmetic: none -> 1.04 us  [per_device(): mine = mine + flip(send, 1).astype(jnp.float32)]
    another operation x1 -> x3, other arithmetic: 0.98 us -> 2 us  [the longest x1 1.03 us: per_device(): mates = flip(jnp.stack([mate, swap[1]]), 2)]
    unnamed x23 -> x13, local copies, waits for them, and re-layouts: 2.03 us -> 2.07 us
  transfers between devices with their start and end apart: 16 -> 10, of which waited for: 6 -> 7; matrix products, arithmetic and copies ran while one was open for 0% -> 2% of each run, Pallas kernels for 0% -> 0%
where the time goes in v2:
time: 61.7 us; the launch traced here: 61.4 us
  starting transfers between devices  25.4 us (41%)
  Pallas kernels  16.1 us (26%)
  waiting for transfers between devices  13.9 us (23%)
  other arithmetic  3.68 us (6%)
  local copies, waits for them, and re-layouts  2.11 us (3%)
    ppermute x10, starting transfers between devices, exchange(): return lax.ppermute(value, AXIS, pairs)  25.4 us
    ppermute x10, waiting for transfers between devices, exchange(): return lax.ppermute(value, AXIS, pairs)  13.9 us
    pallas_call x1, Pallas kernels, pair_call(): pl.pallas_call(pair_kernel, in_specs=[vmem] * len(spectra) + [hbm, vmem,...  11.9 us
    pallas_call x1, Pallas kernels, spectrum_call(): pl.pallas_call(spectrum_kernel, grid=(steps,), in_specs=[pl.BlockSpec(lis...  4.17 us
    unnamed x13, local copies, waits for them, and re-layouts  2.07 us
  transfers between devices with their start and end apart: 10, of which 7 were waited for; matrix products, arithmetic and copies ran while one was open for 2% of the time, Pallas kernels for 0%

profile of v2, /device:TPU:0, one launch (start us, length us, event | category | flops | bytes accessed | tf_op | source)
XLA Modules:
  0.0 61.4 jit_solution(16931177021306170517)
XLA Ops:
  0.0 1.3 %copy.8.bands = s32[1,8,4]{2,1,0:T(8,128)} copy(s32[1,8,4]{1,2,0:T(4,128)} %param.11) | data formatting | bytes 256 | tf_op args[4]
  1.3 4.2 %spectrum.1 = (bf16[272,256]{1,0:T(8,128)(2,1)}, bf16[272,256]{1,0:T(8,128)(2,1)}, bf16[2,272,256]{2,1,0:T(8,128)(2,1)}) custom-call(s32[1,8]{1,0:T(1,128)} %listed.1, s32[1,8,4]{2,1,0:T(8,128)} %copy.8.bands, bf16[256,4096]{1,0:T(8,128)(2,1)} %x3.1, bf16[256,4096]{1,0:T(8,128)(2,1)} %x3.1, bf16[256,4096]{1,0:T(8,128)(2,1)} %x3.1, bf16[256,4096]{1,0:T(8,128)(2,1)} %x3.1, ...), custom_call_target="tpu_custom_call" | custom-call | tf_op jit(solution)/shard_map/spectrum/pallas_call | solution.py:116
  5.5 0.5 collective-permute-start
  6.0 1.4 %collective-permute-done.swap = bf16[2,272,256]{2,1,0:T(8,128)(2,1)S(1)} collective-permute-done((bf16[2,272,256]{2,1,0:T(8,128)(2,1)}, bf16[2,272,256]{2,1,0:T(8,128)(2,1)S(1)}, u32[]{:S(2)}, u32[]{:S(2)}) %collective-permute-start) | collective-permute-done | bytes 278560 | tf_op jit(solution)/shard_map/ppermute | solution.py:268
  7.4 1.0 %pad_maximum_fusion = bf16[2,272,256]{2,1,0:T(8,128)(2,1)S(1)} fusion(bf16[1,272,256]{2,1,0:T(8,128)(2,1)S(1)} %get-tuple-element.18, bf16[1,272,256]{2,1,0:T(8,128)(2,1)} %bitcast.20), kind=kLoop, calls=%fused_computation.1 | loop fusion | flops 139264 | bytes 557056 | tf_op jit(solution)/shard_map/stack | solution.py:280
  8.5 2.9 %collective-permute-start.1 = (bf16[2,272,256]{2,1,0:T(8,128)(2,1)S(1)}, bf16[2,272,256]{2,1,0:T(8,128)(2,1)S(1)}, u32[]{:S(2)}, u32[]{:S(2)}) collective-permute-start(bf16[2,272,256]{2,1,0:T(8,128)(2,1)S(1)} %pad_maximum_fusion), channel_id=1, source_target_pairs={{0,2},{1,3},{2,0},{3,1},{4,6},{5,7},{6,4},{7,5},{8,10},{9,11},{10,... | collective-permute-start | bytes 835592 | tf_op jit(solution)/shard_map/ppermute | solution.py:268
  11.4 0.9 %pad_maximum_fusion.1 = bf16[2,272,256]{2,1,0:T(8,128)(2,1)S(1)} fusion(bf16[1,272,256]{2,1,0:T(8,128)(2,1)S(1)} %get-tuple-element.17, bf16[1,272,256]{2,1,0:T(8,128)(2,1)} %bitcast.19), kind=kLoop, calls=%fused_computation.2 | loop fusion | flops 139264 | bytes 557056 | tf_op jit(solution)/shard_map/stack | solution.py:281
  12.3 1.3 %collective-permute-start.4 = (bf16[2,272,256]{2,1,0:T(8,128)(2,1)S(1)}, bf16[2,272,256]{2,1,0:T(8,128)(2,1)S(1)}, u32[]{:S(2)}, u32[]{:S(2)}) collective-permute-start(bf16[2,272,256]{2,1,0:T(8,128)(2,1)S(1)} %pad_maximum_fusion.1), channel_id=1, source_target_pairs={{4,0},{5,1},{6,2},{7,3},{8,4},{9,5},{10,6},{11,7},{12,8},{13,9},{1... | collective-permute-start | bytes 835592 | tf_op jit(solution)/shard_map/ppermute | solution.py:268
  13.6 4.6 %collective-permute-start.2 = (bf16[2,272,256]{2,1,0:T(8,128)(2,1)S(1)}, bf16[2,272,256]{2,1,0:T(8,128)(2,1)S(1)}, u32[]{:S(2)}, u32[]{:S(2)}) collective-permute-start(bf16[2,272,256]{2,1,0:T(8,128)(2,1)S(1)} %pad_maximum_fusion.1), channel_id=1, source_target_pairs={{0,4},{1,5},{2,6},{3,7},{4,8},{5,9},{6,10},{7,11},{8,12},{9,13},{1... | collective-permute-start | bytes 835592 | tf_op jit(solution)/shard_map/ppermute | solution.py:268
  18.2 0.2 collective-permute-done.1.mate
  18.4 1.3 %collective-permute-start.5 = (bf16[2,272,256]{2,1,0:T(8,128)(2,1)S(1)}, bf16[2,272,256]{2,1,0:T(8,128)(2,1)S(1)}, u32[]{:S(2)}, u32[]{:S(2)}) collective-permute-start(bf16[2,272,256]{2,1,0:T(8,128)(2,1)S(1)} %collective-permute-done.1.mate), channel_id=1, source_target_pairs={{4,0},{5,1},{6,2},{7,3},{8,4},{9,5},{10,6},{11,7},{12,8},{13,9},{1... | collective-permute-start | bytes 835592 | tf_op jit(solution)/shard_map/ppermute | solution.py:268
  19.7 4.6 %collective-permute-start.3 = (bf16[2,272,256]{2,1,0:T(8,128)(2,1)S(1)}, bf16[2,272,256]{2,1,0:T(8,128)(2,1)S(1)}, u32[]{:S(2)}, u32[]{:S(2)}) collective-permute-start(bf16[2,272,256]{2,1,0:T(8,128)(2,1)S(1)} %collective-permute-done.1.mate), channel_id=1, source_target_pairs={{0,4},{1,5},{2,6},{3,7},{4,8},{5,9},{6,10},{7,11},{8,12},{9,13},{1... | collective-permute-start | bytes 835592 | tf_op jit(solution)/shard_map/ppermute | solution.py:268
  24.2 0.0 collective-permute-done.4.near_a
  24.2 0.0 copy-start.2
  24.3 0.0 collective-permute-done.2.near_b
  24.3 0.0 copy-start.3
  24.3 4.4 %collective-permute-done.5.far_a = bf16[2,272,256]{2,1,0:T(8,128)(2,1)S(1)} collective-permute-done((bf16[2,272,256]{2,1,0:T(8,128)(2,1)S(1)}, bf16[2,272,256]{2,1,0:T(8,128)(2,1)S(1)}, u32[]{:S(2)}, u32[]{:S(2)}) %collective-permute-start.5) | collective-permute-done | bytes 278560 | tf_op jit(solution)/shard_map/ppermute | solution.py:268
  28.6 1.2 %collective-permute-done.3.far_b = bf16[2,272,256]{2,1,0:T(8,128)(2,1)S(1)} collective-permute-done((bf16[2,272,256]{2,1,0:T(8,128)(2,1)S(1)}, bf16[2,272,256]{2,1,0:T(8,128)(2,1)S(1)}, u32[]{:S(2)}, u32[]{:S(2)}) %collective-permute-start.3) | collective-permute-done | bytes 278560 | tf_op jit(solution)/shard_map/ppermute | solution.py:268
  29.8 0.0 copy-done
  29.8 0.0 copy-done.3
  29.8 0.7 %copy-done.5 = bf16[2,272,256]{2,1,0:T(8,128)(2,1)} copy-done((bf16[2,272,256]{2,1,0:T(8,128)(2,1)}, bf16[2,272,256]{2,1,0:T(8,128)(2,1)S(1)}, u32[]{:S(2)}) %copy-start.5) | copy-done | bytes 278552
  30.5 11.9 %pairs.1 = (f32[2,3,128,128]{3,2,1,0:T(8,128)}, bf16[2,3,128,128]{3,2,1,0:T(8,128)(2,1)}) custom-call(bf16[272,256]{1,0:T(8,128)(2,1)} %get-tuple-element.10.keep, bf16[2,272,256]{2,1,0:T(8,128)(2,1)} %copy-done, bf16[2,272,256]{2,1,0:T(8,128)(2,1)} %copy-done.1, bf16[2,272,256]{2,1,0:T(8,128)(2,1)} %copy-done.3, bf16[2,272,256]{2,1,0:T(8,128)(2,1)} %copy-done.5, ...), custom_call_target="tpu_custom_call" | custom-call | tf_op jit(solution)/shard_map/pairs/pallas_call | solution.py:244
  42.5 0.1 collective-permute-start.6
  42.5 1.6 %collective-permute-done.6 = bf16[2,3,128,128]{3,2,1,0:T(8,128)(2,1)S(1)} collective-permute-done((bf16[2,3,128,128]{3,2,1,0:T(8,128)(2,1)}, bf16[2,3,128,128]{3,2,1,0:T(8,128)(2,1)S(1)}, u32[]{:S(2)}, u32[]{:S(2)}) %collective-permute-start.6) | collective-permute-done | bytes 196640 | tf_op jit(solution)/shard_map/ppermute | solution.py:268
  44.2 1.0 %convert_add_fusion = f32[2,3,128,128]{3,2,1,0:T(8,128)S(1)} fusion(f32[2,3,128,128]{3,2,1,0:T(8,128)} %get-tuple-element.13, bf16[2,3,128,128]{3,2,1,0:T(8,128)(2,1)S(1)} %collective-permute-done.6), kind=kLoop, calls=%fused_computation | loop fusion | flops 196608 | bytes 983040 | tf_op jit(solution)/shard_map/add | solution.py:286
  45.3 1.3 %collective-permute-start.7 = (bf16[3,128,128]{2,1,0:T(8,128)(2,1)S(1)}, bf16[3,128,128]{2,1,0:T(8,128)(2,1)S(1)}, u32[]{:S(2)}, u32[]{:S(2)}) collective-permute-start(bf16[3,128,128]{2,1,0:T(8,128)(2,1)S(1)} %fusion.1), channel_id=1, source_target_pairs={{0,2},{1,3},{2,0},{3,1},{4,6},{5,7},{6,4},{7,5},{8,10},{9,11},{10,... | collective-permute-start | bytes 294920 | tf_op jit(solution)/shard_map/ppermute | solution.py:268
  46.5 3.6 %collective-permute-done.7 = bf16[3,128,128]{2,1,0:T(8,128)(2,1)S(1)} collective-permute-done((bf16[3,128,128]{2,1,0:T(8,128)(2,1)S(1)}, bf16[3,128,128]{2,1,0:T(8,128)(2,1)S(1)}, u32[]{:S(2)}, u32[]{:S(2)}) %collective-permute-start.7) | collective-permute-done | bytes 98336 | tf_op jit(solution)/shard_map/ppermute | solution.py:268
  50.2 4.4 %collective-permute-start.8 = (bf16[128,128]{1,0:T(8,128)(2,1)S(1)}, bf16[128,128]{1,0:T(8,128)(2,1)S(1)}, u32[]{:S(2)}, u32[]{:S(2)}) collective-permute-start(bf16[128,128]{1,0:T(8,128)(2,1)S(1)} %get-tuple-element.19), channel_id=1, source_target_pairs={{0,4},{1,5},{2,6},{3,7},{4,8},{5,9},{6,10},{7,11},{8,12},{9,13},{1... | collective-permute-start | bytes 98312 | tf_op jit(solution)/shard_map/ppermute | solution.py:268
  54.6 4.5 %collective-permute-start.9 = (bf16[128,128]{1,0:T(8,128)(2,1)S(1)}, bf16[128,128]{1,0:T(8,128)(2,1)S(1)}, u32[]{:S(2)}, u32[]{:S(2)}) collective-permute-start(bf16[128,128]{1,0:T(8,128)(2,1)S(1)} %get-tuple-element.20), channel_id=1, source_target_pairs={{0,8},{4,12},{7,3},{11,7},{15,11},{16,24},{20,28},{23,19},{27,23},... | collective-permute-start | bytes 98312 | tf_op jit(solution)/shard_map/ppermute | solution.py:268
  59.1 0.0 collective-permute-done.8
  59.2 1.6 %collective-permute-done.9 = bf16[128,128]{1,0:T(8,128)(2,1)S(1)} collective-permute-done((bf16[128,128]{1,0:T(8,128)(2,1)S(1)}, bf16[128,128]{1,0:T(8,128)(2,1)S(1)}, u32[]{:S(2)}, u32[]{:S(2)}) %collective-permute-start.9) | collective-permute-done | bytes 32800 | tf_op jit(solution)/shard_map/ppermute | solution.py:268
  60.7 0.6 %fusion.3 = f32[128,128]{1,0:T(8,128)} fusion(f32[3,128,128]{2,1,0:T(8,128)S(1)} %get-tuple-element.16, bf16[128,128]{1,0:T(8,128)(2,1)S(1)} %collective-permute-done.9, bf16[128,128]{1,0:T(8,128)(2,1)S(1)} %collective-permute-done.8), kind=kLoop, calls=%fused_computation.9 | loop fusion | flops 65536 | bytes 196608 | tf_op jit(solution)/shard_map/add | solution.py:298
  (11 shorter events, 0.1 us)
Async XLA Ops:
  5.5 1.9 %collective-permute-start = (bf16[2,272,256]{2,1,0:T(8,128)(2,1)}, bf16[2,272,256]{2,1,0:T(8,128)(2,1)S(1)}, u32[]{:S(2)}, u32[]{:S(2)}) collective-permute-start(bf16[2,272,256]{2,1,0:T(8,128)(2,1)} %get-tuple-element.11), channel_id=1, source_target_pairs={{0,1},{1,0},{2,3},{3,2},{4,5},{5,4},{6,7},{7,6},{8,9},{9,8},{10,11... | collective-permute-start | bytes 835592 | tf_op jit(solution)/shard_map/ppermute | solution.py:268
  7.4 22.4 %copy-start = (bf16[2,272,256]{2,1,0:T(8,128)(2,1)}, bf16[2,272,256]{2,1,0:T(8,128)(2,1)S(1)}, u32[]{:S(2)}) copy-start(bf16[2,272,256]{2,1,0:T(8,128)(2,1)S(1)} %collective-permute-done.swap) | copy-start | bytes 835588
  8.5 9.9 %collective-permute-start.1 = (bf16[2,272,256]{2,1,0:T(8,128)(2,1)S(1)}, bf16[2,272,256]{2,1,0:T(8,128)(2,1)S(1)}, u32[]{:S(2)}, u32[]{:S(2)}) collective-permute-start(bf16[2,272,256]{2,1,0:T(8,128)(2,1)S(1)} %pad_maximum_fusion), channel_id=1, source_target_pairs={{0,2},{1,3},{2,0},{3,1},{4,6},{5,7},{6,4},{7,5},{8,10},{9,11},{10,... | collective-permute-start | bytes 835592 | tf_op jit(solution)/shard_map/ppermute | solution.py:268
  12.3 11.9 %collective-permute-start.4 = (bf16[2,272,256]{2,1,0:T(8,128)(2,1)S(1)}, bf16[2,272,256]{2,1,0:T(8,128)(2,1)S(1)}, u32[]{:S(2)}, u32[]{:S(2)}) collective-permute-start(bf16[2,272,256]{2,1,0:T(8,128)(2,1)S(1)} %pad_maximum_fusion.1), channel_id=1, source_target_pairs={{4,0},{5,1},{6,2},{7,3},{8,4},{9,5},{10,6},{11,7},{12,8},{13,9},{1... | collective-permute-start | bytes 835592 | tf_op jit(solution)/shard_map/ppermute | solution.py:268
  13.6 10.6 %collective-permute-start.2 = (bf16[2,272,256]{2,1,0:T(8,128)(2,1)S(1)}, bf16[2,272,256]{2,1,0:T(8,128)(2,1)S(1)}, u32[]{:S(2)}, u32[]{:S(2)}) collective-permute-start(bf16[2,272,256]{2,1,0:T(8,128)(2,1)S(1)} %pad_maximum_fusion.1), channel_id=1, source_target_pairs={{0,4},{1,5},{2,6},{3,7},{4,8},{5,9},{6,10},{7,11},{8,12},{9,13},{1... | collective-permute-start | bytes 835592 | tf_op jit(solution)/shard_map/ppermute | solution.py:268
  18.4 11.4 %copy-start.1 = (bf16[2,272,256]{2,1,0:T(8,128)(2,1)}, bf16[2,272,256]{2,1,0:T(8,128)(2,1)S(1)}, u32[]{:S(2)}) copy-start(bf16[2,272,256]{2,1,0:T(8,128)(2,1)S(1)} %collective-permute-done.1.mate) | copy-start | bytes 835588
  18.4 10.3 %collective-permute-start.5 = (bf16[2,272,256]{2,1,0:T(8,128)(2,1)S(1)}, bf16[2,272,256]{2,1,0:T(8,128)(2,1)S(1)}, u32[]{:S(2)}, u32[]{:S(2)}) collective-permute-start(bf16[2,272,256]{2,1,0:T(8,128)(2,1)S(1)} %collective-permute-done.1.mate), channel_id=1, source_target_pairs={{4,0},{5,1},{6,2},{7,3},{8,4},{9,5},{10,6},{11,7},{12,8},{13,9},{1... | collective-permute-start | bytes 835592 | tf_op jit(solution)/shard_map/ppermute | solution.py:268
  19.7 10.1 %collective-permute-start.3 = (bf16[2,272,256]{2,1,0:T(8,128)(2,1)S(1)}, bf16[2,272,256]{2,1,0:T(8,128)(2,1)S(1)}, u32[]{:S(2)}, u32[]{:S(2)}) collective-permute-start(bf16[2,272,256]{2,1,0:T(8,128)(2,1)S(1)} %collective-permute-done.1.mate), channel_id=1, source_target_pairs={{0,4},{1,5},{2,6},{3,7},{4,8},{5,9},{6,10},{7,11},{8,12},{9,13},{1... | collective-permute-start | bytes 835592 | tf_op jit(solution)/shard_map/ppermute | solution.py:268
  24.2 5.6 %copy-start.2 = (bf16[2,272,256]{2,1,0:T(8,128)(2,1)}, bf16[2,272,256]{2,1,0:T(8,128)(2,1)S(1)}, u32[]{:S(2)}) copy-start(bf16[2,272,256]{2,1,0:T(8,128)(2,1)S(1)} %collective-permute-done.4.near_a) | copy-start | bytes 835588
  24.3 5.6 %copy-start.3 = (bf16[2,272,256]{2,1,0:T(8,128)(2,1)}, bf16[2,272,256]{2,1,0:T(8,128)(2,1)S(1)}, u32[]{:S(2)}) copy-start(bf16[2,272,256]{2,1,0:T(8,128)(2,1)S(1)} %collective-permute-done.2.near_b) | copy-start | bytes 835588
  28.6 1.2 %copy-start.4 = (bf16[2,272,256]{2,1,0:T(8,128)(2,1)}, bf16[2,272,256]{2,1,0:T(8,128)(2,1)S(1)}, u32[]{:S(2)}) copy-start(bf16[2,272,256]{2,1,0:T(8,128)(2,1)S(1)} %collective-permute-done.5.far_a) | copy-start | bytes 835588
  29.8 0.7 %copy-start.5 = (bf16[2,272,256]{2,1,0:T(8,128)(2,1)}, bf16[2,272,256]{2,1,0:T(8,128)(2,1)S(1)}, u32[]{:S(2)}) copy-start(bf16[2,272,256]{2,1,0:T(8,128)(2,1)S(1)} %collective-permute-done.3.far_b) | copy-start | bytes 835588
  42.5 1.7 %collective-permute-start.6 = (bf16[2,3,128,128]{3,2,1,0:T(8,128)(2,1)}, bf16[2,3,128,128]{3,2,1,0:T(8,128)(2,1)S(1)}, u32[]{:S(2)}, u32[]{:S(2)}) collective-permute-start(bf16[2,3,128,128]{3,2,1,0:T(8,128)(2,1)} %get-tuple-element.14), channel_id=1, source_target_pairs={{0,1},{1,0},{2,3},{3,2},{4,5},{5,4},{6,7},{7,6},{8,9},{9,8},{10,11... | collective-permute-start | bytes 589832 | tf_op jit(solution)/shard_map/ppermute | solution.py:268
  45.3 4.9 %collective-permute-start.7 = (bf16[3,128,128]{2,1,0:T(8,128)(2,1)S(1)}, bf16[3,128,128]{2,1,0:T(8,128)(2,1)S(1)}, u32[]{:S(2)}, u32[]{:S(2)}) collective-permute-start(bf16[3,128,128]{2,1,0:T(8,128)(2,1)S(1)} %fusion.1), channel_id=1, source_target_pairs={{0,2},{1,3},{2,0},{3,1},{4,6},{5,7},{6,4},{7,5},{8,10},{9,11},{10,... | collective-permute-start | bytes 294920 | tf_op jit(solution)/shard_map/ppermute | solution.py:268
  50.2 8.9 %collective-permute-start.8 = (bf16[128,128]{1,0:T(8,128)(2,1)S(1)}, bf16[128,128]{1,0:T(8,128)(2,1)S(1)}, u32[]{:S(2)}, u32[]{:S(2)}) collective-permute-start(bf16[128,128]{1,0:T(8,128)(2,1)S(1)} %get-tuple-element.19), channel_id=1, source_target_pairs={{0,4},{1,5},{2,6},{3,7},{4,8},{5,9},{6,10},{7,11},{8,12},{9,13},{1... | collective-permute-start | bytes 98312 | tf_op jit(solution)/shard_map/ppermute | solution.py:268
  54.6 6.1 %collective-permute-start.9 = (bf16[128,128]{1,0:T(8,128)(2,1)S(1)}, bf16[128,128]{1,0:T(8,128)(2,1)S(1)}, u32[]{:S(2)}, u32[]{:S(2)}) collective-permute-start(bf16[128,128]{1,0:T(8,128)(2,1)S(1)} %get-tuple-element.20), channel_id=1, source_target_pairs={{0,8},{4,12},{7,3},{11,7},{15,11},{16,24},{20,28},{23,19},{27,23},... | collective-permute-start | bytes 98312 | tf_op jit(solution)/shard_map/ppermute | solution.py:268

commit v3 on v2

v3 whole, which is shorter than its diff:
```python
import functools

import jax
import jax.numpy as jnp
import numpy as np
from jax import lax
from jax.experimental import pallas as pl
from jax.experimental.pallas import tpu as pltpu
from jax.sharding import PartitionSpec as P

AXIS = "fib"
F = 512
L = 512
Q = 4


def forward_table(samples):
    freqs = F // Q
    t = np.arange(samples // Q, dtype=np.int64)[None, :, None]
    k = Q * np.arange(freqs, dtype=np.int64)[None, None, :] + np.arange(Q)[:, None, None] + 1
    phase = (t * k % samples) * (2.0 * np.pi / samples)
    table = np.concatenate([np.cos(phase), -np.sin(phase)], axis=2) * samples ** (-0.5)
    return table.astype(jnp.bfloat16)


def inverse_table(samples):
    freqs = F // Q
    k = Q * np.arange(freqs, dtype=np.int64)[None, :, None] + np.arange(Q)[:, None, None] + 1
    lag = np.arange(L, dtype=np.int64)[None, None, :] - L // 2
    theta = (k * lag % samples) * (2.0 * np.pi / samples)
    table = np.concatenate([np.cos(theta), -np.sin(theta)], axis=1) * (2 * F) ** (-0.5)
    return table.astype(jnp.bfloat16)


def in_hbm(value):
    return pltpu.with_memory_space_constraint(value, pltpu.HBM)


def dot(a, b):
    return jnp.dot(a, b, preferred_element_type=jnp.float32)


def spectrum_kernel(listed, bands, x0, x1, x2, x3, table, keep, mate, swap, acc, weight):
    step, steps = pl.program_id(0), pl.num_programs(0)
    half = table.shape[2] // 2
    channels = x0.shape[0]
    me = lax.rem(lax.axis_index(AXIS), Q)

    q0, q1, q2, q3 = (x[...].astype(jnp.float32) for x in (x0, x1, x2, x3))
    even, odd = q0 + q2, q1 + q3
    fold0 = (even + odd).astype(jnp.bfloat16)
    fold2 = (even - odd).astype(jnp.bfloat16)
    a = (q0 - q2).astype(jnp.bfloat16)
    b = (q1 - q3).astype(jnp.bfloat16)
    parts = [
        dot(a, table[0]),
        dot(b, table[0]),
        dot(fold2, table[1]),
        dot(a, table[2]),
        dot(b, table[2]),
        dot(fold0, table[3]),
    ]

    @pl.when(step == 0)
    def _():
        for n, part in enumerate(parts):
            acc[n] = part

    @pl.when((step > 0) & (step < steps - 1))
    def _():
        for n, part in enumerate(parts):
            acc[n] += part

    @pl.when(step == steps - 1)
    def _():
        p1, b1, s2, p3, b3, s0 = (acc[n] + part for n, part in enumerate(parts))
        s1 = jnp.concatenate([p1[:, :half] + b1[:, half:], p1[:, half:] - b1[:, :half]], axis=1)
        s3 = jnp.concatenate([p3[:, :half] - b3[:, half:], p3[:, half:] + b3[:, :half]], axis=1)
        outs = (keep, swap.at[0], mate, swap.at[1])
        for s, value in enumerate((s1, s2, s3, s0)):
            value = value.astype(jnp.bfloat16)
            for p, out in enumerate(outs):

                @pl.when(lax.bitwise_xor(me, s) == p)
                def _():
                    out[:channels, :] = value

        cols = keep.shape[1]
        nbands, rounds = bands.shape[1], bands.shape[2]
        width = L // nbands
        used = (listed[...] * bands[0]).astype(jnp.float32)
        for j in range(nbands):
            part, lane = divmod(j * width, cols)
            for d in range(rounds):
                row = part * rounds + d
                weight[row : row + 1, lane : lane + width] = jnp.broadcast_to(
                    used[j : j + 1, d : d + 1], (1, width)
                )
        for out in outs:
            out[channels:, :] = weight[...].astype(jnp.bfloat16)


def spectrum_call(strain, listed, bands, steps=2):
    channels, samples = strain.shape
    table = forward_table(samples)
    cols = table.shape[2]
    depth = samples // Q // steps
    rows = channels + bands.shape[2] * L // cols
    quarter = [
        pl.BlockSpec((channels, depth), lambda k, q=q: (0, q * steps + k)) for q in range(Q)
    ]
    return pl.pallas_call(
        spectrum_kernel,
        grid=(steps,),
        in_specs=[
            pl.BlockSpec(listed.shape, lambda k: (0, 0)),
            pl.BlockSpec(bands.shape, lambda k: (0, 0, 0)),
            *quarter,
            pl.BlockSpec((Q, depth, cols), lambda k: (0, k, 0)),
        ],
        out_specs=[pl.BlockSpec(memory_space=pltpu.VMEM)] * 3,
        out_shape=[
            pltpu.VMEM((rows, cols), jnp.bfloat16),
            pltpu.VMEM((rows, cols), jnp.bfloat16),
            pltpu.VMEM((2, rows, cols), jnp.bfloat16),
        ],
        scratch_shapes=[
            pltpu.VMEM((6, channels, cols), jnp.float32),
            pltpu.VMEM((rows - channels, cols), jnp.float32),
        ],
        compiler_params=pltpu.CompilerParams(
            dimension_semantics=("arbitrary",), vmem_limit_bytes=LIMIT
        ),
        name="spectrum",
    )(listed, bands, *[in_hbm(strain)] * Q, in_hbm(jnp.asarray(table)))


UNROLL = 3
LIMIT = 16 << 20


def unit_table(rounds):
    early, late = [], []
    for me in range(Q):
        units = ([], [])
        for i in range(2 * Q):
            for j in range(-Q, Q):
                d = i - j
                if not 0 <= d <= rounds or (i >= Q and j >= 0):
                    continue
                p, q = i % Q ^ me, j % Q ^ me
                target = p if i < Q else 2 * Q + p
                source = q if j >= 0 else Q + q
                far = (i >= Q and p >= Q // 2) or (j < 0 and q >= Q // 2)
                mask = p if i < Q else Q + p
                row = d - 1 if d else rounds
                units[far].append((target, source, d, i, mask, row))
        early.append(units[0])
        late.append(units[1])
    return np.asarray(early, np.int32), np.asarray(late, np.int32)


def run_units(table, me, spec, mask, steering, inv, lag_range, window):
    channels, angles = steering.shape[2], steering.shape[1]
    cols = spec.shape[2]
    half = cols // 2

    def body(n, carry):
        units = [
            [table[me, (n * UNROLL + u) * 6 + e] for e in range(6)] for u in range(UNROLL)
        ]
        beams = []
        for target, source, d, _, _, _ in units:
            near_re = spec[target, :channels, :half].astype(jnp.float32)
            near_im = spec[target, :channels, half:].astype(jnp.float32)
            far_re = spec[source, :channels, :half].astype(jnp.float32)
            far_im = spec[source, :channels, half:].astype(jnp.float32)
            real = near_re * far_re + near_im * far_im
            imag = near_im * far_re - near_re * far_im
            cross = jnp.concatenate([real, imag], axis=1).astype(jnp.bfloat16)
            beams.append(dot(steering[d], cross).astype(jnp.bfloat16))
        beams = dot(jnp.concatenate(beams, axis=0), inv[...])
        for u, (_, _, d, slot, target, row) in enumerate(units):
            weight = jnp.concatenate(
                [mask[target, h, pl.ds(row, 1), :] for h in range(L // cols)], axis=1
            )
            masked = (beams[u * angles : (u + 1) * angles, :] * weight).astype(jnp.bfloat16)
            window[slot] += dot(masked, lag_range[d])
        return carry

    lax.fori_loop(0, table.shape[1] // (6 * UNROLL), body, 0)


def fill_mask(mask, entry, spec, slot, channels):
    rounds = mask.shape[2] // 2
    rows = spec[slot, channels:, :].astype(jnp.float32)
    for h in range(mask.shape[1]):
        mask[entry, h, :rounds, :] = rows[h * rounds : (h + 1) * rounds, :]
        mask[entry, h, rounds:, :] = jnp.ones((rounds, mask.shape[3]), jnp.float32)


def early_kernel(
    table, keep, swap, mates, below, above, inv_all, steering, lag_range,
    spec, inv, window, mask, sems,
):
    me = lax.rem(lax.axis_index(AXIS), Q)
    copies = [
        pltpu.make_async_copy(keep, spec.at[0], sems.at[0]),
        pltpu.make_async_copy(swap.at[0], spec.at[1], sems.at[1]),
        pltpu.make_async_copy(mates, spec.at[2:4], sems.at[2]),
        pltpu.make_async_copy(below, spec.at[Q : Q + 2], sems.at[3]),
        pltpu.make_async_copy(above, spec.at[2 * Q : 2 * Q + 2], sems.at[4]),
        pltpu.make_async_copy(inv_all.at[me], inv, sems.at[5]),
    ]
    for copy in copies:
        copy.start()
    window[...] = jnp.zeros_like(window)
    for copy in copies:
        copy.wait()
    channels = steering.shape[2]
    for p in range(Q):
        fill_mask(mask, p, spec, p, channels)
    for p in range(Q // 2):
        fill_mask(mask, Q + p, spec, 2 * Q + p, channels)
    run_units(table, me, spec, mask, steering, inv, lag_range, window)


def late_kernel(
    table, spec_in, inv, window_in, below, above, steering, lag_range,
    own, send, spec, window, mask, segs, sems,
):
    me = lax.rem(lax.axis_index(AXIS), Q)
    copies = [
        pltpu.make_async_copy(below, spec.at[Q + 2 : Q + 4], sems.at[0]),
        pltpu.make_async_copy(above, spec.at[2 * Q + 2 : 2 * Q + 4], sems.at[1]),
    ]
    for copy in copies:
        copy.start()
    for copy in copies:
        copy.wait()
    channels, angles = steering.shape[2], steering.shape[1]
    for p in range(Q):
        fill_mask(mask, p, spec, p, channels)
        fill_mask(mask, Q + p, spec, 2 * Q + p, channels)
    run_units(table, me, spec, mask, steering, inv, lag_range, window)

    width = window.shape[2] // 3

    def segment(s):
        total = None
        for slot, part in ((s, 1), (s - 1, 2), (s + 1, 0)):
            if 0 <= slot < 2 * Q:
                value = window[slot, :, part * width : (part + 1) * width]
                total = value if total is None else total + value
        return total

    for p in range(Q):
        segs[p, 0] = segment(p)
        segs[p, 1] = segment(Q + p)
        if p == 0:
            segs[p, 2] = segment(2 * Q)
        elif p == Q - 1:
            segs[p, 2] = segment(-1)
        else:
            segs[p, 2] = jnp.zeros((angles, width), jnp.float32)
    own[0] = segs[me]
    own[1] = segs[lax.bitwise_xor(me, 2)]
    send[0] = segs[lax.bitwise_xor(me, 1)].astype(jnp.bfloat16)
    send[1] = segs[lax.bitwise_xor(me, 3)].astype(jnp.bfloat16)


def join_kernel(keep, mate, swap, near, mates, sems):
    copies = [
        pltpu.make_async_copy(mate, mates.at[0], sems.at[0]),
        pltpu.make_async_copy(swap.at[1], mates.at[1], sems.at[1]),
        pltpu.make_async_copy(keep, near.at[0], sems.at[2]),
        pltpu.make_async_copy(swap.at[0], near.at[1], sems.at[3]),
    ]
    for copy in copies:
        copy.start()
    for copy in copies:
        copy.wait()


def core_sum_kernel(own, received, mine, send):
    mine[...] = own[0] + received[0].astype(jnp.float32)
    send[...] = (own[1] + received[1].astype(jnp.float32)).astype(jnp.bfloat16)


def plane_sum_kernel(own, received, middle, up, extra):
    middle[...] = own[0] + received[0].astype(jnp.float32)
    up[...] = (own[1] + received[1].astype(jnp.float32)).astype(jnp.bfloat16)
    extra[...] = (own[2] + received[2].astype(jnp.float32)).astype(jnp.bfloat16)


def image_kernel(middle, up, extra, image):
    image[...] = middle[...] + up[...].astype(jnp.float32) + extra[...].astype(jnp.float32)


VMEM_SPEC = pl.BlockSpec(memory_space=pltpu.VMEM)
SMEM_SPEC = pl.BlockSpec(memory_space=pltpu.SMEM)
HBM_SPEC = pl.BlockSpec(memory_space=pl.ANY)


def near_vmem(*values):
    return [pltpu.with_memory_space_constraint(value, pltpu.VMEM) for value in values]


def local_call(kernel, name, outs, *values, scratch=()):
    return pl.pallas_call(
        kernel,
        in_specs=[VMEM_SPEC] * len(values),
        out_specs=[VMEM_SPEC] * len(outs),
        out_shape=outs,
        scratch_shapes=list(scratch),
        compiler_params=pltpu.CompilerParams(vmem_limit_bytes=LIMIT),
        name=name,
    )(*near_vmem(*values))


def early_call(table, keep, swap, mates, below, above, inv_all, steering, lag_range):
    rows, cols = keep.shape
    angles, group = steering.shape[1], lag_range.shape[2]
    rounds = steering.shape[0] - 1
    return pl.pallas_call(
        early_kernel,
        in_specs=[SMEM_SPEC] + [VMEM_SPEC] * 5 + [HBM_SPEC] + [VMEM_SPEC] * 2,
        out_specs=[VMEM_SPEC] * 3,
        out_shape=[
            pltpu.VMEM((3 * Q, rows, cols), jnp.bfloat16),
            pltpu.VMEM((cols, L), jnp.bfloat16),
            pltpu.VMEM((2 * Q, angles, group), jnp.float32),
        ],
        scratch_shapes=[
            pltpu.VMEM((2 * Q, L // cols, 2 * rounds, cols), jnp.float32),
            pltpu.SemaphoreType.DMA((6,)),
        ],
        compiler_params=pltpu.CompilerParams(vmem_limit_bytes=LIMIT),
        name="early_pairs",
    )(table, *near_vmem(keep, swap, mates, below, above), inv_all, *near_vmem(steering, lag_range))


def late_call(table, spec, inv, window, below, above, steering, lag_range):
    cols = spec.shape[2]
    angles, group = steering.shape[1], lag_range.shape[2]
    rounds = steering.shape[0] - 1
    piece = (2, 3, angles, group // 3)
    return pl.pallas_call(
        late_kernel,
        in_specs=[SMEM_SPEC] + [VMEM_SPEC] * 7,
        out_specs=[VMEM_SPEC] * 4,
        out_shape=[
            pltpu.VMEM(piece, jnp.float32),
            pltpu.VMEM(piece, jnp.bfloat16),
            pltpu.VMEM(spec.shape, spec.dtype),
            pltpu.VMEM(window.shape, window.dtype),
        ],
        input_output_aliases={1: 2, 3: 3},
        scratch_shapes=[
            pltpu.VMEM((2 * Q, L // cols, 2 * rounds, cols), jnp.float32),
            pltpu.VMEM((Q,) + piece[1:], jnp.float32),
            pltpu.SemaphoreType.DMA((2,)),
        ],
        compiler_params=pltpu.CompilerParams(vmem_limit_bytes=LIMIT),
        name="late_pairs",
    )(table, *near_vmem(spec, inv, window, below, above, steering, lag_range))[:2]


def exchange(value, devices, target):
    pairs = [(i, target(i)) for i in range(devices) if target(i) is not None]
    pairs = [(i, j) for i, j in pairs if 0 <= j < devices]
    return lax.ppermute(value, AXIS, pairs)


def per_device(devices, strain, steering, lag_range, pair_listed, band_used):
    def shift(value, by):
        return exchange(value, devices, lambda i: i + by)

    def flip(value, by):
        return exchange(value, devices, lambda i: i ^ by)

    keep, mate, swap = spectrum_call(strain, pair_listed, jnp.transpose(band_used, (0, 2, 1)))
    swap = flip(swap, 1)
    pair = pltpu.VMEM((2,) + keep.shape, keep.dtype)
    near, mates = local_call(
        join_kernel, "join", [pair, pair], keep, mate, swap, scratch=[pltpu.SemaphoreType.DMA((4,))]
    )
    mates = flip(mates, 2)
    near_below, near_above = shift(near, Q), shift(near, -Q)
    far_below, far_above = shift(mates, Q), shift(mates, -Q)
    early, late = (jnp.asarray(t.reshape(Q, -1)) for t in unit_table(steering.shape[0] - 1))
    inv_all = jnp.asarray(inverse_table(strain.shape[1]))
    spec, inv, window = early_call(
        early, keep, swap, mates, near_below, near_above, inv_all, steering, lag_range
    )
    mine, send = late_call(
        late, spec, inv, window, far_below, far_above, steering, lag_range
    )
    piece = mine.shape[1:]
    mine, send = local_call(
        core_sum_kernel,
        "core_sum",
        [pltpu.VMEM(piece, jnp.float32), pltpu.VMEM(piece, jnp.bfloat16)],
        mine,
        flip(send, 1),
    )
    middle, up, extra = local_call(
        plane_sum_kernel,
        "plane_sum",
        [pltpu.VMEM(piece[1:], dtype) for dtype in (jnp.float32, jnp.bfloat16, jnp.bfloat16)],
        mine,
        flip(send, 2),
    )

    def ends(i):
        if i % Q == 0:
            return i + 2 * Q
        if i % Q == Q - 1:
            return i - Q
        return None

    up, extra = shift(up, Q), exchange(extra, devices, ends)
    return local_call(
        image_kernel,
        "image",
        [jax.ShapeDtypeStruct(middle.shape, jnp.float32)],
        middle,
        up,
        extra,
    )[0]


def solution(mesh):
    return jax.shard_map(
        functools.partial(per_device, mesh.shape[AXIS]),
        mesh=mesh,
        in_specs=(
            P(("win", AXIS), None),
            P(),
            P(),
            P(("win", AXIS), None),
            P(("win", AXIS), None, None),
        ),
        out_specs=P(None, ("win", AXIS)),
        check_vma=False,
    )
```

time: 61.7 us -> 50.4 us (0.82)
  waiting for transfers between devices: 13.9 us -> 8.26 us
  other arithmetic: 3.68 us -> 0 us
  Pallas kernels: 16.1 us -> 15 us
  local copies, waits for them, and re-layouts: 2.11 us -> 1.35 us
    ppermute x10, waiting for transfers between devices: 13.9 us -> 8.26 us  [exchange(): return lax.ppermute(value, AXIS, pairs)]
    another operation x3 -> x0, other arithmetic: 2 us -> none  [the longest x1 1.03 us: per_device(): mates = flip(jnp.stack([mate, swap[1]]), 2)]
    add x2 -> x0, other arithmetic: 1.68 us -> none  [the longest x1 1.04 us: per_device(): mine = mine + flip(send, 1).astype(jnp.float32)]
    unnamed x13 -> x14, local copies, waits for them, and re-layouts: 2.07 us -> 1.35 us
    pallas_call x1, Pallas kernels: 4.17 us -> 3.49 us  [spectrum_call(): pl.pallas_call(spectrum_kernel, grid=(steps,), in_specs=[pl.BlockSpec(lis...]
    pallas_call x1 -> x6, Pallas kernels: 11.9 us -> 11.5 us  [the longest x1 5.9 us: early_call(): pl.pallas_call(early_kernel, in_specs=[SMEM_SPEC] + [VMEM_SPEC] * 5 + [HB...]
  transfers between devices with their start and end apart: 10 -> 10, of which waited for: 7 -> 5; matrix products, arithmetic and copies ran while one was open for 2% -> 0% of each run, Pallas kernels for 0% -> 12%
where the time goes in v3:
time: 50.4 us; the launch traced here: 50.1 us
  starting transfers between devices  25.3 us (50%)
  Pallas kernels  15 us (30%)
  waiting for transfers between devices  8.26 us (16%)
  local copies, waits for them, and re-layouts  1.35 us (3%)
    ppermute x10, starting transfers between devices, exchange(): return lax.ppermute(value, AXIS, pairs)  25.3 us
    ppermute x10, waiting for transfers between devices, exchange(): return lax.ppermute(value, AXIS, pairs)  8.26 us
    pallas_call x1, Pallas kernels, early_call(): pl.pallas_call(early_kernel, in_specs=[SMEM_SPEC] + [VMEM_SPEC] * 5 + [HB...  5.9 us
    pallas_call x1, Pallas kernels, late_call(): pl.pallas_call(late_kernel, in_specs=[SMEM_SPEC] + [VMEM_SPEC] * 7, out_s...  4.16 us
    pallas_call x1, Pallas kernels, spectrum_call(): pl.pallas_call(spectrum_kernel, grid=(steps,), in_specs=[pl.BlockSpec(lis...  3.49 us
    pallas_call x4, Pallas kernels, local_call(): pl.pallas_call(kernel, in_specs=[VMEM_SPEC] * len(values), out_specs=[VME...  1.42 us
    unnamed x14, local copies, waits for them, and re-layouts  1.35 us
  transfers between devices with their start and end apart: 10, of which 5 were waited for; matrix products, arithmetic and copies ran while one was open for 0% of the time, Pallas kernels for 12%

profile of v3, /device:TPU:0, one launch (start us, length us, event | category | flops | bytes accessed | tf_op | source)
XLA Modules:
  0.0 50.1 jit_solution(11468867688575990833)
XLA Ops:
  0.0 0.7 %copy-done.3 = s32[1,8,4]{1,2,0:T(4,128)S(1)} copy-done((s32[1,8,4]{1,2,0:T(4,128)S(1)}, s32[1,8,4]{1,2,0:T(4,128)}, u32[]{:S(2)}) %copy-start.3) | copy-done | bytes 152
  0.7 0.7 %copy-done.6 = s32[1,8]{1,0:T(1,128)S(1)} copy-done((s32[1,8]{1,0:T(1,128)S(1)}, s32[1,8]{1,0:T(1,128)}, u32[]{:S(2)}) %copy-start.6) | copy-done | bytes 56
  1.3 3.5 %spectrum.1 = (bf16[272,256]{1,0:T(8,128)(2,1)S(1)}, bf16[272,256]{1,0:T(8,128)(2,1)S(1)}, bf16[2,272,256]{2,1,0:T(8,128)(2,1)S(1)}) custom-call(s32[1,8]{1,0:T(1,128)S(1)} %copy-done.6, s32[1,4,8]{2,1,0:T(4,128)S(1)} %bitcast.1, bf16[256,4096]{1,0:T(8,128)(2,1)} %x3.1, bf16[256,4096]{1,0:T(8,128)(2,1)} %x3.1, bf16[256,4096]{1,0:T(8,128)(2,1)} %x3.1, ...), custom_call_target="tpu_custom_call" | custom-call | tf_op jit(solution)/shard_map/spectrum/pallas_call | solution.py:112
  4.8 0.6 %collective-permute-start = (bf16[2,272,256]{2,1,0:T(8,128)(2,1)S(1)}, bf16[2,272,256]{2,1,0:T(8,128)(2,1)S(1)}, u32[]{:S(2)}, u32[]{:S(2)}) collective-permute-start(bf16[2,272,256]{2,1,0:T(8,128)(2,1)S(1)} %get-tuple-element.21), channel_id=1, source_target_pairs={{0,1},{1,0},{2,3},{3,2},{4,5},{5,4},{6,7},{7,6},{8,9},{9,8},{10,11... | collective-permute-start | bytes 835592 | tf_op jit(solution)/shard_map/ppermute | solution.py:372
  5.4 1.2 %collective-permute-done.swap = bf16[2,272,256]{2,1,0:T(8,128)(2,1)S(1)} collective-permute-done((bf16[2,272,256]{2,1,0:T(8,128)(2,1)S(1)}, bf16[2,272,256]{2,1,0:T(8,128)(2,1)S(1)}, u32[]{:S(2)}, u32[]{:S(2)}) %collective-permute-start) | collective-permute-done | bytes 278560 | tf_op jit(solution)/shard_map/ppermute | solution.py:372
  6.6 0.7 %join.1 = (bf16[2,272,256]{2,1,0:T(8,128)(2,1)S(1)}, bf16[2,272,256]{2,1,0:T(8,128)(2,1)S(1)}) custom-call(bf16[272,256]{1,0:T(8,128)(2,1)S(1)} %get-tuple-element.20.keep, bf16[272,256]{1,0:T(8,128)(2,1)S(1)} %get-tuple-element.22.mate, bf16[2,272,256]{2,1,0:T(8,128)(2,1)S(1)} %collective-permute-done.swap), custom_call_target="tpu_custom_call" | custom-call | tf_op jit(solution)/shard_map/join/pallas_call | solution.py:310
  7.3 3.0 %collective-permute-start.1 = (bf16[2,272,256]{2,1,0:T(8,128)(2,1)S(1)}, bf16[2,272,256]{2,1,0:T(8,128)(2,1)S(1)}, u32[]{:S(2)}, u32[]{:S(2)}) collective-permute-start(bf16[2,272,256]{2,1,0:T(8,128)(2,1)S(1)} %get-tuple-element.23), channel_id=1, source_target_pairs={{0,2},{1,3},{2,0},{3,1},{4,6},{5,7},{6,4},{7,5},{8,10},{9,11},{10,... | collective-permute-start | bytes 835592 | tf_op jit(solution)/shard_map/ppermute | solution.py:372
  10.3 1.4 %collective-permute-start.3 = (bf16[2,272,256]{2,1,0:T(8,128)(2,1)S(1)}, bf16[2,272,256]{2,1,0:T(8,128)(2,1)S(1)}, u32[]{:S(2)}, u32[]{:S(2)}) collective-permute-start(bf16[2,272,256]{2,1,0:T(8,128)(2,1)S(1)} %get-tuple-element.24), channel_id=1, source_target_pairs={{4,0},{5,1},{6,2},{7,3},{8,4},{9,5},{10,6},{11,7},{12,8},{13,9},{1... | collective-permute-start | bytes 835592 | tf_op jit(solution)/shard_map/ppermute | solution.py:372
  11.7 4.6 %collective-permute-start.2 = (bf16[2,272,256]{2,1,0:T(8,128)(2,1)S(1)}, bf16[2,272,256]{2,1,0:T(8,128)(2,1)S(1)}, u32[]{:S(2)}, u32[]{:S(2)}) collective-permute-start(bf16[2,272,256]{2,1,0:T(8,128)(2,1)S(1)} %get-tuple-element.24), channel_id=1, source_target_pairs={{0,4},{1,5},{2,6},{3,7},{4,8},{5,9},{6,10},{7,11},{8,12},{9,13},{1... | collective-permute-start | bytes 835592 | tf_op jit(solution)/shard_map/ppermute | solution.py:372
  16.3 1.0 %collective-permute-done.1.mates = bf16[2,272,256]{2,1,0:T(8,128)(2,1)S(1)} collective-permute-done((bf16[2,272,256]{2,1,0:T(8,128)(2,1)S(1)}, bf16[2,272,256]{2,1,0:T(8,128)(2,1)S(1)}, u32[]{:S(2)}, u32[]{:S(2)}) %collective-permute-start.1) | collective-permute-done | bytes 278560 | tf_op jit(solution)/shard_map/ppermute | solution.py:372
  17.2 1.3 %collective-permute-start.5 = (bf16[2,272,256]{2,1,0:T(8,128)(2,1)S(1)}, bf16[2,272,256]{2,1,0:T(8,128)(2,1)S(1)}, u32[]{:S(2)}, u32[]{:S(2)}) collective-permute-start(bf16[2,272,256]{2,1,0:T(8,128)(2,1)S(1)} %collective-permute-done.1.mates), channel_id=1, source_target_pairs={{4,0},{5,1},{6,2},{7,3},{8,4},{9,5},{10,6},{11,7},{12,8},{13,9},{1... | collective-permute-start | bytes 835592 | tf_op jit(solution)/shard_map/ppermute | solution.py:372
  18.5 4.6 %collective-permute-start.4 = (bf16[2,272,256]{2,1,0:T(8,128)(2,1)S(1)}, bf16[2,272,256]{2,1,0:T(8,128)(2,1)S(1)}, u32[]{:S(2)}, u32[]{:S(2)}) collective-permute-start(bf16[2,272,256]{2,1,0:T(8,128)(2,1)S(1)} %collective-permute-done.1.mates), channel_id=1, source_target_pairs={{0,4},{1,5},{2,6},{3,7},{4,8},{5,9},{6,10},{7,11},{8,12},{9,13},{1... | collective-permute-start | bytes 835592 | tf_op jit(solution)/shard_map/ppermute | solution.py:372
  23.1 0.0 collective-permute-done.3.above
  23.1 0.0 collective-permute-done.2.below
  23.1 0.0 copy-done
  23.1 0.0 copy-done.1
  23.1 0.0 copy-done.2
  23.1 0.0 copy-done.5
  23.2 5.9 %early_pairs.1 = (bf16[12,272,256]{2,1,0:T(8,128)(2,1)S(1)}, bf16[256,512]{1,0:T(8,128)(2,1)S(1)}, f32[8,128,384]{2,1,0:T(8,128)S(1)}) custom-call(s32[4,126]{1,0:T(4,128)S(1)} %copy-done.5, bf16[272,256]{1,0:T(8,128)(2,1)S(1)} %get-tuple-element.20.keep, bf16[2,272,256]{2,1,0:T(8,128)(2,1)S(1)} %collective-permute-done.swap, ...), custom_call_target="tpu_custom_call" | custom-call | tf_op jit(solution)/shard_map/early_pairs/pallas_call | solution.py:325
  29.1 0.0 collective-permute-done.5.above
  29.1 0.0 collective-permute-done.4.below
  29.1 0.0 copy-done.4
  29.1 4.2 %late_pairs.1 = (f32[2,3,128,128]{3,2,1,0:T(8,128)S(1)}, bf16[2,3,128,128]{3,2,1,0:T(8,128)(2,1)S(1)}, bf16[12,272,256]{2,1,0:T(8,128)(2,1)S(1)}, f32[8,128,384]{2,1,0:T(8,128)S(1)}) custom-call(s32[4,90]{1,0:T(4,128)S(1)} %copy-done.4, bf16[12,272,256]{2,1,0:T(8,128)(2,1)S(1)} %get-tuple-element.25.spec_in, ...), custom_call_target="tpu_custom_call", output_to_operand_aliasing={{2}: (1, {}), {3}: (3, {})} | custom-call | tf_op jit(solution)/shard_map/late_pairs/pallas_call | solution.py:348
  33.3 0.1 collective-permute-start.6
  33.3 1.4 %collective-permute-done.6.received = bf16[2,3,128,128]{3,2,1,0:T(8,128)(2,1)S(1)} collective-permute-done((bf16[2,3,128,128]{3,2,1,0:T(8,128)(2,1)S(1)}, bf16[2,3,128,128]{3,2,1,0:T(8,128)(2,1)S(1)}, u32[]{:S(2)}, u32[]{:S(2)}) %collective-permute-start.6) | collective-permute-done | bytes 196640 | tf_op jit(solution)/shard_map/ppermute | solution.py:372
  34.8 1.8 %collective-permute-start.7 = (bf16[3,128,128]{2,1,0:T(8,128)(2,1)S(1)}, bf16[3,128,128]{2,1,0:T(8,128)(2,1)S(1)}, u32[]{:S(2)}, u32[]{:S(2)}) collective-permute-start(bf16[3,128,128]{2,1,0:T(8,128)(2,1)S(1)} %get-tuple-element.31), channel_id=1, source_target_pairs={{0,2},{1,3},{2,0},{3,1},{4,6},{5,7},{6,4},{7,5},{8,10},{9,11},{10,... | collective-permute-start | bytes 294920 | tf_op jit(solution)/shard_map/ppermute | solution.py:372
  36.6 3.1 %collective-permute-done.7.received = bf16[3,128,128]{2,1,0:T(8,128)(2,1)S(1)} collective-permute-done((bf16[3,128,128]{2,1,0:T(8,128)(2,1)S(1)}, bf16[3,128,128]{2,1,0:T(8,128)(2,1)S(1)}, u32[]{:S(2)}, u32[]{:S(2)}) %collective-permute-start.7) | collective-permute-done | bytes 98336 | tf_op jit(solution)/shard_map/ppermute | solution.py:372
  39.7 3.7 %collective-permute-start.8 = (bf16[128,128]{1,0:T(8,128)(2,1)S(1)}, bf16[128,128]{1,0:T(8,128)(2,1)S(1)}, u32[]{:S(2)}, u32[]{:S(2)}) collective-permute-start(bf16[128,128]{1,0:T(8,128)(2,1)S(1)} %get-tuple-element.33), channel_id=1, source_target_pairs={{0,4},{1,5},{2,6},{3,7},{4,8},{5,9},{6,10},{7,11},{8,12},{9,13},{1... | collective-permute-start | bytes 98312 | tf_op jit(solution)/shard_map/ppermute | solution.py:372
  43.4 4.4 %collective-permute-start.9 = (bf16[128,128]{1,0:T(8,128)(2,1)S(1)}, bf16[128,128]{1,0:T(8,128)(2,1)S(1)}, u32[]{:S(2)}, u32[]{:S(2)}) collective-permute-start(bf16[128,128]{1,0:T(8,128)(2,1)S(1)} %get-tuple-element.34), channel_id=1, source_target_pairs={{0,8},{4,12},{7,3},{11,7},{15,11},{16,24},{20,28},{23,19},{27,23},... | collective-permute-start | bytes 98312 | tf_op jit(solution)/shard_map/ppermute | solution.py:372
  47.9 0.0 collective-permute-done.8.up
  47.9 1.6 %collective-permute-done.9.extra = bf16[128,128]{1,0:T(8,128)(2,1)S(1)} collective-permute-done((bf16[128,128]{1,0:T(8,128)(2,1)S(1)}, bf16[128,128]{1,0:T(8,128)(2,1)S(1)}, u32[]{:S(2)}, u32[]{:S(2)}) %collective-permute-start.9) | collective-permute-done | bytes 32800 | tf_op jit(solution)/shard_map/ppermute | solution.py:372
  49.5 0.6 %image.1 = f32[128,128]{1,0:T(8,128)} custom-call(f32[128,128]{1,0:T(8,128)S(1)} %get-tuple-element.32.middle, bf16[128,128]{1,0:T(8,128)(2,1)S(1)} %collective-permute-done.8.up, bf16[128,128]{1,0:T(8,128)(2,1)S(1)} %collective-permute-done.9.extra), custom_call_target="tpu_custom_call" | custom-call | tf_op jit(solution)/shard_map/image/pallas_call | solution.py:310
  (9 shorter events, 0.1 us)
Async XLA Ops:
  0.0 0.7 %copy-start.3 = (s32[1,8,4]{1,2,0:T(4,128)S(1)}, s32[1,8,4]{1,2,0:T(4,128)}, u32[]{:S(2)}) copy-start(s32[1,8,4]{1,2,0:T(4,128)} %param.13) | copy-start | bytes 388
  0.7 0.7 %copy-start.6 = (s32[1,8]{1,0:T(1,128)S(1)}, s32[1,8]{1,0:T(1,128)}, u32[]{:S(2)}) copy-start(s32[1,8]{1,0:T(1,128)} %listed.1) | copy-start | bytes 100
  1.3 21.8 %copy-start = (bf16[9,512,384]{2,1,0:T(8,128)(2,1)S(1)}, bf16[9,512,384]{2,1,0:T(8,128)(2,1)}, u32[]{:S(2)}) copy-start(bf16[9,512,384]{2,1,0:T(8,128)(2,1)} %lag_range.3) | copy-start | bytes 10616836
  1.3 21.8 %copy-start.1 = (bf16[9,128,256]{2,1,0:T(8,128)(2,1)S(1)}, bf16[9,128,256]{2,1,0:T(8,128)(2,1)}, u32[]{:S(2)}) copy-start(bf16[9,128,256]{2,1,0:T(8,128)(2,1)} %steering.3) | copy-start | bytes 1769476
  1.3 21.8 %copy-start.2 = (bf16[4,256,512]{2,1,0:T(8,128)(2,1)S(1)}, bf16[4,256,512]{2,1,0:T(8,128)(2,1)}, u32[]{:S(2)}) copy-start(bf16[4,256,512]{2,1,0:T(8,128)(2,1)} %constant.11.clone.inv_all) | copy-start | bytes 3145732
  1.3 21.8 %copy-start.5 = (s32[4,126]{1,0:T(4,128)S(1)}, s32[4,126]{1,0:T(4,128)}, u32[]{:S(2)}) copy-start(s32[4,126]{1,0:T(4,128)} %constant.9.clone.table) | copy-start | bytes 6052
  4.8 1.7 %collective-permute-start = (bf16[2,272,256]{2,1,0:T(8,128)(2,1)S(1)}, bf16[2,272,256]{2,1,0:T(8,128)(2,1)S(1)}, u32[]{:S(2)}, u32[]{:S(2)}) collective-permute-start(bf16[2,272,256]{2,1,0:T(8,128)(2,1)S(1)} %get-tuple-element.21), channel_id=1, source_target_pairs={{0,1},{1,0},{2,3},{3,2},{4,5},{5,4},{6,7},{7,6},{8,9},{9,8},{10,11... | collective-permute-start | bytes 835592 | tf_op jit(solution)/shard_map/ppermute | solution.py:372
  7.3 9.9 %collective-permute-start.1 = (bf16[2,272,256]{2,1,0:T(8,128)(2,1)S(1)}, bf16[2,272,256]{2,1,0:T(8,128)(2,1)S(1)}, u32[]{:S(2)}, u32[]{:S(2)}) collective-permute-start(bf16[2,272,256]{2,1,0:T(8,128)(2,1)S(1)} %get-tuple-element.23), channel_id=1, source_target_pairs={{0,2},{1,3},{2,0},{3,1},{4,6},{5,7},{6,4},{7,5},{8,10},{9,11},{10,... | collective-permute-start | bytes 835592 | tf_op jit(solution)/shard_map/ppermute | solution.py:372
  10.3 18.8 %copy-start.4 = (s32[4,90]{1,0:T(4,128)S(1)}, s32[4,90]{1,0:T(4,128)}, u32[]{:S(2)}) copy-start(s32[4,90]{1,0:T(4,128)} %constant.10.clone.table) | copy-start | bytes 4324
  10.3 12.8 %collective-permute-start.3 = (bf16[2,272,256]{2,1,0:T(8,128)(2,1)S(1)}, bf16[2,272,256]{2,1,0:T(8,128)(2,1)S(1)}, u32[]{:S(2)}, u32[]{:S(2)}) collective-permute-start(bf16[2,272,256]{2,1,0:T(8,128)(2,1)S(1)} %get-tuple-element.24), channel_id=1, source_target_pairs={{4,0},{5,1},{6,2},{7,3},{8,4},{9,5},{10,6},{11,7},{12,8},{13,9},{1... | collective-permute-start | bytes 835592 | tf_op jit(solution)/shard_map/ppermute | solution.py:372
  11.7 11.4 %collective-permute-start.2 = (bf16[2,272,256]{2,1,0:T(8,128)(2,1)S(1)}, bf16[2,272,256]{2,1,0:T(8,128)(2,1)S(1)}, u32[]{:S(2)}, u32[]{:S(2)}) collective-permute-start(bf16[2,272,256]{2,1,0:T(8,128)(2,1)S(1)} %get-tuple-element.24), channel_id=1, source_target_pairs={{0,4},{1,5},{2,6},{3,7},{4,8},{5,9},{6,10},{7,11},{8,12},{9,13},{1... | collective-permute-start | bytes 835592 | tf_op jit(solution)/shard_map/ppermute | solution.py:372
  17.2 11.8 %collective-permute-start.5 = (bf16[2,272,256]{2,1,0:T(8,128)(2,1)S(1)}, bf16[2,272,256]{2,1,0:T(8,128)(2,1)S(1)}, u32[]{:S(2)}, u32[]{:S(2)}) collective-permute-start(bf16[2,272,256]{2,1,0:T(8,128)(2,1)S(1)} %collective-permute-done.1.mates), channel_id=1, source_target_pairs={{4,0},{5,1},{6,2},{7,3},{8,4},{9,5},{10,6},{11,7},{12,8},{13,9},{1... | collective-permute-start | bytes 835592 | tf_op jit(solution)/shard_map/ppermute | solution.py:372
  18.5 10.6 %collective-permute-start.4 = (bf16[2,272,256]{2,1,0:T(8,128)(2,1)S(1)}, bf16[2,272,256]{2,1,0:T(8,128)(2,1)S(1)}, u32[]{:S(2)}, u32[]{:S(2)}) collective-permute-start(bf16[2,272,256]{2,1,0:T(8,128)(2,1)S(1)} %collective-permute-done.1.mates), channel_id=1, source_target_pairs={{0,4},{1,5},{2,6},{3,7},{4,8},{5,9},{6,10},{7,11},{8,12},{9,13},{1... | collective-permute-start | bytes 835592 | tf_op jit(solution)/shard_map/ppermute | solution.py:372
  33.3 1.5 %collective-permute-start.6 = (bf16[2,3,128,128]{3,2,1,0:T(8,128)(2,1)S(1)}, bf16[2,3,128,128]{3,2,1,0:T(8,128)(2,1)S(1)}, u32[]{:S(2)}, u32[]{:S(2)}) collective-permute-start(bf16[2,3,128,128]{3,2,1,0:T(8,128)(2,1)S(1)} %get-tuple-element.29), channel_id=1, source_target_pairs={{0,1},{1,0},{2,3},{3,2},{4,5},{5,4},{6,7},{7,6},{8,9},{9,8},{10,11... | collective-permute-start | bytes 589832 | tf_op jit(solution)/shard_map/ppermute | solution.py:372
  34.8 4.9 %collective-permute-start.7 = (bf16[3,128,128]{2,1,0:T(8,128)(2,1)S(1)}, bf16[3,128,128]{2,1,0:T(8,128)(2,1)S(1)}, u32[]{:S(2)}, u32[]{:S(2)}) collective-permute-start(bf16[3,128,128]{2,1,0:T(8,128)(2,1)S(1)} %get-tuple-element.31), channel_id=1, source_target_pairs={{0,2},{1,3},{2,0},{3,1},{4,6},{5,7},{6,4},{7,5},{8,10},{9,11},{10,... | collective-permute-start | bytes 294920 | tf_op jit(solution)/shard_map/ppermute | solution.py:372
  39.7 8.2 %collective-permute-start.8 = (bf16[128,128]{1,0:T(8,128)(2,1)S(1)}, bf16[128,128]{1,0:T(8,128)(2,1)S(1)}, u32[]{:S(2)}, u32[]{:S(2)}) collective-permute-start(bf16[128,128]{1,0:T(8,128)(2,1)S(1)} %get-tuple-element.33), channel_id=1, source_target_pairs={{0,4},{1,5},{2,6},{3,7},{4,8},{5,9},{6,10},{7,11},{8,12},{9,13},{1... | collective-permute-start | bytes 98312 | tf_op jit(solution)/shard_map/ppermute | solution.py:372
  43.4 6.0 %collective-permute-start.9 = (bf16[128,128]{1,0:T(8,128)(2,1)S(1)}, bf16[128,128]{1,0:T(8,128)(2,1)S(1)}, u32[]{:S(2)}, u32[]{:S(2)}) collective-permute-start(bf16[128,128]{1,0:T(8,128)(2,1)S(1)} %get-tuple-element.34), channel_id=1, source_target_pairs={{0,8},{4,12},{7,3},{11,7},{15,11},{16,24},{20,28},{23,19},{27,23},... | collective-permute-start | bytes 98312 | tf_op jit(solution)/shard_map/ppermute | solution.py:372

commit v4 on v3

--- a/solution.py
+++ b/solution.py
@@ -40,7 +40,7 @@
     return jnp.dot(a, b, preferred_element_type=jnp.float32)
 
 
-def spectrum_kernel(listed, bands, x0, x1, x2, x3, table, keep, mate, swap, acc, weight):
+def spectrum_kernel(listed, bands, x0, x1, x2, x3, table, near, mates, swap, acc, weight):
     step, steps = pl.program_id(0), pl.num_programs(0)
     half = table.shape[2] // 2
     channels = x0.shape[0]
@@ -76,7 +76,7 @@
         p1, b1, s2, p3, b3, s0 = (acc[n] + part for n, part in enumerate(parts))
         s1 = jnp.concatenate([p1[:, :half] + b1[:, half:], p1[:, half:] - b1[:, :half]], axis=1)
         s3 = jnp.concatenate([p3[:, :half] - b3[:, half:], p3[:, half:] + b3[:, :half]], axis=1)
-        outs = (keep, swap.at[0], mate, swap.at[1])
+        outs = (near.at[0], swap.at[0], mates.at[0], swap.at[1])
         for s, value in enumerate((s1, s2, s3, s0)):
             value = value.astype(jnp.bfloat16)
             for p, out in enumerate(outs):
@@ -85,7 +85,7 @@
                 def _():
                     out[:channels, :] = value
 
-        cols = keep.shape[1]
+        cols = near.shape[2]
         nbands, rounds = bands.shape[1], bands.shape[2]
         width = L // nbands
         used = (listed[...] * bands[0]).astype(jnp.float32)
@@ -120,8 +120,8 @@
         ],
         out_specs=[pl.BlockSpec(memory_space=pltpu.VMEM)] * 3,
         out_shape=[
-            pltpu.VMEM((rows, cols), jnp.bfloat16),
-            pltpu.VMEM((rows, cols), jnp.bfloat16),
+            pltpu.VMEM((2, rows, cols), jnp.bfloat16),
+            pltpu.VMEM((2, rows, cols), jnp.bfloat16),
             pltpu.VMEM((2, rows, cols), jnp.bfloat16),
         ],
         scratch_shapes=[
@@ -132,7 +132,7 @@
             dimension_semantics=("arbitrary",), vmem_limit_bytes=LIMIT
         ),
         name="spectrum",
-    )(listed, bands, *[in_hbm(strain)] * Q, in_hbm(jnp.asarray(table)))
+    )(in_hbm(listed), in_hbm(bands), *[in_hbm(strain)] * Q, in_hbm(jnp.asarray(table)))
 
 
 UNROLL = 3
@@ -200,49 +200,34 @@
 
 
 def early_kernel(
-    table, keep, swap, mates, below, above, inv_all, steering, lag_range,
-    spec, inv, window, mask, sems,
+    table, near, mates, below, above, inv, steering, lag_range, spec, window, mask
 ):
     me = lax.rem(lax.axis_index(AXIS), Q)
-    copies = [
-        pltpu.make_async_copy(keep, spec.at[0], sems.at[0]),
-        pltpu.make_async_copy(swap.at[0], spec.at[1], sems.at[1]),
-        pltpu.make_async_copy(mates, spec.at[2:4], sems.at[2]),
-        pltpu.make_async_copy(below, spec.at[Q : Q + 2], sems.at[3]),
-        pltpu.make_async_copy(above, spec.at[2 * Q : 2 * Q + 2], sems.at[4]),
-        pltpu.make_async_copy(inv_all.at[me], inv, sems.at[5]),
-    ]
-    for copy in copies:
-        copy.start()
+    spec[0:2] = near[...]
+    spec[2:4] = mates[...]
+    spec[Q : Q + 2] = below[...]
+    spec[2 * Q : 2 * Q + 2] = above[...]
     window[...] = jnp.zeros_like(window)
-    for copy in copies:
-        copy.wait()
     channels = steering.shape[2]
     for p in range(Q):
         fill_mask(mask, p, spec, p, channels)
     for p in range(Q // 2):
         fill_mask(mask, Q + p, spec, 2 * Q + p, channels)
-    run_units(table, me, spec, mask, steering, inv, lag_range, window)
+    run_units(table, me, spec, mask, steering, inv.at[me], lag_range, window)
 
 
 def late_kernel(
-    table, spec_in, inv, window_in, below, above, steering, lag_range,
-    own, send, spec, window, mask, segs, sems,
+    table, spec_in, window_in, below, above, inv, steering, lag_range,
+    keep, send, spec, window, mask,
 ):
     me = lax.rem(lax.axis_index(AXIS), Q)
-    copies = [
-        pltpu.make_async_copy(below, spec.at[Q + 2 : Q + 4], sems.at[0]),
-        pltpu.make_async_copy(above, spec.at[2 * Q + 2 : 2 * Q + 4], sems.at[1]),
-    ]
-    for copy in copies:
-        copy.start()
-    for copy in copies:
-        copy.wait()
-    channels, angles = steering.shape[2], steering.shape[1]
+    spec[Q + 2 : Q + 4] = below[...]
+    spec[2 * Q + 2 : 2 * Q + 4] = above[...]
+    channels = steering.shape[2]
     for p in range(Q):
         fill_mask(mask, p, spec, p, channels)
         fill_mask(mask, Q + p, spec, 2 * Q + p, channels)
-    run_units(table, me, spec, mask, steering, inv, lag_range, window)
+    run_units(table, me, spec, mask, steering, inv.at[me], lag_range, window)
 
     width = window.shape[2] // 3
 
@@ -254,47 +239,88 @@
                 total = value if total is None else total + value
         return total
 
-    for p in range(Q):
-        segs[p, 0] = segment(p)
-        segs[p, 1] = segment(Q + p)
-        if p == 0:
-            segs[p, 2] = segment(2 * Q)
-        elif p == Q - 1:
-            segs[p, 2] = segment(-1)
-        else:
-            segs[p, 2] = jnp.zeros((angles, width), jnp.float32)
-    own[0] = segs[me]
-    own[1] = segs[lax.bitwise_xor(me, 2)]
-    send[0] = segs[lax.bitwise_xor(me, 1)].astype(jnp.bfloat16)
-    send[1] = segs[lax.bitwise_xor(me, 3)].astype(jnp.bfloat16)
-
-
-def join_kernel(keep, mate, swap, near, mates, sems):
-    copies = [
-        pltpu.make_async_copy(mate, mates.at[0], sems.at[0]),
-        pltpu.make_async_copy(swap.at[1], mates.at[1], sems.at[1]),
-        pltpu.make_async_copy(keep, near.at[0], sems.at[2]),
-        pltpu.make_async_copy(swap.at[0], near.at[1], sems.at[3]),
-    ]
-    for copy in copies:
-        copy.start()
-    for copy in copies:
-        copy.wait()
-
-
-def core_sum_kernel(own, received, mine, send):
-    mine[...] = own[0] + received[0].astype(jnp.float32)
-    send[...] = (own[1] + received[1].astype(jnp.float32)).astype(jnp.bfloat16)
-
-
-def plane_sum_kernel(own, received, middle, up, extra):
-    middle[...] = own[0] + received[0].astype(jnp.float32)
-    up[...] = (own[1] + received[1].astype(jnp.float32)).astype(jnp.bfloat16)
-    extra[...] = (own[2] + received[2].astype(jnp.float32)).astype(jnp.bfloat16)
-
-
-def image_kernel(middle, up, extra, image):
-    image[...] = middle[...] + up[...].astype(jnp.float32) + extra[...].astype(jnp.float32)
+    core = lax.rem(me, 2)
+    here = [segment(s) for s in list(range(Q)) + [2 * Q, -1]]
+    there = [segment(Q + p) for p in range(Q)]
+
+    @pl.when(core == 0)
+    def _():
+        for n, value in enumerate(there):
+            keep[n] = value
+        for n in range(Q, Q + 2):
+            keep[n] = jnp.zeros_like(there[0])
+        for n, value in enumerate(here):
+            send[n] = value.astype(jnp.bfloat16)
+
+    @pl.when(core == 1)
+    def _():
+        for n, value in enumerate(here):
+            keep[n] = value
+        for n, value in enumerate(there):
+            send[n] = value.astype(jnp.bfloat16)
+        for n in range(Q, Q + 2):
+            send[n] = jnp.zeros_like(there[0]).astype(jnp.bfloat16)
+
+
+def join_kernel(swap, near_in, mates_in, near, mates):
+    near[1] = swap[0]
+    mates[1] = swap[1]
+
+
+def core_sum_kernel(kept, received, mine, send):
+    side = lax.rem(lax.axis_index(AXIS), Q) // 2
+
+    def total(n):
+        return kept[n] + received[n].astype(jnp.float32)
+
+    for n in range(2):
+        mine[n] = total(2 * side + n)
+        send[n] = total(2 * (1 - side) + n).astype(jnp.bfloat16)
+    mine[2] = total(Q + side)
+    send[2] = total(Q + 1 - side).astype(jnp.bfloat16)
+
+
+def plane_sum_kernel(kept, received, mine, send):
+    core = lax.rem(lax.axis_index(AXIS), 2)
+    totals = [kept[n] + received[n].astype(jnp.float32) for n in range(3)]
+    mine[0] = totals[0]
+    mine[1] = totals[1]
+
+    @pl.when(core == 0)
+    def _():
+        send[0] = totals[0].astype(jnp.bfloat16)
+        send[1] = totals[1].astype(jnp.bfloat16)
+
+    @pl.when(core == 1)
+    def _():
+        send[0] = totals[2].astype(jnp.bfloat16)
+        send[1] = jnp.zeros_like(totals[2]).astype(jnp.bfloat16)
+
+
+def end_sum_kernel(kept, received, mine, send):
+    me = lax.rem(lax.axis_index(AXIS), Q)
+    first = received[0].astype(jnp.float32)
+    second = received[1].astype(jnp.float32)
+    core, side = lax.rem(me, 2), me // 2
+
+    @pl.when(core == 0)
+    def _():
+        mine[...] = first
+        send[...] = second
+
+    @pl.when((core == 1) & (side == 0))
+    def _():
+        mine[...] = kept[1]
+        send[...] = kept[0] + first
+
+    @pl.when((core == 1) & (side == 1))
+    def _():
+        mine[...] = kept[1] + first
+        send[...] = kept[0]
+
+
+def image_kernel(kept, received, image):
+    image[...] = kept[...] + received[...]
 
 
 VMEM_SPEC = pl.BlockSpec(memory_space=pltpu.VMEM)
@@ -306,64 +332,56 @@
     return [pltpu.with_memory_space_constraint(value, pltpu.VMEM) for value in values]
 
 
-def local_call(kernel, name, outs, *values, scratch=()):
+def local_call(kernel, name, outs, *values, aliases={}):
     return pl.pallas_call(
         kernel,
         in_specs=[VMEM_SPEC] * len(values),
         out_specs=[VMEM_SPEC] * len(outs),
         out_shape=outs,
-        scratch_shapes=list(scratch),
+        input_output_aliases=aliases,
         compiler_params=pltpu.CompilerParams(vmem_limit_bytes=LIMIT),
         name=name,
     )(*near_vmem(*values))
 
 
-def early_call(table, keep, swap, mates, below, above, inv_all, steering, lag_range):
-    rows, cols = keep.shape
+def early_call(table, near, mates, below, above, inv, steering, lag_range):
+    _, rows, cols = near.shape
     angles, group = steering.shape[1], lag_range.shape[2]
     rounds = steering.shape[0] - 1
     return pl.pallas_call(
         early_kernel,
-        in_specs=[SMEM_SPEC] + [VMEM_SPEC] * 5 + [HBM_SPEC] + [VMEM_SPEC] * 2,
-        out_specs=[VMEM_SPEC] * 3,
+        in_specs=[SMEM_SPEC] + [VMEM_SPEC] * 7,
+        out_specs=[VMEM_SPEC] * 2,
         out_shape=[
             pltpu.VMEM((3 * Q, rows, cols), jnp.bfloat16),
-            pltpu.VMEM((cols, L), jnp.bfloat16),
             pltpu.VMEM((2 * Q, angles, group), jnp.float32),
         ],
-        scratch_shapes=[
-            pltpu.VMEM((2 * Q, L // cols, 2 * rounds, cols), jnp.float32),
-            pltpu.SemaphoreType.DMA((6,)),
-        ],
+        scratch_shapes=[pltpu.VMEM((2 * Q, L // cols, 2 * rounds, cols), jnp.float32)],
         compiler_params=pltpu.CompilerParams(vmem_limit_bytes=LIMIT),
         name="early_pairs",
-    )(table, *near_vmem(keep, swap, mates, below, above), inv_all, *near_vmem(steering, lag_range))
-
-
-def late_call(table, spec, inv, window, below, above, steering, lag_range):
+    )(table, *near_vmem(near, mates, below, above, inv, steering, lag_range))
+
+
+def late_call(table, spec, window, below, above, inv, steering, lag_range):
     cols = spec.shape[2]
     angles, group = steering.shape[1], lag_range.shape[2]
     rounds = steering.shape[0] - 1
-    piece = (2, 3, angles, group // 3)
+    pieces = (Q + 2, angles, group // 3)
     return pl.pallas_call(
         late_kernel,
         in_specs=[SMEM_SPEC] + [VMEM_SPEC] * 7,
         out_specs=[VMEM_SPEC] * 4,
         out_shape=[
-            pltpu.VMEM(piece, jnp.float32),
-            pltpu.VMEM(piece, jnp.bfloat16),
+            pltpu.VMEM(pieces, jnp.float32),
+            pltpu.VMEM(pieces, jnp.bfloat16),
             pltpu.VMEM(spec.shape, spec.dtype),
             pltpu.VMEM(window.shape, window.dtype),
         ],
-        input_output_aliases={1: 2, 3: 3},
-        scratch_shapes=[
-            pltpu.VMEM((2 * Q, L // cols, 2 * rounds, cols), jnp.float32),
-            pltpu.VMEM((Q,) + piece[1:], jnp.float32),
-            pltpu.SemaphoreType.DMA((2,)),
-        ],
+        input_output_aliases={1: 2, 2: 3},
+        scratch_shapes=[pltpu.VMEM((2 * Q, L // cols, 2 * rounds, cols), jnp.float32)],
         compiler_params=pltpu.CompilerParams(vmem_limit_bytes=LIMIT),
         name="late_pairs",
-    )(table, *near_vmem(spec, inv, window, below, above, steering, lag_range))[:2]
+    )(table, *near_vmem(spec, window, below, above, inv, steering, lag_range))[:2]
 
 
 def exchange(value, devices, target):
@@ -379,54 +397,55 @@
     def flip(value, by):
         return exchange(value, devices, lambda i: i ^ by)
 
-    keep, mate, swap = spectrum_call(strain, pair_listed, jnp.transpose(band_used, (0, 2, 1)))
-    swap = flip(swap, 1)
-    pair = pltpu.VMEM((2,) + keep.shape, keep.dtype)
+    near, mates, swap = spectrum_call(strain, pair_listed, jnp.transpose(band_used, (0, 2, 1)))
+    joined = pltpu.VMEM(near.shape, near.dtype)
     near, mates = local_call(
-        join_kernel, "join", [pair, pair], keep, mate, swap, scratch=[pltpu.SemaphoreType.DMA((4,))]
+        join_kernel, "join", [joined, joined], flip(swap, 1), near, mates, aliases={1: 0, 2: 1}
     )
     mates = flip(mates, 2)
     near_below, near_above = shift(near, Q), shift(near, -Q)
     far_below, far_above = shift(mates, Q), shift(mates, -Q)
     early, late = (jnp.asarray(t.reshape(Q, -1)) for t in unit_table(steering.shape[0] - 1))
-    inv_all = jnp.asarray(inverse_table(strain.shape[1]))
-    spec, inv, window = early_call(
-        early, keep, swap, mates, near_below, near_above, inv_all, steering, lag_range
-    )
-    mine, send = late_call(
-        late, spec, inv, window, far_below, far_above, steering, lag_range
-    )
-    piece = mine.shape[1:]
-    mine, send = local_call(
+    inv = jnp.asarray(inverse_table(strain.shape[1]))
+    shared = (inv, steering, lag_range)
+    spec, window = early_call(early, near, mates, near_below, near_above, *shared)
+    kept, send = late_call(late, spec, window, far_below, far_above, *shared)
+
+    def pieces(count, dtype):
+        return pltpu.VMEM(((count,) if count else ()) + kept.shape[1:], dtype)
+
+    def ends(i):
+        if i % 2 == 0:
+            return i + Q
+        return i + 2 * Q if i % Q < 2 else i - Q
+
+    kept, send = local_call(
         core_sum_kernel,
         "core_sum",
-        [pltpu.VMEM(piece, jnp.float32), pltpu.VMEM(piece, jnp.bfloat16)],
-        mine,
+        [pieces(3, jnp.float32), pieces(3, jnp.bfloat16)],
+        kept,
         flip(send, 1),
     )
-    middle, up, extra = local_call(
+    kept, send = local_call(
         plane_sum_kernel,
         "plane_sum",
-        [pltpu.VMEM(piece[1:], dtype) for dtype in (jnp.float32, jnp.bfloat16, jnp.bfloat16)],
-        mine,
+        [pieces(2, jnp.float32), pieces(2, jnp.bfloat16)],
+        kept,
         flip(send, 2),
     )
-
-    def ends(i):
-        if i % Q == 0:
-            return i + 2 * Q
-        if i % Q == Q - 1:
-            return i - Q
-        return None
-
-    up, extra = shift(up, Q), exchange(extra, devices, ends)
+    kept, send = local_call(
+        end_sum_kernel,
+        "end_sum",
+        [pieces(0, jnp.float32), pieces(0, jnp.float32)],
+        kept,
+        exchange(send, devices, ends),
+    )
     return local_call(
         image_kernel,
         "image",
-        [jax.ShapeDtypeStruct(middle.shape, jnp.float32)],
-        middle,
-        up,
-        extra,
+        [jax.ShapeDtypeStruct(kept.shape, jnp.float32)],
+        kept,
+        flip(send, 1),
     )[0]
 
 

time: 50.4 us -> 45.7 us (0.907)
  starting transfers between devices: 25.3 us -> 21.4 us
  waiting for transfers between devices: 8.26 us -> 9.82 us
  local copies, waits for them, and re-layouts: 1.35 us -> 0.02 us
  Pallas kernels: 15 us -> 13.8 us
    ppermute x10, starting transfers between devices: 25.3 us -> 21.4 us  [exchange(): return lax.ppermute(value, AXIS, pairs)]
    ppermute x10, waiting for transfers between devices: 8.26 us -> 9.82 us  [exchange(): return lax.ppermute(value, AXIS, pairs)]
    unnamed x14 -> x10, local copies, waits for them, and re-layouts: 1.35 us -> 0.02 us
    pallas_call x4 -> x5, Pallas kernels: 1.42 us -> 0.73 us  [local_call(): pl.pallas_call(kernel, in_specs=[VMEM_SPEC] * len(values), out_specs=[VME...]
  transfers between devices with their start and end apart: 10 -> 10, of which waited for: 5 -> 6; matrix products, arithmetic and copies ran while one was open for 0% -> 0% of each run, Pallas kernels for 12% -> 12%
where the time goes in v4:
time: 45.7 us; the launch traced here: 45.3 us
  starting transfers between devices  21.4 us (47%)
  Pallas kernels  13.8 us (30%)
  waiting for transfers between devices  9.82 us (21%)
    ppermute x10, starting transfers between devices, exchange(): return lax.ppermute(value, AXIS, pairs)  21.4 us
    ppermute x10, waiting for transfers between devices, exchange(): return lax.ppermute(value, AXIS, pairs)  9.82 us
    pallas_call x1, Pallas kernels, early_call(): pl.pallas_call(early_kernel, in_specs=[SMEM_SPEC] + [VMEM_SPEC] * 7, out_...  5.48 us
    pallas_call x1, Pallas kernels, late_call(): pl.pallas_call(late_kernel, in_specs=[SMEM_SPEC] + [VMEM_SPEC] * 7, out_s...  4.11 us
    pallas_call x1, Pallas kernels, spectrum_call(): pl.pallas_call(spectrum_kernel, grid=(steps,), in_specs=[pl.BlockSpec(lis...  3.5 us
  transfers between devices with their start and end apart: 10, of which 6 were waited for; matrix products, arithmetic and copies ran while one was open for 0% of the time, Pallas kernels for 12%

profile of v4, /device:TPU:0, one launch (start us, length us, event | category | flops | bytes accessed | tf_op | source)
XLA Modules:
  0.0 45.3 jit_solution(17574220375252642961)
XLA Ops:
  0.0 0.0 copy-start
  0.0 0.0 copy-start.1
  0.0 0.0 copy-start.2
  0.0 3.5 %spectrum.1 = (bf16[2,272,256]{2,1,0:T(8,128)(2,1)S(1)}, bf16[2,272,256]{2,1,0:T(8,128)(2,1)S(1)}, bf16[2,272,256]{2,1,0:T(8,128)(2,1)S(1)}) custom-call(s32[1,8]{1,0:T(1,128)} %listed.1, s32[1,4,8]{2,1,0:T(4,128)} %bitcast.1, bf16[256,4096]{1,0:T(8,128)(2,1)} %x3.1, bf16[256,4096]{1,0:T(8,128)(2,1)} %x3.1, bf16[256,4096]{1,0:T(8,128)(2,1)} %x3.1, ...), custom_call_target="tpu_custom_call" | custom-call | tf_op jit(solution)/shard_map/spectrum/pallas_call | solution.py:112
  3.5 0.6 %collective-permute-start = (bf16[2,272,256]{2,1,0:T(8,128)(2,1)S(1)}, bf16[2,272,256]{2,1,0:T(8,128)(2,1)S(1)}, u32[]{:S(2)}, u32[]{:S(2)}) collective-permute-start(bf16[2,272,256]{2,1,0:T(8,128)(2,1)S(1)} %get-tuple-element.20), channel_id=1, source_target_pairs={{0,1},{1,0},{2,3},{3,2},{4,5},{5,4},{6,7},{7,6},{8,9},{9,8},{10,11... | collective-permute-start | bytes 835592 | tf_op jit(solution)/shard_map/ppermute | solution.py:390
  4.1 1.2 %collective-permute-done.swap = bf16[2,272,256]{2,1,0:T(8,128)(2,1)S(1)} collective-permute-done((bf16[2,272,256]{2,1,0:T(8,128)(2,1)S(1)}, bf16[2,272,256]{2,1,0:T(8,128)(2,1)S(1)}, u32[]{:S(2)}, u32[]{:S(2)}) %collective-permute-start) | collective-permute-done | bytes 278560 | tf_op jit(solution)/shard_map/ppermute | solution.py:390
  5.3 2.9 %collective-permute-start.1 = (bf16[2,272,256]{2,1,0:T(8,128)(2,1)S(1)}, bf16[2,272,256]{2,1,0:T(8,128)(2,1)S(1)}, u32[]{:S(2)}, u32[]{:S(2)}) collective-permute-start(bf16[2,272,256]{2,1,0:T(8,128)(2,1)S(1)} %get-tuple-element.24), channel_id=1, source_target_pairs={{0,2},{1,3},{2,0},{3,1},{4,6},{5,7},{6,4},{7,5},{8,10},{9,11},{10,... | collective-permute-start | bytes 835592 | tf_op jit(solution)/shard_map/ppermute | solution.py:390
  8.2 1.4 %collective-permute-start.3 = (bf16[2,272,256]{2,1,0:T(8,128)(2,1)S(1)}, bf16[2,272,256]{2,1,0:T(8,128)(2,1)S(1)}, u32[]{:S(2)}, u32[]{:S(2)}) collective-permute-start(bf16[2,272,256]{2,1,0:T(8,128)(2,1)S(1)} %get-tuple-element.23.near), channel_id=1, source_target_pairs={{4,0},{5,1},{6,2},{7,3},{8,4},{9,5},{10,6},{11,7},{12,8},{13,9},{1... | collective-permute-start | bytes 835592 | tf_op jit(solution)/shard_map/ppermute | solution.py:390
  9.7 4.6 %collective-permute-start.2 = (bf16[2,272,256]{2,1,0:T(8,128)(2,1)S(1)}, bf16[2,272,256]{2,1,0:T(8,128)(2,1)S(1)}, u32[]{:S(2)}, u32[]{:S(2)}) collective-permute-start(bf16[2,272,256]{2,1,0:T(8,128)(2,1)S(1)} %get-tuple-element.23.near), channel_id=1, source_target_pairs={{0,4},{1,5},{2,6},{3,7},{4,8},{5,9},{6,10},{7,11},{8,12},{9,13},{1... | collective-permute-start | bytes 835592 | tf_op jit(solution)/shard_map/ppermute | solution.py:390
  14.2 1.0 %collective-permute-done.1.mates = bf16[2,272,256]{2,1,0:T(8,128)(2,1)S(1)} collective-permute-done((bf16[2,272,256]{2,1,0:T(8,128)(2,1)S(1)}, bf16[2,272,256]{2,1,0:T(8,128)(2,1)S(1)}, u32[]{:S(2)}, u32[]{:S(2)}) %collective-permute-start.1) | collective-permute-done | bytes 278560 | tf_op jit(solution)/shard_map/ppermute | solution.py:390
  15.2 1.3 %collective-permute-start.5 = (bf16[2,272,256]{2,1,0:T(8,128)(2,1)S(1)}, bf16[2,272,256]{2,1,0:T(8,128)(2,1)S(1)}, u32[]{:S(2)}, u32[]{:S(2)}) collective-permute-start(bf16[2,272,256]{2,1,0:T(8,128)(2,1)S(1)} %collective-permute-done.1.mates), channel_id=1, source_target_pairs={{4,0},{5,1},{6,2},{7,3},{8,4},{9,5},{10,6},{11,7},{12,8},{13,9},{1... | collective-permute-start | bytes 835592 | tf_op jit(solution)/shard_map/ppermute | solution.py:390
  16.5 4.6 %collective-permute-start.4 = (bf16[2,272,256]{2,1,0:T(8,128)(2,1)S(1)}, bf16[2,272,256]{2,1,0:T(8,128)(2,1)S(1)}, u32[]{:S(2)}, u32[]{:S(2)}) collective-permute-start(bf16[2,272,256]{2,1,0:T(8,128)(2,1)S(1)} %collective-permute-done.1.mates), channel_id=1, source_target_pairs={{0,4},{1,5},{2,6},{3,7},{4,8},{5,9},{6,10},{7,11},{8,12},{9,13},{1... | collective-permute-start | bytes 835592 | tf_op jit(solution)/shard_map/ppermute | solution.py:390
  21.1 0.0 collective-permute-done.3.above
  21.1 0.0 collective-permute-done.2.below
  21.1 0.0 copy-done
  21.1 0.0 copy-done.1
  21.1 0.0 copy-done.2
  21.1 0.0 copy-done.4
  21.1 5.5 %early_pairs.1 = (bf16[12,272,256]{2,1,0:T(8,128)(2,1)S(1)}, f32[8,128,384]{2,1,0:T(8,128)S(1)}) custom-call(s32[4,126]{1,0:T(4,128)S(1)} %copy-done.4, bf16[2,272,256]{2,1,0:T(8,128)(2,1)S(1)} %get-tuple-element.23.near, bf16[2,272,256]{2,1,0:T(8,128)(2,1)S(1)} %collective-permute-done.1.mates, bf16[2,272,256]{2,1,0:T(8,128)(2,1)S(1)} %collective-permute-done.2.below, ...), custom_call_target="tpu_custom_call" | custom-call | tf_op jit(solution)/shard_map/early_pairs/pallas_call | solution.py:351
  26.6 0.0 collective-permute-done.5.above
  26.6 0.0 collective-permute-done.4.below
  26.6 0.0 copy-done.3
  26.6 4.1 %late_pairs.1 = (f32[6,128,128]{2,1,0:T(8,128)S(1)}, bf16[6,128,128]{2,1,0:T(8,128)(2,1)S(1)}, bf16[12,272,256]{2,1,0:T(8,128)(2,1)S(1)}, f32[8,128,384]{2,1,0:T(8,128)S(1)}) custom-call(s32[4,90]{1,0:T(4,128)S(1)} %copy-done.3, bf16[12,272,256]{2,1,0:T(8,128)(2,1)S(1)} %get-tuple-element.25.spec_in, ...), custom_call_target="tpu_custom_call", output_to_operand_aliasing={{2}: (1, {}), {3}: (2, {})} | custom-call | tf_op jit(solution)/shard_map/late_pairs/pallas_call | solution.py:370
  30.8 0.1 collective-permute-start.6
  30.8 1.4 %collective-permute-done.6.received = bf16[6,128,128]{2,1,0:T(8,128)(2,1)S(1)} collective-permute-done((bf16[6,128,128]{2,1,0:T(8,128)(2,1)S(1)}, bf16[6,128,128]{2,1,0:T(8,128)(2,1)S(1)}, u32[]{:S(2)}, u32[]{:S(2)}) %collective-permute-start.6) | collective-permute-done | bytes 196640 | tf_op jit(solution)/shard_map/ppermute | solution.py:390
  32.3 1.8 %collective-permute-start.7 = (bf16[3,128,128]{2,1,0:T(8,128)(2,1)S(1)}, bf16[3,128,128]{2,1,0:T(8,128)(2,1)S(1)}, u32[]{:S(2)}, u32[]{:S(2)}) collective-permute-start(bf16[3,128,128]{2,1,0:T(8,128)(2,1)S(1)} %get-tuple-element.30), channel_id=1, source_target_pairs={{0,2},{1,3},{2,0},{3,1},{4,6},{5,7},{6,4},{7,5},{8,10},{9,11},{10,... | collective-permute-start | bytes 294920 | tf_op jit(solution)/shard_map/ppermute | solution.py:390
  34.1 3.1 %collective-permute-done.7.received = bf16[3,128,128]{2,1,0:T(8,128)(2,1)S(1)} collective-permute-done((bf16[3,128,128]{2,1,0:T(8,128)(2,1)S(1)}, bf16[3,128,128]{2,1,0:T(8,128)(2,1)S(1)}, u32[]{:S(2)}, u32[]{:S(2)}) %collective-permute-start.7) | collective-permute-done | bytes 98336 | tf_op jit(solution)/shard_map/ppermute | solution.py:390
  37.2 4.1 %collective-permute-start.8 = (bf16[2,128,128]{2,1,0:T(8,128)(2,1)S(1)}, bf16[2,128,128]{2,1,0:T(8,128)(2,1)S(1)}, u32[]{:S(2)}, u32[]{:S(2)}) collective-permute-start(bf16[2,128,128]{2,1,0:T(8,128)(2,1)S(1)} %get-tuple-element.32), channel_id=1, source_target_pairs={{0,4},{1,9},{2,6},{4,8},{5,13},{6,10},{7,3},{8,12},{10,14},{11,7},... | collective-permute-start | bytes 196616 | tf_op jit(solution)/shard_map/ppermute | solution.py:390
  41.4 1.9 %collective-permute-done.8.received = bf16[2,128,128]{2,1,0:T(8,128)(2,1)S(1)} collective-permute-done((bf16[2,128,128]{2,1,0:T(8,128)(2,1)S(1)}, bf16[2,128,128]{2,1,0:T(8,128)(2,1)S(1)}, u32[]{:S(2)}, u32[]{:S(2)}) %collective-permute-start.8) | collective-permute-done | bytes 65568 | tf_op jit(solution)/shard_map/ppermute | solution.py:390
  43.3 0.1 collective-permute-start.9
  43.4 1.2 %collective-permute-done.9.received = f32[128,128]{1,0:T(8,128)S(1)} collective-permute-done((f32[128,128]{1,0:T(8,128)S(1)}, f32[128,128]{1,0:T(8,128)S(1)}, u32[]{:S(2)}, u32[]{:S(2)}) %collective-permute-start.9) | collective-permute-done | bytes 65568 | tf_op jit(solution)/shard_map/ppermute | solution.py:390
  44.6 0.6 %image.1 = f32[128,128]{1,0:T(8,128)} custom-call(f32[128,128]{1,0:T(8,128)S(1)} %get-tuple-element.33.kept, f32[128,128]{1,0:T(8,128)S(1)} %collective-permute-done.9.received), custom_call_target="tpu_custom_call" | custom-call | tf_op jit(solution)/shard_map/image/pallas_call | solution.py:336
  (6 shorter events, 0.1 us)
Async XLA Ops:
  0.0 21.1 %copy-start = (bf16[9,512,384]{2,1,0:T(8,128)(2,1)S(1)}, bf16[9,512,384]{2,1,0:T(8,128)(2,1)}, u32[]{:S(2)}) copy-start(bf16[9,512,384]{2,1,0:T(8,128)(2,1)} %lag_range.3) | copy-start | bytes 10616836
  0.0 21.1 %copy-start.1 = (bf16[4,256,512]{2,1,0:T(8,128)(2,1)S(1)}, bf16[4,256,512]{2,1,0:T(8,128)(2,1)}, u32[]{:S(2)}) copy-start(bf16[4,256,512]{2,1,0:T(8,128)(2,1)} %constant.11.clone.inv) | copy-start | bytes 3145732
  0.0 21.1 %copy-start.2 = (bf16[9,128,256]{2,1,0:T(8,128)(2,1)S(1)}, bf16[9,128,256]{2,1,0:T(8,128)(2,1)}, u32[]{:S(2)}) copy-start(bf16[9,128,256]{2,1,0:T(8,128)(2,1)} %steering.3) | copy-start | bytes 1769476
  0.0 21.1 %copy-start.4 = (s32[4,126]{1,0:T(4,128)S(1)}, s32[4,126]{1,0:T(4,128)}, u32[]{:S(2)}) copy-start(s32[4,126]{1,0:T(4,128)} %constant.9.clone.table) | copy-start | bytes 6052
  3.5 1.8 %collective-permute-start = (bf16[2,272,256]{2,1,0:T(8,128)(2,1)S(1)}, bf16[2,272,256]{2,1,0:T(8,128)(2,1)S(1)}, u32[]{:S(2)}, u32[]{:S(2)}) collective-permute-start(bf16[2,272,256]{2,1,0:T(8,128)(2,1)S(1)} %get-tuple-element.20), channel_id=1, source_target_pairs={{0,1},{1,0},{2,3},{3,2},{4,5},{5,4},{6,7},{7,6},{8,9},{9,8},{10,11... | collective-permute-start | bytes 835592 | tf_op jit(solution)/shard_map/ppermute | solution.py:390
  5.3 9.9 %collective-permute-start.1 = (bf16[2,272,256]{2,1,0:T(8,128)(2,1)S(1)}, bf16[2,272,256]{2,1,0:T(8,128)(2,1)S(1)}, u32[]{:S(2)}, u32[]{:S(2)}) collective-permute-start(bf16[2,272,256]{2,1,0:T(8,128)(2,1)S(1)} %get-tuple-element.24), channel_id=1, source_target_pairs={{0,2},{1,3},{2,0},{3,1},{4,6},{5,7},{6,4},{7,5},{8,10},{9,11},{10,... | collective-permute-start | bytes 835592 | tf_op jit(solution)/shard_map/ppermute | solution.py:390
  8.2 18.4 %copy-start.3 = (s32[4,90]{1,0:T(4,128)S(1)}, s32[4,90]{1,0:T(4,128)}, u32[]{:S(2)}) copy-start(s32[4,90]{1,0:T(4,128)} %constant.10.clone.table) | copy-start | bytes 4324
  8.2 12.8 %collective-permute-start.3 = (bf16[2,272,256]{2,1,0:T(8,128)(2,1)S(1)}, bf16[2,272,256]{2,1,0:T(8,128)(2,1)S(1)}, u32[]{:S(2)}, u32[]{:S(2)}) collective-permute-start(bf16[2,272,256]{2,1,0:T(8,128)(2,1)S(1)} %get-tuple-element.23.near), channel_id=1, source_target_pairs={{4,0},{5,1},{6,2},{7,3},{8,4},{9,5},{10,6},{11,7},{12,8},{13,9},{1... | collective-permute-start | bytes 835592 | tf_op jit(solution)/shard_map/ppermute | solution.py:390
  9.7 11.4 %collective-permute-start.2 = (bf16[2,272,256]{2,1,0:T(8,128)(2,1)S(1)}, bf16[2,272,256]{2,1,0:T(8,128)(2,1)S(1)}, u32[]{:S(2)}, u32[]{:S(2)}) collective-permute-start(bf16[2,272,256]{2,1,0:T(8,128)(2,1)S(1)} %get-tuple-element.23.near), channel_id=1, source_target_pairs={{0,4},{1,5},{2,6},{3,7},{4,8},{5,9},{6,10},{7,11},{8,12},{9,13},{1... | collective-permute-start | bytes 835592 | tf_op jit(solution)/shard_map/ppermute | solution.py:390
  15.2 11.4 %collective-permute-start.5 = (bf16[2,272,256]{2,1,0:T(8,128)(2,1)S(1)}, bf16[2,272,256]{2,1,0:T(8,128)(2,1)S(1)}, u32[]{:S(2)}, u32[]{:S(2)}) collective-permute-start(bf16[2,272,256]{2,1,0:T(8,128)(2,1)S(1)} %collective-permute-done.1.mates), channel_id=1, source_target_pairs={{4,0},{5,1},{6,2},{7,3},{8,4},{9,5},{10,6},{11,7},{12,8},{13,9},{1... | collective-permute-start | bytes 835592 | tf_op jit(solution)/shard_map/ppermute | solution.py:390
  16.5 10.1 %collective-permute-start.4 = (bf16[2,272,256]{2,1,0:T(8,128)(2,1)S(1)}, bf16[2,272,256]{2,1,0:T(8,128)(2,1)S(1)}, u32[]{:S(2)}, u32[]{:S(2)}) collective-permute-start(bf16[2,272,256]{2,1,0:T(8,128)(2,1)S(1)} %collective-permute-done.1.mates), channel_id=1, source_target_pairs={{0,4},{1,5},{2,6},{3,7},{4,8},{5,9},{6,10},{7,11},{8,12},{9,13},{1... | collective-permute-start | bytes 835592 | tf_op jit(solution)/shard_map/ppermute | solution.py:390
  30.8 1.5 %collective-permute-start.6 = (bf16[6,128,128]{2,1,0:T(8,128)(2,1)S(1)}, bf16[6,128,128]{2,1,0:T(8,128)(2,1)S(1)}, u32[]{:S(2)}, u32[]{:S(2)}) collective-permute-start(bf16[6,128,128]{2,1,0:T(8,128)(2,1)S(1)} %get-tuple-element.28), channel_id=1, source_target_pairs={{0,1},{1,0},{2,3},{3,2},{4,5},{5,4},{6,7},{7,6},{8,9},{9,8},{10,11... | collective-permute-start | bytes 589832 | tf_op jit(solution)/shard_map/ppermute | solution.py:390
  32.3 4.9 %collective-permute-start.7 = (bf16[3,128,128]{2,1,0:T(8,128)(2,1)S(1)}, bf16[3,128,128]{2,1,0:T(8,128)(2,1)S(1)}, u32[]{:S(2)}, u32[]{:S(2)}) collective-permute-start(bf16[3,128,128]{2,1,0:T(8,128)(2,1)S(1)} %get-tuple-element.30), channel_id=1, source_target_pairs={{0,2},{1,3},{2,0},{3,1},{4,6},{5,7},{6,4},{7,5},{8,10},{9,11},{10,... | collective-permute-start | bytes 294920 | tf_op jit(solution)/shard_map/ppermute | solution.py:390
  37.2 6.0 %collective-permute-start.8 = (bf16[2,128,128]{2,1,0:T(8,128)(2,1)S(1)}, bf16[2,128,128]{2,1,0:T(8,128)(2,1)S(1)}, u32[]{:S(2)}, u32[]{:S(2)}) collective-permute-start(bf16[2,128,128]{2,1,0:T(8,128)(2,1)S(1)} %get-tuple-element.32), channel_id=1, source_target_pairs={{0,4},{1,9},{2,6},{4,8},{5,13},{6,10},{7,3},{8,12},{10,14},{11,7},... | collective-permute-start | bytes 196616 | tf_op jit(solution)/shard_map/ppermute | solution.py:390
  43.3 1.3 %collective-permute-start.9 = (f32[128,128]{1,0:T(8,128)S(1)}, f32[128,128]{1,0:T(8,128)S(1)}, u32[]{:S(2)}, u32[]{:S(2)}) collective-permute-start(f32[128,128]{1,0:T(8,128)S(1)} %get-tuple-element.34), channel_id=1, source_target_pairs={{0,1},{1,0},{2,3},{3,2},{4,5},{5,4},{6,7},{7,6},{8,9},{9,8},{10,11... | collective-permute-start | bytes 196616 | tf_op jit(solution)/shard_map/ppermute | solution.py:390

commit v5 on v4

--- a/solution.py
+++ b/solution.py
@@ -199,14 +199,20 @@
         mask[entry, h, rounds:, :] = jnp.ones((rounds, mask.shape[3]), jnp.float32)
 
 
+def neighbour_slots():
+    parity = lax.rem(lax.axis_index(AXIS) // Q, 2)
+    return Q * (2 - parity), Q * (1 + parity)
+
+
 def early_kernel(
-    table, near, mates, below, above, inv, steering, lag_range, spec, window, mask
+    table, near, mates, even, odd, inv, steering, lag_range, spec, window, mask
 ):
     me = lax.rem(lax.axis_index(AXIS), Q)
+    even_slot, odd_slot = neighbour_slots()
     spec[0:2] = near[...]
     spec[2:4] = mates[...]
-    spec[Q : Q + 2] = below[...]
-    spec[2 * Q : 2 * Q + 2] = above[...]
+    spec[pl.ds(even_slot, 2)] = even[...]
+    spec[pl.ds(odd_slot, 2)] = odd[...]
     window[...] = jnp.zeros_like(window)
     channels = steering.shape[2]
     for p in range(Q):
@@ -217,12 +223,13 @@
 
 
 def late_kernel(
-    table, spec_in, window_in, below, above, inv, steering, lag_range,
+    table, spec_in, window_in, even, odd, inv, steering, lag_range,
     keep, send, spec, window, mask,
 ):
     me = lax.rem(lax.axis_index(AXIS), Q)
-    spec[Q + 2 : Q + 4] = below[...]
-    spec[2 * Q + 2 : 2 * Q + 4] = above[...]
+    even_slot, odd_slot = neighbour_slots()
+    spec[pl.ds(even_slot + 2, 2)] = even[...]
+    spec[pl.ds(odd_slot + 2, 2)] = odd[...]
     channels = steering.shape[2]
     for p in range(Q):
         fill_mask(mask, p, spec, p, channels)
@@ -344,7 +351,7 @@
     )(*near_vmem(*values))
 
 
-def early_call(table, near, mates, below, above, inv, steering, lag_range):
+def early_call(table, near, mates, even, odd, inv, steering, lag_range):
     _, rows, cols = near.shape
     angles, group = steering.shape[1], lag_range.shape[2]
     rounds = steering.shape[0] - 1
@@ -359,10 +366,10 @@
         scratch_shapes=[pltpu.VMEM((2 * Q, L // cols, 2 * rounds, cols), jnp.float32)],
         compiler_params=pltpu.CompilerParams(vmem_limit_bytes=LIMIT),
         name="early_pairs",
-    )(table, *near_vmem(near, mates, below, above, inv, steering, lag_range))
-
-
-def late_call(table, spec, window, below, above, inv, steering, lag_range):
+    )(table, *near_vmem(near, mates, even, odd, inv, steering, lag_range))
+
+
+def late_call(table, spec, window, even, odd, inv, steering, lag_range):
     cols = spec.shape[2]
     angles, group = steering.shape[1], lag_range.shape[2]
     rounds = steering.shape[0] - 1
@@ -381,7 +388,7 @@
         scratch_shapes=[pltpu.VMEM((2 * Q, L // cols, 2 * rounds, cols), jnp.float32)],
         compiler_params=pltpu.CompilerParams(vmem_limit_bytes=LIMIT),
         name="late_pairs",
-    )(table, *near_vmem(spec, window, below, above, inv, steering, lag_range))[:2]
+    )(table, *near_vmem(spec, window, even, odd, inv, steering, lag_range))[:2]
 
 
 def exchange(value, devices, target):
@@ -391,8 +398,8 @@
 
 
 def per_device(devices, strain, steering, lag_range, pair_listed, band_used):
-    def shift(value, by):
-        return exchange(value, devices, lambda i: i + by)
+    def planes(value, parity):
+        return exchange(value, devices, lambda i: i + (Q if i // Q % 2 == parity else -Q))
 
     def flip(value, by):
         return exchange(value, devices, lambda i: i ^ by)
@@ -403,13 +410,14 @@
         join_kernel, "join", [joined, joined], flip(swap, 1), near, mates, aliases={1: 0, 2: 1}
     )
     mates = flip(mates, 2)
-    near_below, near_above = shift(near, Q), shift(near, -Q)
-    far_below, far_above = shift(mates, Q), shift(mates, -Q)
+    near_odd, near_even = planes(near, 1), planes(near, 0)
+    far_odd, far_even = planes(mates, 1), planes(mates, 0)
     early, late = (jnp.asarray(t.reshape(Q, -1)) for t in unit_table(steering.shape[0] - 1))
     inv = jnp.asarray(inverse_table(strain.shape[1]))
+    near, steering, lag_range, inv = lax.optimization_barrier((near, steering, lag_range, inv))
     shared = (inv, steering, lag_range)
-    spec, window = early_call(early, near, mates, near_below, near_above, *shared)
-    kept, send = late_call(late, spec, window, far_below, far_above, *shared)
+    spec, window = early_call(early, near, mates, near_even, near_odd, *shared)
+    kept, send = late_call(late, spec, window, far_even, far_odd, *shared)
 
     def pieces(count, dtype):
         return pltpu.VMEM(((count,) if count else ()) + kept.shape[1:], dtype)

time: 45.7 us -> 44.7 us (0.978)
  starting transfers between devices: 21.4 us -> 19.5 us
  waiting for transfers between devices: 9.82 us -> 11.1 us
    ppermute x10, starting transfers between devices: 21.4 us -> 19.5 us  [exchange(): return lax.ppermute(value, AXIS, pairs)]
    ppermute x10, waiting for transfers between devices: 9.82 us -> 11.1 us  [exchange(): return lax.ppermute(value, AXIS, pairs)]
  transfers between devices with their start and end apart: 10 -> 10, of which waited for: 6 -> 7; matrix products, arithmetic and copies ran while one was open for 0% -> 0% of each run, Pallas kernels for 12% -> 12%
where the time goes in v5:
time: 44.7 us; the launch traced here: 44.5 us
  starting transfers between devices  19.5 us (44%)
  Pallas kernels  13.8 us (31%)
  waiting for transfers between devices  11.1 us (25%)
    ppermute x10, starting transfers between devices, exchange(): return lax.ppermute(value, AXIS, pairs)  19.5 us
    ppermute x10, waiting for transfers between devices, exchange(): return lax.ppermute(value, AXIS, pairs)  11.1 us
    pallas_call x1, Pallas kernels, early_call(): pl.pallas_call(early_kernel, in_specs=[SMEM_SPEC] + [VMEM_SPEC] * 7, out_...  5.47 us
    pallas_call x1, Pallas kernels, late_call(): pl.pallas_call(late_kernel, in_specs=[SMEM_SPEC] + [VMEM_SPEC] * 7, out_s...  4.13 us
    pallas_call x1, Pallas kernels, spectrum_call(): pl.pallas_call(spectrum_kernel, grid=(steps,), in_specs=[pl.BlockSpec(lis...  3.5 us
  transfers between devices with their start and end apart: 10, of which 7 were waited for; matrix products, arithmetic and copies ran while one was open for 0% of the time, Pallas kernels for 12%

profile of v5, /device:TPU:0, one launch (start us, length us, event | category | flops | bytes accessed | tf_op | source)
XLA Modules:
  0.0 44.5 jit_solution(96231097905835969)
XLA Ops:
  0.0 0.0 copy-start
  0.0 0.0 copy-start.1
  0.0 0.0 copy-start.2
  0.0 3.5 %spectrum.1 = (bf16[2,272,256]{2,1,0:T(8,128)(2,1)S(1)}, bf16[2,272,256]{2,1,0:T(8,128)(2,1)S(1)}, bf16[2,272,256]{2,1,0:T(8,128)(2,1)S(1)}) custom-call(s32[1,8]{1,0:T(1,128)} %listed.1, s32[1,4,8]{2,1,0:T(4,128)} %bitcast.1, bf16[256,4096]{1,0:T(8,128)(2,1)} %x3.1, bf16[256,4096]{1,0:T(8,128)(2,1)} %x3.1, bf16[256,4096]{1,0:T(8,128)(2,1)} %x3.1, ...), custom_call_target="tpu_custom_call" | custom-call | tf_op jit(solution)/shard_map/spectrum/pallas_call | solution.py:112
  3.5 0.6 %collective-permute-start = (bf16[2,272,256]{2,1,0:T(8,128)(2,1)S(1)}, bf16[2,272,256]{2,1,0:T(8,128)(2,1)S(1)}, u32[]{:S(2)}, u32[]{:S(2)}) collective-permute-start(bf16[2,272,256]{2,1,0:T(8,128)(2,1)S(1)} %get-tuple-element.24), channel_id=1, source_target_pairs={{0,1},{1,0},{2,3},{3,2},{4,5},{5,4},{6,7},{7,6},{8,9},{9,8},{10,11... | collective-permute-start | bytes 835592 | tf_op jit(solution)/shard_map/ppermute | solution.py:397
  4.1 1.2 %collective-permute-done.swap = bf16[2,272,256]{2,1,0:T(8,128)(2,1)S(1)} collective-permute-done((bf16[2,272,256]{2,1,0:T(8,128)(2,1)S(1)}, bf16[2,272,256]{2,1,0:T(8,128)(2,1)S(1)}, u32[]{:S(2)}, u32[]{:S(2)}) %collective-permute-start) | collective-permute-done | bytes 278560 | tf_op jit(solution)/shard_map/ppermute | solution.py:397
  5.3 2.9 %collective-permute-start.1 = (bf16[2,272,256]{2,1,0:T(8,128)(2,1)S(1)}, bf16[2,272,256]{2,1,0:T(8,128)(2,1)S(1)}, u32[]{:S(2)}, u32[]{:S(2)}) collective-permute-start(bf16[2,272,256]{2,1,0:T(8,128)(2,1)S(1)} %get-tuple-element.29), channel_id=1, source_target_pairs={{0,2},{1,3},{2,0},{3,1},{4,6},{5,7},{6,4},{7,5},{8,10},{9,11},{10,... | collective-permute-start | bytes 835592 | tf_op jit(solution)/shard_map/ppermute | solution.py:397
  8.2 0.8 %collective-permute-start.3 = (bf16[2,272,256]{2,1,0:T(8,128)(2,1)S(1)}, bf16[2,272,256]{2,1,0:T(8,128)(2,1)S(1)}, u32[]{:S(2)}, u32[]{:S(2)}) collective-permute-start(bf16[2,272,256]{2,1,0:T(8,128)(2,1)S(1)} %get-tuple-element.28.near), channel_id=1, source_target_pairs={{4,8},{5,9},{6,10},{7,11},{8,4},{9,5},{10,6},{11,7},{20,24},{21,25... | collective-permute-start | bytes 835592 | tf_op jit(solution)/shard_map/ppermute | solution.py:397
  9.0 4.5 %collective-permute-start.2 = (bf16[2,272,256]{2,1,0:T(8,128)(2,1)S(1)}, bf16[2,272,256]{2,1,0:T(8,128)(2,1)S(1)}, u32[]{:S(2)}, u32[]{:S(2)}) collective-permute-start(bf16[2,272,256]{2,1,0:T(8,128)(2,1)S(1)} %get-tuple-element.28.near), channel_id=1, source_target_pairs={{0,4},{1,5},{2,6},{3,7},{4,0},{5,1},{6,2},{7,3},{8,12},{9,13},{10,... | collective-permute-start | bytes 835592 | tf_op jit(solution)/shard_map/ppermute | solution.py:397
  13.5 1.7 %collective-permute-done.1.mates = bf16[2,272,256]{2,1,0:T(8,128)(2,1)S(1)} collective-permute-done((bf16[2,272,256]{2,1,0:T(8,128)(2,1)S(1)}, bf16[2,272,256]{2,1,0:T(8,128)(2,1)S(1)}, u32[]{:S(2)}, u32[]{:S(2)}) %collective-permute-start.1) | collective-permute-done | bytes 278560 | tf_op jit(solution)/shard_map/ppermute | solution.py:397
  15.2 0.7 %collective-permute-start.5 = (bf16[2,272,256]{2,1,0:T(8,128)(2,1)S(1)}, bf16[2,272,256]{2,1,0:T(8,128)(2,1)S(1)}, u32[]{:S(2)}, u32[]{:S(2)}) collective-permute-start(bf16[2,272,256]{2,1,0:T(8,128)(2,1)S(1)} %collective-permute-done.1.mates), channel_id=1, source_target_pairs={{4,8},{5,9},{6,10},{7,11},{8,4},{9,5},{10,6},{11,7},{20,24},{21,25... | collective-permute-start | bytes 835592 | tf_op jit(solution)/shard_map/ppermute | solution.py:397
  15.9 4.7 %collective-permute-start.4 = (bf16[2,272,256]{2,1,0:T(8,128)(2,1)S(1)}, bf16[2,272,256]{2,1,0:T(8,128)(2,1)S(1)}, u32[]{:S(2)}, u32[]{:S(2)}) collective-permute-start(bf16[2,272,256]{2,1,0:T(8,128)(2,1)S(1)} %collective-permute-done.1.mates), channel_id=1, source_target_pairs={{0,4},{1,5},{2,6},{3,7},{4,0},{5,1},{6,2},{7,3},{8,12},{9,13},{10,... | collective-permute-start | bytes 835592 | tf_op jit(solution)/shard_map/ppermute | solution.py:397
  20.5 0.0 collective-permute-done.3.odd
  20.5 0.0 collective-permute-done.2.even
  20.5 0.0 copy-done
  20.6 0.0 copy-done.1
  20.6 0.0 copy-done.2
  20.6 0.0 copy-done.4
  20.6 5.5 %early_pairs.1 = (bf16[12,272,256]{2,1,0:T(8,128)(2,1)S(1)}, f32[8,128,384]{2,1,0:T(8,128)S(1)}) custom-call(s32[4,126]{1,0:T(4,128)S(1)} %copy-done.4, bf16[2,272,256]{2,1,0:T(8,128)(2,1)S(1)} %get-tuple-element.28.near, bf16[2,272,256]{2,1,0:T(8,128)(2,1)S(1)} %collective-permute-done.1.mates, bf16[2,272,256]{2,1,0:T(8,128)(2,1)S(1)} %collective-permute-done.2.even, ...), custom_call_target="tpu_custom_call" | custom-call | tf_op jit(solution)/shard_map/early_pairs/pallas_call | solution.py:358
  26.1 0.0 collective-permute-done.5.odd
  26.1 0.3 collective-permute-done.4.even
  26.4 0.0 copy-done.3
  26.4 4.1 %late_pairs.1 = (f32[6,128,128]{2,1,0:T(8,128)S(1)}, bf16[6,128,128]{2,1,0:T(8,128)(2,1)S(1)}, bf16[12,272,256]{2,1,0:T(8,128)(2,1)S(1)}, f32[8,128,384]{2,1,0:T(8,128)S(1)}) custom-call(s32[4,90]{1,0:T(4,128)S(1)} %copy-done.3, bf16[12,272,256]{2,1,0:T(8,128)(2,1)S(1)} %get-tuple-element.33.spec_in, ...), custom_call_target="tpu_custom_call", output_to_operand_aliasing={{2}: (1, {}), {3}: (2, {})} | custom-call | tf_op jit(solution)/shard_map/late_pairs/pallas_call | solution.py:377
  30.5 0.1 collective-permute-start.6
  30.6 1.4 %collective-permute-done.6.received = bf16[6,128,128]{2,1,0:T(8,128)(2,1)S(1)} collective-permute-done((bf16[6,128,128]{2,1,0:T(8,128)(2,1)S(1)}, bf16[6,128,128]{2,1,0:T(8,128)(2,1)S(1)}, u32[]{:S(2)}, u32[]{:S(2)}) %collective-permute-start.6) | collective-permute-done | bytes 196640 | tf_op jit(solution)/shard_map/ppermute | solution.py:397
  32.1 1.6 %collective-permute-start.7 = (bf16[3,128,128]{2,1,0:T(8,128)(2,1)S(1)}, bf16[3,128,128]{2,1,0:T(8,128)(2,1)S(1)}, u32[]{:S(2)}, u32[]{:S(2)}) collective-permute-start(bf16[3,128,128]{2,1,0:T(8,128)(2,1)S(1)} %get-tuple-element.38), channel_id=1, source_target_pairs={{0,2},{1,3},{2,0},{3,1},{4,6},{5,7},{6,4},{7,5},{8,10},{9,11},{10,... | collective-permute-start | bytes 294920 | tf_op jit(solution)/shard_map/ppermute | solution.py:397
  33.6 3.3 %collective-permute-done.7.received = bf16[3,128,128]{2,1,0:T(8,128)(2,1)S(1)} collective-permute-done((bf16[3,128,128]{2,1,0:T(8,128)(2,1)S(1)}, bf16[3,128,128]{2,1,0:T(8,128)(2,1)S(1)}, u32[]{:S(2)}, u32[]{:S(2)}) %collective-permute-start.7) | collective-permute-done | bytes 98336 | tf_op jit(solution)/shard_map/ppermute | solution.py:397
  37.0 3.6 %collective-permute-start.8 = (bf16[2,128,128]{2,1,0:T(8,128)(2,1)S(1)}, bf16[2,128,128]{2,1,0:T(8,128)(2,1)S(1)}, u32[]{:S(2)}, u32[]{:S(2)}) collective-permute-start(bf16[2,128,128]{2,1,0:T(8,128)(2,1)S(1)} %get-tuple-element.40), channel_id=1, source_target_pairs={{0,4},{1,9},{2,6},{4,8},{5,13},{6,10},{7,3},{8,12},{10,14},{11,7},... | collective-permute-start | bytes 196616 | tf_op jit(solution)/shard_map/ppermute | solution.py:397
  40.6 1.9 %collective-permute-done.8.received = bf16[2,128,128]{2,1,0:T(8,128)(2,1)S(1)} collective-permute-done((bf16[2,128,128]{2,1,0:T(8,128)(2,1)S(1)}, bf16[2,128,128]{2,1,0:T(8,128)(2,1)S(1)}, u32[]{:S(2)}, u32[]{:S(2)}) %collective-permute-start.8) | collective-permute-done | bytes 65568 | tf_op jit(solution)/shard_map/ppermute | solution.py:397
  42.6 0.1 collective-permute-start.9
  42.6 1.2 %collective-permute-done.9.received = f32[128,128]{1,0:T(8,128)S(1)} collective-permute-done((f32[128,128]{1,0:T(8,128)S(1)}, f32[128,128]{1,0:T(8,128)S(1)}, u32[]{:S(2)}, u32[]{:S(2)}) %collective-permute-start.9) | collective-permute-done | bytes 65568 | tf_op jit(solution)/shard_map/ppermute | solution.py:397
  43.9 0.6 %image.1 = f32[128,128]{1,0:T(8,128)} custom-call(f32[128,128]{1,0:T(8,128)S(1)} %get-tuple-element.41.kept, f32[128,128]{1,0:T(8,128)S(1)} %collective-permute-done.9.received), custom_call_target="tpu_custom_call" | custom-call | tf_op jit(solution)/shard_map/image/pallas_call | solution.py:343
  (6 shorter events, 0.1 us)
Async XLA Ops:
  0.0 20.6 %copy-start = (bf16[9,512,384]{2,1,0:T(8,128)(2,1)S(1)}, bf16[9,512,384]{2,1,0:T(8,128)(2,1)}, u32[]{:S(2)}) copy-start(bf16[9,512,384]{2,1,0:T(8,128)(2,1)} %lag_range.1) | copy-start | bytes 10616836
  0.0 20.6 %copy-start.1 = (bf16[4,256,512]{2,1,0:T(8,128)(2,1)S(1)}, bf16[4,256,512]{2,1,0:T(8,128)(2,1)}, u32[]{:S(2)}) copy-start(bf16[4,256,512]{2,1,0:T(8,128)(2,1)} %constant.11.clone.inv) | copy-start | bytes 3145732
  0.0 20.6 %copy-start.2 = (bf16[9,128,256]{2,1,0:T(8,128)(2,1)S(1)}, bf16[9,128,256]{2,1,0:T(8,128)(2,1)}, u32[]{:S(2)}) copy-start(bf16[9,128,256]{2,1,0:T(8,128)(2,1)} %steering.1) | copy-start | bytes 1769476
  0.0 20.6 %copy-start.4 = (s32[4,126]{1,0:T(4,128)S(1)}, s32[4,126]{1,0:T(4,128)}, u32[]{:S(2)}) copy-start(s32[4,126]{1,0:T(4,128)} %constant.9.clone.table) | copy-start | bytes 6052
  3.5 1.8 %collective-permute-start = (bf16[2,272,256]{2,1,0:T(8,128)(2,1)S(1)}, bf16[2,272,256]{2,1,0:T(8,128)(2,1)S(1)}, u32[]{:S(2)}, u32[]{:S(2)}) collective-permute-start(bf16[2,272,256]{2,1,0:T(8,128)(2,1)S(1)} %get-tuple-element.24), channel_id=1, source_target_pairs={{0,1},{1,0},{2,3},{3,2},{4,5},{5,4},{6,7},{7,6},{8,9},{9,8},{10,11... | collective-permute-start | bytes 835592 | tf_op jit(solution)/shard_map/ppermute | solution.py:397
  5.3 9.9 %collective-permute-start.1 = (bf16[2,272,256]{2,1,0:T(8,128)(2,1)S(1)}, bf16[2,272,256]{2,1,0:T(8,128)(2,1)S(1)}, u32[]{:S(2)}, u32[]{:S(2)}) collective-permute-start(bf16[2,272,256]{2,1,0:T(8,128)(2,1)S(1)} %get-tuple-element.29), channel_id=1, source_target_pairs={{0,2},{1,3},{2,0},{3,1},{4,6},{5,7},{6,4},{7,5},{8,10},{9,11},{10,... | collective-permute-start | bytes 835592 | tf_op jit(solution)/shard_map/ppermute | solution.py:397
  8.2 18.1 %copy-start.3 = (s32[4,90]{1,0:T(4,128)S(1)}, s32[4,90]{1,0:T(4,128)}, u32[]{:S(2)}) copy-start(s32[4,90]{1,0:T(4,128)} %constant.10.clone.table) | copy-start | bytes 4324
  8.2 12.3 %collective-permute-start.3 = (bf16[2,272,256]{2,1,0:T(8,128)(2,1)S(1)}, bf16[2,272,256]{2,1,0:T(8,128)(2,1)S(1)}, u32[]{:S(2)}, u32[]{:S(2)}) collective-permute-start(bf16[2,272,256]{2,1,0:T(8,128)(2,1)S(1)} %get-tuple-element.28.near), channel_id=1, source_target_pairs={{4,8},{5,9},{6,10},{7,11},{8,4},{9,5},{10,6},{11,7},{20,24},{21,25... | collective-permute-start | bytes 835592 | tf_op jit(solution)/shard_map/ppermute | solution.py:397
  9.0 11.5 %collective-permute-start.2 = (bf16[2,272,256]{2,1,0:T(8,128)(2,1)S(1)}, bf16[2,272,256]{2,1,0:T(8,128)(2,1)S(1)}, u32[]{:S(2)}, u32[]{:S(2)}) collective-permute-start(bf16[2,272,256]{2,1,0:T(8,128)(2,1)S(1)} %get-tuple-element.28.near), channel_id=1, source_target_pairs={{0,4},{1,5},{2,6},{3,7},{4,0},{5,1},{6,2},{7,3},{8,12},{9,13},{10,... | collective-permute-start | bytes 835592 | tf_op jit(solution)/shard_map/ppermute | solution.py:397
  15.2 10.9 %collective-permute-start.5 = (bf16[2,272,256]{2,1,0:T(8,128)(2,1)S(1)}, bf16[2,272,256]{2,1,0:T(8,128)(2,1)S(1)}, u32[]{:S(2)}, u32[]{:S(2)}) collective-permute-start(bf16[2,272,256]{2,1,0:T(8,128)(2,1)S(1)} %collective-permute-done.1.mates), channel_id=1, source_target_pairs={{4,8},{5,9},{6,10},{7,11},{8,4},{9,5},{10,6},{11,7},{20,24},{21,25... | collective-permute-start | bytes 835592 | tf_op jit(solution)/shard_map/ppermute | solution.py:397
  15.9 10.5 %collective-permute-start.4 = (bf16[2,272,256]{2,1,0:T(8,128)(2,1)S(1)}, bf16[2,272,256]{2,1,0:T(8,128)(2,1)S(1)}, u32[]{:S(2)}, u32[]{:S(2)}) collective-permute-start(bf16[2,272,256]{2,1,0:T(8,128)(2,1)S(1)} %collective-permute-done.1.mates), channel_id=1, source_target_pairs={{0,4},{1,5},{2,6},{3,7},{4,0},{5,1},{6,2},{7,3},{8,12},{9,13},{10,... | collective-permute-start | bytes 835592 | tf_op jit(solution)/shard_map/ppermute | solution.py:397
  30.5 1.5 %collective-permute-start.6 = (bf16[6,128,128]{2,1,0:T(8,128)(2,1)S(1)}, bf16[6,128,128]{2,1,0:T(8,128)(2,1)S(1)}, u32[]{:S(2)}, u32[]{:S(2)}) collective-permute-start(bf16[6,128,128]{2,1,0:T(8,128)(2,1)S(1)} %get-tuple-element.36), channel_id=1, source_target_pairs={{0,1},{1,0},{2,3},{3,2},{4,5},{5,4},{6,7},{7,6},{8,9},{9,8},{10,11... | collective-permute-start | bytes 589832 | tf_op jit(solution)/shard_map/ppermute | solution.py:397
  32.1 4.9 %collective-permute-start.7 = (bf16[3,128,128]{2,1,0:T(8,128)(2,1)S(1)}, bf16[3,128,128]{2,1,0:T(8,128)(2,1)S(1)}, u32[]{:S(2)}, u32[]{:S(2)}) collective-permute-start(bf16[3,128,128]{2,1,0:T(8,128)(2,1)S(1)} %get-tuple-element.38), channel_id=1, source_target_pairs={{0,2},{1,3},{2,0},{3,1},{4,6},{5,7},{6,4},{7,5},{8,10},{9,11},{10,... | collective-permute-start | bytes 294920 | tf_op jit(solution)/shard_map/ppermute | solution.py:397
  37.0 5.5 %collective-permute-start.8 = (bf16[2,128,128]{2,1,0:T(8,128)(2,1)S(1)}, bf16[2,128,128]{2,1,0:T(8,128)(2,1)S(1)}, u32[]{:S(2)}, u32[]{:S(2)}) collective-permute-start(bf16[2,128,128]{2,1,0:T(8,128)(2,1)S(1)} %get-tuple-element.40), channel_id=1, source_target_pairs={{0,4},{1,9},{2,6},{4,8},{5,13},{6,10},{7,3},{8,12},{10,14},{11,7},... | collective-permute-start | bytes 196616 | tf_op jit(solution)/shard_map/ppermute | solution.py:397
  42.6 1.3 %collective-permute-start.9 = (f32[128,128]{1,0:T(8,128)S(1)}, f32[128,128]{1,0:T(8,128)S(1)}, u32[]{:S(2)}, u32[]{:S(2)}) collective-permute-start(f32[128,128]{1,0:T(8,128)S(1)} %get-tuple-element.42), channel_id=1, source_target_pairs={{0,1},{1,0},{2,3},{3,2},{4,5},{5,4},{6,7},{7,6},{8,9},{9,8},{10,11... | collective-permute-start | bytes 196616 | tf_op jit(solution)/shard_map/ppermute | solution.py:397

commit v6 on v5

--- a/solution.py
+++ b/solution.py
@@ -12,6 +12,10 @@
 F = 512
 L = 512
 Q = 4
+LIMIT = 16 << 20
+VMEM_SPEC = pl.BlockSpec(memory_space=pltpu.VMEM)
+SMEM_SPEC = pl.BlockSpec(memory_space=pltpu.SMEM)
+HBM_SPEC = pl.BlockSpec(memory_space=pl.ANY)
 
 
 def forward_table(samples):
@@ -20,7 +24,7 @@
     k = Q * np.arange(freqs, dtype=np.int64)[None, None, :] + np.arange(Q)[:, None, None] + 1
     phase = (t * k % samples) * (2.0 * np.pi / samples)
     table = np.concatenate([np.cos(phase), -np.sin(phase)], axis=2) * samples ** (-0.5)
-    return table.astype(jnp.bfloat16)
+    return np.stack([table[0::2], table[1::2]]).astype(jnp.bfloat16)
 
 
 def inverse_table(samples):
@@ -40,103 +44,146 @@
     return jnp.dot(a, b, preferred_element_type=jnp.float32)
 
 
-def spectrum_kernel(listed, bands, x0, x1, x2, x3, table, near, mates, swap, acc, weight):
-    step, steps = pl.program_id(0), pl.num_programs(0)
+def complex_classes(folds, table):
+    channels = folds.shape[1]
     half = table.shape[2] // 2
-    channels = x0.shape[0]
+    both = folds[...].reshape(2 * channels, folds.shape[2])
+    values = []
+    for n, sign in ((0, 1.0), (1, -1.0)):
+        product = dot(both, table[n])
+        a, b = product[:channels], product[channels:] * sign
+        values.append(
+            jnp.concatenate([a[:, :half] + b[:, half:], a[:, half:] - b[:, :half]], axis=1)
+        )
+    return values
+
+
+def real_classes(folds, table):
+    return [dot(folds[n], table[n]) for n in range(2)]
+
+
+def send_kernel(strain, table, listed, bands, swap, folds, kept_table, time, sent_table, sems):
     me = lax.rem(lax.axis_index(AXIS), Q)
-
-    q0, q1, q2, q3 = (x[...].astype(jnp.float32) for x in (x0, x1, x2, x3))
-    even, odd = q0 + q2, q1 + q3
-    fold0 = (even + odd).astype(jnp.bfloat16)
-    fold2 = (even - odd).astype(jnp.bfloat16)
-    a = (q0 - q2).astype(jnp.bfloat16)
-    b = (q1 - q3).astype(jnp.bfloat16)
-    parts = [
-        dot(a, table[0]),
-        dot(b, table[0]),
-        dot(fold2, table[1]),
-        dot(a, table[2]),
-        dot(b, table[2]),
-        dot(fold0, table[3]),
+    core, side = lax.rem(me, 2), me // 2
+    channels, samples = strain.shape
+    quarter = samples // Q
+    depth = quarter // 2
+    copies = []
+    for h in range(2):
+        for q in range(Q):
+            part = (slice(None), pl.ds(q * quarter + h * depth, depth))
+            copies.append(
+                pltpu.make_async_copy(strain.at[part], time.at[part], sems.at[h * Q + q])
+            )
+    tables = [
+        pltpu.make_async_copy(table.at[1 - core], sent_table, sems.at[2 * Q]),
+        pltpu.make_async_copy(table.at[core], kept_table, sems.at[2 * Q + 1]),
     ]
-
-    @pl.when(step == 0)
-    def _():
-        for n, part in enumerate(parts):
-            acc[n] = part
-
-    @pl.when((step > 0) & (step < steps - 1))
-    def _():
-        for n, part in enumerate(parts):
-            acc[n] += part
-
-    @pl.when(step == steps - 1)
-    def _():
-        p1, b1, s2, p3, b3, s0 = (acc[n] + part for n, part in enumerate(parts))
-        s1 = jnp.concatenate([p1[:, :half] + b1[:, half:], p1[:, half:] - b1[:, :half]], axis=1)
-        s3 = jnp.concatenate([p3[:, :half] - b3[:, half:], p3[:, half:] + b3[:, :half]], axis=1)
-        outs = (near.at[0], swap.at[0], mates.at[0], swap.at[1])
-        for s, value in enumerate((s1, s2, s3, s0)):
+    for copy in copies + tables:
+        copy.start()
+
+    nbands = bands.shape[1]
+    width = swap.shape[2] // nbands
+    rounds = bands.shape[2]
+    used = (listed[...] * bands[0]).astype(jnp.float32)
+    pick = lax.broadcasted_iota(jnp.int32, (rounds, rounds), 0) == lax.broadcasted_iota(
+        jnp.int32, (rounds, rounds), 1
+    )
+    weight = jnp.concatenate(
+        [
+            jnp.broadcast_to(
+                jnp.sum(
+                    jnp.where(pick, jnp.broadcast_to(used[j : j + 1], (rounds, rounds)), 0.0),
+                    axis=1,
+                    keepdims=True,
+                ),
+                (rounds, width),
+            )
+            for j in range(nbands)
+        ],
+        axis=1,
+    ).astype(jnp.bfloat16)
+    for n in range(2):
+        swap[n, channels:, :] = weight
+
+    for h in range(2):
+        for copy in copies[h * Q : (h + 1) * Q]:
+            copy.wait()
+        here = pl.ds(h * depth, depth)
+        q0, q1, q2, q3 = (time[:, pl.ds(q * quarter + h * depth, depth)] for q in range(Q))
+        folds[0, 0, :, here] = q0 - q2
+        folds[0, 1, :, here] = q1 - q3
+        even = q0.astype(jnp.float32) + q2.astype(jnp.float32)
+        odd = q1.astype(jnp.float32) + q3.astype(jnp.float32)
+        folds[1, 0, :, here] = (even - odd).astype(jnp.bfloat16)
+        folds[1, 1, :, here] = (even + odd).astype(jnp.bfloat16)
+    tables[0].wait()
+
+    def store(values):
+        for n, value in enumerate(values):
+            swap[lax.bitwise_xor(side, n), :channels, :] = value.astype(jnp.bfloat16)
+
+    @pl.when(core == 0)
+    def _():
+        store(real_classes(folds.at[1], sent_table))
+
+    @pl.when(core == 1)
+    def _():
+        store(complex_classes(folds.at[0], sent_table))
+
+    tables[1].wait()
+
+
+def keep_kernel(swap, folds, table, near, mates):
+    me = lax.rem(lax.axis_index(AXIS), Q)
+    core, side = lax.rem(me, 2), me // 2
+    channels = folds.shape[2]
+    near[0, channels:, :] = swap[0, channels:, :]
+    mates[0, channels:, :] = swap[0, channels:, :]
+
+    def store(values):
+        for n, value in enumerate(values):
             value = value.astype(jnp.bfloat16)
-            for p, out in enumerate(outs):
-
-                @pl.when(lax.bitwise_xor(me, s) == p)
-                def _():
-                    out[:channels, :] = value
-
-        cols = near.shape[2]
-        nbands, rounds = bands.shape[1], bands.shape[2]
-        width = L // nbands
-        used = (listed[...] * bands[0]).astype(jnp.float32)
-        for j in range(nbands):
-            part, lane = divmod(j * width, cols)
-            for d in range(rounds):
-                row = part * rounds + d
-                weight[row : row + 1, lane : lane + width] = jnp.broadcast_to(
-                    used[j : j + 1, d : d + 1], (1, width)
-                )
-        for out in outs:
-            out[channels:, :] = weight[...].astype(jnp.bfloat16)
-
-
-def spectrum_call(strain, listed, bands, steps=2):
+
+            @pl.when(side == n)
+            def _():
+                near[0, :channels, :] = value
+
+            @pl.when(side != n)
+            def _():
+                mates[0, :channels, :] = value
+
+    @pl.when(core == 0)
+    def _():
+        store(complex_classes(folds.at[0], table))
+
+    @pl.when(core == 1)
+    def _():
+        store(real_classes(folds.at[1], table))
+
+
+def send_call(strain, listed, bands):
     channels, samples = strain.shape
     table = forward_table(samples)
-    cols = table.shape[2]
-    depth = samples // Q // steps
-    rows = channels + bands.shape[2] * L // cols
-    quarter = [
-        pl.BlockSpec((channels, depth), lambda k, q=q: (0, q * steps + k)) for q in range(Q)
-    ]
+    rows, cols = channels + bands.shape[2], table.shape[3]
+    quarter = samples // Q
     return pl.pallas_call(
-        spectrum_kernel,
-        grid=(steps,),
-        in_specs=[
-            pl.BlockSpec(listed.shape, lambda k: (0, 0)),
-            pl.BlockSpec(bands.shape, lambda k: (0, 0, 0)),
-            *quarter,
-            pl.BlockSpec((Q, depth, cols), lambda k: (0, k, 0)),
-        ],
-        out_specs=[pl.BlockSpec(memory_space=pltpu.VMEM)] * 3,
+        send_kernel,
+        in_specs=[HBM_SPEC, HBM_SPEC, VMEM_SPEC, VMEM_SPEC],
+        out_specs=[VMEM_SPEC] * 3,
         out_shape=[
             pltpu.VMEM((2, rows, cols), jnp.bfloat16),
-            pltpu.VMEM((2, rows, cols), jnp.bfloat16),
-            pltpu.VMEM((2, rows, cols), jnp.bfloat16),
+            pltpu.VMEM((2, 2, channels, quarter), jnp.bfloat16),
+            pltpu.VMEM((2, quarter, cols), jnp.bfloat16),
         ],
         scratch_shapes=[
-            pltpu.VMEM((6, channels, cols), jnp.float32),
-            pltpu.VMEM((rows - channels, cols), jnp.float32),
+            pltpu.VMEM((channels, samples), jnp.bfloat16),
+            pltpu.VMEM((2, quarter, cols), jnp.bfloat16),
+            pltpu.SemaphoreType.DMA((2 * Q + 2,)),
         ],
-        compiler_params=pltpu.CompilerParams(
-            dimension_semantics=("arbitrary",), vmem_limit_bytes=LIMIT
-        ),
-        name="spectrum",
-    )(in_hbm(listed), in_hbm(bands), *[in_hbm(strain)] * Q, in_hbm(jnp.asarray(table)))
-
-
-UNROLL = 3
-LIMIT = 16 << 20
+        compiler_params=pltpu.CompilerParams(vmem_limit_bytes=LIMIT),
+        name="spectrum_sent",
+    )(in_hbm(strain), in_hbm(jnp.asarray(table)), in_hbm(listed), in_hbm(bands))
 
 
 def unit_table(rounds):
@@ -157,46 +204,73 @@
                 units[far].append((target, source, d, i, mask, row))
         early.append(units[0])
         late.append(units[1])
-    return np.asarray(early, np.int32), np.asarray(late, np.int32)
-
-
-def run_units(table, me, spec, mask, steering, inv, lag_range, window):
+    return twins_first(early), twins_first(late)
+
+
+def twins_first(tables):
+    ordered = []
+    for units in tables:
+        twins, single = [], {}
+        for unit in units:
+            if unit[2] in single:
+                twins.append((single.pop(unit[2]), unit))
+            else:
+                single[unit[2]] = unit
+        ordered.append((twins, list(single.values())))
+    count = min(len(twins) for twins, _ in ordered)
+    table = []
+    for twins, rest in ordered:
+        flat = [unit for pair in twins for unit in pair] + rest
+        table.append(flat)
+    return np.asarray(table, np.int32).reshape(len(tables), -1), count
+
+
+def run_units(table, me, spec, mask, steering, inv, lag_range, window, unroll, twins):
     channels, angles = steering.shape[2], steering.shape[1]
     cols = spec.shape[2]
     half = cols // 2
 
     def body(n, carry):
         units = [
-            [table[me, (n * UNROLL + u) * 6 + e] for e in range(6)] for u in range(UNROLL)
+            [table[me, (n * unroll + u) * 6 + e] for e in range(6)] for u in range(unroll)
         ]
         beams = []
         for target, source, d, _, _, _ in units:
-            near_re = spec[target, :channels, :half].astype(jnp.float32)
-            near_im = spec[target, :channels, half:].astype(jnp.float32)
-            far_re = spec[source, :channels, :half].astype(jnp.float32)
-            far_im = spec[source, :channels, half:].astype(jnp.float32)
+            near_re, near_im = spec[target, :channels, :half], spec[target, :channels, half:]
+            far_re, far_im = spec[source, :channels, :half], spec[source, :channels, half:]
             real = near_re * far_re + near_im * far_im
             imag = near_im * far_re - near_re * far_im
-            cross = jnp.concatenate([real, imag], axis=1).astype(jnp.bfloat16)
+            cross = jnp.concatenate([real, imag], axis=1)
             beams.append(dot(steering[d], cross).astype(jnp.bfloat16))
         beams = dot(jnp.concatenate(beams, axis=0), inv[...])
-        for u, (_, _, d, slot, target, row) in enumerate(units):
+        masked = []
+        for u, (_, _, _, _, target, row) in enumerate(units):
             weight = jnp.concatenate(
                 [mask[target, h, pl.ds(row, 1), :] for h in range(L // cols)], axis=1
             )
-            masked = (beams[u * angles : (u + 1) * angles, :] * weight).astype(jnp.bfloat16)
-            window[slot] += dot(masked, lag_range[d])
+            masked.append((beams[u * angles : (u + 1) * angles, :] * weight).astype(jnp.bfloat16))
+        for u in range(0, 2 * twins, 2):
+            part = dot(jnp.concatenate(masked[u : u + 2], axis=0), lag_range[units[u][2]])
+            window[units[u][3]] += part[:angles]
+            window[units[u + 1][3]] += part[angles:]
+        for u in range(2 * twins, unroll):
+            window[units[u][3]] += dot(masked[u], lag_range[units[u][2]])
         return carry
 
-    lax.fori_loop(0, table.shape[1] // (6 * UNROLL), body, 0)
-
-
-def fill_mask(mask, entry, spec, slot, channels):
+    lax.fori_loop(0, table.shape[1] // (6 * unroll), body, 0)
+
+
+def fill_mask(mask, entry, spec, slot, channels, nbands):
     rounds = mask.shape[2] // 2
     rows = spec[slot, channels:, :].astype(jnp.float32)
-    for h in range(mask.shape[1]):
-        mask[entry, h, :rounds, :] = rows[h * rounds : (h + 1) * rounds, :]
-        mask[entry, h, rounds:, :] = jnp.ones((rounds, mask.shape[3]), jnp.float32)
+    cols = mask.shape[3]
+    for j in range(nbands):
+        h, lane = divmod(j * (mask.shape[1] * cols // nbands), cols)
+        width = mask.shape[1] * cols // nbands
+        mask[entry, h, :rounds, lane : lane + width] = jnp.broadcast_to(
+            rows[:, j * (cols // nbands) : j * (cols // nbands) + 1], (rounds, width)
+        )
+    mask[entry, :, rounds:, :] = jnp.ones((mask.shape[1], rounds, cols), jnp.float32)
 
 
 def neighbour_slots():
@@ -205,7 +279,7 @@
 
 
 def early_kernel(
-    table, near, mates, even, odd, inv, steering, lag_range, spec, window, mask
+    nbands, unroll, twins, table, near, mates, even, odd, inv, steering, lag_range, spec, window, mask
 ):
     me = lax.rem(lax.axis_index(AXIS), Q)
     even_slot, odd_slot = neighbour_slots()
@@ -216,14 +290,14 @@
     window[...] = jnp.zeros_like(window)
     channels = steering.shape[2]
     for p in range(Q):
-        fill_mask(mask, p, spec, p, channels)
+        fill_mask(mask, p, spec, p, channels, nbands)
     for p in range(Q // 2):
-        fill_mask(mask, Q + p, spec, 2 * Q + p, channels)
-    run_units(table, me, spec, mask, steering, inv.at[me], lag_range, window)
+        fill_mask(mask, Q + p, spec, 2 * Q + p, channels, nbands)
+    run_units(table, me, spec, mask, steering, inv.at[me], lag_range, window, unroll, twins)
 
 
 def late_kernel(
-    table, spec_in, window_in, even, odd, inv, steering, lag_range,
+    nbands, unroll, twins, table, spec_in, window_in, even, odd, inv, steering, lag_range,
     keep, send, spec, window, mask,
 ):
     me = lax.rem(lax.axis_index(AXIS), Q)
@@ -232,9 +306,9 @@
     spec[pl.ds(odd_slot + 2, 2)] = odd[...]
     channels = steering.shape[2]
     for p in range(Q):
-        fill_mask(mask, p, spec, p, channels)
-        fill_mask(mask, Q + p, spec, 2 * Q + p, channels)
-    run_units(table, me, spec, mask, steering, inv.at[me], lag_range, window)
+        fill_mask(mask, p, spec, p, channels, nbands)
+        fill_mask(mask, Q + p, spec, 2 * Q + p, channels, nbands)
+    run_units(table, me, spec, mask, steering, inv.at[me], lag_range, window, unroll, twins)
 
     width = window.shape[2] // 3
 
@@ -328,11 +402,6 @@
 
 def image_kernel(kept, received, image):
     image[...] = kept[...] + received[...]
-
-
-VMEM_SPEC = pl.BlockSpec(memory_space=pltpu.VMEM)
-SMEM_SPEC = pl.BlockSpec(memory_space=pltpu.SMEM)
-HBM_SPEC = pl.BlockSpec(memory_space=pl.ANY)
 
 
 def near_vmem(*values):
@@ -351,12 +420,17 @@
     )(*near_vmem(*values))
 
 
-def early_call(table, near, mates, even, odd, inv, steering, lag_range):
+def divide(count, most=8):
+    return max(n for n in range(1, most + 1) if count % n == 0)
+
+
+def early_call(plan, nbands, near, mates, even, odd, inv, steering, lag_range):
     _, rows, cols = near.shape
     angles, group = steering.shape[1], lag_range.shape[2]
     rounds = steering.shape[0] - 1
+    table, _ = plan
     return pl.pallas_call(
-        early_kernel,
+        functools.partial(early_kernel, nbands, divide(table.shape[1] // 6), 0),
         in_specs=[SMEM_SPEC] + [VMEM_SPEC] * 7,
         out_specs=[VMEM_SPEC] * 2,
         out_shape=[
@@ -366,16 +440,17 @@
         scratch_shapes=[pltpu.VMEM((2 * Q, L // cols, 2 * rounds, cols), jnp.float32)],
         compiler_params=pltpu.CompilerParams(vmem_limit_bytes=LIMIT),
         name="early_pairs",
-    )(table, *near_vmem(near, mates, even, odd, inv, steering, lag_range))
-
-
-def late_call(table, spec, window, even, odd, inv, steering, lag_range):
+    )(jnp.asarray(table), *near_vmem(near, mates, even, odd, inv, steering, lag_range))
+
+
+def late_call(plan, nbands, spec, window, even, odd, inv, steering, lag_range):
     cols = spec.shape[2]
     angles, group = steering.shape[1], lag_range.shape[2]
     rounds = steering.shape[0] - 1
     pieces = (Q + 2, angles, group // 3)
+    table, twins = plan
     return pl.pallas_call(
-        late_kernel,
+        functools.partial(late_kernel, nbands, table.shape[1] // 6, twins),
         in_specs=[SMEM_SPEC] + [VMEM_SPEC] * 7,
         out_specs=[VMEM_SPEC] * 4,
         out_shape=[
@@ -388,7 +463,7 @@
         scratch_shapes=[pltpu.VMEM((2 * Q, L // cols, 2 * rounds, cols), jnp.float32)],
         compiler_params=pltpu.CompilerParams(vmem_limit_bytes=LIMIT),
         name="late_pairs",
-    )(table, *near_vmem(spec, window, even, odd, inv, steering, lag_range))[:2]
+    )(jnp.asarray(table), *near_vmem(spec, window, even, odd, inv, steering, lag_range))[:2]
 
 
 def exchange(value, devices, target):
@@ -404,20 +479,21 @@
     def flip(value, by):
         return exchange(value, devices, lambda i: i ^ by)
 
-    near, mates, swap = spectrum_call(strain, pair_listed, jnp.transpose(band_used, (0, 2, 1)))
-    joined = pltpu.VMEM(near.shape, near.dtype)
+    swap, folds, table = send_call(strain, pair_listed, jnp.transpose(band_used, (0, 2, 1)))
+    joined = pltpu.VMEM(swap.shape, swap.dtype)
+    near, mates = local_call(keep_kernel, "spectrum_kept", [joined, joined], swap, folds, table)
     near, mates = local_call(
         join_kernel, "join", [joined, joined], flip(swap, 1), near, mates, aliases={1: 0, 2: 1}
     )
     mates = flip(mates, 2)
     near_odd, near_even = planes(near, 1), planes(near, 0)
     far_odd, far_even = planes(mates, 1), planes(mates, 0)
-    early, late = (jnp.asarray(t.reshape(Q, -1)) for t in unit_table(steering.shape[0] - 1))
+    early, late = unit_table(steering.shape[0] - 1)
+    nbands = band_used.shape[2]
     inv = jnp.asarray(inverse_table(strain.shape[1]))
-    near, steering, lag_range, inv = lax.optimization_barrier((near, steering, lag_range, inv))
     shared = (inv, steering, lag_range)
-    spec, window = early_call(early, near, mates, near_even, near_odd, *shared)
-    kept, send = late_call(late, spec, window, far_even, far_odd, *shared)
+    spec, window = early_call(early, nbands, near, mates, near_even, near_odd, *shared)
+    kept, send = late_call(late, nbands, spec, window, far_even, far_odd, *shared)
 
     def pieces(count, dtype):
         return pltpu.VMEM(((count,) if count else ()) + kept.shape[1:], dtype)

time: 44.7 us -> 43.1 us (0.964)
  Pallas kernels: 13.8 us -> 12.2 us
    pallas_call x3, Pallas kernels: 13.1 us -> 10.7 us  [the longest x1 4.25 us: early_call(): pl.pallas_call(functools.partial(early_kernel, nbands, divide(table.shape...]
    pallas_call x5 -> x6, Pallas kernels: 0.73 us -> 1.48 us  [local_call(): pl.pallas_call(kernel, in_specs=[VMEM_SPEC] * len(values), out_specs=[VME...]
where the time goes in v6:
time: 43.1 us; the launch traced here: 42.9 us
  starting transfers between devices  19.5 us (45%)
  Pallas kernels  12.2 us (28%)
  waiting for transfers between devices  11.1 us (26%)
    ppermute x10, starting transfers between devices, exchange(): return lax.ppermute(value, AXIS, pairs)  19.5 us
    ppermute x10, waiting for transfers between devices, exchange(): return lax.ppermute(value, AXIS, pairs)  11.1 us
    pallas_call x1, Pallas kernels, early_call(): pl.pallas_call(functools.partial(early_kernel, nbands, divide(table.shape...  4.25 us
    pallas_call x1, Pallas kernels, send_call(): pl.pallas_call(send_kernel, in_specs=[HBM_SPEC, HBM_SPEC, VMEM_SPEC, VMEM...  3.22 us
    pallas_call x1, Pallas kernels, late_call(): pl.pallas_call(functools.partial(late_kernel, nbands, table.shape[1] // 6...  3.21 us
    pallas_call x6, Pallas kernels, local_call(): pl.pallas_call(kernel, in_specs=[VMEM_SPEC] * len(values), out_specs=[VME...  1.48 us
  transfers between devices with their start and end apart: 10, of which 7 were waited for; matrix products, arithmetic and copies ran while one was open for 0% of the time, Pallas kernels for 12%

profile of v6, /device:TPU:0, one launch (start us, length us, event | category | flops | bytes accessed | tf_op | source)
XLA Modules:
  0.0 42.9 jit_solution(339150065886027385)
XLA Ops:
  0.0 0.0 copy-start.1
  0.0 3.2 %spectrum_sent.1 = (bf16[2,264,256]{2,1,0:T(8,128)(2,1)S(1)}, bf16[2,2,256,1024]{3,2,1,0:T(8,128)(2,1)S(1)}, bf16[2,1024,256]{2,1,0:T(8,128)(2,1)S(1)}) custom-call(bf16[256,4096]{1,0:T(8,128)(2,1)} %strain.1, bf16[2,2,1024,256]{3,2,1,0:T(8,128)(2,1)} %constant.8.clone.table, s32[1,8]{1,0:T(1,128)} %listed.1, s32[1,4,8]{2,1,0:T(4,128)} %bitcast.1), custom_call_target="tpu_custom_call" | custom-call | tf_op jit(solution)/shard_map/spectrum_sent/pallas_call | solution.py:170
  3.2 0.8 %collective-permute-start = (bf16[2,264,256]{2,1,0:T(8,128)(2,1)S(1)}, bf16[2,264,256]{2,1,0:T(8,128)(2,1)S(1)}, u32[]{:S(2)}, u32[]{:S(2)}) collective-permute-start(bf16[2,264,256]{2,1,0:T(8,128)(2,1)S(1)} %get-tuple-element.22.swap), channel_id=1, source_target_pairs={{0,1},{1,0},{2,3},{3,2},{4,5},{5,4},{6,7},{7,6},{8,9},{9,8},{10,11... | collective-permute-start | bytes 811016 | tf_op jit(solution)/shard_map/ppermute | solution.py:472
  4.1 0.0 copy-start
  4.1 0.7 %spectrum_kept.1 = (bf16[2,264,256]{2,1,0:T(8,128)(2,1)S(1)}, bf16[2,264,256]{2,1,0:T(8,128)(2,1)S(1)}) custom-call(bf16[2,264,256]{2,1,0:T(8,128)(2,1)S(1)} %get-tuple-element.22.swap, bf16[2,2,256,1024]{3,2,1,0:T(8,128)(2,1)S(1)} %get-tuple-element.23.folds, bf16[2,1024,256]{2,1,0:T(8,128)(2,1)S(1)} %get-tuple-element.24.table), custom_call_target="tpu_custom_call" | custom-call | tf_op jit(solution)/shard_map/spectrum_kept/pallas_call | solution.py:412
  4.8 0.4 collective-permute-done.swap
  5.2 2.7 %collective-permute-start.1 = (bf16[2,264,256]{2,1,0:T(8,128)(2,1)S(1)}, bf16[2,264,256]{2,1,0:T(8,128)(2,1)S(1)}, u32[]{:S(2)}, u32[]{:S(2)}) collective-permute-start(bf16[2,264,256]{2,1,0:T(8,128)(2,1)S(1)} %get-tuple-element.28), channel_id=1, source_target_pairs={{0,2},{1,3},{2,0},{3,1},{4,6},{5,7},{6,4},{7,5},{8,10},{9,11},{10,... | collective-permute-start | bytes 811016 | tf_op jit(solution)/shard_map/ppermute | solution.py:472
  7.9 0.8 %collective-permute-start.3 = (bf16[2,264,256]{2,1,0:T(8,128)(2,1)S(1)}, bf16[2,264,256]{2,1,0:T(8,128)(2,1)S(1)}, u32[]{:S(2)}, u32[]{:S(2)}) collective-permute-start(bf16[2,264,256]{2,1,0:T(8,128)(2,1)S(1)} %get-tuple-element.27.near), channel_id=1, source_target_pairs={{4,8},{5,9},{6,10},{7,11},{8,4},{9,5},{10,6},{11,7},{20,24},{21,25... | collective-permute-start | bytes 811016 | tf_op jit(solution)/shard_map/ppermute | solution.py:472
  8.7 4.4 %collective-permute-start.2 = (bf16[2,264,256]{2,1,0:T(8,128)(2,1)S(1)}, bf16[2,264,256]{2,1,0:T(8,128)(2,1)S(1)}, u32[]{:S(2)}, u32[]{:S(2)}) collective-permute-start(bf16[2,264,256]{2,1,0:T(8,128)(2,1)S(1)} %get-tuple-element.27.near), channel_id=1, source_target_pairs={{0,4},{1,5},{2,6},{3,7},{4,0},{5,1},{6,2},{7,3},{8,12},{9,13},{10,... | collective-permute-start | bytes 811016 | tf_op jit(solution)/shard_map/ppermute | solution.py:472
  13.2 1.5 %collective-permute-done.1.mates = bf16[2,264,256]{2,1,0:T(8,128)(2,1)S(1)} collective-permute-done((bf16[2,264,256]{2,1,0:T(8,128)(2,1)S(1)}, bf16[2,264,256]{2,1,0:T(8,128)(2,1)S(1)}, u32[]{:S(2)}, u32[]{:S(2)}) %collective-permute-start.1) | collective-permute-done | bytes 270368 | tf_op jit(solution)/shard_map/ppermute | solution.py:472
  14.7 0.7 %collective-permute-start.5 = (bf16[2,264,256]{2,1,0:T(8,128)(2,1)S(1)}, bf16[2,264,256]{2,1,0:T(8,128)(2,1)S(1)}, u32[]{:S(2)}, u32[]{:S(2)}) collective-permute-start(bf16[2,264,256]{2,1,0:T(8,128)(2,1)S(1)} %collective-permute-done.1.mates), channel_id=1, source_target_pairs={{4,8},{5,9},{6,10},{7,11},{8,4},{9,5},{10,6},{11,7},{20,24},{21,25... | collective-permute-start | bytes 811016 | tf_op jit(solution)/shard_map/ppermute | solution.py:472
  15.4 4.7 %collective-permute-start.4 = (bf16[2,264,256]{2,1,0:T(8,128)(2,1)S(1)}, bf16[2,264,256]{2,1,0:T(8,128)(2,1)S(1)}, u32[]{:S(2)}, u32[]{:S(2)}) collective-permute-start(bf16[2,264,256]{2,1,0:T(8,128)(2,1)S(1)} %collective-permute-done.1.mates), channel_id=1, source_target_pairs={{0,4},{1,5},{2,6},{3,7},{4,0},{5,1},{6,2},{7,3},{8,12},{9,13},{10,... | collective-permute-start | bytes 811016 | tf_op jit(solution)/shard_map/ppermute | solution.py:472
  20.1 0.0 collective-permute-done.3.odd
  20.1 0.0 collective-permute-done.2.even
  20.1 0.0 copy-done.1
  20.1 0.0 copy-done
  20.1 0.0 copy-done.2
  20.1 0.0 copy-done.4
  20.1 4.2 %early_pairs.1 = (bf16[12,264,256]{2,1,0:T(8,128)(2,1)S(1)}, f32[8,128,384]{2,1,0:T(8,128)S(1)}) custom-call(s32[4,126]{1,0:T(4,128)S(1)} %copy-done.4, bf16[2,264,256]{2,1,0:T(8,128)(2,1)S(1)} %get-tuple-element.27.near, bf16[2,264,256]{2,1,0:T(8,128)(2,1)S(1)} %collective-permute-done.1.mates, bf16[2,264,256]{2,1,0:T(8,128)(2,1)S(1)} %collective-permute-done.2.even, ...), custom_call_target="tpu_custom_call" | custom-call | tf_op jit(solution)/shard_map/early_pairs/pallas_call | solution.py:432
  24.4 0.0 collective-permute-done.5.odd
  24.4 1.3 %collective-permute-done.4.even = bf16[2,264,256]{2,1,0:T(8,128)(2,1)S(1)} collective-permute-done((bf16[2,264,256]{2,1,0:T(8,128)(2,1)S(1)}, bf16[2,264,256]{2,1,0:T(8,128)(2,1)S(1)}, u32[]{:S(2)}, u32[]{:S(2)}) %collective-permute-start.4) | collective-permute-done | bytes 270368 | tf_op jit(solution)/shard_map/ppermute | solution.py:472
  25.7 0.0 copy-done.3
  25.7 3.2 %late_pairs.1 = (f32[6,128,128]{2,1,0:T(8,128)S(1)}, bf16[6,128,128]{2,1,0:T(8,128)(2,1)S(1)}, bf16[12,264,256]{2,1,0:T(8,128)(2,1)S(1)}, f32[8,128,384]{2,1,0:T(8,128)S(1)}) custom-call(s32[4,90]{1,0:T(4,128)S(1)} %copy-done.3, bf16[12,264,256]{2,1,0:T(8,128)(2,1)S(1)} %get-tuple-element.29.spec_in, ...), custom_call_target="tpu_custom_call", output_to_operand_aliasing={{2}: (1, {}), {3}: (2, {})} | custom-call | tf_op jit(solution)/shard_map/late_pairs/pallas_call | solution.py:452
  28.9 0.1 collective-permute-start.6
  29.0 1.4 %collective-permute-done.6.received = bf16[6,128,128]{2,1,0:T(8,128)(2,1)S(1)} collective-permute-done((bf16[6,128,128]{2,1,0:T(8,128)(2,1)S(1)}, bf16[6,128,128]{2,1,0:T(8,128)(2,1)S(1)}, u32[]{:S(2)}, u32[]{:S(2)}) %collective-permute-start.6) | collective-permute-done | bytes 196640 | tf_op jit(solution)/shard_map/ppermute | solution.py:472
  30.5 1.6 %collective-permute-start.7 = (bf16[3,128,128]{2,1,0:T(8,128)(2,1)S(1)}, bf16[3,128,128]{2,1,0:T(8,128)(2,1)S(1)}, u32[]{:S(2)}, u32[]{:S(2)}) collective-permute-start(bf16[3,128,128]{2,1,0:T(8,128)(2,1)S(1)} %get-tuple-element.34), channel_id=1, source_target_pairs={{0,2},{1,3},{2,0},{3,1},{4,6},{5,7},{6,4},{7,5},{8,10},{9,11},{10,... | collective-permute-start | bytes 294920 | tf_op jit(solution)/shard_map/ppermute | solution.py:472
  32.1 3.3 %collective-permute-done.7.received = bf16[3,128,128]{2,1,0:T(8,128)(2,1)S(1)} collective-permute-done((bf16[3,128,128]{2,1,0:T(8,128)(2,1)S(1)}, bf16[3,128,128]{2,1,0:T(8,128)(2,1)S(1)}, u32[]{:S(2)}, u32[]{:S(2)}) %collective-permute-start.7) | collective-permute-done | bytes 98336 | tf_op jit(solution)/shard_map/ppermute | solution.py:472
  35.4 3.7 %collective-permute-start.8 = (bf16[2,128,128]{2,1,0:T(8,128)(2,1)S(1)}, bf16[2,128,128]{2,1,0:T(8,128)(2,1)S(1)}, u32[]{:S(2)}, u32[]{:S(2)}) collective-permute-start(bf16[2,128,128]{2,1,0:T(8,128)(2,1)S(1)} %get-tuple-element.36), channel_id=1, source_target_pairs={{0,4},{1,9},{2,6},{4,8},{5,13},{6,10},{7,3},{8,12},{10,14},{11,7},... | collective-permute-start | bytes 196616 | tf_op jit(solution)/shard_map/ppermute | solution.py:472
  39.1 1.9 %collective-permute-done.8.received = bf16[2,128,128]{2,1,0:T(8,128)(2,1)S(1)} collective-permute-done((bf16[2,128,128]{2,1,0:T(8,128)(2,1)S(1)}, bf16[2,128,128]{2,1,0:T(8,128)(2,1)S(1)}, u32[]{:S(2)}, u32[]{:S(2)}) %collective-permute-start.8) | collective-permute-done | bytes 65568 | tf_op jit(solution)/shard_map/ppermute | solution.py:472
  41.0 0.1 collective-permute-start.9
  41.1 1.2 %collective-permute-done.9.received = f32[128,128]{1,0:T(8,128)S(1)} collective-permute-done((f32[128,128]{1,0:T(8,128)S(1)}, f32[128,128]{1,0:T(8,128)S(1)}, u32[]{:S(2)}, u32[]{:S(2)}) %collective-permute-start.9) | collective-permute-done | bytes 65568 | tf_op jit(solution)/shard_map/ppermute | solution.py:472
  42.3 0.6 %image.1 = f32[128,128]{1,0:T(8,128)} custom-call(f32[128,128]{1,0:T(8,128)S(1)} %get-tuple-element.37.kept, f32[128,128]{1,0:T(8,128)S(1)} %collective-permute-done.9.received), custom_call_target="tpu_custom_call" | custom-call | tf_op jit(solution)/shard_map/image/pallas_call | solution.py:412
  (7 shorter events, 0.1 us)
Async XLA Ops:
  0.0 20.1 %copy-start.1 = (bf16[4,256,512]{2,1,0:T(8,128)(2,1)S(1)}, bf16[4,256,512]{2,1,0:T(8,128)(2,1)}, u32[]{:S(2)}) copy-start(bf16[4,256,512]{2,1,0:T(8,128)(2,1)} %constant.9.clone.inv) | copy-start | bytes 3145732
  3.2 2.0 %collective-permute-start = (bf16[2,264,256]{2,1,0:T(8,128)(2,1)S(1)}, bf16[2,264,256]{2,1,0:T(8,128)(2,1)S(1)}, u32[]{:S(2)}, u32[]{:S(2)}) collective-permute-start(bf16[2,264,256]{2,1,0:T(8,128)(2,1)S(1)} %get-tuple-element.22.swap), channel_id=1, source_target_pairs={{0,1},{1,0},{2,3},{3,2},{4,5},{5,4},{6,7},{7,6},{8,9},{9,8},{10,11... | collective-permute-start | bytes 811016 | tf_op jit(solution)/shard_map/ppermute | solution.py:472
  4.1 16.0 %copy-start = (bf16[9,512,384]{2,1,0:T(8,128)(2,1)S(1)}, bf16[9,512,384]{2,1,0:T(8,128)(2,1)}, u32[]{:S(2)}) copy-start(bf16[9,512,384]{2,1,0:T(8,128)(2,1)} %lag_range.3) | copy-start | bytes 10616836
  4.1 16.0 %copy-start.2 = (bf16[9,128,256]{2,1,0:T(8,128)(2,1)S(1)}, bf16[9,128,256]{2,1,0:T(8,128)(2,1)}, u32[]{:S(2)}) copy-start(bf16[9,128,256]{2,1,0:T(8,128)(2,1)} %steering.3) | copy-start | bytes 1769476
  4.1 16.0 %copy-start.4 = (s32[4,126]{1,0:T(4,128)S(1)}, s32[4,126]{1,0:T(4,128)}, u32[]{:S(2)}) copy-start(s32[4,126]{1,0:T(4,128)} %constant.10.clone.table) | copy-start | bytes 6052
  5.2 9.5 %collective-permute-start.1 = (bf16[2,264,256]{2,1,0:T(8,128)(2,1)S(1)}, bf16[2,264,256]{2,1,0:T(8,128)(2,1)S(1)}, u32[]{:S(2)}, u32[]{:S(2)}) collective-permute-start(bf16[2,264,256]{2,1,0:T(8,128)(2,1)S(1)} %get-tuple-element.28), channel_id=1, source_target_pairs={{0,2},{1,3},{2,0},{3,1},{4,6},{5,7},{6,4},{7,5},{8,10},{9,11},{10,... | collective-permute-start | bytes 811016 | tf_op jit(solution)/shard_map/ppermute | solution.py:472
  7.9 17.8 %copy-start.3 = (s32[4,90]{1,0:T(4,128)S(1)}, s32[4,90]{1,0:T(4,128)}, u32[]{:S(2)}) copy-start(s32[4,90]{1,0:T(4,128)} %constant.11.clone.table) | copy-start | bytes 4324
  7.9 12.1 %collective-permute-start.3 = (bf16[2,264,256]{2,1,0:T(8,128)(2,1)S(1)}, bf16[2,264,256]{2,1,0:T(8,128)(2,1)S(1)}, u32[]{:S(2)}, u32[]{:S(2)}) collective-permute-start(bf16[2,264,256]{2,1,0:T(8,128)(2,1)S(1)} %get-tuple-element.27.near), channel_id=1, source_target_pairs={{4,8},{5,9},{6,10},{7,11},{8,4},{9,5},{10,6},{11,7},{20,24},{21,25... | collective-permute-start | bytes 811016 | tf_op jit(solution)/shard_map/ppermute | solution.py:472
  8.7 11.3 %collective-permute-start.2 = (bf16[2,264,256]{2,1,0:T(8,128)(2,1)S(1)}, bf16[2,264,256]{2,1,0:T(8,128)(2,1)S(1)}, u32[]{:S(2)}, u32[]{:S(2)}) collective-permute-start(bf16[2,264,256]{2,1,0:T(8,128)(2,1)S(1)} %get-tuple-element.27.near), channel_id=1, source_target_pairs={{0,4},{1,5},{2,6},{3,7},{4,0},{5,1},{6,2},{7,3},{8,12},{9,13},{10,... | collective-permute-start | bytes 811016 | tf_op jit(solution)/shard_map/ppermute | solution.py:472
  14.7 9.6 %collective-permute-start.5 = (bf16[2,264,256]{2,1,0:T(8,128)(2,1)S(1)}, bf16[2,264,256]{2,1,0:T(8,128)(2,1)S(1)}, u32[]{:S(2)}, u32[]{:S(2)}) collective-permute-start(bf16[2,264,256]{2,1,0:T(8,128)(2,1)S(1)} %collective-permute-done.1.mates), channel_id=1, source_target_pairs={{4,8},{5,9},{6,10},{7,11},{8,4},{9,5},{10,6},{11,7},{20,24},{21,25... | collective-permute-start | bytes 811016 | tf_op jit(solution)/shard_map/ppermute | solution.py:472
  15.4 10.3 %collective-permute-start.4 = (bf16[2,264,256]{2,1,0:T(8,128)(2,1)S(1)}, bf16[2,264,256]{2,1,0:T(8,128)(2,1)S(1)}, u32[]{:S(2)}, u32[]{:S(2)}) collective-permute-start(bf16[2,264,256]{2,1,0:T(8,128)(2,1)S(1)} %collective-permute-done.1.mates), channel_id=1, source_target_pairs={{0,4},{1,5},{2,6},{3,7},{4,0},{5,1},{6,2},{7,3},{8,12},{9,13},{10,... | collective-permute-start | bytes 811016 | tf_op jit(solution)/shard_map/ppermute | solution.py:472
  28.9 1.5 %collective-permute-start.6 = (bf16[6,128,128]{2,1,0:T(8,128)(2,1)S(1)}, bf16[6,128,128]{2,1,0:T(8,128)(2,1)S(1)}, u32[]{:S(2)}, u32[]{:S(2)}) collective-permute-start(bf16[6,128,128]{2,1,0:T(8,128)(2,1)S(1)} %get-tuple-element.32), channel_id=1, source_target_pairs={{0,1},{1,0},{2,3},{3,2},{4,5},{5,4},{6,7},{7,6},{8,9},{9,8},{10,11... | collective-permute-start | bytes 589832 | tf_op jit(solution)/shard_map/ppermute | solution.py:472
  30.5 4.9 %collective-permute-start.7 = (bf16[3,128,128]{2,1,0:T(8,128)(2,1)S(1)}, bf16[3,128,128]{2,1,0:T(8,128)(2,1)S(1)}, u32[]{:S(2)}, u32[]{:S(2)}) collective-permute-start(bf16[3,128,128]{2,1,0:T(8,128)(2,1)S(1)} %get-tuple-element.34), channel_id=1, source_target_pairs={{0,2},{1,3},{2,0},{3,1},{4,6},{5,7},{6,4},{7,5},{8,10},{9,11},{10,... | collective-permute-start | bytes 294920 | tf_op jit(solution)/shard_map/ppermute | solution.py:472
  35.4 5.5 %collective-permute-start.8 = (bf16[2,128,128]{2,1,0:T(8,128)(2,1)S(1)}, bf16[2,128,128]{2,1,0:T(8,128)(2,1)S(1)}, u32[]{:S(2)}, u32[]{:S(2)}) collective-permute-start(bf16[2,128,128]{2,1,0:T(8,128)(2,1)S(1)} %get-tuple-element.36), channel_id=1, source_target_pairs={{0,4},{1,9},{2,6},{4,8},{5,13},{6,10},{7,3},{8,12},{10,14},{11,7},... | collective-permute-start | bytes 196616 | tf_op jit(solution)/shard_map/ppermute | solution.py:472
  41.0 1.3 %collective-permute-start.9 = (f32[128,128]{1,0:T(8,128)S(1)}, f32[128,128]{1,0:T(8,128)S(1)}, u32[]{:S(2)}, u32[]{:S(2)}) collective-permute-start(f32[128,128]{1,0:T(8,128)S(1)} %get-tuple-element.38), channel_id=1, source_target_pairs={{0,1},{1,0},{2,3},{3,2},{4,5},{5,4},{6,7},{7,6},{8,9},{9,8},{10,11... | collective-permute-start | bytes 196616 | tf_op jit(solution)/shard_map/ppermute | solution.py:472

commit v7 on v6

--- a/solution.py
+++ b/solution.py
@@ -18,13 +18,21 @@
 HBM_SPEC = pl.BlockSpec(memory_space=pl.ANY)
 
 
-def forward_table(samples):
-    freqs = F // Q
-    t = np.arange(samples // Q, dtype=np.int64)[None, :, None]
-    k = Q * np.arange(freqs, dtype=np.int64)[None, None, :] + np.arange(Q)[:, None, None] + 1
-    phase = (t * k % samples) * (2.0 * np.pi / samples)
-    table = np.concatenate([np.cos(phase), -np.sin(phase)], axis=2) * samples ** (-0.5)
-    return np.stack([table[0::2], table[1::2]]).astype(jnp.bfloat16)
+STEP = 32
+
+
+def forward_factors(samples):
+    m = np.arange(F // Q, dtype=np.int64)
+    k = (Q * m[None, :] + np.arange(Q)[:, None] + 1)[:, None, :]
+    scale = samples ** (-0.5)
+    parts = []
+    for step, factor in ((STEP, scale), (1, 1.0)):
+        count = samples // Q // STEP if step == STEP else STEP
+        t = step * np.arange(count, dtype=np.int64)[None, :, None]
+        phase = (t * k % samples) * (2.0 * np.pi / samples)
+        parts += [np.cos(phase) * factor, np.sin(phase) * factor]
+    table = np.stack(parts)
+    return np.stack([table[:, 0::2], table[:, 1::2]]).astype(np.float32)
 
 
 def inverse_table(samples):
@@ -44,17 +52,18 @@
     return jnp.dot(a, b, preferred_element_type=jnp.float32)
 
 
+def combine(a, b):
+    half = a.shape[1] // 2
+    return jnp.concatenate([a[:, :half] + b[:, half:], a[:, half:] - b[:, :half]], axis=1)
+
+
 def complex_classes(folds, table):
     channels = folds.shape[1]
-    half = table.shape[2] // 2
     both = folds[...].reshape(2 * channels, folds.shape[2])
     values = []
     for n, sign in ((0, 1.0), (1, -1.0)):
         product = dot(both, table[n])
-        a, b = product[:channels], product[channels:] * sign
-        values.append(
-            jnp.concatenate([a[:, :half] + b[:, half:], a[:, half:] - b[:, :half]], axis=1)
-        )
+        values.append(combine(product[:channels], product[channels:] * sign))
     return values
 
 
@@ -62,12 +71,32 @@
     return [dot(folds[n], table[n]) for n in range(2)]
 
 
-def send_kernel(strain, table, listed, bands, swap, folds, kept_table, time, sent_table, sems):
+def fill_table(factors, table):
+    half = table.shape[2] // 2
+    for n in range(2):
+        cos_v, sin_v = factors[2, n], factors[3, n]
+        for u in range(factors.shape[2]):
+            cos_u, sin_u = factors[0, n, u : u + 1, :], factors[1, n, u : u + 1, :]
+            rows = slice(u * STEP, (u + 1) * STEP)
+            table[n, rows, :half] = (cos_u * cos_v - sin_u * sin_v).astype(jnp.bfloat16)
+            table[n, rows, half:] = (-sin_u * cos_v - cos_u * sin_v).astype(jnp.bfloat16)
+
+
+def send_kernel(
+    strain, factors, listed, bands,
+    swap, folds, kept_table,
+    time, sent_table, factors_in, listed_in, bands_in, sems,
+):
     me = lax.rem(lax.axis_index(AXIS), Q)
     core, side = lax.rem(me, 2), me // 2
     channels, samples = strain.shape
     quarter = samples // Q
     depth = quarter // 2
+    small = [
+        pltpu.make_async_copy(factors, factors_in, sems.at[2 * Q]),
+        pltpu.make_async_copy(listed, listed_in, sems.at[2 * Q + 1]),
+        pltpu.make_async_copy(bands, bands_in, sems.at[2 * Q + 2]),
+    ]
     copies = []
     for h in range(2):
         for q in range(Q):
@@ -75,17 +104,16 @@
             copies.append(
                 pltpu.make_async_copy(strain.at[part], time.at[part], sems.at[h * Q + q])
             )
-    tables = [
-        pltpu.make_async_copy(table.at[1 - core], sent_table, sems.at[2 * Q]),
-        pltpu.make_async_copy(table.at[core], kept_table, sems.at[2 * Q + 1]),
-    ]
-    for copy in copies + tables:
+    for copy in small + copies:
         copy.start()
-
+    for copy in small:
+        copy.wait()
+
+    fill_table(factors_in.at[1 - core], sent_table)
     nbands = bands.shape[1]
     width = swap.shape[2] // nbands
     rounds = bands.shape[2]
-    used = (listed[...] * bands[0]).astype(jnp.float32)
+    used = (listed_in[...] * bands_in[0]).astype(jnp.float32)
     pick = lax.broadcasted_iota(jnp.int32, (rounds, rounds), 0) == lax.broadcasted_iota(
         jnp.int32, (rounds, rounds), 1
     )
@@ -105,6 +133,7 @@
     ).astype(jnp.bfloat16)
     for n in range(2):
         swap[n, channels:, :] = weight
+    fill_table(factors_in.at[core], kept_table)
 
     for h in range(2):
         for copy in copies[h * Q : (h + 1) * Q]:
@@ -117,7 +146,6 @@
         odd = q1.astype(jnp.float32) + q3.astype(jnp.float32)
         folds[1, 0, :, here] = (even - odd).astype(jnp.bfloat16)
         folds[1, 1, :, here] = (even + odd).astype(jnp.bfloat16)
-    tables[0].wait()
 
     def store(values):
         for n, value in enumerate(values):
@@ -130,8 +158,6 @@
     @pl.when(core == 1)
     def _():
         store(complex_classes(folds.at[0], sent_table))
-
-    tables[1].wait()
 
 
 def keep_kernel(swap, folds, table, near, mates):
@@ -164,12 +190,12 @@
 
 def send_call(strain, listed, bands):
     channels, samples = strain.shape
-    table = forward_table(samples)
-    rows, cols = channels + bands.shape[2], table.shape[3]
+    factors = forward_factors(samples)
+    rows, cols = channels + bands.shape[2], 2 * factors.shape[4]
     quarter = samples // Q
     return pl.pallas_call(
         send_kernel,
-        in_specs=[HBM_SPEC, HBM_SPEC, VMEM_SPEC, VMEM_SPEC],
+        in_specs=[HBM_SPEC] * 4,
         out_specs=[VMEM_SPEC] * 3,
         out_shape=[
             pltpu.VMEM((2, rows, cols), jnp.bfloat16),
@@ -179,11 +205,14 @@
         scratch_shapes=[
             pltpu.VMEM((channels, samples), jnp.bfloat16),
             pltpu.VMEM((2, quarter, cols), jnp.bfloat16),
-            pltpu.SemaphoreType.DMA((2 * Q + 2,)),
+            pltpu.VMEM(factors.shape, jnp.float32),
+            pltpu.VMEM(listed.shape, listed.dtype),
+            pltpu.VMEM(bands.shape, bands.dtype),
+            pltpu.SemaphoreType.DMA((2 * Q + 3,)),
         ],
         compiler_params=pltpu.CompilerParams(vmem_limit_bytes=LIMIT),
         name="spectrum_sent",
-    )(in_hbm(strain), in_hbm(jnp.asarray(table)), in_hbm(listed), in_hbm(bands))
+    )(in_hbm(strain), in_hbm(jnp.asarray(factors)), in_hbm(listed), in_hbm(bands))
 
 
 def unit_table(rounds):
@@ -279,9 +308,12 @@
 
 
 def early_kernel(
-    nbands, unroll, twins, table, near, mates, even, odd, inv, steering, lag_range, spec, window, mask
+    nbands, unroll, twins, table, near, mates, even, odd, inv_all, steering, lag_range,
+    spec, window, inv, mask, sem,
 ):
     me = lax.rem(lax.axis_index(AXIS), Q)
+    copy = pltpu.make_async_copy(inv_all.at[me], inv, sem)
+    copy.start()
     even_slot, odd_slot = neighbour_slots()
     spec[0:2] = near[...]
     spec[2:4] = mates[...]
@@ -293,7 +325,8 @@
         fill_mask(mask, p, spec, p, channels, nbands)
     for p in range(Q // 2):
         fill_mask(mask, Q + p, spec, 2 * Q + p, channels, nbands)
-    run_units(table, me, spec, mask, steering, inv.at[me], lag_range, window, unroll, twins)
+    copy.wait()
+    run_units(table, me, spec, mask, steering, inv, lag_range, window, unroll, twins)
 
 
 def late_kernel(
@@ -308,7 +341,7 @@
     for p in range(Q):
         fill_mask(mask, p, spec, p, channels, nbands)
         fill_mask(mask, Q + p, spec, 2 * Q + p, channels, nbands)
-    run_units(table, me, spec, mask, steering, inv.at[me], lag_range, window, unroll, twins)
+    run_units(table, me, spec, mask, steering, inv, lag_range, window, unroll, twins)
 
     width = window.shape[2] // 3
 
@@ -431,16 +464,20 @@
     table, _ = plan
     return pl.pallas_call(
         functools.partial(early_kernel, nbands, divide(table.shape[1] // 6), 0),
-        in_specs=[SMEM_SPEC] + [VMEM_SPEC] * 7,
-        out_specs=[VMEM_SPEC] * 2,
+        in_specs=[SMEM_SPEC] + [VMEM_SPEC] * 4 + [HBM_SPEC] + [VMEM_SPEC] * 2,
+        out_specs=[VMEM_SPEC] * 3,
         out_shape=[
             pltpu.VMEM((3 * Q, rows, cols), jnp.bfloat16),
             pltpu.VMEM((2 * Q, angles, group), jnp.float32),
+            pltpu.VMEM(inv.shape[1:], inv.dtype),
         ],
-        scratch_shapes=[pltpu.VMEM((2 * Q, L // cols, 2 * rounds, cols), jnp.float32)],
+        scratch_shapes=[
+            pltpu.VMEM((2 * Q, L // cols, 2 * rounds, cols), jnp.float32),
+            pltpu.SemaphoreType.DMA(()),
+        ],
         compiler_params=pltpu.CompilerParams(vmem_limit_bytes=LIMIT),
         name="early_pairs",
-    )(jnp.asarray(table), *near_vmem(near, mates, even, odd, inv, steering, lag_range))
+    )(jnp.asarray(table), *near_vmem(near, mates, even, odd), in_hbm(inv), *near_vmem(steering, lag_range))
 
 
 def late_call(plan, nbands, spec, window, even, odd, inv, steering, lag_range):
@@ -491,9 +528,12 @@
     early, late = unit_table(steering.shape[0] - 1)
     nbands = band_used.shape[2]
     inv = jnp.asarray(inverse_table(strain.shape[1]))
-    shared = (inv, steering, lag_range)
-    spec, window = early_call(early, nbands, near, mates, near_even, near_odd, *shared)
-    kept, send = late_call(late, nbands, spec, window, far_even, far_odd, *shared)
+    spec, window, inv = early_call(
+        early, nbands, near, mates, near_even, near_odd, inv, steering, lag_range
+    )
+    kept, send = late_call(
+        late, nbands, spec, window, far_even, far_odd, inv, steering, lag_range
+    )
 
     def pieces(count, dtype):
         return pltpu.VMEM(((count,) if count else ()) + kept.shape[1:], dtype)

time: 43.1 us -> 42.5 us (0.986)
  waiting for transfers between devices: 11.1 us -> 10.5 us
    pallas_call x1, Pallas kernels: 4.25 us -> 4.91 us  [early_call(): pl.pallas_call(functools.partial(early_kernel, nbands, divide(table.shape...]
    ppermute x10, waiting for transfers between devices: 11.1 us -> 10.5 us  [exchange(): return lax.ppermute(value, AXIS, pairs)]
    pallas_call x1, Pallas kernels: 3.22 us -> 2.66 us  [send_call(): pl.pallas_call(send_kernel, in_specs=[HBM_SPEC] * 4, out_specs=[VMEM_SPEC...]
  transfers between devices with their start and end apart: 10 -> 10, of which waited for: 7 -> 7; matrix products, arithmetic and copies ran while one was open for 0% -> 0% of each run, Pallas kernels for 12% -> 13%
where the time goes in v7:
time: 42.5 us; the launch traced here: 42.3 us
  starting transfers between devices  19.5 us (46%)
  Pallas kernels  12.2 us (29%)
  waiting for transfers between devices  10.5 us (25%)
    ppermute x10, starting transfers between devices, exchange(): return lax.ppermute(value, AXIS, pairs)  19.5 us
    ppermute x10, waiting for transfers between devices, exchange(): return lax.ppermute(value, AXIS, pairs)  10.5 us
    pallas_call x1, Pallas kernels, early_call(): pl.pallas_call(functools.partial(early_kernel, nbands, divide(table.shape...  4.91 us
    pallas_call x1, Pallas kernels, late_call(): pl.pallas_call(functools.partial(late_kernel, nbands, table.shape[1] // 6...  3.17 us
    pallas_call x1, Pallas kernels, send_call(): pl.pallas_call(send_kernel, in_specs=[HBM_SPEC] * 4, out_specs=[VMEM_SPEC...  2.66 us
    pallas_call x6, Pallas kernels, local_call(): pl.pallas_call(kernel, in_specs=[VMEM_SPEC] * len(values), out_specs=[VME...  1.48 us
  transfers between devices with their start and end apart: 10, of which 7 were waited for; matrix products, arithmetic and copies ran while one was open for 0% of the time, Pallas kernels for 13%

profile of v7, /device:TPU:0, one launch (start us, length us, event | category | flops | bytes accessed | tf_op | source)
XLA Modules:
  0.0 42.3 jit_solution(17141954675845648656)
XLA Ops:
  0.0 2.7 %spectrum_sent.1 = (bf16[2,264,256]{2,1,0:T(8,128)(2,1)S(1)}, bf16[2,2,256,1024]{3,2,1,0:T(8,128)(2,1)S(1)}, bf16[2,1024,256]{2,1,0:T(8,128)(2,1)S(1)}) custom-call(bf16[256,4096]{1,0:T(8,128)(2,1)} %strain.1, f32[2,4,2,32,128]{4,3,2,1,0:T(8,128)} %constant.8.clone.factors, s32[1,8]{1,0:T(1,128)} %listed.1, s32[1,4,8]{2,1,0:T(4,128)} %bitcast.1), custom_call_target="tpu_custom_call" | custom-call | tf_op jit(solution)/shard_map/spectrum_sent/pallas_call | solution.py:196
  2.7 0.8 %collective-permute-start = (bf16[2,264,256]{2,1,0:T(8,128)(2,1)S(1)}, bf16[2,264,256]{2,1,0:T(8,128)(2,1)S(1)}, u32[]{:S(2)}, u32[]{:S(2)}) collective-permute-start(bf16[2,264,256]{2,1,0:T(8,128)(2,1)S(1)} %get-tuple-element.23.swap), channel_id=1, source_target_pairs={{0,1},{1,0},{2,3},{3,2},{4,5},{5,4},{6,7},{7,6},{8,9},{9,8},{10,11... | collective-permute-start | bytes 811016 | tf_op jit(solution)/shard_map/ppermute | solution.py:509
  3.5 0.0 copy-start
  3.5 0.0 copy-start.1
  3.5 0.0 copy-start.3
  3.5 0.7 %spectrum_kept.1 = (bf16[2,264,256]{2,1,0:T(8,128)(2,1)S(1)}, bf16[2,264,256]{2,1,0:T(8,128)(2,1)S(1)}) custom-call(bf16[2,264,256]{2,1,0:T(8,128)(2,1)S(1)} %get-tuple-element.23.swap, bf16[2,2,256,1024]{3,2,1,0:T(8,128)(2,1)S(1)} %get-tuple-element.24.folds, bf16[2,1024,256]{2,1,0:T(8,128)(2,1)S(1)} %get-tuple-element.25.table), custom_call_target="tpu_custom_call" | custom-call | tf_op jit(solution)/shard_map/spectrum_kept/pallas_call | solution.py:445
  4.2 0.4 collective-permute-done.swap
  4.7 2.7 %collective-permute-start.1 = (bf16[2,264,256]{2,1,0:T(8,128)(2,1)S(1)}, bf16[2,264,256]{2,1,0:T(8,128)(2,1)S(1)}, u32[]{:S(2)}, u32[]{:S(2)}) collective-permute-start(bf16[2,264,256]{2,1,0:T(8,128)(2,1)S(1)} %get-tuple-element.29), channel_id=1, source_target_pairs={{0,2},{1,3},{2,0},{3,1},{4,6},{5,7},{6,4},{7,5},{8,10},{9,11},{10,... | collective-permute-start | bytes 811016 | tf_op jit(solution)/shard_map/ppermute | solution.py:509
  7.4 0.8 %collective-permute-start.3 = (bf16[2,264,256]{2,1,0:T(8,128)(2,1)S(1)}, bf16[2,264,256]{2,1,0:T(8,128)(2,1)S(1)}, u32[]{:S(2)}, u32[]{:S(2)}) collective-permute-start(bf16[2,264,256]{2,1,0:T(8,128)(2,1)S(1)} %get-tuple-element.28.near), channel_id=1, source_target_pairs={{4,8},{5,9},{6,10},{7,11},{8,4},{9,5},{10,6},{11,7},{20,24},{21,25... | collective-permute-start | bytes 811016 | tf_op jit(solution)/shard_map/ppermute | solution.py:509
  8.2 4.4 %collective-permute-start.2 = (bf16[2,264,256]{2,1,0:T(8,128)(2,1)S(1)}, bf16[2,264,256]{2,1,0:T(8,128)(2,1)S(1)}, u32[]{:S(2)}, u32[]{:S(2)}) collective-permute-start(bf16[2,264,256]{2,1,0:T(8,128)(2,1)S(1)} %get-tuple-element.28.near), channel_id=1, source_target_pairs={{0,4},{1,5},{2,6},{3,7},{4,0},{5,1},{6,2},{7,3},{8,12},{9,13},{10,... | collective-permute-start | bytes 811016 | tf_op jit(solution)/shard_map/ppermute | solution.py:509
  12.6 1.5 %collective-permute-done.1.mates = bf16[2,264,256]{2,1,0:T(8,128)(2,1)S(1)} collective-permute-done((bf16[2,264,256]{2,1,0:T(8,128)(2,1)S(1)}, bf16[2,264,256]{2,1,0:T(8,128)(2,1)S(1)}, u32[]{:S(2)}, u32[]{:S(2)}) %collective-permute-start.1) | collective-permute-done | bytes 270368 | tf_op jit(solution)/shard_map/ppermute | solution.py:509
  14.1 0.7 %collective-permute-start.5 = (bf16[2,264,256]{2,1,0:T(8,128)(2,1)S(1)}, bf16[2,264,256]{2,1,0:T(8,128)(2,1)S(1)}, u32[]{:S(2)}, u32[]{:S(2)}) collective-permute-start(bf16[2,264,256]{2,1,0:T(8,128)(2,1)S(1)} %collective-permute-done.1.mates), channel_id=1, source_target_pairs={{4,8},{5,9},{6,10},{7,11},{8,4},{9,5},{10,6},{11,7},{20,24},{21,25... | collective-permute-start | bytes 811016 | tf_op jit(solution)/shard_map/ppermute | solution.py:509
  14.8 4.7 %collective-permute-start.4 = (bf16[2,264,256]{2,1,0:T(8,128)(2,1)S(1)}, bf16[2,264,256]{2,1,0:T(8,128)(2,1)S(1)}, u32[]{:S(2)}, u32[]{:S(2)}) collective-permute-start(bf16[2,264,256]{2,1,0:T(8,128)(2,1)S(1)} %collective-permute-done.1.mates), channel_id=1, source_target_pairs={{0,4},{1,5},{2,6},{3,7},{4,0},{5,1},{6,2},{7,3},{8,12},{9,13},{10,... | collective-permute-start | bytes 811016 | tf_op jit(solution)/shard_map/ppermute | solution.py:509
  19.5 0.0 collective-permute-done.3.odd
  19.5 0.0 collective-permute-done.2.even
  19.5 0.0 copy-done
  19.5 0.0 copy-done.1
  19.5 0.0 copy-done.3
  19.5 4.9 %early_pairs.1 = (bf16[12,264,256]{2,1,0:T(8,128)(2,1)S(1)}, f32[8,128,384]{2,1,0:T(8,128)S(1)}, bf16[256,512]{1,0:T(8,128)(2,1)S(1)}) custom-call(s32[4,126]{1,0:T(4,128)S(1)} %copy-done.3, bf16[2,264,256]{2,1,0:T(8,128)(2,1)S(1)} %get-tuple-element.28.near, bf16[2,264,256]{2,1,0:T(8,128)(2,1)S(1)} %collective-permute-done.1.mates, ...), custom_call_target="tpu_custom_call" | custom-call | tf_op jit(solution)/shard_map/early_pairs/pallas_call | solution.py:465
  24.4 0.0 collective-permute-done.5.odd
  24.5 0.7 %collective-permute-done.4.even = bf16[2,264,256]{2,1,0:T(8,128)(2,1)S(1)} collective-permute-done((bf16[2,264,256]{2,1,0:T(8,128)(2,1)S(1)}, bf16[2,264,256]{2,1,0:T(8,128)(2,1)S(1)}, u32[]{:S(2)}, u32[]{:S(2)}) %collective-permute-start.4) | collective-permute-done | bytes 270368 | tf_op jit(solution)/shard_map/ppermute | solution.py:509
  25.1 0.0 copy-done.2
  25.1 3.2 %late_pairs.1 = (f32[6,128,128]{2,1,0:T(8,128)S(1)}, bf16[6,128,128]{2,1,0:T(8,128)(2,1)S(1)}, bf16[12,264,256]{2,1,0:T(8,128)(2,1)S(1)}, f32[8,128,384]{2,1,0:T(8,128)S(1)}) custom-call(s32[4,90]{1,0:T(4,128)S(1)} %copy-done.2, bf16[12,264,256]{2,1,0:T(8,128)(2,1)S(1)} %get-tuple-element.30.spec_in, ...), custom_call_target="tpu_custom_call", output_to_operand_aliasing={{2}: (1, {}), {3}: (2, {})} | custom-call | tf_op jit(solution)/shard_map/late_pairs/pallas_call | solution.py:489
  28.3 0.1 collective-permute-start.6
  28.4 1.4 %collective-permute-done.6.received = bf16[6,128,128]{2,1,0:T(8,128)(2,1)S(1)} collective-permute-done((bf16[6,128,128]{2,1,0:T(8,128)(2,1)S(1)}, bf16[6,128,128]{2,1,0:T(8,128)(2,1)S(1)}, u32[]{:S(2)}, u32[]{:S(2)}) %collective-permute-start.6) | collective-permute-done | bytes 196640 | tf_op jit(solution)/shard_map/ppermute | solution.py:509
  29.9 1.6 %collective-permute-start.7 = (bf16[3,128,128]{2,1,0:T(8,128)(2,1)S(1)}, bf16[3,128,128]{2,1,0:T(8,128)(2,1)S(1)}, u32[]{:S(2)}, u32[]{:S(2)}) collective-permute-start(bf16[3,128,128]{2,1,0:T(8,128)(2,1)S(1)} %get-tuple-element.36), channel_id=1, source_target_pairs={{0,2},{1,3},{2,0},{3,1},{4,6},{5,7},{6,4},{7,5},{8,10},{9,11},{10,... | collective-permute-start | bytes 294920 | tf_op jit(solution)/shard_map/ppermute | solution.py:509
  31.5 3.3 %collective-permute-done.7.received = bf16[3,128,128]{2,1,0:T(8,128)(2,1)S(1)} collective-permute-done((bf16[3,128,128]{2,1,0:T(8,128)(2,1)S(1)}, bf16[3,128,128]{2,1,0:T(8,128)(2,1)S(1)}, u32[]{:S(2)}, u32[]{:S(2)}) %collective-permute-start.7) | collective-permute-done | bytes 98336 | tf_op jit(solution)/shard_map/ppermute | solution.py:509
  34.8 3.6 %collective-permute-start.8 = (bf16[2,128,128]{2,1,0:T(8,128)(2,1)S(1)}, bf16[2,128,128]{2,1,0:T(8,128)(2,1)S(1)}, u32[]{:S(2)}, u32[]{:S(2)}) collective-permute-start(bf16[2,128,128]{2,1,0:T(8,128)(2,1)S(1)} %get-tuple-element.38), channel_id=1, source_target_pairs={{0,4},{1,9},{2,6},{4,8},{5,13},{6,10},{7,3},{8,12},{10,14},{11,7},... | collective-permute-start | bytes 196616 | tf_op jit(solution)/shard_map/ppermute | solution.py:509
  38.5 1.9 %collective-permute-done.8.received = bf16[2,128,128]{2,1,0:T(8,128)(2,1)S(1)} collective-permute-done((bf16[2,128,128]{2,1,0:T(8,128)(2,1)S(1)}, bf16[2,128,128]{2,1,0:T(8,128)(2,1)S(1)}, u32[]{:S(2)}, u32[]{:S(2)}) %collective-permute-start.8) | collective-permute-done | bytes 65568 | tf_op jit(solution)/shard_map/ppermute | solution.py:509
  40.4 0.1 collective-permute-start.9
  40.4 1.2 %collective-permute-done.9.received = f32[128,128]{1,0:T(8,128)S(1)} collective-permute-done((f32[128,128]{1,0:T(8,128)S(1)}, f32[128,128]{1,0:T(8,128)S(1)}, u32[]{:S(2)}, u32[]{:S(2)}) %collective-permute-start.9) | collective-permute-done | bytes 65568 | tf_op jit(solution)/shard_map/ppermute | solution.py:509
  41.7 0.6 %image.1 = f32[128,128]{1,0:T(8,128)} custom-call(f32[128,128]{1,0:T(8,128)S(1)} %get-tuple-element.39.kept, f32[128,128]{1,0:T(8,128)S(1)} %collective-permute-done.9.received), custom_call_target="tpu_custom_call" | custom-call | tf_op jit(solution)/shard_map/image/pallas_call | solution.py:445
  (5 shorter events, 0.1 us)
Async XLA Ops:
  2.7 2.0 %collective-permute-start = (bf16[2,264,256]{2,1,0:T(8,128)(2,1)S(1)}, bf16[2,264,256]{2,1,0:T(8,128)(2,1)S(1)}, u32[]{:S(2)}, u32[]{:S(2)}) collective-permute-start(bf16[2,264,256]{2,1,0:T(8,128)(2,1)S(1)} %get-tuple-element.23.swap), channel_id=1, source_target_pairs={{0,1},{1,0},{2,3},{3,2},{4,5},{5,4},{6,7},{7,6},{8,9},{9,8},{10,11... | collective-permute-start | bytes 811016 | tf_op jit(solution)/shard_map/ppermute | solution.py:509
  3.5 16.0 %copy-start = (bf16[9,512,384]{2,1,0:T(8,128)(2,1)S(1)}, bf16[9,512,384]{2,1,0:T(8,128)(2,1)}, u32[]{:S(2)}) copy-start(bf16[9,512,384]{2,1,0:T(8,128)(2,1)} %lag_range.3) | copy-start | bytes 10616836
  3.5 16.0 %copy-start.1 = (bf16[9,128,256]{2,1,0:T(8,128)(2,1)S(1)}, bf16[9,128,256]{2,1,0:T(8,128)(2,1)}, u32[]{:S(2)}) copy-start(bf16[9,128,256]{2,1,0:T(8,128)(2,1)} %steering.3) | copy-start | bytes 1769476
  3.5 16.0 %copy-start.3 = (s32[4,126]{1,0:T(4,128)S(1)}, s32[4,126]{1,0:T(4,128)}, u32[]{:S(2)}) copy-start(s32[4,126]{1,0:T(4,128)} %constant.10.clone.table) | copy-start | bytes 6052
  4.7 9.5 %collective-permute-start.1 = (bf16[2,264,256]{2,1,0:T(8,128)(2,1)S(1)}, bf16[2,264,256]{2,1,0:T(8,128)(2,1)S(1)}, u32[]{:S(2)}, u32[]{:S(2)}) collective-permute-start(bf16[2,264,256]{2,1,0:T(8,128)(2,1)S(1)} %get-tuple-element.29), channel_id=1, source_target_pairs={{0,2},{1,3},{2,0},{3,1},{4,6},{5,7},{6,4},{7,5},{8,10},{9,11},{10,... | collective-permute-start | bytes 811016 | tf_op jit(solution)/shard_map/ppermute | solution.py:509
  7.4 17.8 %copy-start.2 = (s32[4,90]{1,0:T(4,128)S(1)}, s32[4,90]{1,0:T(4,128)}, u32[]{:S(2)}) copy-start(s32[4,90]{1,0:T(4,128)} %constant.11.clone.table) | copy-start | bytes 4324
  7.4 12.1 %collective-permute-start.3 = (bf16[2,264,256]{2,1,0:T(8,128)(2,1)S(1)}, bf16[2,264,256]{2,1,0:T(8,128)(2,1)S(1)}, u32[]{:S(2)}, u32[]{:S(2)}) collective-permute-start(bf16[2,264,256]{2,1,0:T(8,128)(2,1)S(1)} %get-tuple-element.28.near), channel_id=1, source_target_pairs={{4,8},{5,9},{6,10},{7,11},{8,4},{9,5},{10,6},{11,7},{20,24},{21,25... | collective-permute-start | bytes 811016 | tf_op jit(solution)/shard_map/ppermute | solution.py:509
  8.2 11.3 %collective-permute-start.2 = (bf16[2,264,256]{2,1,0:T(8,128)(2,1)S(1)}, bf16[2,264,256]{2,1,0:T(8,128)(2,1)S(1)}, u32[]{:S(2)}, u32[]{:S(2)}) collective-permute-start(bf16[2,264,256]{2,1,0:T(8,128)(2,1)S(1)} %get-tuple-element.28.near), channel_id=1, source_target_pairs={{0,4},{1,5},{2,6},{3,7},{4,0},{5,1},{6,2},{7,3},{8,12},{9,13},{10,... | collective-permute-start | bytes 811016 | tf_op jit(solution)/shard_map/ppermute | solution.py:509
  14.1 10.3 %collective-permute-start.5 = (bf16[2,264,256]{2,1,0:T(8,128)(2,1)S(1)}, bf16[2,264,256]{2,1,0:T(8,128)(2,1)S(1)}, u32[]{:S(2)}, u32[]{:S(2)}) collective-permute-start(bf16[2,264,256]{2,1,0:T(8,128)(2,1)S(1)} %collective-permute-done.1.mates), channel_id=1, source_target_pairs={{4,8},{5,9},{6,10},{7,11},{8,4},{9,5},{10,6},{11,7},{20,24},{21,25... | collective-permute-start | bytes 811016 | tf_op jit(solution)/shard_map/ppermute | solution.py:509
  14.8 10.3 %collective-permute-start.4 = (bf16[2,264,256]{2,1,0:T(8,128)(2,1)S(1)}, bf16[2,264,256]{2,1,0:T(8,128)(2,1)S(1)}, u32[]{:S(2)}, u32[]{:S(2)}) collective-permute-start(bf16[2,264,256]{2,1,0:T(8,128)(2,1)S(1)} %collective-permute-done.1.mates), channel_id=1, source_target_pairs={{0,4},{1,5},{2,6},{3,7},{4,0},{5,1},{6,2},{7,3},{8,12},{9,13},{10,... | collective-permute-start | bytes 811016 | tf_op jit(solution)/shard_map/ppermute | solution.py:509
  28.3 1.5 %collective-permute-start.6 = (bf16[6,128,128]{2,1,0:T(8,128)(2,1)S(1)}, bf16[6,128,128]{2,1,0:T(8,128)(2,1)S(1)}, u32[]{:S(2)}, u32[]{:S(2)}) collective-permute-start(bf16[6,128,128]{2,1,0:T(8,128)(2,1)S(1)} %get-tuple-element.34), channel_id=1, source_target_pairs={{0,1},{1,0},{2,3},{3,2},{4,5},{5,4},{6,7},{7,6},{8,9},{9,8},{10,11... | collective-permute-start | bytes 589832 | tf_op jit(solution)/shard_map/ppermute | solution.py:509
  29.9 4.9 %collective-permute-start.7 = (bf16[3,128,128]{2,1,0:T(8,128)(2,1)S(1)}, bf16[3,128,128]{2,1,0:T(8,128)(2,1)S(1)}, u32[]{:S(2)}, u32[]{:S(2)}) collective-permute-start(bf16[3,128,128]{2,1,0:T(8,128)(2,1)S(1)} %get-tuple-element.36), channel_id=1, source_target_pairs={{0,2},{1,3},{2,0},{3,1},{4,6},{5,7},{6,4},{7,5},{8,10},{9,11},{10,... | collective-permute-start | bytes 294920 | tf_op jit(solution)/shard_map/ppermute | solution.py:509
  34.8 5.5 %collective-permute-start.8 = (bf16[2,128,128]{2,1,0:T(8,128)(2,1)S(1)}, bf16[2,128,128]{2,1,0:T(8,128)(2,1)S(1)}, u32[]{:S(2)}, u32[]{:S(2)}) collective-permute-start(bf16[2,128,128]{2,1,0:T(8,128)(2,1)S(1)} %get-tuple-element.38), channel_id=1, source_target_pairs={{0,4},{1,9},{2,6},{4,8},{5,13},{6,10},{7,3},{8,12},{10,14},{11,7},... | collective-permute-start | bytes 196616 | tf_op jit(solution)/shard_map/ppermute | solution.py:509
  40.4 1.3 %collective-permute-start.9 = (f32[128,128]{1,0:T(8,128)S(1)}, f32[128,128]{1,0:T(8,128)S(1)}, u32[]{:S(2)}, u32[]{:S(2)}) collective-permute-start(f32[128,128]{1,0:T(8,128)S(1)} %get-tuple-element.40), channel_id=1, source_target_pairs={{0,1},{1,0},{2,3},{3,2},{4,5},{5,4},{6,7},{7,6},{8,9},{9,8},{10,11... | collective-permute-start | bytes 196616 | tf_op jit(solution)/shard_map/ppermute | solution.py:509

commit v8 on v7

--- a/solution.py
+++ b/solution.py
@@ -14,7 +14,6 @@
 Q = 4
 LIMIT = 16 << 20
 VMEM_SPEC = pl.BlockSpec(memory_space=pltpu.VMEM)
-SMEM_SPEC = pl.BlockSpec(memory_space=pltpu.SMEM)
 HBM_SPEC = pl.BlockSpec(memory_space=pl.ANY)
 
 
@@ -215,78 +214,86 @@
     )(in_hbm(strain), in_hbm(jnp.asarray(factors)), in_hbm(listed), in_hbm(bands))
 
 
-def unit_table(rounds):
-    early, late = [], []
-    for me in range(Q):
-        units = ([], [])
-        for i in range(2 * Q):
-            for j in range(-Q, Q):
-                d = i - j
-                if not 0 <= d <= rounds or (i >= Q and j >= 0):
-                    continue
-                p, q = i % Q ^ me, j % Q ^ me
-                target = p if i < Q else 2 * Q + p
-                source = q if j >= 0 else Q + q
-                far = (i >= Q and p >= Q // 2) or (j < 0 and q >= Q // 2)
-                mask = p if i < Q else Q + p
-                row = d - 1 if d else rounds
-                units[far].append((target, source, d, i, mask, row))
-        early.append(units[0])
-        late.append(units[1])
-    return twins_first(early), twins_first(late)
-
-
-def twins_first(tables):
-    ordered = []
-    for units in tables:
-        twins, single = [], {}
-        for unit in units:
-            if unit[2] in single:
-                twins.append((single.pop(unit[2]), unit))
-            else:
-                single[unit[2]] = unit
-        ordered.append((twins, list(single.values())))
-    count = min(len(twins) for twins, _ in ordered)
-    table = []
-    for twins, rest in ordered:
-        flat = [unit for pair in twins for unit in pair] + rest
-        table.append(flat)
-    return np.asarray(table, np.int32).reshape(len(tables), -1), count
-
-
-def run_units(table, me, spec, mask, steering, inv, lag_range, window, unroll, twins):
+def make_unit(me, rounds, i, j):
+    target_plane, i = i
+    source_plane, j = j
+    p, q = lax.bitwise_xor(me, i), lax.bitwise_xor(me, j)
+    d = (target_plane + source_plane) * Q + i - j
+    target = 2 * Q * target_plane + p
+    source = Q * source_plane + q
+    row = d - 1 if target_plane + source_plane or i != j else rounds
+    return target, source, d, target_plane * Q + i, target_plane * Q + p, row
+
+
+def early_units(me, rounds):
+    base = 2 * (me // 2)
+
+    def unit(i, j):
+        return make_unit(me, rounds, i, j)
+
+    def own(i, j):
+        return unit((0, i), (0, j))
+
+    def low(i, e):
+        return unit((0, i), (1, base + e))
+
+    def mid(e, f):
+        return unit((1, base + e), (1, base + f))
+
+    twins, rest = [], []
+    for d in range(Q):
+        group = [own(i, i - d) for i in range(d, Q)]
+        twins += [group[n : n + 2] for n in range(0, len(group) // 2 * 2, 2)]
+        rest += group[len(group) // 2 * 2 :]
+    twins += [[low(i, 0), low(i + 1, 1)] for i in range(Q - 1)]
+    twins.append([mid(0, 0), mid(1, 1)])
+    rest += [low(Q - 1, 0), low(0, 1), mid(0, 1)]
+    return twins, rest
+
+
+def late_units(me, rounds):
+    base = 2 * (1 - me // 2)
+
+    def low(i, e):
+        return make_unit(me, rounds, (0, i), (1, base + e))
+
+    def mid(i, j):
+        return make_unit(me, rounds, (1, i), (1, j))
+
+    twins = [[low(i, 0), low(i + 1, 1)] for i in range(Q - 1)]
+    twins.append([mid(base, base), mid(base + 1, base + 1)])
+    twins.append([mid(0, 2), mid(1, 3)])
+    twins.append([mid(1, 2), mid(base, base + 1)])
+    return twins, [low(Q - 1, 0), low(0, 1), mid(0, 3)]
+
+
+def run_units(plan, spec, mask, steering, inv, lag_range, window):
     channels, angles = steering.shape[2], steering.shape[1]
     cols = spec.shape[2]
     half = cols // 2
-
-    def body(n, carry):
-        units = [
-            [table[me, (n * unroll + u) * 6 + e] for e in range(6)] for u in range(unroll)
-        ]
-        beams = []
-        for target, source, d, _, _, _ in units:
-            near_re, near_im = spec[target, :channels, :half], spec[target, :channels, half:]
-            far_re, far_im = spec[source, :channels, :half], spec[source, :channels, half:]
-            real = near_re * far_re + near_im * far_im
-            imag = near_im * far_re - near_re * far_im
-            cross = jnp.concatenate([real, imag], axis=1)
-            beams.append(dot(steering[d], cross).astype(jnp.bfloat16))
-        beams = dot(jnp.concatenate(beams, axis=0), inv[...])
-        masked = []
-        for u, (_, _, _, _, target, row) in enumerate(units):
-            weight = jnp.concatenate(
-                [mask[target, h, pl.ds(row, 1), :] for h in range(L // cols)], axis=1
-            )
-            masked.append((beams[u * angles : (u + 1) * angles, :] * weight).astype(jnp.bfloat16))
-        for u in range(0, 2 * twins, 2):
-            part = dot(jnp.concatenate(masked[u : u + 2], axis=0), lag_range[units[u][2]])
-            window[units[u][3]] += part[:angles]
-            window[units[u + 1][3]] += part[angles:]
-        for u in range(2 * twins, unroll):
-            window[units[u][3]] += dot(masked[u], lag_range[units[u][2]])
-        return carry
-
-    lax.fori_loop(0, table.shape[1] // (6 * unroll), body, 0)
+    twins, rest = plan
+    units = [unit for pair in twins for unit in pair] + rest
+    beams = []
+    for target, source, d, _, _, _ in units:
+        near_re, near_im = spec[target, :channels, :half], spec[target, :channels, half:]
+        far_re, far_im = spec[source, :channels, :half], spec[source, :channels, half:]
+        real = near_re * far_re + near_im * far_im
+        imag = near_im * far_re - near_re * far_im
+        cross = jnp.concatenate([real, imag], axis=1)
+        beams.append(dot(steering[d], cross).astype(jnp.bfloat16))
+    beams = dot(jnp.concatenate(beams, axis=0), inv[...])
+    masked = []
+    for u, (_, _, _, _, target, row) in enumerate(units):
+        weight = jnp.concatenate(
+            [mask[target, h, pl.ds(row, 1), :] for h in range(L // cols)], axis=1
+        )
+        masked.append((beams[u * angles : (u + 1) * angles, :] * weight).astype(jnp.bfloat16))
+    for u in range(0, 2 * len(twins), 2):
+        part = dot(jnp.concatenate(masked[u : u + 2], axis=0), lag_range[units[u][2]])
+        window[units[u][3]] += part[:angles]
+        window[units[u + 1][3]] += part[angles:]
+    for u in range(2 * len(twins), len(units)):
+        window[units[u][3]] += dot(masked[u], lag_range[units[u][2]])
 
 
 def fill_mask(mask, entry, spec, slot, channels, nbands):
@@ -308,7 +315,7 @@
 
 
 def early_kernel(
-    nbands, unroll, twins, table, near, mates, even, odd, inv_all, steering, lag_range,
+    nbands, near, mates, even, odd, inv_all, steering, lag_range,
     spec, window, inv, mask, sem,
 ):
     me = lax.rem(lax.axis_index(AXIS), Q)
@@ -326,11 +333,12 @@
     for p in range(Q // 2):
         fill_mask(mask, Q + p, spec, 2 * Q + p, channels, nbands)
     copy.wait()
-    run_units(table, me, spec, mask, steering, inv, lag_range, window, unroll, twins)
+    plan = early_units(me, steering.shape[0] - 1)
+    run_units(plan, spec, mask, steering, inv, lag_range, window)
 
 
 def late_kernel(
-    nbands, unroll, twins, table, spec_in, window_in, even, odd, inv, steering, lag_range,
+    nbands, spec_in, window_in, even, odd, inv, steering, lag_range,
     keep, send, spec, window, mask,
 ):
     me = lax.rem(lax.axis_index(AXIS), Q)
@@ -341,7 +349,8 @@
     for p in range(Q):
         fill_mask(mask, p, spec, p, channels, nbands)
         fill_mask(mask, Q + p, spec, 2 * Q + p, channels, nbands)
-    run_units(table, me, spec, mask, steering, inv, lag_range, window, unroll, twins)
+    plan = late_units(me, steering.shape[0] - 1)
+    run_units(plan, spec, mask, steering, inv, lag_range, window)
 
     width = window.shape[2] // 3
 
@@ -453,18 +462,13 @@
     )(*near_vmem(*values))
 
 
-def divide(count, most=8):
-    return max(n for n in range(1, most + 1) if count % n == 0)
-
-
-def early_call(plan, nbands, near, mates, even, odd, inv, steering, lag_range):
+def early_call(nbands, near, mates, even, odd, inv, steering, lag_range):
     _, rows, cols = near.shape
     angles, group = steering.shape[1], lag_range.shape[2]
     rounds = steering.shape[0] - 1
-    table, _ = plan
     return pl.pallas_call(
-        functools.partial(early_kernel, nbands, divide(table.shape[1] // 6), 0),
-        in_specs=[SMEM_SPEC] + [VMEM_SPEC] * 4 + [HBM_SPEC] + [VMEM_SPEC] * 2,
+        functools.partial(early_kernel, nbands),
+        in_specs=[VMEM_SPEC] * 4 + [HBM_SPEC] + [VMEM_SPEC] * 2,
         out_specs=[VMEM_SPEC] * 3,
         out_shape=[
             pltpu.VMEM((3 * Q, rows, cols), jnp.bfloat16),
@@ -477,18 +481,17 @@
         ],
         compiler_params=pltpu.CompilerParams(vmem_limit_bytes=LIMIT),
         name="early_pairs",
-    )(jnp.asarray(table), *near_vmem(near, mates, even, odd), in_hbm(inv), *near_vmem(steering, lag_range))
-
-
-def late_call(plan, nbands, spec, window, even, odd, inv, steering, lag_range):
+    )(*near_vmem(near, mates, even, odd), in_hbm(inv), *near_vmem(steering, lag_range))
+
+
+def late_call(nbands, spec, window, even, odd, inv, steering, lag_range):
     cols = spec.shape[2]
     angles, group = steering.shape[1], lag_range.shape[2]
     rounds = steering.shape[0] - 1
     pieces = (Q + 2, angles, group // 3)
-    table, twins = plan
     return pl.pallas_call(
-        functools.partial(late_kernel, nbands, table.shape[1] // 6, twins),
-        in_specs=[SMEM_SPEC] + [VMEM_SPEC] * 7,
+        functools.partial(late_kernel, nbands),
+        in_specs=[VMEM_SPEC] * 7,
         out_specs=[VMEM_SPEC] * 4,
         out_shape=[
             pltpu.VMEM(pieces, jnp.float32),
@@ -496,11 +499,11 @@
             pltpu.VMEM(spec.shape, spec.dtype),
             pltpu.VMEM(window.shape, window.dtype),
         ],
-        input_output_aliases={1: 2, 2: 3},
+        input_output_aliases={0: 2, 1: 3},
         scratch_shapes=[pltpu.VMEM((2 * Q, L // cols, 2 * rounds, cols), jnp.float32)],
         compiler_params=pltpu.CompilerParams(vmem_limit_bytes=LIMIT),
         name="late_pairs",
-    )(jnp.asarray(table), *near_vmem(spec, window, even, odd, inv, steering, lag_range))[:2]
+    )(*near_vmem(spec, window, even, odd, inv, steering, lag_range))[:2]
 
 
 def exchange(value, devices, target):
@@ -525,14 +528,13 @@
     mates = flip(mates, 2)
     near_odd, near_even = planes(near, 1), planes(near, 0)
     far_odd, far_even = planes(mates, 1), planes(mates, 0)
-    early, late = unit_table(steering.shape[0] - 1)
     nbands = band_used.shape[2]
     inv = jnp.asarray(inverse_table(strain.shape[1]))
     spec, window, inv = early_call(
-        early, nbands, near, mates, near_even, near_odd, inv, steering, lag_range
+        nbands, near, mates, near_even, near_odd, inv, steering, lag_range
     )
     kept, send = late_call(
-        late, nbands, spec, window, far_even, far_odd, inv, steering, lag_range
+        nbands, spec, window, far_even, far_odd, inv, steering, lag_range
     )
 
     def pieces(count, dtype):

time: 42.5 us -> 41.8 us (0.984)
  Pallas kernels: 12.2 us -> 10.9 us
  waiting for transfers between devices: 10.5 us -> 11.3 us
    pallas_call x2, Pallas kernels: 8.09 us -> 6.73 us  [the longest x1 4.26 us: early_call(): pl.pallas_call(functools.partial(early_kernel, nbands), in_specs=[VMEM_SP...]
    ppermute x10, waiting for transfers between devices: 10.5 us -> 11.3 us  [exchange(): return lax.ppermute(value, AXIS, pairs)]
  transfers between devices with their start and end apart: 10 -> 10, of which waited for: 7 -> 7; matrix products, arithmetic and copies ran while one was open for 0% -> 0% of each run, Pallas kernels for 13% -> 12%
where the time goes in v8:
time: 41.8 us; the launch traced here: 41.6 us
  starting transfers between devices  19.3 us (46%)
  waiting for transfers between devices  11.3 us (27%)
  Pallas kernels  10.9 us (26%)
    ppermute x10, starting transfers between devices, exchange(): return lax.ppermute(value, AXIS, pairs)  19.3 us
    ppermute x10, waiting for transfers between devices, exchange(): return lax.ppermute(value, AXIS, pairs)  11.3 us
    pallas_call x1, Pallas kernels, early_call(): pl.pallas_call(functools.partial(early_kernel, nbands), in_specs=[VMEM_SP...  4.26 us
    pallas_call x1, Pallas kernels, send_call(): pl.pallas_call(send_kernel, in_specs=[HBM_SPEC] * 4, out_specs=[VMEM_SPEC...  2.66 us
    pallas_call x1, Pallas kernels, late_call(): pl.pallas_call(functools.partial(late_kernel, nbands), in_specs=[VMEM_SPE...  2.47 us
    pallas_call x6, Pallas kernels, local_call(): pl.pallas_call(kernel, in_specs=[VMEM_SPEC] * len(values), out_specs=[VME...  1.48 us
  transfers between devices with their start and end apart: 10, of which 7 were waited for; matrix products, arithmetic and copies ran while one was open for 0% of the time, Pallas kernels for 12%

profile of v8, /device:TPU:0, one launch (start us, length us, event | category | flops | bytes accessed | tf_op | source)
XLA Modules:
  0.0 41.6 jit_solution(15050552962266556143)
XLA Ops:
  0.0 2.7 %spectrum_sent.1 = (bf16[2,264,256]{2,1,0:T(8,128)(2,1)S(1)}, bf16[2,2,256,1024]{3,2,1,0:T(8,128)(2,1)S(1)}, bf16[2,1024,256]{2,1,0:T(8,128)(2,1)S(1)}) custom-call(bf16[256,4096]{1,0:T(8,128)(2,1)} %strain.1, f32[2,4,2,32,128]{4,3,2,1,0:T(8,128)} %constant.4.clone.factors, s32[1,8]{1,0:T(1,128)} %listed.1, s32[1,4,8]{2,1,0:T(4,128)} %bitcast.1), custom_call_target="tpu_custom_call" | custom-call | tf_op jit(solution)/shard_map/spectrum_sent/pallas_call | solution.py:195
  2.7 0.8 %collective-permute-start = (bf16[2,264,256]{2,1,0:T(8,128)(2,1)S(1)}, bf16[2,264,256]{2,1,0:T(8,128)(2,1)S(1)}, u32[]{:S(2)}, u32[]{:S(2)}) collective-permute-start(bf16[2,264,256]{2,1,0:T(8,128)(2,1)S(1)} %get-tuple-element.23.swap), channel_id=1, source_target_pairs={{0,1},{1,0},{2,3},{3,2},{4,5},{5,4},{6,7},{7,6},{8,9},{9,8},{10,11... | collective-permute-start | bytes 811016 | tf_op jit(solution)/shard_map/ppermute | solution.py:512
  3.5 0.0 copy-start
  3.5 0.0 copy-start.1
  3.5 0.7 %spectrum_kept.1 = (bf16[2,264,256]{2,1,0:T(8,128)(2,1)S(1)}, bf16[2,264,256]{2,1,0:T(8,128)(2,1)S(1)}) custom-call(bf16[2,264,256]{2,1,0:T(8,128)(2,1)S(1)} %get-tuple-element.23.swap, bf16[2,2,256,1024]{3,2,1,0:T(8,128)(2,1)S(1)} %get-tuple-element.24.folds, bf16[2,1024,256]{2,1,0:T(8,128)(2,1)S(1)} %get-tuple-element.25.table), custom_call_target="tpu_custom_call" | custom-call | tf_op jit(solution)/shard_map/spectrum_kept/pallas_call | solution.py:454
  4.2 0.4 collective-permute-done.swap
  4.7 2.7 %collective-permute-start.1 = (bf16[2,264,256]{2,1,0:T(8,128)(2,1)S(1)}, bf16[2,264,256]{2,1,0:T(8,128)(2,1)S(1)}, u32[]{:S(2)}, u32[]{:S(2)}) collective-permute-start(bf16[2,264,256]{2,1,0:T(8,128)(2,1)S(1)} %get-tuple-element.29), channel_id=1, source_target_pairs={{0,2},{1,3},{2,0},{3,1},{4,6},{5,7},{6,4},{7,5},{8,10},{9,11},{10,... | collective-permute-start | bytes 811016 | tf_op jit(solution)/shard_map/ppermute | solution.py:512
  7.4 0.7 %collective-permute-start.3 = (bf16[2,264,256]{2,1,0:T(8,128)(2,1)S(1)}, bf16[2,264,256]{2,1,0:T(8,128)(2,1)S(1)}, u32[]{:S(2)}, u32[]{:S(2)}) collective-permute-start(bf16[2,264,256]{2,1,0:T(8,128)(2,1)S(1)} %get-tuple-element.28.near), channel_id=1, source_target_pairs={{4,8},{5,9},{6,10},{7,11},{8,4},{9,5},{10,6},{11,7},{20,24},{21,25... | collective-permute-start | bytes 811016 | tf_op jit(solution)/shard_map/ppermute | solution.py:512
  8.0 4.4 %collective-permute-start.2 = (bf16[2,264,256]{2,1,0:T(8,128)(2,1)S(1)}, bf16[2,264,256]{2,1,0:T(8,128)(2,1)S(1)}, u32[]{:S(2)}, u32[]{:S(2)}) collective-permute-start(bf16[2,264,256]{2,1,0:T(8,128)(2,1)S(1)} %get-tuple-element.28.near), channel_id=1, source_target_pairs={{0,4},{1,5},{2,6},{3,7},{4,0},{5,1},{6,2},{7,3},{8,12},{9,13},{10,... | collective-permute-start | bytes 811016 | tf_op jit(solution)/shard_map/ppermute | solution.py:512
  12.5 1.7 %collective-permute-done.1.mates = bf16[2,264,256]{2,1,0:T(8,128)(2,1)S(1)} collective-permute-done((bf16[2,264,256]{2,1,0:T(8,128)(2,1)S(1)}, bf16[2,264,256]{2,1,0:T(8,128)(2,1)S(1)}, u32[]{:S(2)}, u32[]{:S(2)}) %collective-permute-start.1) | collective-permute-done | bytes 270368 | tf_op jit(solution)/shard_map/ppermute | solution.py:512
  14.1 0.7 %collective-permute-start.5 = (bf16[2,264,256]{2,1,0:T(8,128)(2,1)S(1)}, bf16[2,264,256]{2,1,0:T(8,128)(2,1)S(1)}, u32[]{:S(2)}, u32[]{:S(2)}) collective-permute-start(bf16[2,264,256]{2,1,0:T(8,128)(2,1)S(1)} %collective-permute-done.1.mates), channel_id=1, source_target_pairs={{4,8},{5,9},{6,10},{7,11},{8,4},{9,5},{10,6},{11,7},{20,24},{21,25... | collective-permute-start | bytes 811016 | tf_op jit(solution)/shard_map/ppermute | solution.py:512
  14.8 4.7 %collective-permute-start.4 = (bf16[2,264,256]{2,1,0:T(8,128)(2,1)S(1)}, bf16[2,264,256]{2,1,0:T(8,128)(2,1)S(1)}, u32[]{:S(2)}, u32[]{:S(2)}) collective-permute-start(bf16[2,264,256]{2,1,0:T(8,128)(2,1)S(1)} %collective-permute-done.1.mates), channel_id=1, source_target_pairs={{0,4},{1,5},{2,6},{3,7},{4,0},{5,1},{6,2},{7,3},{8,12},{9,13},{10,... | collective-permute-start | bytes 811016 | tf_op jit(solution)/shard_map/ppermute | solution.py:512
  19.5 0.0 collective-permute-done.3.odd
  19.5 0.0 collective-permute-done.2.even
  19.5 0.0 copy-done
  19.5 0.0 copy-done.1
  19.5 4.3 %early_pairs.1 = (bf16[12,264,256]{2,1,0:T(8,128)(2,1)S(1)}, f32[8,128,384]{2,1,0:T(8,128)S(1)}, bf16[256,512]{1,0:T(8,128)(2,1)S(1)}) custom-call(bf16[2,264,256]{2,1,0:T(8,128)(2,1)S(1)} %get-tuple-element.28.near, bf16[2,264,256]{2,1,0:T(8,128)(2,1)S(1)} %collective-permute-done.1.mates, bf16[2,264,256]{2,1,0:T(8,128)(2,1)S(1)} %collective-permute-done.2.even, ...), custom_call_target="tpu_custom_call" | custom-call | tf_op jit(solution)/shard_map/early_pairs/pallas_call | solution.py:469
  23.8 0.0 collective-permute-done.5.odd
  23.8 1.4 %collective-permute-done.4.even = bf16[2,264,256]{2,1,0:T(8,128)(2,1)S(1)} collective-permute-done((bf16[2,264,256]{2,1,0:T(8,128)(2,1)S(1)}, bf16[2,264,256]{2,1,0:T(8,128)(2,1)S(1)}, u32[]{:S(2)}, u32[]{:S(2)}) %collective-permute-start.4) | collective-permute-done | bytes 270368 | tf_op jit(solution)/shard_map/ppermute | solution.py:512
  25.1 2.5 %late_pairs.1 = (f32[6,128,128]{2,1,0:T(8,128)S(1)}, bf16[6,128,128]{2,1,0:T(8,128)(2,1)S(1)}, bf16[12,264,256]{2,1,0:T(8,128)(2,1)S(1)}, f32[8,128,384]{2,1,0:T(8,128)S(1)}) custom-call(bf16[12,264,256]{2,1,0:T(8,128)(2,1)S(1)} %get-tuple-element.30.spec_in, ...), custom_call_target="tpu_custom_call", output_to_operand_aliasing={{2}: (0, {}), {3}: (1, {})} | custom-call | tf_op jit(solution)/shard_map/late_pairs/pallas_call | solution.py:492
  27.6 0.1 collective-permute-start.6
  27.7 1.4 %collective-permute-done.6.received = bf16[6,128,128]{2,1,0:T(8,128)(2,1)S(1)} collective-permute-done((bf16[6,128,128]{2,1,0:T(8,128)(2,1)S(1)}, bf16[6,128,128]{2,1,0:T(8,128)(2,1)S(1)}, u32[]{:S(2)}, u32[]{:S(2)}) %collective-permute-start.6) | collective-permute-done | bytes 196640 | tf_op jit(solution)/shard_map/ppermute | solution.py:512
  29.2 1.6 %collective-permute-start.7 = (bf16[3,128,128]{2,1,0:T(8,128)(2,1)S(1)}, bf16[3,128,128]{2,1,0:T(8,128)(2,1)S(1)}, u32[]{:S(2)}, u32[]{:S(2)}) collective-permute-start(bf16[3,128,128]{2,1,0:T(8,128)(2,1)S(1)} %get-tuple-element.36), channel_id=1, source_target_pairs={{0,2},{1,3},{2,0},{3,1},{4,6},{5,7},{6,4},{7,5},{8,10},{9,11},{10,... | collective-permute-start | bytes 294920 | tf_op jit(solution)/shard_map/ppermute | solution.py:512
  30.7 3.3 %collective-permute-done.7.received = bf16[3,128,128]{2,1,0:T(8,128)(2,1)S(1)} collective-permute-done((bf16[3,128,128]{2,1,0:T(8,128)(2,1)S(1)}, bf16[3,128,128]{2,1,0:T(8,128)(2,1)S(1)}, u32[]{:S(2)}, u32[]{:S(2)}) %collective-permute-start.7) | collective-permute-done | bytes 98336 | tf_op jit(solution)/shard_map/ppermute | solution.py:512
  34.1 3.6 %collective-permute-start.8 = (bf16[2,128,128]{2,1,0:T(8,128)(2,1)S(1)}, bf16[2,128,128]{2,1,0:T(8,128)(2,1)S(1)}, u32[]{:S(2)}, u32[]{:S(2)}) collective-permute-start(bf16[2,128,128]{2,1,0:T(8,128)(2,1)S(1)} %get-tuple-element.38), channel_id=1, source_target_pairs={{0,4},{1,9},{2,6},{4,8},{5,13},{6,10},{7,3},{8,12},{10,14},{11,7},... | collective-permute-start | bytes 196616 | tf_op jit(solution)/shard_map/ppermute | solution.py:512
  37.8 1.9 %collective-permute-done.8.received = bf16[2,128,128]{2,1,0:T(8,128)(2,1)S(1)} collective-permute-done((bf16[2,128,128]{2,1,0:T(8,128)(2,1)S(1)}, bf16[2,128,128]{2,1,0:T(8,128)(2,1)S(1)}, u32[]{:S(2)}, u32[]{:S(2)}) %collective-permute-start.8) | collective-permute-done | bytes 65568 | tf_op jit(solution)/shard_map/ppermute | solution.py:512
  39.7 0.1 collective-permute-start.9
  39.7 1.2 %collective-permute-done.9.received = f32[128,128]{1,0:T(8,128)S(1)} collective-permute-done((f32[128,128]{1,0:T(8,128)S(1)}, f32[128,128]{1,0:T(8,128)S(1)}, u32[]{:S(2)}, u32[]{:S(2)}) %collective-permute-start.9) | collective-permute-done | bytes 65568 | tf_op jit(solution)/shard_map/ppermute | solution.py:512
  41.0 0.6 %image.1 = f32[128,128]{1,0:T(8,128)} custom-call(f32[128,128]{1,0:T(8,128)S(1)} %get-tuple-element.39.kept, f32[128,128]{1,0:T(8,128)S(1)} %collective-permute-done.9.received), custom_call_target="tpu_custom_call" | custom-call | tf_op jit(solution)/shard_map/image/pallas_call | solution.py:454
  (4 shorter events, 0.1 us)
Async XLA Ops:
  2.7 2.0 %collective-permute-start = (bf16[2,264,256]{2,1,0:T(8,128)(2,1)S(1)}, bf16[2,264,256]{2,1,0:T(8,128)(2,1)S(1)}, u32[]{:S(2)}, u32[]{:S(2)}) collective-permute-start(bf16[2,264,256]{2,1,0:T(8,128)(2,1)S(1)} %get-tuple-element.23.swap), channel_id=1, source_target_pairs={{0,1},{1,0},{2,3},{3,2},{4,5},{5,4},{6,7},{7,6},{8,9},{9,8},{10,11... | collective-permute-start | bytes 811016 | tf_op jit(solution)/shard_map/ppermute | solution.py:512
  3.5 16.0 %copy-start = (bf16[9,512,384]{2,1,0:T(8,128)(2,1)S(1)}, bf16[9,512,384]{2,1,0:T(8,128)(2,1)}, u32[]{:S(2)}) copy-start(bf16[9,512,384]{2,1,0:T(8,128)(2,1)} %lag_range.3) | copy-start | bytes 10616836
  3.5 16.0 %copy-start.1 = (bf16[9,128,256]{2,1,0:T(8,128)(2,1)S(1)}, bf16[9,128,256]{2,1,0:T(8,128)(2,1)}, u32[]{:S(2)}) copy-start(bf16[9,128,256]{2,1,0:T(8,128)(2,1)} %steering.3) | copy-start | bytes 1769476
  4.7 9.5 %collective-permute-start.1 = (bf16[2,264,256]{2,1,0:T(8,128)(2,1)S(1)}, bf16[2,264,256]{2,1,0:T(8,128)(2,1)S(1)}, u32[]{:S(2)}, u32[]{:S(2)}) collective-permute-start(bf16[2,264,256]{2,1,0:T(8,128)(2,1)S(1)} %get-tuple-element.29), channel_id=1, source_target_pairs={{0,2},{1,3},{2,0},{3,1},{4,6},{5,7},{6,4},{7,5},{8,10},{9,11},{10,... | collective-permute-start | bytes 811016 | tf_op jit(solution)/shard_map/ppermute | solution.py:512
  7.4 12.1 %collective-permute-start.3 = (bf16[2,264,256]{2,1,0:T(8,128)(2,1)S(1)}, bf16[2,264,256]{2,1,0:T(8,128)(2,1)S(1)}, u32[]{:S(2)}, u32[]{:S(2)}) collective-permute-start(bf16[2,264,256]{2,1,0:T(8,128)(2,1)S(1)} %get-tuple-element.28.near), channel_id=1, source_target_pairs={{4,8},{5,9},{6,10},{7,11},{8,4},{9,5},{10,6},{11,7},{20,24},{21,25... | collective-permute-start | bytes 811016 | tf_op jit(solution)/shard_map/ppermute | solution.py:512
  8.0 11.5 %collective-permute-start.2 = (bf16[2,264,256]{2,1,0:T(8,128)(2,1)S(1)}, bf16[2,264,256]{2,1,0:T(8,128)(2,1)S(1)}, u32[]{:S(2)}, u32[]{:S(2)}) collective-permute-start(bf16[2,264,256]{2,1,0:T(8,128)(2,1)S(1)} %get-tuple-element.28.near), channel_id=1, source_target_pairs={{0,4},{1,5},{2,6},{3,7},{4,0},{5,1},{6,2},{7,3},{8,12},{9,13},{10,... | collective-permute-start | bytes 811016 | tf_op jit(solution)/shard_map/ppermute | solution.py:512
  14.1 9.6 %collective-permute-start.5 = (bf16[2,264,256]{2,1,0:T(8,128)(2,1)S(1)}, bf16[2,264,256]{2,1,0:T(8,128)(2,1)S(1)}, u32[]{:S(2)}, u32[]{:S(2)}) collective-permute-start(bf16[2,264,256]{2,1,0:T(8,128)(2,1)S(1)} %collective-permute-done.1.mates), channel_id=1, source_target_pairs={{4,8},{5,9},{6,10},{7,11},{8,4},{9,5},{10,6},{11,7},{20,24},{21,25... | collective-permute-start | bytes 811016 | tf_op jit(solution)/shard_map/ppermute | solution.py:512
  14.8 10.3 %collective-permute-start.4 = (bf16[2,264,256]{2,1,0:T(8,128)(2,1)S(1)}, bf16[2,264,256]{2,1,0:T(8,128)(2,1)S(1)}, u32[]{:S(2)}, u32[]{:S(2)}) collective-permute-start(bf16[2,264,256]{2,1,0:T(8,128)(2,1)S(1)} %collective-permute-done.1.mates), channel_id=1, source_target_pairs={{0,4},{1,5},{2,6},{3,7},{4,0},{5,1},{6,2},{7,3},{8,12},{9,13},{10,... | collective-permute-start | bytes 811016 | tf_op jit(solution)/shard_map/ppermute | solution.py:512
  27.6 1.5 %collective-permute-start.6 = (bf16[6,128,128]{2,1,0:T(8,128)(2,1)S(1)}, bf16[6,128,128]{2,1,0:T(8,128)(2,1)S(1)}, u32[]{:S(2)}, u32[]{:S(2)}) collective-permute-start(bf16[6,128,128]{2,1,0:T(8,128)(2,1)S(1)} %get-tuple-element.34), channel_id=1, source_target_pairs={{0,1},{1,0},{2,3},{3,2},{4,5},{5,4},{6,7},{7,6},{8,9},{9,8},{10,11... | collective-permute-start | bytes 589832 | tf_op jit(solution)/shard_map/ppermute | solution.py:512
  29.2 4.9 %collective-permute-start.7 = (bf16[3,128,128]{2,1,0:T(8,128)(2,1)S(1)}, bf16[3,128,128]{2,1,0:T(8,128)(2,1)S(1)}, u32[]{:S(2)}, u32[]{:S(2)}) collective-permute-start(bf16[3,128,128]{2,1,0:T(8,128)(2,1)S(1)} %get-tuple-element.36), channel_id=1, source_target_pairs={{0,2},{1,3},{2,0},{3,1},{4,6},{5,7},{6,4},{7,5},{8,10},{9,11},{10,... | collective-permute-start | bytes 294920 | tf_op jit(solution)/shard_map/ppermute | solution.py:512
  34.1 5.5 %collective-permute-start.8 = (bf16[2,128,128]{2,1,0:T(8,128)(2,1)S(1)}, bf16[2,128,128]{2,1,0:T(8,128)(2,1)S(1)}, u32[]{:S(2)}, u32[]{:S(2)}) collective-permute-start(bf16[2,128,128]{2,1,0:T(8,128)(2,1)S(1)} %get-tuple-element.38), channel_id=1, source_target_pairs={{0,4},{1,9},{2,6},{4,8},{5,13},{6,10},{7,3},{8,12},{10,14},{11,7},... | collective-permute-start | bytes 196616 | tf_op jit(solution)/shard_map/ppermute | solution.py:512
  39.7 1.3 %collective-permute-start.9 = (f32[128,128]{1,0:T(8,128)S(1)}, f32[128,128]{1,0:T(8,128)S(1)}, u32[]{:S(2)}, u32[]{:S(2)}) collective-permute-start(f32[128,128]{1,0:T(8,128)S(1)} %get-tuple-element.40), channel_id=1, source_target_pairs={{0,1},{1,0},{2,3},{3,2},{4,5},{5,4},{6,7},{7,6},{8,9},{9,8},{10,11... | collective-permute-start | bytes 196616 | tf_op jit(solution)/shard_map/ppermute | solution.py:512

commit v9 on v8

--- a/solution.py
+++ b/solution.py
@@ -391,33 +391,44 @@
 
 
 def core_sum_kernel(kept, received, mine, send):
-    side = lax.rem(lax.axis_index(AXIS), Q) // 2
+    me = lax.rem(lax.axis_index(AXIS), Q)
+    core, side = lax.rem(me, 2), me // 2
 
     def total(n):
         return kept[n] + received[n].astype(jnp.float32)
 
-    for n in range(2):
-        mine[n] = total(2 * side + n)
-        send[n] = total(2 * (1 - side) + n).astype(jnp.bfloat16)
-    mine[2] = total(Q + side)
-    send[2] = total(Q + 1 - side).astype(jnp.bfloat16)
+    @pl.when(core == 0)
+    def _():
+        for n in range(Q):
+            send[n] = total(n).astype(jnp.bfloat16)
+        mine[...] = jnp.zeros_like(mine)
+
+    @pl.when(core == 1)
+    def _():
+        for n in range(2):
+            mine[n] = total(2 * side + n)
+            send[n] = total(2 * (1 - side) + n).astype(jnp.bfloat16)
+        mine[2] = total(Q + side)
+        send[2] = total(Q + 1 - side).astype(jnp.bfloat16)
+        send[3] = jnp.zeros_like(send[2])
 
 
 def plane_sum_kernel(kept, received, mine, send):
-    core = lax.rem(lax.axis_index(AXIS), 2)
-    totals = [kept[n] + received[n].astype(jnp.float32) for n in range(3)]
-    mine[0] = totals[0]
-    mine[1] = totals[1]
+    me = lax.rem(lax.axis_index(AXIS), Q)
+    core, side = lax.rem(me, 2), me // 2
 
     @pl.when(core == 0)
     def _():
-        send[0] = totals[0].astype(jnp.bfloat16)
-        send[1] = totals[1].astype(jnp.bfloat16)
+        for n in range(2):
+            mine[n] = received[2 * side + n].astype(jnp.float32)
+            send[n] = received[2 * (1 - side) + n]
 
     @pl.when(core == 1)
     def _():
-        send[0] = totals[2].astype(jnp.bfloat16)
-        send[1] = jnp.zeros_like(totals[2]).astype(jnp.bfloat16)
+        for n in range(2):
+            mine[n] = kept[n] + received[n].astype(jnp.float32)
+        send[0] = (kept[2] + received[2].astype(jnp.float32)).astype(jnp.bfloat16)
+        send[1] = jnp.zeros_like(send[0])
 
 
 def end_sum_kernel(kept, received, mine, send):
@@ -428,8 +439,8 @@
 
     @pl.when(core == 0)
     def _():
-        mine[...] = first
-        send[...] = second
+        mine[...] = kept[0] + first
+        send[...] = kept[1] + second
 
     @pl.when((core == 1) & (side == 0))
     def _():
@@ -540,15 +551,18 @@
     def pieces(count, dtype):
         return pltpu.VMEM(((count,) if count else ()) + kept.shape[1:], dtype)
 
-    def ends(i):
+    def first(i):
+        return i + Q if i % 2 == 0 else i ^ 2
+
+    def second(i):
         if i % 2 == 0:
-            return i + Q
+            return i ^ 2
         return i + 2 * Q if i % Q < 2 else i - Q
 
     kept, send = local_call(
         core_sum_kernel,
         "core_sum",
-        [pieces(3, jnp.float32), pieces(3, jnp.bfloat16)],
+        [pieces(3, jnp.float32), pieces(Q, jnp.bfloat16)],
         kept,
         flip(send, 1),
     )
@@ -557,14 +571,14 @@
         "plane_sum",
         [pieces(2, jnp.float32), pieces(2, jnp.bfloat16)],
         kept,
-        flip(send, 2),
+        exchange(send, devices, first),
     )
     kept, send = local_call(
         end_sum_kernel,
         "end_sum",
         [pieces(0, jnp.float32), pieces(0, jnp.float32)],
         kept,
-        exchange(send, devices, ends),
+        exchange(send, devices, second),
     )
     return local_call(
         image_kernel,

time: 41.8 us -> 43.7 us (1.045)
  starting transfers between devices: 19.3 us -> 21.2 us
    ppermute x10, starting transfers between devices: 19.3 us -> 21.2 us  [exchange(): return lax.ppermute(value, AXIS, pairs)]
  transfers between devices with their start and end apart: 10 -> 10, of which waited for: 7 -> 7; matrix products, arithmetic and copies ran while one was open for 0% -> 0% of each run, Pallas kernels for 12% -> 11%
where the time goes in v9:
time: 43.7 us; the launch traced here: 43.5 us
  starting transfers between devices  21.2 us (49%)
  waiting for transfers between devices  11.3 us (26%)
  Pallas kernels  10.9 us (25%)
    ppermute x10, starting transfers between devices, exchange(): return lax.ppermute(value, AXIS, pairs)  21.2 us
    ppermute x10, waiting for transfers between devices, exchange(): return lax.ppermute(value, AXIS, pairs)  11.3 us
    pallas_call x1, Pallas kernels, early_call(): pl.pallas_call(functools.partial(early_kernel, nbands), in_specs=[VMEM_SP...  4.26 us
    pallas_call x1, Pallas kernels, send_call(): pl.pallas_call(send_kernel, in_specs=[HBM_SPEC] * 4, out_specs=[VMEM_SPEC...  2.66 us
    pallas_call x1, Pallas kernels, late_call(): pl.pallas_call(functools.partial(late_kernel, nbands), in_specs=[VMEM_SPE...  2.47 us
    pallas_call x6, Pallas kernels, local_call(): pl.pallas_call(kernel, in_specs=[VMEM_SPEC] * len(values), out_specs=[VME...  1.47 us
  transfers between devices with their start and end apart: 10, of which 7 were waited for; matrix products, arithmetic and copies ran while one was open for 0% of the time, Pallas kernels for 11%

profile of v9, /device:TPU:0, one launch (start us, length us, event | category | flops | bytes accessed | tf_op | source)
XLA Modules:
  0.0 43.5 jit_solution(2343511587480643683)
XLA Ops:
  0.0 2.7 %spectrum_sent.1 = (bf16[2,264,256]{2,1,0:T(8,128)(2,1)S(1)}, bf16[2,2,256,1024]{3,2,1,0:T(8,128)(2,1)S(1)}, bf16[2,1024,256]{2,1,0:T(8,128)(2,1)S(1)}) custom-call(bf16[256,4096]{1,0:T(8,128)(2,1)} %strain.1, f32[2,4,2,32,128]{4,3,2,1,0:T(8,128)} %constant.4.clone.factors, s32[1,8]{1,0:T(1,128)} %listed.1, s32[1,4,8]{2,1,0:T(4,128)} %bitcast.1), custom_call_target="tpu_custom_call" | custom-call | tf_op jit(solution)/shard_map/spectrum_sent/pallas_call | solution.py:195
  2.7 0.8 %collective-permute-start = (bf16[2,264,256]{2,1,0:T(8,128)(2,1)S(1)}, bf16[2,264,256]{2,1,0:T(8,128)(2,1)S(1)}, u32[]{:S(2)}, u32[]{:S(2)}) collective-permute-start(bf16[2,264,256]{2,1,0:T(8,128)(2,1)S(1)} %get-tuple-element.23.swap), channel_id=1, source_target_pairs={{0,1},{1,0},{2,3},{3,2},{4,5},{5,4},{6,7},{7,6},{8,9},{9,8},{10,11... | collective-permute-start | bytes 811016 | tf_op jit(solution)/shard_map/ppermute | solution.py:523
  3.5 0.0 copy-start
  3.5 0.0 copy-start.1
  3.5 0.7 %spectrum_kept.1 = (bf16[2,264,256]{2,1,0:T(8,128)(2,1)S(1)}, bf16[2,264,256]{2,1,0:T(8,128)(2,1)S(1)}) custom-call(bf16[2,264,256]{2,1,0:T(8,128)(2,1)S(1)} %get-tuple-element.23.swap, bf16[2,2,256,1024]{3,2,1,0:T(8,128)(2,1)S(1)} %get-tuple-element.24.folds, bf16[2,1024,256]{2,1,0:T(8,128)(2,1)S(1)} %get-tuple-element.25.table), custom_call_target="tpu_custom_call" | custom-call | tf_op jit(solution)/shard_map/spectrum_kept/pallas_call | solution.py:465
  4.2 0.4 collective-permute-done.swap
  4.7 2.7 %collective-permute-start.1 = (bf16[2,264,256]{2,1,0:T(8,128)(2,1)S(1)}, bf16[2,264,256]{2,1,0:T(8,128)(2,1)S(1)}, u32[]{:S(2)}, u32[]{:S(2)}) collective-permute-start(bf16[2,264,256]{2,1,0:T(8,128)(2,1)S(1)} %get-tuple-element.29), channel_id=1, source_target_pairs={{0,2},{1,3},{2,0},{3,1},{4,6},{5,7},{6,4},{7,5},{8,10},{9,11},{10,... | collective-permute-start | bytes 811016 | tf_op jit(solution)/shard_map/ppermute | solution.py:523
  7.4 0.7 %collective-permute-start.3 = (bf16[2,264,256]{2,1,0:T(8,128)(2,1)S(1)}, bf16[2,264,256]{2,1,0:T(8,128)(2,1)S(1)}, u32[]{:S(2)}, u32[]{:S(2)}) collective-permute-start(bf16[2,264,256]{2,1,0:T(8,128)(2,1)S(1)} %get-tuple-element.28.near), channel_id=1, source_target_pairs={{4,8},{5,9},{6,10},{7,11},{8,4},{9,5},{10,6},{11,7},{20,24},{21,25... | collective-permute-start | bytes 811016 | tf_op jit(solution)/shard_map/ppermute | solution.py:523
  8.0 4.4 %collective-permute-start.2 = (bf16[2,264,256]{2,1,0:T(8,128)(2,1)S(1)}, bf16[2,264,256]{2,1,0:T(8,128)(2,1)S(1)}, u32[]{:S(2)}, u32[]{:S(2)}) collective-permute-start(bf16[2,264,256]{2,1,0:T(8,128)(2,1)S(1)} %get-tuple-element.28.near), channel_id=1, source_target_pairs={{0,4},{1,5},{2,6},{3,7},{4,0},{5,1},{6,2},{7,3},{8,12},{9,13},{10,... | collective-permute-start | bytes 811016 | tf_op jit(solution)/shard_map/ppermute | solution.py:523
  12.5 1.7 %collective-permute-done.1.mates = bf16[2,264,256]{2,1,0:T(8,128)(2,1)S(1)} collective-permute-done((bf16[2,264,256]{2,1,0:T(8,128)(2,1)S(1)}, bf16[2,264,256]{2,1,0:T(8,128)(2,1)S(1)}, u32[]{:S(2)}, u32[]{:S(2)}) %collective-permute-start.1) | collective-permute-done | bytes 270368 | tf_op jit(solution)/shard_map/ppermute | solution.py:523
  14.1 0.7 %collective-permute-start.5 = (bf16[2,264,256]{2,1,0:T(8,128)(2,1)S(1)}, bf16[2,264,256]{2,1,0:T(8,128)(2,1)S(1)}, u32[]{:S(2)}, u32[]{:S(2)}) collective-permute-start(bf16[2,264,256]{2,1,0:T(8,128)(2,1)S(1)} %collective-permute-done.1.mates), channel_id=1, source_target_pairs={{4,8},{5,9},{6,10},{7,11},{8,4},{9,5},{10,6},{11,7},{20,24},{21,25... | collective-permute-start | bytes 811016 | tf_op jit(solution)/shard_map/ppermute | solution.py:523
  14.8 4.7 %collective-permute-start.4 = (bf16[2,264,256]{2,1,0:T(8,128)(2,1)S(1)}, bf16[2,264,256]{2,1,0:T(8,128)(2,1)S(1)}, u32[]{:S(2)}, u32[]{:S(2)}) collective-permute-start(bf16[2,264,256]{2,1,0:T(8,128)(2,1)S(1)} %collective-permute-done.1.mates), channel_id=1, source_target_pairs={{0,4},{1,5},{2,6},{3,7},{4,0},{5,1},{6,2},{7,3},{8,12},{9,13},{10,... | collective-permute-start | bytes 811016 | tf_op jit(solution)/shard_map/ppermute | solution.py:523
  19.5 0.0 collective-permute-done.3.odd
  19.5 0.0 collective-permute-done.2.even
  19.5 0.0 copy-done
  19.5 0.0 copy-done.1
  19.5 4.3 %early_pairs.1 = (bf16[12,264,256]{2,1,0:T(8,128)(2,1)S(1)}, f32[8,128,384]{2,1,0:T(8,128)S(1)}, bf16[256,512]{1,0:T(8,128)(2,1)S(1)}) custom-call(bf16[2,264,256]{2,1,0:T(8,128)(2,1)S(1)} %get-tuple-element.28.near, bf16[2,264,256]{2,1,0:T(8,128)(2,1)S(1)} %collective-permute-done.1.mates, bf16[2,264,256]{2,1,0:T(8,128)(2,1)S(1)} %collective-permute-done.2.even, ...), custom_call_target="tpu_custom_call" | custom-call | tf_op jit(solution)/shard_map/early_pairs/pallas_call | solution.py:480
  23.8 0.0 collective-permute-done.5.odd
  23.8 1.4 %collective-permute-done.4.even = bf16[2,264,256]{2,1,0:T(8,128)(2,1)S(1)} collective-permute-done((bf16[2,264,256]{2,1,0:T(8,128)(2,1)S(1)}, bf16[2,264,256]{2,1,0:T(8,128)(2,1)S(1)}, u32[]{:S(2)}, u32[]{:S(2)}) %collective-permute-start.4) | collective-permute-done | bytes 270368 | tf_op jit(solution)/shard_map/ppermute | solution.py:523
  25.1 2.5 %late_pairs.1 = (f32[6,128,128]{2,1,0:T(8,128)S(1)}, bf16[6,128,128]{2,1,0:T(8,128)(2,1)S(1)}, bf16[12,264,256]{2,1,0:T(8,128)(2,1)S(1)}, f32[8,128,384]{2,1,0:T(8,128)S(1)}) custom-call(bf16[12,264,256]{2,1,0:T(8,128)(2,1)S(1)} %get-tuple-element.30.spec_in, ...), custom_call_target="tpu_custom_call", output_to_operand_aliasing={{2}: (0, {}), {3}: (1, {})} | custom-call | tf_op jit(solution)/shard_map/late_pairs/pallas_call | solution.py:503
  27.6 0.1 collective-permute-start.6
  27.7 1.4 %collective-permute-done.6.received = bf16[6,128,128]{2,1,0:T(8,128)(2,1)S(1)} collective-permute-done((bf16[6,128,128]{2,1,0:T(8,128)(2,1)S(1)}, bf16[6,128,128]{2,1,0:T(8,128)(2,1)S(1)}, u32[]{:S(2)}, u32[]{:S(2)}) %collective-permute-start.6) | collective-permute-done | bytes 196640 | tf_op jit(solution)/shard_map/ppermute | solution.py:523
  29.2 3.7 %collective-permute-start.7 = (bf16[4,128,128]{2,1,0:T(8,128)(2,1)S(1)}, bf16[4,128,128]{2,1,0:T(8,128)(2,1)S(1)}, u32[]{:S(2)}, u32[]{:S(2)}) collective-permute-start(bf16[4,128,128]{2,1,0:T(8,128)(2,1)S(1)} %get-tuple-element.36), channel_id=1, source_target_pairs={{0,4},{1,3},{2,6},{3,1},{4,8},{5,7},{6,10},{7,5},{8,12},{9,11},{10... | collective-permute-start | bytes 393224 | tf_op jit(solution)/shard_map/ppermute | solution.py:523
  32.8 2.5 %collective-permute-done.7.received = bf16[4,128,128]{2,1,0:T(8,128)(2,1)S(1)} collective-permute-done((bf16[4,128,128]{2,1,0:T(8,128)(2,1)S(1)}, bf16[4,128,128]{2,1,0:T(8,128)(2,1)S(1)}, u32[]{:S(2)}, u32[]{:S(2)}) %collective-permute-start.7) | collective-permute-done | bytes 131104 | tf_op jit(solution)/shard_map/ppermute | solution.py:523
  35.3 3.4 %collective-permute-start.8 = (bf16[2,128,128]{2,1,0:T(8,128)(2,1)S(1)}, bf16[2,128,128]{2,1,0:T(8,128)(2,1)S(1)}, u32[]{:S(2)}, u32[]{:S(2)}) collective-permute-start(bf16[2,128,128]{2,1,0:T(8,128)(2,1)S(1)} %get-tuple-element.38), channel_id=1, source_target_pairs={{0,2},{1,9},{2,0},{4,6},{5,13},{6,4},{7,3},{8,10},{10,8},{11,7},{1... | collective-permute-start | bytes 196616 | tf_op jit(solution)/shard_map/ppermute | solution.py:523
  38.8 2.7 %collective-permute-done.8.received = bf16[2,128,128]{2,1,0:T(8,128)(2,1)S(1)} collective-permute-done((bf16[2,128,128]{2,1,0:T(8,128)(2,1)S(1)}, bf16[2,128,128]{2,1,0:T(8,128)(2,1)S(1)}, u32[]{:S(2)}, u32[]{:S(2)}) %collective-permute-start.8) | collective-permute-done | bytes 65568 | tf_op jit(solution)/shard_map/ppermute | solution.py:523
  41.5 0.1 collective-permute-start.9
  41.6 1.2 %collective-permute-done.9.received = f32[128,128]{1,0:T(8,128)S(1)} collective-permute-done((f32[128,128]{1,0:T(8,128)S(1)}, f32[128,128]{1,0:T(8,128)S(1)}, u32[]{:S(2)}, u32[]{:S(2)}) %collective-permute-start.9) | collective-permute-done | bytes 65568 | tf_op jit(solution)/shard_map/ppermute | solution.py:523
  42.9 0.6 %image.1 = f32[128,128]{1,0:T(8,128)} custom-call(f32[128,128]{1,0:T(8,128)S(1)} %get-tuple-element.39.kept, f32[128,128]{1,0:T(8,128)S(1)} %collective-permute-done.9.received), custom_call_target="tpu_custom_call" | custom-call | tf_op jit(solution)/shard_map/image/pallas_call | solution.py:465
  (4 shorter events, 0.1 us)
Async XLA Ops:
  2.7 2.0 %collective-permute-start = (bf16[2,264,256]{2,1,0:T(8,128)(2,1)S(1)}, bf16[2,264,256]{2,1,0:T(8,128)(2,1)S(1)}, u32[]{:S(2)}, u32[]{:S(2)}) collective-permute-start(bf16[2,264,256]{2,1,0:T(8,128)(2,1)S(1)} %get-tuple-element.23.swap), channel_id=1, source_target_pairs={{0,1},{1,0},{2,3},{3,2},{4,5},{5,4},{6,7},{7,6},{8,9},{9,8},{10,11... | collective-permute-start | bytes 811016 | tf_op jit(solution)/shard_map/ppermute | solution.py:523
  3.5 16.0 %copy-start = (bf16[9,512,384]{2,1,0:T(8,128)(2,1)S(1)}, bf16[9,512,384]{2,1,0:T(8,128)(2,1)}, u32[]{:S(2)}) copy-start(bf16[9,512,384]{2,1,0:T(8,128)(2,1)} %lag_range.3) | copy-start | bytes 10616836
  3.5 16.0 %copy-start.1 = (bf16[9,128,256]{2,1,0:T(8,128)(2,1)S(1)}, bf16[9,128,256]{2,1,0:T(8,128)(2,1)}, u32[]{:S(2)}) copy-start(bf16[9,128,256]{2,1,0:T(8,128)(2,1)} %steering.3) | copy-start | bytes 1769476
  4.7 9.5 %collective-permute-start.1 = (bf16[2,264,256]{2,1,0:T(8,128)(2,1)S(1)}, bf16[2,264,256]{2,1,0:T(8,128)(2,1)S(1)}, u32[]{:S(2)}, u32[]{:S(2)}) collective-permute-start(bf16[2,264,256]{2,1,0:T(8,128)(2,1)S(1)} %get-tuple-element.29), channel_id=1, source_target_pairs={{0,2},{1,3},{2,0},{3,1},{4,6},{5,7},{6,4},{7,5},{8,10},{9,11},{10,... | collective-permute-start | bytes 811016 | tf_op jit(solution)/shard_map/ppermute | solution.py:523
  7.4 12.1 %collective-permute-start.3 = (bf16[2,264,256]{2,1,0:T(8,128)(2,1)S(1)}, bf16[2,264,256]{2,1,0:T(8,128)(2,1)S(1)}, u32[]{:S(2)}, u32[]{:S(2)}) collective-permute-start(bf16[2,264,256]{2,1,0:T(8,128)(2,1)S(1)} %get-tuple-element.28.near), channel_id=1, source_target_pairs={{4,8},{5,9},{6,10},{7,11},{8,4},{9,5},{10,6},{11,7},{20,24},{21,25... | collective-permute-start | bytes 811016 | tf_op jit(solution)/shard_map/ppermute | solution.py:523
  8.0 11.5 %collective-permute-start.2 = (bf16[2,264,256]{2,1,0:T(8,128)(2,1)S(1)}, bf16[2,264,256]{2,1,0:T(8,128)(2,1)S(1)}, u32[]{:S(2)}, u32[]{:S(2)}) collective-permute-start(bf16[2,264,256]{2,1,0:T(8,128)(2,1)S(1)} %get-tuple-element.28.near), channel_id=1, source_target_pairs={{0,4},{1,5},{2,6},{3,7},{4,0},{5,1},{6,2},{7,3},{8,12},{9,13},{10,... | collective-permute-start | bytes 811016 | tf_op jit(solution)/shard_map/ppermute | solution.py:523
  14.1 9.6 %collective-permute-start.5 = (bf16[2,264,256]{2,1,0:T(8,128)(2,1)S(1)}, bf16[2,264,256]{2,1,0:T(8,128)(2,1)S(1)}, u32[]{:S(2)}, u32[]{:S(2)}) collective-permute-start(bf16[2,264,256]{2,1,0:T(8,128)(2,1)S(1)} %collective-permute-done.1.mates), channel_id=1, source_target_pairs={{4,8},{5,9},{6,10},{7,11},{8,4},{9,5},{10,6},{11,7},{20,24},{21,25... | collective-permute-start | bytes 811016 | tf_op jit(solution)/shard_map/ppermute | solution.py:523
  14.8 10.3 %collective-permute-start.4 = (bf16[2,264,256]{2,1,0:T(8,128)(2,1)S(1)}, bf16[2,264,256]{2,1,0:T(8,128)(2,1)S(1)}, u32[]{:S(2)}, u32[]{:S(2)}) collective-permute-start(bf16[2,264,256]{2,1,0:T(8,128)(2,1)S(1)} %collective-permute-done.1.mates), channel_id=1, source_target_pairs={{0,4},{1,5},{2,6},{3,7},{4,0},{5,1},{6,2},{7,3},{8,12},{9,13},{10,... | collective-permute-start | bytes 811016 | tf_op jit(solution)/shard_map/ppermute | solution.py:523
  27.6 1.5 %collective-permute-start.6 = (bf16[6,128,128]{2,1,0:T(8,128)(2,1)S(1)}, bf16[6,128,128]{2,1,0:T(8,128)(2,1)S(1)}, u32[]{:S(2)}, u32[]{:S(2)}) collective-permute-start(bf16[6,128,128]{2,1,0:T(8,128)(2,1)S(1)} %get-tuple-element.34), channel_id=1, source_target_pairs={{0,1},{1,0},{2,3},{3,2},{4,5},{5,4},{6,7},{7,6},{8,9},{9,8},{10,11... | collective-permute-start | bytes 589832 | tf_op jit(solution)/shard_map/ppermute | solution.py:523
  29.2 6.2 %collective-permute-start.7 = (bf16[4,128,128]{2,1,0:T(8,128)(2,1)S(1)}, bf16[4,128,128]{2,1,0:T(8,128)(2,1)S(1)}, u32[]{:S(2)}, u32[]{:S(2)}) collective-permute-start(bf16[4,128,128]{2,1,0:T(8,128)(2,1)S(1)} %get-tuple-element.36), channel_id=1, source_target_pairs={{0,4},{1,3},{2,6},{3,1},{4,8},{5,7},{6,10},{7,5},{8,12},{9,11},{10... | collective-permute-start | bytes 393224 | tf_op jit(solution)/shard_map/ppermute | solution.py:523
  35.3 6.2 %collective-permute-start.8 = (bf16[2,128,128]{2,1,0:T(8,128)(2,1)S(1)}, bf16[2,128,128]{2,1,0:T(8,128)(2,1)S(1)}, u32[]{:S(2)}, u32[]{:S(2)}) collective-permute-start(bf16[2,128,128]{2,1,0:T(8,128)(2,1)S(1)} %get-tuple-element.38), channel_id=1, source_target_pairs={{0,2},{1,9},{2,0},{4,6},{5,13},{6,4},{7,3},{8,10},{10,8},{11,7},{1... | collective-permute-start | bytes 196616 | tf_op jit(solution)/shard_map/ppermute | solution.py:523
  41.5 1.3 %collective-permute-start.9 = (f32[128,128]{1,0:T(8,128)S(1)}, f32[128,128]{1,0:T(8,128)S(1)}, u32[]{:S(2)}, u32[]{:S(2)}) collective-permute-start(f32[128,128]{1,0:T(8,128)S(1)} %get-tuple-element.40), channel_id=1, source_target_pairs={{0,1},{1,0},{2,3},{3,2},{4,5},{5,4},{6,7},{7,6},{8,9},{9,8},{10,11... | collective-permute-start | bytes 196616 | tf_op jit(solution)/shard_map/ppermute | solution.py:523

commit v10 on v8

--- a/solution.py
+++ b/solution.py
@@ -310,7 +310,8 @@
 
 
 def neighbour_slots():
-    parity = lax.rem(lax.axis_index(AXIS) // Q, 2)
+    me = lax.axis_index(AXIS)
+    parity = lax.rem(me // Q + me, 2)
     return Q * (2 - parity), Q * (1 + parity)
 
 
@@ -514,7 +515,7 @@
 
 def per_device(devices, strain, steering, lag_range, pair_listed, band_used):
     def planes(value, parity):
-        return exchange(value, devices, lambda i: i + (Q if i // Q % 2 == parity else -Q))
+        return exchange(value, devices, lambda i: i + (Q if (i // Q + i) % 2 == parity else -Q))
 
     def flip(value, by):
         return exchange(value, devices, lambda i: i ^ by)

time: 41.8 us -> 42.8 us (1.024)
  starting transfers between devices: 19.3 us -> 23.1 us
  waiting for transfers between devices: 11.3 us -> 8.41 us
    ppermute x10, starting transfers between devices: 19.3 us -> 23.1 us  [exchange(): return lax.ppermute(value, AXIS, pairs)]
    ppermute x10, waiting for transfers between devices: 11.3 us -> 8.41 us  [exchange(): return lax.ppermute(value, AXIS, pairs)]
  transfers between devices with their start and end apart: 10 -> 10, of which waited for: 7 -> 6; matrix products, arithmetic and copies ran while one was open for 0% -> 0% of each run, Pallas kernels for 12% -> 12%
where the time goes in v10:
time: 42.8 us; the launch traced here: 42.5 us
  starting transfers between devices  23.1 us (54%)
  Pallas kernels  10.9 us (25%)
  waiting for transfers between devices  8.41 us (20%)
    ppermute x10, starting transfers between devices, exchange(): return lax.ppermute(value, AXIS, pairs)  23.1 us
    ppermute x10, waiting for transfers between devices, exchange(): return lax.ppermute(value, AXIS, pairs)  8.41 us
    pallas_call x1, Pallas kernels, early_call(): pl.pallas_call(functools.partial(early_kernel, nbands), in_specs=[VMEM_SP...  4.26 us
    pallas_call x1, Pallas kernels, send_call(): pl.pallas_call(send_kernel, in_specs=[HBM_SPEC] * 4, out_specs=[VMEM_SPEC...  2.66 us
    pallas_call x1, Pallas kernels, late_call(): pl.pallas_call(functools.partial(late_kernel, nbands), in_specs=[VMEM_SPE...  2.48 us
    pallas_call x6, Pallas kernels, local_call(): pl.pallas_call(kernel, in_specs=[VMEM_SPEC] * len(values), out_specs=[VME...  1.48 us
  transfers between devices with their start and end apart: 10, of which 6 were waited for; matrix products, arithmetic and copies ran while one was open for 0% of the time, Pallas kernels for 12%

profile of v10, /device:TPU:0, one launch (start us, length us, event | category | flops | bytes accessed | tf_op | source)
XLA Modules:
  0.0 42.5 jit_solution(9412708353010478203)
XLA Ops:
  0.0 2.7 %spectrum_sent.1 = (bf16[2,264,256]{2,1,0:T(8,128)(2,1)S(1)}, bf16[2,2,256,1024]{3,2,1,0:T(8,128)(2,1)S(1)}, bf16[2,1024,256]{2,1,0:T(8,128)(2,1)S(1)}) custom-call(bf16[256,4096]{1,0:T(8,128)(2,1)} %strain.1, f32[2,4,2,32,128]{4,3,2,1,0:T(8,128)} %constant.4.clone.factors, s32[1,8]{1,0:T(1,128)} %listed.1, s32[1,4,8]{2,1,0:T(4,128)} %bitcast.1), custom_call_target="tpu_custom_call" | custom-call | tf_op jit(solution)/shard_map/spectrum_sent/pallas_call | solution.py:195
  2.7 0.8 %collective-permute-start = (bf16[2,264,256]{2,1,0:T(8,128)(2,1)S(1)}, bf16[2,264,256]{2,1,0:T(8,128)(2,1)S(1)}, u32[]{:S(2)}, u32[]{:S(2)}) collective-permute-start(bf16[2,264,256]{2,1,0:T(8,128)(2,1)S(1)} %get-tuple-element.23.swap), channel_id=1, source_target_pairs={{0,1},{1,0},{2,3},{3,2},{4,5},{5,4},{6,7},{7,6},{8,9},{9,8},{10,11... | collective-permute-start | bytes 811016 | tf_op jit(solution)/shard_map/ppermute | solution.py:513
  3.5 0.0 copy-start
  3.5 0.0 copy-start.1
  3.5 0.7 %spectrum_kept.1 = (bf16[2,264,256]{2,1,0:T(8,128)(2,1)S(1)}, bf16[2,264,256]{2,1,0:T(8,128)(2,1)S(1)}) custom-call(bf16[2,264,256]{2,1,0:T(8,128)(2,1)S(1)} %get-tuple-element.23.swap, bf16[2,2,256,1024]{3,2,1,0:T(8,128)(2,1)S(1)} %get-tuple-element.24.folds, bf16[2,1024,256]{2,1,0:T(8,128)(2,1)S(1)} %get-tuple-element.25.table), custom_call_target="tpu_custom_call" | custom-call | tf_op jit(solution)/shard_map/spectrum_kept/pallas_call | solution.py:455
  4.2 0.4 collective-permute-done.swap
  4.7 2.7 %collective-permute-start.1 = (bf16[2,264,256]{2,1,0:T(8,128)(2,1)S(1)}, bf16[2,264,256]{2,1,0:T(8,128)(2,1)S(1)}, u32[]{:S(2)}, u32[]{:S(2)}) collective-permute-start(bf16[2,264,256]{2,1,0:T(8,128)(2,1)S(1)} %get-tuple-element.29), channel_id=1, source_target_pairs={{0,2},{1,3},{2,0},{3,1},{4,6},{5,7},{6,4},{7,5},{8,10},{9,11},{10,... | collective-permute-start | bytes 811016 | tf_op jit(solution)/shard_map/ppermute | solution.py:513
  7.4 0.7 %collective-permute-start.3 = (bf16[2,264,256]{2,1,0:T(8,128)(2,1)S(1)}, bf16[2,264,256]{2,1,0:T(8,128)(2,1)S(1)}, u32[]{:S(2)}, u32[]{:S(2)}) collective-permute-start(bf16[2,264,256]{2,1,0:T(8,128)(2,1)S(1)} %get-tuple-element.28.near), channel_id=1, source_target_pairs={{1,5},{3,7},{4,8},{5,1},{6,10},{7,3},{8,4},{9,13},{10,6},{11,15},{... | collective-permute-start | bytes 811016 | tf_op jit(solution)/shard_map/ppermute | solution.py:513
  8.0 6.3 %collective-permute-start.2 = (bf16[2,264,256]{2,1,0:T(8,128)(2,1)S(1)}, bf16[2,264,256]{2,1,0:T(8,128)(2,1)S(1)}, u32[]{:S(2)}, u32[]{:S(2)}) collective-permute-start(bf16[2,264,256]{2,1,0:T(8,128)(2,1)S(1)} %get-tuple-element.28.near), channel_id=1, source_target_pairs={{0,4},{2,6},{4,0},{5,9},{6,2},{7,11},{8,12},{9,5},{10,14},{11,7},{... | collective-permute-start | bytes 811016 | tf_op jit(solution)/shard_map/ppermute | solution.py:513
  14.3 0.0 collective-permute-done.1.mates
  14.3 0.7 %collective-permute-start.5 = (bf16[2,264,256]{2,1,0:T(8,128)(2,1)S(1)}, bf16[2,264,256]{2,1,0:T(8,128)(2,1)S(1)}, u32[]{:S(2)}, u32[]{:S(2)}) collective-permute-start(bf16[2,264,256]{2,1,0:T(8,128)(2,1)S(1)} %collective-permute-done.1.mates), channel_id=1, source_target_pairs={{1,5},{3,7},{4,8},{5,1},{6,10},{7,3},{8,4},{9,13},{10,6},{11,15},{... | collective-permute-start | bytes 811016 | tf_op jit(solution)/shard_map/ppermute | solution.py:513
  15.0 6.3 %collective-permute-start.4 = (bf16[2,264,256]{2,1,0:T(8,128)(2,1)S(1)}, bf16[2,264,256]{2,1,0:T(8,128)(2,1)S(1)}, u32[]{:S(2)}, u32[]{:S(2)}) collective-permute-start(bf16[2,264,256]{2,1,0:T(8,128)(2,1)S(1)} %collective-permute-done.1.mates), channel_id=1, source_target_pairs={{0,4},{2,6},{4,0},{5,9},{6,2},{7,11},{8,12},{9,5},{10,14},{11,7},{... | collective-permute-start | bytes 811016 | tf_op jit(solution)/shard_map/ppermute | solution.py:513
  21.3 0.0 collective-permute-done.3.odd
  21.3 0.0 collective-permute-done.2.even
  21.4 0.0 copy-done
  21.4 0.0 copy-done.1
  21.4 4.3 %early_pairs.1 = (bf16[12,264,256]{2,1,0:T(8,128)(2,1)S(1)}, f32[8,128,384]{2,1,0:T(8,128)S(1)}, bf16[256,512]{1,0:T(8,128)(2,1)S(1)}) custom-call(bf16[2,264,256]{2,1,0:T(8,128)(2,1)S(1)} %get-tuple-element.28.near, bf16[2,264,256]{2,1,0:T(8,128)(2,1)S(1)} %collective-permute-done.1.mates, bf16[2,264,256]{2,1,0:T(8,128)(2,1)S(1)} %collective-permute-done.2.even, ...), custom_call_target="tpu_custom_call" | custom-call | tf_op jit(solution)/shard_map/early_pairs/pallas_call | solution.py:470
  25.6 0.0 collective-permute-done.5.odd
  25.7 0.1 collective-permute-done.4.even
  25.8 2.5 %late_pairs.1 = (f32[6,128,128]{2,1,0:T(8,128)S(1)}, bf16[6,128,128]{2,1,0:T(8,128)(2,1)S(1)}, bf16[12,264,256]{2,1,0:T(8,128)(2,1)S(1)}, f32[8,128,384]{2,1,0:T(8,128)S(1)}) custom-call(bf16[12,264,256]{2,1,0:T(8,128)(2,1)S(1)} %get-tuple-element.30.spec_in, ...), custom_call_target="tpu_custom_call", output_to_operand_aliasing={{2}: (0, {}), {3}: (1, {})} | custom-call | tf_op jit(solution)/shard_map/late_pairs/pallas_call | solution.py:493
  28.2 0.1 collective-permute-start.6
  28.3 1.4 %collective-permute-done.6.received = bf16[6,128,128]{2,1,0:T(8,128)(2,1)S(1)} collective-permute-done((bf16[6,128,128]{2,1,0:T(8,128)(2,1)S(1)}, bf16[6,128,128]{2,1,0:T(8,128)(2,1)S(1)}, u32[]{:S(2)}, u32[]{:S(2)}) %collective-permute-start.6) | collective-permute-done | bytes 196640 | tf_op jit(solution)/shard_map/ppermute | solution.py:513
  29.8 1.6 %collective-permute-start.7 = (bf16[3,128,128]{2,1,0:T(8,128)(2,1)S(1)}, bf16[3,128,128]{2,1,0:T(8,128)(2,1)S(1)}, u32[]{:S(2)}, u32[]{:S(2)}) collective-permute-start(bf16[3,128,128]{2,1,0:T(8,128)(2,1)S(1)} %get-tuple-element.36), channel_id=1, source_target_pairs={{0,2},{1,3},{2,0},{3,1},{4,6},{5,7},{6,4},{7,5},{8,10},{9,11},{10,... | collective-permute-start | bytes 294920 | tf_op jit(solution)/shard_map/ppermute | solution.py:513
  31.4 3.3 %collective-permute-done.7.received = bf16[3,128,128]{2,1,0:T(8,128)(2,1)S(1)} collective-permute-done((bf16[3,128,128]{2,1,0:T(8,128)(2,1)S(1)}, bf16[3,128,128]{2,1,0:T(8,128)(2,1)S(1)}, u32[]{:S(2)}, u32[]{:S(2)}) %collective-permute-start.7) | collective-permute-done | bytes 98336 | tf_op jit(solution)/shard_map/ppermute | solution.py:513
  34.7 3.9 %collective-permute-start.8 = (bf16[2,128,128]{2,1,0:T(8,128)(2,1)S(1)}, bf16[2,128,128]{2,1,0:T(8,128)(2,1)S(1)}, u32[]{:S(2)}, u32[]{:S(2)}) collective-permute-start(bf16[2,128,128]{2,1,0:T(8,128)(2,1)S(1)} %get-tuple-element.38), channel_id=1, source_target_pairs={{0,4},{1,9},{2,6},{4,8},{5,13},{6,10},{7,3},{8,12},{10,14},{11,7},... | collective-permute-start | bytes 196616 | tf_op jit(solution)/shard_map/ppermute | solution.py:513
  38.7 1.9 %collective-permute-done.8.received = bf16[2,128,128]{2,1,0:T(8,128)(2,1)S(1)} collective-permute-done((bf16[2,128,128]{2,1,0:T(8,128)(2,1)S(1)}, bf16[2,128,128]{2,1,0:T(8,128)(2,1)S(1)}, u32[]{:S(2)}, u32[]{:S(2)}) %collective-permute-start.8) | collective-permute-done | bytes 65568 | tf_op jit(solution)/shard_map/ppermute | solution.py:513
  40.6 0.1 collective-permute-start.9
  40.6 1.2 %collective-permute-done.9.received = f32[128,128]{1,0:T(8,128)S(1)} collective-permute-done((f32[128,128]{1,0:T(8,128)S(1)}, f32[128,128]{1,0:T(8,128)S(1)}, u32[]{:S(2)}, u32[]{:S(2)}) %collective-permute-start.9) | collective-permute-done | bytes 65568 | tf_op jit(solution)/shard_map/ppermute | solution.py:513
  41.9 0.6 %image.1 = f32[128,128]{1,0:T(8,128)} custom-call(f32[128,128]{1,0:T(8,128)S(1)} %get-tuple-element.39.kept, f32[128,128]{1,0:T(8,128)S(1)} %collective-permute-done.9.received), custom_call_target="tpu_custom_call" | custom-call | tf_op jit(solution)/shard_map/image/pallas_call | solution.py:455
  (4 shorter events, 0.1 us)
Async XLA Ops:
  2.7 2.0 %collective-permute-start = (bf16[2,264,256]{2,1,0:T(8,128)(2,1)S(1)}, bf16[2,264,256]{2,1,0:T(8,128)(2,1)S(1)}, u32[]{:S(2)}, u32[]{:S(2)}) collective-permute-start(bf16[2,264,256]{2,1,0:T(8,128)(2,1)S(1)} %get-tuple-element.23.swap), channel_id=1, source_target_pairs={{0,1},{1,0},{2,3},{3,2},{4,5},{5,4},{6,7},{7,6},{8,9},{9,8},{10,11... | collective-permute-start | bytes 811016 | tf_op jit(solution)/shard_map/ppermute | solution.py:513
  3.5 17.9 %copy-start = (bf16[9,512,384]{2,1,0:T(8,128)(2,1)S(1)}, bf16[9,512,384]{2,1,0:T(8,128)(2,1)}, u32[]{:S(2)}) copy-start(bf16[9,512,384]{2,1,0:T(8,128)(2,1)} %lag_range.3) | copy-start | bytes 10616836
  3.5 17.9 %copy-start.1 = (bf16[9,128,256]{2,1,0:T(8,128)(2,1)S(1)}, bf16[9,128,256]{2,1,0:T(8,128)(2,1)}, u32[]{:S(2)}) copy-start(bf16[9,128,256]{2,1,0:T(8,128)(2,1)} %steering.3) | copy-start | bytes 1769476
  4.7 9.7 %collective-permute-start.1 = (bf16[2,264,256]{2,1,0:T(8,128)(2,1)S(1)}, bf16[2,264,256]{2,1,0:T(8,128)(2,1)S(1)}, u32[]{:S(2)}, u32[]{:S(2)}) collective-permute-start(bf16[2,264,256]{2,1,0:T(8,128)(2,1)S(1)} %get-tuple-element.29), channel_id=1, source_target_pairs={{0,2},{1,3},{2,0},{3,1},{4,6},{5,7},{6,4},{7,5},{8,10},{9,11},{10,... | collective-permute-start | bytes 811016 | tf_op jit(solution)/shard_map/ppermute | solution.py:513
  7.4 14.0 %collective-permute-start.3 = (bf16[2,264,256]{2,1,0:T(8,128)(2,1)S(1)}, bf16[2,264,256]{2,1,0:T(8,128)(2,1)S(1)}, u32[]{:S(2)}, u32[]{:S(2)}) collective-permute-start(bf16[2,264,256]{2,1,0:T(8,128)(2,1)S(1)} %get-tuple-element.28.near), channel_id=1, source_target_pairs={{1,5},{3,7},{4,8},{5,1},{6,10},{7,3},{8,4},{9,13},{10,6},{11,15},{... | collective-permute-start | bytes 811016 | tf_op jit(solution)/shard_map/ppermute | solution.py:513
  8.0 13.3 %collective-permute-start.2 = (bf16[2,264,256]{2,1,0:T(8,128)(2,1)S(1)}, bf16[2,264,256]{2,1,0:T(8,128)(2,1)S(1)}, u32[]{:S(2)}, u32[]{:S(2)}) collective-permute-start(bf16[2,264,256]{2,1,0:T(8,128)(2,1)S(1)} %get-tuple-element.28.near), channel_id=1, source_target_pairs={{0,4},{2,6},{4,0},{5,9},{6,2},{7,11},{8,12},{9,5},{10,14},{11,7},{... | collective-permute-start | bytes 811016 | tf_op jit(solution)/shard_map/ppermute | solution.py:513
  14.3 11.3 %collective-permute-start.5 = (bf16[2,264,256]{2,1,0:T(8,128)(2,1)S(1)}, bf16[2,264,256]{2,1,0:T(8,128)(2,1)S(1)}, u32[]{:S(2)}, u32[]{:S(2)}) collective-permute-start(bf16[2,264,256]{2,1,0:T(8,128)(2,1)S(1)} %collective-permute-done.1.mates), channel_id=1, source_target_pairs={{1,5},{3,7},{4,8},{5,1},{6,10},{7,3},{8,4},{9,13},{10,6},{11,15},{... | collective-permute-start | bytes 811016 | tf_op jit(solution)/shard_map/ppermute | solution.py:513
  15.0 10.7 %collective-permute-start.4 = (bf16[2,264,256]{2,1,0:T(8,128)(2,1)S(1)}, bf16[2,264,256]{2,1,0:T(8,128)(2,1)S(1)}, u32[]{:S(2)}, u32[]{:S(2)}) collective-permute-start(bf16[2,264,256]{2,1,0:T(8,128)(2,1)S(1)} %collective-permute-done.1.mates), channel_id=1, source_target_pairs={{0,4},{2,6},{4,0},{5,9},{6,2},{7,11},{8,12},{9,5},{10,14},{11,7},{... | collective-permute-start | bytes 811016 | tf_op jit(solution)/shard_map/ppermute | solution.py:513
  28.2 1.5 %collective-permute-start.6 = (bf16[6,128,128]{2,1,0:T(8,128)(2,1)S(1)}, bf16[6,128,128]{2,1,0:T(8,128)(2,1)S(1)}, u32[]{:S(2)}, u32[]{:S(2)}) collective-permute-start(bf16[6,128,128]{2,1,0:T(8,128)(2,1)S(1)} %get-tuple-element.34), channel_id=1, source_target_pairs={{0,1},{1,0},{2,3},{3,2},{4,5},{5,4},{6,7},{7,6},{8,9},{9,8},{10,11... | collective-permute-start | bytes 589832 | tf_op jit(solution)/shard_map/ppermute | solution.py:513
  29.8 4.9 %collective-permute-start.7 = (bf16[3,128,128]{2,1,0:T(8,128)(2,1)S(1)}, bf16[3,128,128]{2,1,0:T(8,128)(2,1)S(1)}, u32[]{:S(2)}, u32[]{:S(2)}) collective-permute-start(bf16[3,128,128]{2,1,0:T(8,128)(2,1)S(1)} %get-tuple-element.36), channel_id=1, source_target_pairs={{0,2},{1,3},{2,0},{3,1},{4,6},{5,7},{6,4},{7,5},{8,10},{9,11},{10,... | collective-permute-start | bytes 294920 | tf_op jit(solution)/shard_map/ppermute | solution.py:513
  34.7 5.8 %collective-permute-start.8 = (bf16[2,128,128]{2,1,0:T(8,128)(2,1)S(1)}, bf16[2,128,128]{2,1,0:T(8,128)(2,1)S(1)}, u32[]{:S(2)}, u32[]{:S(2)}) collective-permute-start(bf16[2,128,128]{2,1,0:T(8,128)(2,1)S(1)} %get-tuple-element.38), channel_id=1, source_target_pairs={{0,4},{1,9},{2,6},{4,8},{5,13},{6,10},{7,3},{8,12},{10,14},{11,7},... | collective-permute-start | bytes 196616 | tf_op jit(solution)/shard_map/ppermute | solution.py:513
  40.6 1.3 %collective-permute-start.9 = (f32[128,128]{1,0:T(8,128)S(1)}, f32[128,128]{1,0:T(8,128)S(1)}, u32[]{:S(2)}, u32[]{:S(2)}) collective-permute-start(f32[128,128]{1,0:T(8,128)S(1)} %get-tuple-element.40), channel_id=1, source_target_pairs={{0,1},{1,0},{2,3},{3,2},{4,5},{5,4},{6,7},{7,6},{8,9},{9,8},{10,11... | collective-permute-start | bytes 196616 | tf_op jit(solution)/shard_map/ppermute | solution.py:513

commit v11 on v8

--- a/solution.py
+++ b/solution.py
@@ -254,25 +254,35 @@
 def late_units(me, rounds):
     base = 2 * (1 - me // 2)
 
-    def low(i, e):
-        return make_unit(me, rounds, (0, i), (1, base + e))
-
     def mid(i, j):
         return make_unit(me, rounds, (1, i), (1, j))
 
-    twins = [[low(i, 0), low(i + 1, 1)] for i in range(Q - 1)]
-    twins.append([mid(base, base), mid(base + 1, base + 1)])
+    twins = [[mid(base, base), mid(base + 1, base + 1)]]
     twins.append([mid(0, 2), mid(1, 3)])
     twins.append([mid(1, 2), mid(base, base + 1)])
-    return twins, [low(Q - 1, 0), low(0, 1), mid(0, 3)]
-
-
-def run_units(plan, spec, mask, steering, inv, lag_range, window):
-    channels, angles = steering.shape[2], steering.shape[1]
-    cols = spec.shape[2]
-    half = cols // 2
-    twins, rest = plan
-    units = [unit for pair in twins for unit in pair] + rest
+    return twins, [mid(0, 3)]
+
+
+def mask_row(mask, target, row):
+    return jnp.concatenate([mask[target, h, pl.ds(row, 1), :] for h in range(mask.shape[1])], axis=1)
+
+
+def low_units(me, rounds):
+    base = 2 * (1 - me // 2)
+    return [
+        make_unit(me, rounds, (0, i), (1, base + e)) for i in range(Q) for e in range(2)
+    ]
+
+
+def prepare_maps(units, mask, inv, lag_range, maps):
+    for n, (_, _, d, _, target, row) in enumerate(units):
+        weight = mask_row(mask, target, row).astype(jnp.bfloat16)
+        maps[n] = dot(inv[...] * weight, lag_range[d]).astype(jnp.bfloat16)
+
+
+def steered(units, spec, steering):
+    channels = steering.shape[2]
+    half = spec.shape[2] // 2
     beams = []
     for target, source, d, _, _, _ in units:
         near_re, near_im = spec[target, :channels, :half], spec[target, :channels, half:]
@@ -281,12 +291,19 @@
         imag = near_im * far_re - near_re * far_im
         cross = jnp.concatenate([real, imag], axis=1)
         beams.append(dot(steering[d], cross).astype(jnp.bfloat16))
-    beams = dot(jnp.concatenate(beams, axis=0), inv[...])
+    return beams
+
+
+def run_units(plan, spec, mask, steering, inv, lag_range, window, mapped=(), maps=None):
+    angles = steering.shape[1]
+    twins, rest = plan
+    units = [unit for pair in twins for unit in pair] + rest
+    beams = steered(units + list(mapped), spec, steering)
+    mapped_beams = beams[len(units) :]
+    beams = dot(jnp.concatenate(beams[: len(units)], axis=0), inv[...])
     masked = []
     for u, (_, _, _, _, target, row) in enumerate(units):
-        weight = jnp.concatenate(
-            [mask[target, h, pl.ds(row, 1), :] for h in range(L // cols)], axis=1
-        )
+        weight = mask_row(mask, target, row)
         masked.append((beams[u * angles : (u + 1) * angles, :] * weight).astype(jnp.bfloat16))
     for u in range(0, 2 * len(twins), 2):
         part = dot(jnp.concatenate(masked[u : u + 2], axis=0), lag_range[units[u][2]])
@@ -294,6 +311,9 @@
         window[units[u + 1][3]] += part[angles:]
     for u in range(2 * len(twins), len(units)):
         window[units[u][3]] += dot(masked[u], lag_range[units[u][2]])
+    for n in range(0, len(mapped), 2):
+        both = jnp.concatenate(mapped_beams[n : n + 2], axis=1)
+        window[mapped[n][3]] += dot(both, maps[n : n + 2].reshape(both.shape[1], -1))
 
 
 def fill_mask(mask, entry, spec, slot, channels, nbands):
@@ -316,7 +336,7 @@
 
 def early_kernel(
     nbands, near, mates, even, odd, inv_all, steering, lag_range,
-    spec, window, inv, mask, sem,
+    spec, window, inv, maps, mask, sem,
 ):
     me = lax.rem(lax.axis_index(AXIS), Q)
     copy = pltpu.make_async_copy(inv_all.at[me], inv, sem)
@@ -335,10 +355,11 @@
     copy.wait()
     plan = early_units(me, steering.shape[0] - 1)
     run_units(plan, spec, mask, steering, inv, lag_range, window)
+    prepare_maps(low_units(me, steering.shape[0] - 1), mask, inv, lag_range, maps)
 
 
 def late_kernel(
-    nbands, spec_in, window_in, even, odd, inv, steering, lag_range,
+    nbands, spec_in, window_in, even, odd, inv, maps, steering, lag_range,
     keep, send, spec, window, mask,
 ):
     me = lax.rem(lax.axis_index(AXIS), Q)
@@ -350,7 +371,8 @@
         fill_mask(mask, p, spec, p, channels, nbands)
         fill_mask(mask, Q + p, spec, 2 * Q + p, channels, nbands)
     plan = late_units(me, steering.shape[0] - 1)
-    run_units(plan, spec, mask, steering, inv, lag_range, window)
+    mapped = low_units(me, steering.shape[0] - 1)
+    run_units(plan, spec, mask, steering, inv, lag_range, window, mapped, maps)
 
     width = window.shape[2] // 3
 
@@ -469,11 +491,12 @@
     return pl.pallas_call(
         functools.partial(early_kernel, nbands),
         in_specs=[VMEM_SPEC] * 4 + [HBM_SPEC] + [VMEM_SPEC] * 2,
-        out_specs=[VMEM_SPEC] * 3,
+        out_specs=[VMEM_SPEC] * 4,
         out_shape=[
             pltpu.VMEM((3 * Q, rows, cols), jnp.bfloat16),
             pltpu.VMEM((2 * Q, angles, group), jnp.float32),
             pltpu.VMEM(inv.shape[1:], inv.dtype),
+            pltpu.VMEM((2 * Q, cols, group), jnp.bfloat16),
         ],
         scratch_shapes=[
             pltpu.VMEM((2 * Q, L // cols, 2 * rounds, cols), jnp.float32),
@@ -484,14 +507,14 @@
     )(*near_vmem(near, mates, even, odd), in_hbm(inv), *near_vmem(steering, lag_range))
 
 
-def late_call(nbands, spec, window, even, odd, inv, steering, lag_range):
+def late_call(nbands, spec, window, even, odd, inv, maps, steering, lag_range):
     cols = spec.shape[2]
     angles, group = steering.shape[1], lag_range.shape[2]
     rounds = steering.shape[0] - 1
     pieces = (Q + 2, angles, group // 3)
     return pl.pallas_call(
         functools.partial(late_kernel, nbands),
-        in_specs=[VMEM_SPEC] * 7,
+        in_specs=[VMEM_SPEC] * 8,
         out_specs=[VMEM_SPEC] * 4,
         out_shape=[
             pltpu.VMEM(pieces, jnp.float32),
@@ -503,7 +526,7 @@
         scratch_shapes=[pltpu.VMEM((2 * Q, L // cols, 2 * rounds, cols), jnp.float32)],
         compiler_params=pltpu.CompilerParams(vmem_limit_bytes=LIMIT),
         name="late_pairs",
-    )(*near_vmem(spec, window, even, odd, inv, steering, lag_range))[:2]
+    )(*near_vmem(spec, window, even, odd, inv, maps, steering, lag_range))[:2]
 
 
 def exchange(value, devices, target):
@@ -530,11 +553,11 @@
     far_odd, far_even = planes(mates, 1), planes(mates, 0)
     nbands = band_used.shape[2]
     inv = jnp.asarray(inverse_table(strain.shape[1]))
-    spec, window, inv = early_call(
+    spec, window, inv, maps = early_call(
         nbands, near, mates, near_even, near_odd, inv, steering, lag_range
     )
     kept, send = late_call(
-        nbands, spec, window, far_even, far_odd, inv, steering, lag_range
+        nbands, spec, window, far_even, far_odd, inv, maps, steering, lag_range
     )
 
     def pieces(count, dtype):

time: 41.8 us -> 41.3 us (0.988)
  waiting for transfers between devices: 11.3 us -> 10.2 us
  Pallas kernels: 10.9 us -> 11.4 us
    pallas_call x1, Pallas kernels: 4.26 us -> 5.34 us  [early_call(): pl.pallas_call(functools.partial(early_kernel, nbands), in_specs=[VMEM_SP...]
    ppermute x10, waiting for transfers between devices: 11.3 us -> 10.2 us  [exchange(): return lax.ppermute(value, AXIS, pairs)]
    pallas_call x1, Pallas kernels: 2.47 us -> 1.93 us  [late_call(): pl.pallas_call(functools.partial(late_kernel, nbands), in_specs=[VMEM_SPE...]
  transfers between devices with their start and end apart: 10 -> 10, of which waited for: 7 -> 7; matrix products, arithmetic and copies ran while one was open for 0% -> 0% of each run, Pallas kernels for 12% -> 15%
where the time goes in v11:
time: 41.3 us; the launch traced here: 41.1 us
  starting transfers between devices  19.3 us (47%)
  Pallas kernels  11.4 us (28%)
  waiting for transfers between devices  10.2 us (25%)
    ppermute x10, starting transfers between devices, exchange(): return lax.ppermute(value, AXIS, pairs)  19.3 us
    ppermute x10, waiting for transfers between devices, exchange(): return lax.ppermute(value, AXIS, pairs)  10.2 us
    pallas_call x1, Pallas kernels, early_call(): pl.pallas_call(functools.partial(early_kernel, nbands), in_specs=[VMEM_SP...  5.34 us
    pallas_call x1, Pallas kernels, send_call(): pl.pallas_call(send_kernel, in_specs=[HBM_SPEC] * 4, out_specs=[VMEM_SPEC...  2.66 us
    pallas_call x1, Pallas kernels, late_call(): pl.pallas_call(functools.partial(late_kernel, nbands), in_specs=[VMEM_SPE...  1.93 us
    pallas_call x6, Pallas kernels, local_call(): pl.pallas_call(kernel, in_specs=[VMEM_SPEC] * len(values), out_specs=[VME...  1.48 us
  transfers between devices with their start and end apart: 10, of which 7 were waited for; matrix products, arithmetic and copies ran while one was open for 0% of the time, Pallas kernels for 15%

profile of v11, /device:TPU:0, one launch (start us, length us, event | category | flops | bytes accessed | tf_op | source)
XLA Modules:
  0.0 41.1 jit_solution(14808184924779880201)
XLA Ops:
  0.0 2.7 %spectrum_sent.1 = (bf16[2,264,256]{2,1,0:T(8,128)(2,1)S(1)}, bf16[2,2,256,1024]{3,2,1,0:T(8,128)(2,1)S(1)}, bf16[2,1024,256]{2,1,0:T(8,128)(2,1)S(1)}) custom-call(bf16[256,4096]{1,0:T(8,128)(2,1)} %strain.1, f32[2,4,2,32,128]{4,3,2,1,0:T(8,128)} %constant.4.clone.factors, s32[1,8]{1,0:T(1,128)} %listed.1, s32[1,4,8]{2,1,0:T(4,128)} %bitcast.1), custom_call_target="tpu_custom_call" | custom-call | tf_op jit(solution)/shard_map/spectrum_sent/pallas_call | solution.py:195
  2.7 0.8 %collective-permute-start = (bf16[2,264,256]{2,1,0:T(8,128)(2,1)S(1)}, bf16[2,264,256]{2,1,0:T(8,128)(2,1)S(1)}, u32[]{:S(2)}, u32[]{:S(2)}) collective-permute-start(bf16[2,264,256]{2,1,0:T(8,128)(2,1)S(1)} %get-tuple-element.24.swap), channel_id=1, source_target_pairs={{0,1},{1,0},{2,3},{3,2},{4,5},{5,4},{6,7},{7,6},{8,9},{9,8},{10,11... | collective-permute-start | bytes 811016 | tf_op jit(solution)/shard_map/ppermute | solution.py:535
  3.5 0.0 copy-start
  3.5 0.0 copy-start.1
  3.5 0.7 %spectrum_kept.1 = (bf16[2,264,256]{2,1,0:T(8,128)(2,1)S(1)}, bf16[2,264,256]{2,1,0:T(8,128)(2,1)S(1)}) custom-call(bf16[2,264,256]{2,1,0:T(8,128)(2,1)S(1)} %get-tuple-element.24.swap, bf16[2,2,256,1024]{3,2,1,0:T(8,128)(2,1)S(1)} %get-tuple-element.25.folds, bf16[2,1024,256]{2,1,0:T(8,128)(2,1)S(1)} %get-tuple-element.26.table), custom_call_target="tpu_custom_call" | custom-call | tf_op jit(solution)/shard_map/spectrum_kept/pallas_call | solution.py:476
  4.2 0.4 %collective-permute-done.swap = bf16[2,264,256]{2,1,0:T(8,128)(2,1)S(1)} collective-permute-done((bf16[2,264,256]{2,1,0:T(8,128)(2,1)S(1)}, bf16[2,264,256]{2,1,0:T(8,128)(2,1)S(1)}, u32[]{:S(2)}, u32[]{:S(2)}) %collective-permute-start) | collective-permute-done | bytes 270368 | tf_op jit(solution)/shard_map/ppermute | solution.py:535
  4.7 2.7 %collective-permute-start.1 = (bf16[2,264,256]{2,1,0:T(8,128)(2,1)S(1)}, bf16[2,264,256]{2,1,0:T(8,128)(2,1)S(1)}, u32[]{:S(2)}, u32[]{:S(2)}) collective-permute-start(bf16[2,264,256]{2,1,0:T(8,128)(2,1)S(1)} %get-tuple-element.30), channel_id=1, source_target_pairs={{0,2},{1,3},{2,0},{3,1},{4,6},{5,7},{6,4},{7,5},{8,10},{9,11},{10,... | collective-permute-start | bytes 811016 | tf_op jit(solution)/shard_map/ppermute | solution.py:535
  7.4 0.7 %collective-permute-start.3 = (bf16[2,264,256]{2,1,0:T(8,128)(2,1)S(1)}, bf16[2,264,256]{2,1,0:T(8,128)(2,1)S(1)}, u32[]{:S(2)}, u32[]{:S(2)}) collective-permute-start(bf16[2,264,256]{2,1,0:T(8,128)(2,1)S(1)} %get-tuple-element.29.near), channel_id=1, source_target_pairs={{4,8},{5,9},{6,10},{7,11},{8,4},{9,5},{10,6},{11,7},{20,24},{21,25... | collective-permute-start | bytes 811016 | tf_op jit(solution)/shard_map/ppermute | solution.py:535
  8.0 4.4 %collective-permute-start.2 = (bf16[2,264,256]{2,1,0:T(8,128)(2,1)S(1)}, bf16[2,264,256]{2,1,0:T(8,128)(2,1)S(1)}, u32[]{:S(2)}, u32[]{:S(2)}) collective-permute-start(bf16[2,264,256]{2,1,0:T(8,128)(2,1)S(1)} %get-tuple-element.29.near), channel_id=1, source_target_pairs={{0,4},{1,5},{2,6},{3,7},{4,0},{5,1},{6,2},{7,3},{8,12},{9,13},{10,... | collective-permute-start | bytes 811016 | tf_op jit(solution)/shard_map/ppermute | solution.py:535
  12.5 1.7 %collective-permute-done.1.mates = bf16[2,264,256]{2,1,0:T(8,128)(2,1)S(1)} collective-permute-done((bf16[2,264,256]{2,1,0:T(8,128)(2,1)S(1)}, bf16[2,264,256]{2,1,0:T(8,128)(2,1)S(1)}, u32[]{:S(2)}, u32[]{:S(2)}) %collective-permute-start.1) | collective-permute-done | bytes 270368 | tf_op jit(solution)/shard_map/ppermute | solution.py:535
  14.1 0.7 %collective-permute-start.5 = (bf16[2,264,256]{2,1,0:T(8,128)(2,1)S(1)}, bf16[2,264,256]{2,1,0:T(8,128)(2,1)S(1)}, u32[]{:S(2)}, u32[]{:S(2)}) collective-permute-start(bf16[2,264,256]{2,1,0:T(8,128)(2,1)S(1)} %collective-permute-done.1.mates), channel_id=1, source_target_pairs={{4,8},{5,9},{6,10},{7,11},{8,4},{9,5},{10,6},{11,7},{20,24},{21,25... | collective-permute-start | bytes 811016 | tf_op jit(solution)/shard_map/ppermute | solution.py:535
  14.8 4.7 %collective-permute-start.4 = (bf16[2,264,256]{2,1,0:T(8,128)(2,1)S(1)}, bf16[2,264,256]{2,1,0:T(8,128)(2,1)S(1)}, u32[]{:S(2)}, u32[]{:S(2)}) collective-permute-start(bf16[2,264,256]{2,1,0:T(8,128)(2,1)S(1)} %collective-permute-done.1.mates), channel_id=1, source_target_pairs={{0,4},{1,5},{2,6},{3,7},{4,0},{5,1},{6,2},{7,3},{8,12},{9,13},{10,... | collective-permute-start | bytes 811016 | tf_op jit(solution)/shard_map/ppermute | solution.py:535
  19.5 0.0 collective-permute-done.3.odd
  19.5 0.0 collective-permute-done.2.even
  19.5 0.0 copy-done
  19.5 0.0 copy-done.1
  19.5 5.3 %early_pairs.1 = (bf16[12,264,256]{2,1,0:T(8,128)(2,1)S(1)}, f32[8,128,384]{2,1,0:T(8,128)S(1)}, bf16[256,512]{1,0:T(8,128)(2,1)S(1)}, bf16[8,256,384]{2,1,0:T(8,128)(2,1)S(1)}) custom-call(bf16[2,264,256]{2,1,0:T(8,128)(2,1)S(1)} %get-tuple-element.29.near, bf16[2,264,256]{2,1,0:T(8,128)(2,1)S(1)} %collective-permute-done.1.mates, ...), custom_call_target="tpu_custom_call" | custom-call | tf_op jit(solution)/shard_map/early_pairs/pallas_call | solution.py:491
  24.9 0.0 collective-permute-done.5.odd
  24.9 0.3 collective-permute-done.4.even
  25.1 1.9 %late_pairs.1 = (f32[6,128,128]{2,1,0:T(8,128)S(1)}, bf16[6,128,128]{2,1,0:T(8,128)(2,1)S(1)}, bf16[12,264,256]{2,1,0:T(8,128)(2,1)S(1)}, f32[8,128,384]{2,1,0:T(8,128)S(1)}) custom-call(bf16[12,264,256]{2,1,0:T(8,128)(2,1)S(1)} %get-tuple-element.31.spec_in, ...), custom_call_target="tpu_custom_call", output_to_operand_aliasing={{2}: (0, {}), {3}: (1, {})} | custom-call | tf_op jit(solution)/shard_map/late_pairs/pallas_call | solution.py:515
  27.1 0.1 collective-permute-start.6
  27.2 1.4 %collective-permute-done.6.received = bf16[6,128,128]{2,1,0:T(8,128)(2,1)S(1)} collective-permute-done((bf16[6,128,128]{2,1,0:T(8,128)(2,1)S(1)}, bf16[6,128,128]{2,1,0:T(8,128)(2,1)S(1)}, u32[]{:S(2)}, u32[]{:S(2)}) %collective-permute-start.6) | collective-permute-done | bytes 196640 | tf_op jit(solution)/shard_map/ppermute | solution.py:535
  28.6 1.6 %collective-permute-start.7 = (bf16[3,128,128]{2,1,0:T(8,128)(2,1)S(1)}, bf16[3,128,128]{2,1,0:T(8,128)(2,1)S(1)}, u32[]{:S(2)}, u32[]{:S(2)}) collective-permute-start(bf16[3,128,128]{2,1,0:T(8,128)(2,1)S(1)} %get-tuple-element.38), channel_id=1, source_target_pairs={{0,2},{1,3},{2,0},{3,1},{4,6},{5,7},{6,4},{7,5},{8,10},{9,11},{10,... | collective-permute-start | bytes 294920 | tf_op jit(solution)/shard_map/ppermute | solution.py:535
  30.2 3.3 %collective-permute-done.7.received = bf16[3,128,128]{2,1,0:T(8,128)(2,1)S(1)} collective-permute-done((bf16[3,128,128]{2,1,0:T(8,128)(2,1)S(1)}, bf16[3,128,128]{2,1,0:T(8,128)(2,1)S(1)}, u32[]{:S(2)}, u32[]{:S(2)}) %collective-permute-start.7) | collective-permute-done | bytes 98336 | tf_op jit(solution)/shard_map/ppermute | solution.py:535
  33.6 3.6 %collective-permute-start.8 = (bf16[2,128,128]{2,1,0:T(8,128)(2,1)S(1)}, bf16[2,128,128]{2,1,0:T(8,128)(2,1)S(1)}, u32[]{:S(2)}, u32[]{:S(2)}) collective-permute-start(bf16[2,128,128]{2,1,0:T(8,128)(2,1)S(1)} %get-tuple-element.40), channel_id=1, source_target_pairs={{0,4},{1,9},{2,6},{4,8},{5,13},{6,10},{7,3},{8,12},{10,14},{11,7},... | collective-permute-start | bytes 196616 | tf_op jit(solution)/shard_map/ppermute | solution.py:535
  37.2 1.9 %collective-permute-done.8.received = bf16[2,128,128]{2,1,0:T(8,128)(2,1)S(1)} collective-permute-done((bf16[2,128,128]{2,1,0:T(8,128)(2,1)S(1)}, bf16[2,128,128]{2,1,0:T(8,128)(2,1)S(1)}, u32[]{:S(2)}, u32[]{:S(2)}) %collective-permute-start.8) | collective-permute-done | bytes 65568 | tf_op jit(solution)/shard_map/ppermute | solution.py:535
  39.1 0.1 collective-permute-start.9
  39.2 1.2 %collective-permute-done.9.received = f32[128,128]{1,0:T(8,128)S(1)} collective-permute-done((f32[128,128]{1,0:T(8,128)S(1)}, f32[128,128]{1,0:T(8,128)S(1)}, u32[]{:S(2)}, u32[]{:S(2)}) %collective-permute-start.9) | collective-permute-done | bytes 65568 | tf_op jit(solution)/shard_map/ppermute | solution.py:535
  40.4 0.6 %image.1 = f32[128,128]{1,0:T(8,128)} custom-call(f32[128,128]{1,0:T(8,128)S(1)} %get-tuple-element.41.kept, f32[128,128]{1,0:T(8,128)S(1)} %collective-permute-done.9.received), custom_call_target="tpu_custom_call" | custom-call | tf_op jit(solution)/shard_map/image/pallas_call | solution.py:476
  (4 shorter events, 0.1 us)
Async XLA Ops:
  2.7 2.0 %collective-permute-start = (bf16[2,264,256]{2,1,0:T(8,128)(2,1)S(1)}, bf16[2,264,256]{2,1,0:T(8,128)(2,1)S(1)}, u32[]{:S(2)}, u32[]{:S(2)}) collective-permute-start(bf16[2,264,256]{2,1,0:T(8,128)(2,1)S(1)} %get-tuple-element.24.swap), channel_id=1, source_target_pairs={{0,1},{1,0},{2,3},{3,2},{4,5},{5,4},{6,7},{7,6},{8,9},{9,8},{10,11... | collective-permute-start | bytes 811016 | tf_op jit(solution)/shard_map/ppermute | solution.py:535
  3.5 16.0 %copy-start = (bf16[9,512,384]{2,1,0:T(8,128)(2,1)S(1)}, bf16[9,512,384]{2,1,0:T(8,128)(2,1)}, u32[]{:S(2)}) copy-start(bf16[9,512,384]{2,1,0:T(8,128)(2,1)} %lag_range.3) | copy-start | bytes 10616836
  3.5 16.0 %copy-start.1 = (bf16[9,128,256]{2,1,0:T(8,128)(2,1)S(1)}, bf16[9,128,256]{2,1,0:T(8,128)(2,1)}, u32[]{:S(2)}) copy-start(bf16[9,128,256]{2,1,0:T(8,128)(2,1)} %steering.3) | copy-start | bytes 1769476
  4.7 9.5 %collective-permute-start.1 = (bf16[2,264,256]{2,1,0:T(8,128)(2,1)S(1)}, bf16[2,264,256]{2,1,0:T(8,128)(2,1)S(1)}, u32[]{:S(2)}, u32[]{:S(2)}) collective-permute-start(bf16[2,264,256]{2,1,0:T(8,128)(2,1)S(1)} %get-tuple-element.30), channel_id=1, source_target_pairs={{0,2},{1,3},{2,0},{3,1},{4,6},{5,7},{6,4},{7,5},{8,10},{9,11},{10,... | collective-permute-start | bytes 811016 | tf_op jit(solution)/shard_map/ppermute | solution.py:535
  7.4 12.1 %collective-permute-start.3 = (bf16[2,264,256]{2,1,0:T(8,128)(2,1)S(1)}, bf16[2,264,256]{2,1,0:T(8,128)(2,1)S(1)}, u32[]{:S(2)}, u32[]{:S(2)}) collective-permute-start(bf16[2,264,256]{2,1,0:T(8,128)(2,1)S(1)} %get-tuple-element.29.near), channel_id=1, source_target_pairs={{4,8},{5,9},{6,10},{7,11},{8,4},{9,5},{10,6},{11,7},{20,24},{21,25... | collective-permute-start | bytes 811016 | tf_op jit(solution)/shard_map/ppermute | solution.py:535
  8.0 11.5 %collective-permute-start.2 = (bf16[2,264,256]{2,1,0:T(8,128)(2,1)S(1)}, bf16[2,264,256]{2,1,0:T(8,128)(2,1)S(1)}, u32[]{:S(2)}, u32[]{:S(2)}) collective-permute-start(bf16[2,264,256]{2,1,0:T(8,128)(2,1)S(1)} %get-tuple-element.29.near), channel_id=1, source_target_pairs={{0,4},{1,5},{2,6},{3,7},{4,0},{5,1},{6,2},{7,3},{8,12},{9,13},{10,... | collective-permute-start | bytes 811016 | tf_op jit(solution)/shard_map/ppermute | solution.py:535
  14.1 10.7 %collective-permute-start.5 = (bf16[2,264,256]{2,1,0:T(8,128)(2,1)S(1)}, bf16[2,264,256]{2,1,0:T(8,128)(2,1)S(1)}, u32[]{:S(2)}, u32[]{:S(2)}) collective-permute-start(bf16[2,264,256]{2,1,0:T(8,128)(2,1)S(1)} %collective-permute-done.1.mates), channel_id=1, source_target_pairs={{4,8},{5,9},{6,10},{7,11},{8,4},{9,5},{10,6},{11,7},{20,24},{21,25... | collective-permute-start | bytes 811016 | tf_op jit(solution)/shard_map/ppermute | solution.py:535
  14.8 10.3 %collective-permute-start.4 = (bf16[2,264,256]{2,1,0:T(8,128)(2,1)S(1)}, bf16[2,264,256]{2,1,0:T(8,128)(2,1)S(1)}, u32[]{:S(2)}, u32[]{:S(2)}) collective-permute-start(bf16[2,264,256]{2,1,0:T(8,128)(2,1)S(1)} %collective-permute-done.1.mates), channel_id=1, source_target_pairs={{0,4},{1,5},{2,6},{3,7},{4,0},{5,1},{6,2},{7,3},{8,12},{9,13},{10,... | collective-permute-start | bytes 811016 | tf_op jit(solution)/shard_map/ppermute | solution.py:535
  27.1 1.5 %collective-permute-start.6 = (bf16[6,128,128]{2,1,0:T(8,128)(2,1)S(1)}, bf16[6,128,128]{2,1,0:T(8,128)(2,1)S(1)}, u32[]{:S(2)}, u32[]{:S(2)}) collective-permute-start(bf16[6,128,128]{2,1,0:T(8,128)(2,1)S(1)} %get-tuple-element.36), channel_id=1, source_target_pairs={{0,1},{1,0},{2,3},{3,2},{4,5},{5,4},{6,7},{7,6},{8,9},{9,8},{10,11... | collective-permute-start | bytes 589832 | tf_op jit(solution)/shard_map/ppermute | solution.py:535
  28.6 4.9 %collective-permute-start.7 = (bf16[3,128,128]{2,1,0:T(8,128)(2,1)S(1)}, bf16[3,128,128]{2,1,0:T(8,128)(2,1)S(1)}, u32[]{:S(2)}, u32[]{:S(2)}) collective-permute-start(bf16[3,128,128]{2,1,0:T(8,128)(2,1)S(1)} %get-tuple-element.38), channel_id=1, source_target_pairs={{0,2},{1,3},{2,0},{3,1},{4,6},{5,7},{6,4},{7,5},{8,10},{9,11},{10,... | collective-permute-start | bytes 294920 | tf_op jit(solution)/shard_map/ppermute | solution.py:535
  33.6 5.5 %collective-permute-start.8 = (bf16[2,128,128]{2,1,0:T(8,128)(2,1)S(1)}, bf16[2,128,128]{2,1,0:T(8,128)(2,1)S(1)}, u32[]{:S(2)}, u32[]{:S(2)}) collective-permute-start(bf16[2,128,128]{2,1,0:T(8,128)(2,1)S(1)} %get-tuple-element.40), channel_id=1, source_target_pairs={{0,4},{1,9},{2,6},{4,8},{5,13},{6,10},{7,3},{8,12},{10,14},{11,7},... | collective-permute-start | bytes 196616 | tf_op jit(solution)/shard_map/ppermute | solution.py:535
  39.1 1.3 %collective-permute-start.9 = (f32[128,128]{1,0:T(8,128)S(1)}, f32[128,128]{1,0:T(8,128)S(1)}, u32[]{:S(2)}, u32[]{:S(2)}) collective-permute-start(f32[128,128]{1,0:T(8,128)S(1)} %get-tuple-element.42), channel_id=1, source_target_pairs={{0,1},{1,0},{2,3},{3,2},{4,5},{5,4},{6,7},{7,6},{8,9},{9,8},{10,11... | collective-permute-start | bytes 196616 | tf_op jit(solution)/shard_map/ppermute | solution.py:535

commit v12 on v11

--- a/solution.py
+++ b/solution.py
@@ -164,7 +164,7 @@
     core, side = lax.rem(me, 2), me // 2
     channels = folds.shape[2]
     near[0, channels:, :] = swap[0, channels:, :]
-    mates[0, channels:, :] = swap[0, channels:, :]
+    mates[channels:, :] = swap[0, channels:, :]
 
     def store(values):
         for n, value in enumerate(values):
@@ -176,7 +176,7 @@
 
             @pl.when(side != n)
             def _():
-                mates[0, :channels, :] = value
+                mates[:channels, :] = value
 
     @pl.when(core == 0)
     def _():
@@ -407,9 +407,14 @@
             send[n] = jnp.zeros_like(there[0]).astype(jnp.bfloat16)
 
 
-def join_kernel(swap, near_in, mates_in, near, mates):
+def join_kernel(swap, near_in, near, other):
     near[1] = swap[0]
-    mates[1] = swap[1]
+    other[...] = swap[1]
+
+
+def stack_kernel(first, second, both):
+    both[0] = first[...]
+    both[1] = second[...]
 
 
 def core_sum_kernel(kept, received, mine, send):
@@ -544,11 +549,14 @@
 
     swap, folds, table = send_call(strain, pair_listed, jnp.transpose(band_used, (0, 2, 1)))
     joined = pltpu.VMEM(swap.shape, swap.dtype)
-    near, mates = local_call(keep_kernel, "spectrum_kept", [joined, joined], swap, folds, table)
-    near, mates = local_call(
-        join_kernel, "join", [joined, joined], flip(swap, 1), near, mates, aliases={1: 0, 2: 1}
-    )
-    mates = flip(mates, 2)
+    single = pltpu.VMEM(swap.shape[1:], swap.dtype)
+    near, mate = local_call(keep_kernel, "spectrum_kept", [joined, single], swap, folds, table)
+    mate = flip(mate, 2)
+    near, other = local_call(
+        join_kernel, "join", [joined, single], flip(swap, 1), near, aliases={1: 0}
+    )
+    other = flip(other, 2)
+    mates = local_call(stack_kernel, "stack", [joined], mate, other)[0]
     near_odd, near_even = planes(near, 1), planes(near, 0)
     far_odd, far_even = planes(mates, 1), planes(mates, 0)
     nbands = band_used.shape[2]

time: 41.3 us -> 40.6 us (0.983)
  waiting for transfers between devices: 10.2 us -> 9.17 us
    ppermute x10 -> x11, waiting for transfers between devices: 10.2 us -> 9.17 us  [exchange(): return lax.ppermute(value, AXIS, pairs)]
    ppermute x10 -> x11, starting transfers between devices: 19.3 us -> 19.7 us  [exchange(): return lax.ppermute(value, AXIS, pairs)]
    pallas_call x6 -> x7, Pallas kernels: 1.48 us -> 1.5 us  [local_call(): pl.pallas_call(kernel, in_specs=[VMEM_SPEC] * len(values), out_specs=[VME...]
  transfers between devices with their start and end apart: 10 -> 11, of which waited for: 7 -> 6; matrix products, arithmetic and copies ran while one was open for 0% -> 0% of each run, Pallas kernels for 15% -> 15%
where the time goes in v12:
time: 40.6 us; the launch traced here: 40.4 us
  starting transfers between devices  19.7 us (49%)
  Pallas kernels  11.4 us (28%)
  waiting for transfers between devices  9.17 us (23%)
    ppermute x11, starting transfers between devices, exchange(): return lax.ppermute(value, AXIS, pairs)  19.7 us
    ppermute x11, waiting for transfers between devices, exchange(): return lax.ppermute(value, AXIS, pairs)  9.17 us
    pallas_call x1, Pallas kernels, early_call(): pl.pallas_call(functools.partial(early_kernel, nbands), in_specs=[VMEM_SP...  5.34 us
    pallas_call x1, Pallas kernels, send_call(): pl.pallas_call(send_kernel, in_specs=[HBM_SPEC] * 4, out_specs=[VMEM_SPEC...  2.66 us
    pallas_call x1, Pallas kernels, late_call(): pl.pallas_call(functools.partial(late_kernel, nbands), in_specs=[VMEM_SPE...  1.93 us
    pallas_call x7, Pallas kernels, local_call(): pl.pallas_call(kernel, in_specs=[VMEM_SPEC] * len(values), out_specs=[VME...  1.5 us
  transfers between devices with their start and end apart: 11, of which 6 were waited for; matrix products, arithmetic and copies ran while one was open for 0% of the time, Pallas kernels for 15%

profile of v12, /device:TPU:0, one launch (start us, length us, event | category | flops | bytes accessed | tf_op | source)
XLA Modules:
  0.0 40.4 jit_solution(7164560165195758888)
XLA Ops:
  0.0 2.7 %spectrum_sent.1 = (bf16[2,264,256]{2,1,0:T(8,128)(2,1)S(1)}, bf16[2,2,256,1024]{3,2,1,0:T(8,128)(2,1)S(1)}, bf16[2,1024,256]{2,1,0:T(8,128)(2,1)S(1)}) custom-call(bf16[256,4096]{1,0:T(8,128)(2,1)} %strain.1, f32[2,4,2,32,128]{4,3,2,1,0:T(8,128)} %constant.4.clone.factors, s32[1,8]{1,0:T(1,128)} %listed.1, s32[1,4,8]{2,1,0:T(4,128)} %bitcast.1), custom_call_target="tpu_custom_call" | custom-call | tf_op jit(solution)/shard_map/spectrum_sent/pallas_call | solution.py:195
  2.7 0.8 %collective-permute-start = (bf16[2,264,256]{2,1,0:T(8,128)(2,1)S(1)}, bf16[2,264,256]{2,1,0:T(8,128)(2,1)S(1)}, u32[]{:S(2)}, u32[]{:S(2)}) collective-permute-start(bf16[2,264,256]{2,1,0:T(8,128)(2,1)S(1)} %get-tuple-element.24.swap), channel_id=1, source_target_pairs={{0,1},{1,0},{2,3},{3,2},{4,5},{5,4},{6,7},{7,6},{8,9},{9,8},{10,11... | collective-permute-start | bytes 811016 | tf_op jit(solution)/shard_map/ppermute | solution.py:540
  3.5 0.0 copy-start
  3.5 0.0 copy-start.1
  3.5 0.8 %spectrum_kept.1 = (bf16[2,264,256]{2,1,0:T(8,128)(2,1)S(1)}, bf16[264,256]{1,0:T(8,128)(2,1)S(1)}) custom-call(bf16[2,264,256]{2,1,0:T(8,128)(2,1)S(1)} %get-tuple-element.24.swap, bf16[2,2,256,1024]{3,2,1,0:T(8,128)(2,1)S(1)} %get-tuple-element.25.folds, bf16[2,1024,256]{2,1,0:T(8,128)(2,1)S(1)} %get-tuple-element.26.table), custom_call_target="tpu_custom_call" | custom-call | tf_op jit(solution)/shard_map/spectrum_kept/pallas_call | solution.py:481
  4.2 2.4 %collective-permute-start.1 = (bf16[264,256]{1,0:T(8,128)(2,1)S(1)}, bf16[264,256]{1,0:T(8,128)(2,1)S(1)}, u32[]{:S(2)}, u32[]{:S(2)}) collective-permute-start(bf16[264,256]{1,0:T(8,128)(2,1)S(1)} %get-tuple-element.29), channel_id=1, source_target_pairs={{0,2},{1,3},{2,0},{3,1},{4,6},{5,7},{6,4},{7,5},{8,10},{9,11},{10,... | collective-permute-start | bytes 405512 | tf_op jit(solution)/shard_map/ppermute | solution.py:540
  6.6 0.0 collective-permute-done.swap
  6.7 0.7 %collective-permute-start.2 = (bf16[264,256]{1,0:T(8,128)(2,1)S(1)}, bf16[264,256]{1,0:T(8,128)(2,1)S(1)}, u32[]{:S(2)}, u32[]{:S(2)}) collective-permute-start(bf16[264,256]{1,0:T(8,128)(2,1)S(1)} %get-tuple-element.30), channel_id=1, source_target_pairs={{0,2},{1,3},{2,0},{3,1},{4,6},{5,7},{6,4},{7,5},{8,10},{9,11},{10,... | collective-permute-start | bytes 405512 | tf_op jit(solution)/shard_map/ppermute | solution.py:540
  7.4 0.7 %collective-permute-start.4 = (bf16[2,264,256]{2,1,0:T(8,128)(2,1)S(1)}, bf16[2,264,256]{2,1,0:T(8,128)(2,1)S(1)}, u32[]{:S(2)}, u32[]{:S(2)}) collective-permute-start(bf16[2,264,256]{2,1,0:T(8,128)(2,1)S(1)} %get-tuple-element.28.near), channel_id=1, source_target_pairs={{4,8},{5,9},{6,10},{7,11},{8,4},{9,5},{10,6},{11,7},{20,24},{21,25... | collective-permute-start | bytes 811016 | tf_op jit(solution)/shard_map/ppermute | solution.py:540
  8.0 4.4 %collective-permute-start.3 = (bf16[2,264,256]{2,1,0:T(8,128)(2,1)S(1)}, bf16[2,264,256]{2,1,0:T(8,128)(2,1)S(1)}, u32[]{:S(2)}, u32[]{:S(2)}) collective-permute-start(bf16[2,264,256]{2,1,0:T(8,128)(2,1)S(1)} %get-tuple-element.28.near), channel_id=1, source_target_pairs={{0,4},{1,5},{2,6},{3,7},{4,0},{5,1},{6,2},{7,3},{8,12},{9,13},{10,... | collective-permute-start | bytes 811016 | tf_op jit(solution)/shard_map/ppermute | solution.py:540
  12.5 0.0 collective-permute-done.1.first
  12.5 1.0 %collective-permute-done.2.second = bf16[264,256]{1,0:T(8,128)(2,1)S(1)} collective-permute-done((bf16[264,256]{1,0:T(8,128)(2,1)S(1)}, bf16[264,256]{1,0:T(8,128)(2,1)S(1)}, u32[]{:S(2)}, u32[]{:S(2)}) %collective-permute-start.2) | collective-permute-done | bytes 135200 | tf_op jit(solution)/shard_map/ppermute | solution.py:540
  13.5 0.7 %collective-permute-start.6 = (bf16[2,264,256]{2,1,0:T(8,128)(2,1)S(1)}, bf16[2,264,256]{2,1,0:T(8,128)(2,1)S(1)}, u32[]{:S(2)}, u32[]{:S(2)}) collective-permute-start(bf16[2,264,256]{2,1,0:T(8,128)(2,1)S(1)} %stack.1.mates), channel_id=1, source_target_pairs={{4,8},{5,9},{6,10},{7,11},{8,4},{9,5},{10,6},{11,7},{20,24},{21,25... | collective-permute-start | bytes 811016 | tf_op jit(solution)/shard_map/ppermute | solution.py:540
  14.2 4.7 %collective-permute-start.5 = (bf16[2,264,256]{2,1,0:T(8,128)(2,1)S(1)}, bf16[2,264,256]{2,1,0:T(8,128)(2,1)S(1)}, u32[]{:S(2)}, u32[]{:S(2)}) collective-permute-start(bf16[2,264,256]{2,1,0:T(8,128)(2,1)S(1)} %stack.1.mates), channel_id=1, source_target_pairs={{0,4},{1,5},{2,6},{3,7},{4,0},{5,1},{6,2},{7,3},{8,12},{9,13},{10,... | collective-permute-start | bytes 811016 | tf_op jit(solution)/shard_map/ppermute | solution.py:540
  18.8 0.0 collective-permute-done.4.odd
  18.8 0.0 collective-permute-done.3.even
  18.8 0.0 copy-done
  18.8 0.0 copy-done.1
  18.8 5.3 %early_pairs.1 = (bf16[12,264,256]{2,1,0:T(8,128)(2,1)S(1)}, f32[8,128,384]{2,1,0:T(8,128)S(1)}, bf16[256,512]{1,0:T(8,128)(2,1)S(1)}, bf16[8,256,384]{2,1,0:T(8,128)(2,1)S(1)}) custom-call(bf16[2,264,256]{2,1,0:T(8,128)(2,1)S(1)} %get-tuple-element.28.near, bf16[2,264,256]{2,1,0:T(8,128)(2,1)S(1)} %stack.1.mates, ...), custom_call_target="tpu_custom_call" | custom-call | tf_op jit(solution)/shard_map/early_pairs/pallas_call | solution.py:496
  24.2 0.0 collective-permute-done.6.odd
  24.2 0.3 collective-permute-done.5.even
  24.5 1.9 %late_pairs.1 = (f32[6,128,128]{2,1,0:T(8,128)S(1)}, bf16[6,128,128]{2,1,0:T(8,128)(2,1)S(1)}, bf16[12,264,256]{2,1,0:T(8,128)(2,1)S(1)}, f32[8,128,384]{2,1,0:T(8,128)S(1)}) custom-call(bf16[12,264,256]{2,1,0:T(8,128)(2,1)S(1)} %get-tuple-element.31.spec_in, ...), custom_call_target="tpu_custom_call", output_to_operand_aliasing={{2}: (0, {}), {3}: (1, {})} | custom-call | tf_op jit(solution)/shard_map/late_pairs/pallas_call | solution.py:520
  26.4 0.1 collective-permute-start.7
  26.5 1.4 %collective-permute-done.7.received = bf16[6,128,128]{2,1,0:T(8,128)(2,1)S(1)} collective-permute-done((bf16[6,128,128]{2,1,0:T(8,128)(2,1)S(1)}, bf16[6,128,128]{2,1,0:T(8,128)(2,1)S(1)}, u32[]{:S(2)}, u32[]{:S(2)}) %collective-permute-start.7) | collective-permute-done | bytes 196640 | tf_op jit(solution)/shard_map/ppermute | solution.py:540
  28.0 1.6 %collective-permute-start.8 = (bf16[3,128,128]{2,1,0:T(8,128)(2,1)S(1)}, bf16[3,128,128]{2,1,0:T(8,128)(2,1)S(1)}, u32[]{:S(2)}, u32[]{:S(2)}) collective-permute-start(bf16[3,128,128]{2,1,0:T(8,128)(2,1)S(1)} %get-tuple-element.38), channel_id=1, source_target_pairs={{0,2},{1,3},{2,0},{3,1},{4,6},{5,7},{6,4},{7,5},{8,10},{9,11},{10,... | collective-permute-start | bytes 294920 | tf_op jit(solution)/shard_map/ppermute | solution.py:540
  29.5 3.3 %collective-permute-done.8.received = bf16[3,128,128]{2,1,0:T(8,128)(2,1)S(1)} collective-permute-done((bf16[3,128,128]{2,1,0:T(8,128)(2,1)S(1)}, bf16[3,128,128]{2,1,0:T(8,128)(2,1)S(1)}, u32[]{:S(2)}, u32[]{:S(2)}) %collective-permute-start.8) | collective-permute-done | bytes 98336 | tf_op jit(solution)/shard_map/ppermute | solution.py:540
  32.9 3.6 %collective-permute-start.9 = (bf16[2,128,128]{2,1,0:T(8,128)(2,1)S(1)}, bf16[2,128,128]{2,1,0:T(8,128)(2,1)S(1)}, u32[]{:S(2)}, u32[]{:S(2)}) collective-permute-start(bf16[2,128,128]{2,1,0:T(8,128)(2,1)S(1)} %get-tuple-element.40), channel_id=1, source_target_pairs={{0,4},{1,9},{2,6},{4,8},{5,13},{6,10},{7,3},{8,12},{10,14},{11,7},... | collective-permute-start | bytes 196616 | tf_op jit(solution)/shard_map/ppermute | solution.py:540
  36.6 1.9 %collective-permute-done.9.received = bf16[2,128,128]{2,1,0:T(8,128)(2,1)S(1)} collective-permute-done((bf16[2,128,128]{2,1,0:T(8,128)(2,1)S(1)}, bf16[2,128,128]{2,1,0:T(8,128)(2,1)S(1)}, u32[]{:S(2)}, u32[]{:S(2)}) %collective-permute-start.9) | collective-permute-done | bytes 65568 | tf_op jit(solution)/shard_map/ppermute | solution.py:540
  38.5 0.1 collective-permute-start.10
  38.6 1.2 %collective-permute-done.10.received = f32[128,128]{1,0:T(8,128)S(1)} collective-permute-done((f32[128,128]{1,0:T(8,128)S(1)}, f32[128,128]{1,0:T(8,128)S(1)}, u32[]{:S(2)}, u32[]{:S(2)}) %collective-permute-start.10) | collective-permute-done | bytes 65568 | tf_op jit(solution)/shard_map/ppermute | solution.py:540
  39.8 0.6 %image.1 = f32[128,128]{1,0:T(8,128)} custom-call(f32[128,128]{1,0:T(8,128)S(1)} %get-tuple-element.41.kept, f32[128,128]{1,0:T(8,128)S(1)} %collective-permute-done.10.received), custom_call_target="tpu_custom_call" | custom-call | tf_op jit(solution)/shard_map/image/pallas_call | solution.py:481
  (5 shorter events, 0.1 us)
Async XLA Ops:
  2.7 4.0 %collective-permute-start = (bf16[2,264,256]{2,1,0:T(8,128)(2,1)S(1)}, bf16[2,264,256]{2,1,0:T(8,128)(2,1)S(1)}, u32[]{:S(2)}, u32[]{:S(2)}) collective-permute-start(bf16[2,264,256]{2,1,0:T(8,128)(2,1)S(1)} %get-tuple-element.24.swap), channel_id=1, source_target_pairs={{0,1},{1,0},{2,3},{3,2},{4,5},{5,4},{6,7},{7,6},{8,9},{9,8},{10,11... | collective-permute-start | bytes 811016 | tf_op jit(solution)/shard_map/ppermute | solution.py:540
  3.5 15.3 %copy-start = (bf16[9,512,384]{2,1,0:T(8,128)(2,1)S(1)}, bf16[9,512,384]{2,1,0:T(8,128)(2,1)}, u32[]{:S(2)}) copy-start(bf16[9,512,384]{2,1,0:T(8,128)(2,1)} %lag_range.3) | copy-start | bytes 10616836
  3.5 15.4 %copy-start.1 = (bf16[9,128,256]{2,1,0:T(8,128)(2,1)S(1)}, bf16[9,128,256]{2,1,0:T(8,128)(2,1)}, u32[]{:S(2)}) copy-start(bf16[9,128,256]{2,1,0:T(8,128)(2,1)} %steering.3) | copy-start | bytes 1769476
  4.2 8.2 %collective-permute-start.1 = (bf16[264,256]{1,0:T(8,128)(2,1)S(1)}, bf16[264,256]{1,0:T(8,128)(2,1)S(1)}, u32[]{:S(2)}, u32[]{:S(2)}) collective-permute-start(bf16[264,256]{1,0:T(8,128)(2,1)S(1)} %get-tuple-element.29), channel_id=1, source_target_pairs={{0,2},{1,3},{2,0},{3,1},{4,6},{5,7},{6,4},{7,5},{8,10},{9,11},{10,... | collective-permute-start | bytes 405512 | tf_op jit(solution)/shard_map/ppermute | solution.py:540
  6.7 6.8 %collective-permute-start.2 = (bf16[264,256]{1,0:T(8,128)(2,1)S(1)}, bf16[264,256]{1,0:T(8,128)(2,1)S(1)}, u32[]{:S(2)}, u32[]{:S(2)}) collective-permute-start(bf16[264,256]{1,0:T(8,128)(2,1)S(1)} %get-tuple-element.30), channel_id=1, source_target_pairs={{0,2},{1,3},{2,0},{3,1},{4,6},{5,7},{6,4},{7,5},{8,10},{9,11},{10,... | collective-permute-start | bytes 405512 | tf_op jit(solution)/shard_map/ppermute | solution.py:540
  7.4 11.5 %collective-permute-start.4 = (bf16[2,264,256]{2,1,0:T(8,128)(2,1)S(1)}, bf16[2,264,256]{2,1,0:T(8,128)(2,1)S(1)}, u32[]{:S(2)}, u32[]{:S(2)}) collective-permute-start(bf16[2,264,256]{2,1,0:T(8,128)(2,1)S(1)} %get-tuple-element.28.near), channel_id=1, source_target_pairs={{4,8},{5,9},{6,10},{7,11},{8,4},{9,5},{10,6},{11,7},{20,24},{21,25... | collective-permute-start | bytes 811016 | tf_op jit(solution)/shard_map/ppermute | solution.py:540
  8.0 10.8 %collective-permute-start.3 = (bf16[2,264,256]{2,1,0:T(8,128)(2,1)S(1)}, bf16[2,264,256]{2,1,0:T(8,128)(2,1)S(1)}, u32[]{:S(2)}, u32[]{:S(2)}) collective-permute-start(bf16[2,264,256]{2,1,0:T(8,128)(2,1)S(1)} %get-tuple-element.28.near), channel_id=1, source_target_pairs={{0,4},{1,5},{2,6},{3,7},{4,0},{5,1},{6,2},{7,3},{8,12},{9,13},{10,... | collective-permute-start | bytes 811016 | tf_op jit(solution)/shard_map/ppermute | solution.py:540
  13.5 10.7 %collective-permute-start.6 = (bf16[2,264,256]{2,1,0:T(8,128)(2,1)S(1)}, bf16[2,264,256]{2,1,0:T(8,128)(2,1)S(1)}, u32[]{:S(2)}, u32[]{:S(2)}) collective-permute-start(bf16[2,264,256]{2,1,0:T(8,128)(2,1)S(1)} %stack.1.mates), channel_id=1, source_target_pairs={{4,8},{5,9},{6,10},{7,11},{8,4},{9,5},{10,6},{11,7},{20,24},{21,25... | collective-permute-start | bytes 811016 | tf_op jit(solution)/shard_map/ppermute | solution.py:540
  14.2 10.3 %collective-permute-start.5 = (bf16[2,264,256]{2,1,0:T(8,128)(2,1)S(1)}, bf16[2,264,256]{2,1,0:T(8,128)(2,1)S(1)}, u32[]{:S(2)}, u32[]{:S(2)}) collective-permute-start(bf16[2,264,256]{2,1,0:T(8,128)(2,1)S(1)} %stack.1.mates), channel_id=1, source_target_pairs={{0,4},{1,5},{2,6},{3,7},{4,0},{5,1},{6,2},{7,3},{8,12},{9,13},{10,... | collective-permute-start | bytes 811016 | tf_op jit(solution)/shard_map/ppermute | solution.py:540
  26.4 1.5 %collective-permute-start.7 = (bf16[6,128,128]{2,1,0:T(8,128)(2,1)S(1)}, bf16[6,128,128]{2,1,0:T(8,128)(2,1)S(1)}, u32[]{:S(2)}, u32[]{:S(2)}) collective-permute-start(bf16[6,128,128]{2,1,0:T(8,128)(2,1)S(1)} %get-tuple-element.36), channel_id=1, source_target_pairs={{0,1},{1,0},{2,3},{3,2},{4,5},{5,4},{6,7},{7,6},{8,9},{9,8},{10,11... | collective-permute-start | bytes 589832 | tf_op jit(solution)/shard_map/ppermute | solution.py:540
  28.0 4.9 %collective-permute-start.8 = (bf16[3,128,128]{2,1,0:T(8,128)(2,1)S(1)}, bf16[3,128,128]{2,1,0:T(8,128)(2,1)S(1)}, u32[]{:S(2)}, u32[]{:S(2)}) collective-permute-start(bf16[3,128,128]{2,1,0:T(8,128)(2,1)S(1)} %get-tuple-element.38), channel_id=1, source_target_pairs={{0,2},{1,3},{2,0},{3,1},{4,6},{5,7},{6,4},{7,5},{8,10},{9,11},{10,... | collective-permute-start | bytes 294920 | tf_op jit(solution)/shard_map/ppermute | solution.py:540
  32.9 5.5 %collective-permute-start.9 = (bf16[2,128,128]{2,1,0:T(8,128)(2,1)S(1)}, bf16[2,128,128]{2,1,0:T(8,128)(2,1)S(1)}, u32[]{:S(2)}, u32[]{:S(2)}) collective-permute-start(bf16[2,128,128]{2,1,0:T(8,128)(2,1)S(1)} %get-tuple-element.40), channel_id=1, source_target_pairs={{0,4},{1,9},{2,6},{4,8},{5,13},{6,10},{7,3},{8,12},{10,14},{11,7},... | collective-permute-start | bytes 196616 | tf_op jit(solution)/shard_map/ppermute | solution.py:540
  38.5 1.3 %collective-permute-start.10 = (f32[128,128]{1,0:T(8,128)S(1)}, f32[128,128]{1,0:T(8,128)S(1)}, u32[]{:S(2)}, u32[]{:S(2)}) collective-permute-start(f32[128,128]{1,0:T(8,128)S(1)} %get-tuple-element.42), channel_id=1, source_target_pairs={{0,1},{1,0},{2,3},{3,2},{4,5},{5,4},{6,7},{7,6},{8,9},{9,8},{10,11... | collective-permute-start | bytes 196616 | tf_op jit(solution)/shard_map/ppermute | solution.py:540

commit v13 on v12

--- a/solution.py
+++ b/solution.py
@@ -417,41 +417,48 @@
     both[1] = second[...]
 
 
-def core_sum_kernel(kept, received, mine, send):
-    side = lax.rem(lax.axis_index(AXIS), Q) // 2
+def core_sum_kernel(kept, received, mine, send, later):
+    me = lax.rem(lax.axis_index(AXIS), Q)
+    core, side = lax.rem(me, 2), me // 2
 
     def total(n):
         return kept[n] + received[n].astype(jnp.float32)
 
     for n in range(2):
         mine[n] = total(2 * side + n)
-        send[n] = total(2 * (1 - side) + n).astype(jnp.bfloat16)
+        later[n] = total(2 * (1 - side) + n).astype(jnp.bfloat16)
     mine[2] = total(Q + side)
-    send[2] = total(Q + 1 - side).astype(jnp.bfloat16)
-
-
-def plane_sum_kernel(kept, received, mine, send):
+
+    @pl.when(core == 0)
+    def _():
+        send[...] = later[...]
+
+    @pl.when(core == 1)
+    def _():
+        send[0] = total(Q + 1 - side).astype(jnp.bfloat16)
+        send[1] = jnp.zeros_like(send[0])
+
+
+def plane_sum_kernel(kept, received, send):
     core = lax.rem(lax.axis_index(AXIS), 2)
-    totals = [kept[n] + received[n].astype(jnp.float32) for n in range(3)]
-    mine[0] = totals[0]
-    mine[1] = totals[1]
 
     @pl.when(core == 0)
     def _():
-        send[0] = totals[0].astype(jnp.bfloat16)
-        send[1] = totals[1].astype(jnp.bfloat16)
+        for n in range(2):
+            send[n] = (kept[n] + received[n].astype(jnp.float32)).astype(jnp.bfloat16)
 
     @pl.when(core == 1)
     def _():
-        send[0] = totals[2].astype(jnp.bfloat16)
-        send[1] = jnp.zeros_like(totals[2]).astype(jnp.bfloat16)
-
-
-def end_sum_kernel(kept, received, mine, send):
+        send[0] = (kept[2] + received[0].astype(jnp.float32)).astype(jnp.bfloat16)
+        send[1] = jnp.zeros_like(send[0])
+
+
+def end_sum_kernel(kept, later, received, mine, send):
     me = lax.rem(lax.axis_index(AXIS), Q)
     first = received[0].astype(jnp.float32)
     second = received[1].astype(jnp.float32)
     core, side = lax.rem(me, 2), me // 2
+    own = [kept[n] + later[n].astype(jnp.float32) for n in range(2)]
 
     @pl.when(core == 0)
     def _():
@@ -460,13 +467,13 @@
 
     @pl.when((core == 1) & (side == 0))
     def _():
-        mine[...] = kept[1]
-        send[...] = kept[0] + first
+        mine[...] = own[1]
+        send[...] = own[0] + first
 
     @pl.when((core == 1) & (side == 1))
     def _():
-        mine[...] = kept[1] + first
-        send[...] = kept[0]
+        mine[...] = own[1] + first
+        send[...] = own[0]
 
 
 def image_kernel(kept, received, image):
@@ -576,25 +583,24 @@
             return i + Q
         return i + 2 * Q if i % Q < 2 else i - Q
 
-    kept, send = local_call(
+    kept, send, later = local_call(
         core_sum_kernel,
         "core_sum",
-        [pieces(3, jnp.float32), pieces(3, jnp.bfloat16)],
+        [pieces(3, jnp.float32), pieces(2, jnp.bfloat16), pieces(2, jnp.bfloat16)],
         kept,
         flip(send, 1),
     )
-    kept, send = local_call(
-        plane_sum_kernel,
-        "plane_sum",
-        [pieces(2, jnp.float32), pieces(2, jnp.bfloat16)],
-        kept,
-        flip(send, 2),
-    )
+    received = flip(send, 2)
+    later = exchange(later, devices, lambda i: i ^ 2 if i % 2 else None)
+    send = local_call(
+        plane_sum_kernel, "plane_sum", [pieces(2, jnp.bfloat16)], kept, received
+    )[0]
     kept, send = local_call(
         end_sum_kernel,
         "end_sum",
         [pieces(0, jnp.float32), pieces(0, jnp.float32)],
         kept,
+        later,
         exchange(send, devices, ends),
     )
     return local_call(

time: 40.6 us -> 40.1 us (0.988)
  waiting for transfers between devices: 9.17 us -> 7.93 us
  starting transfers between devices: 19.7 us -> 20.4 us
    ppermute x11 -> x12, waiting for transfers between devices: 9.17 us -> 7.93 us  [exchange(): return lax.ppermute(value, AXIS, pairs)]
    ppermute x11 -> x12, starting transfers between devices: 19.7 us -> 20.4 us  [exchange(): return lax.ppermute(value, AXIS, pairs)]
  transfers between devices with their start and end apart: 11 -> 12, of which waited for: 6 -> 6; matrix products, arithmetic and copies ran while one was open for 0% -> 0% of each run, Pallas kernels for 15% -> 15%
where the time goes in v13:
time: 40.1 us; the launch traced here: 39.9 us
  starting transfers between devices  20.4 us (51%)
  Pallas kernels  11.4 us (28%)
  waiting for transfers between devices  7.93 us (20%)
    ppermute x12, starting transfers between devices, exchange(): return lax.ppermute(value, AXIS, pairs)  20.4 us
    ppermute x12, waiting for transfers between devices, exchange(): return lax.ppermute(value, AXIS, pairs)  7.93 us
    pallas_call x1, Pallas kernels, early_call(): pl.pallas_call(functools.partial(early_kernel, nbands), in_specs=[VMEM_SP...  5.34 us
    pallas_call x1, Pallas kernels, send_call(): pl.pallas_call(send_kernel, in_specs=[HBM_SPEC] * 4, out_specs=[VMEM_SPEC...  2.66 us
    pallas_call x1, Pallas kernels, late_call(): pl.pallas_call(functools.partial(late_kernel, nbands), in_specs=[VMEM_SPE...  1.93 us
    pallas_call x7, Pallas kernels, local_call(): pl.pallas_call(kernel, in_specs=[VMEM_SPEC] * len(values), out_specs=[VME...  1.51 us
  transfers between devices with their start and end apart: 12, of which 6 were waited for; matrix products, arithmetic and copies ran while one was open for 0% of the time, Pallas kernels for 15%

profile of v13, /device:TPU:0, one launch (start us, length us, event | category | flops | bytes accessed | tf_op | source)
XLA Modules:
  0.0 39.9 jit_solution(17191967660049235293)
XLA Ops:
  0.0 2.7 %spectrum_sent.1 = (bf16[2,264,256]{2,1,0:T(8,128)(2,1)S(1)}, bf16[2,2,256,1024]{3,2,1,0:T(8,128)(2,1)S(1)}, bf16[2,1024,256]{2,1,0:T(8,128)(2,1)S(1)}) custom-call(bf16[256,4096]{1,0:T(8,128)(2,1)} %strain.1, f32[2,4,2,32,128]{4,3,2,1,0:T(8,128)} %constant.4.clone.factors, s32[1,8]{1,0:T(1,128)} %listed.1, s32[1,4,8]{2,1,0:T(4,128)} %bitcast.1), custom_call_target="tpu_custom_call" | custom-call | tf_op jit(solution)/shard_map/spectrum_sent/pallas_call | solution.py:195
  2.7 0.8 %collective-permute-start = (bf16[2,264,256]{2,1,0:T(8,128)(2,1)S(1)}, bf16[2,264,256]{2,1,0:T(8,128)(2,1)S(1)}, u32[]{:S(2)}, u32[]{:S(2)}) collective-permute-start(bf16[2,264,256]{2,1,0:T(8,128)(2,1)S(1)} %get-tuple-element.23.swap), channel_id=1, source_target_pairs={{0,1},{1,0},{2,3},{3,2},{4,5},{5,4},{6,7},{7,6},{8,9},{9,8},{10,11... | collective-permute-start | bytes 811016 | tf_op jit(solution)/shard_map/ppermute | solution.py:547
  3.5 0.0 copy-start
  3.5 0.8 %spectrum_kept.1 = (bf16[2,264,256]{2,1,0:T(8,128)(2,1)S(1)}, bf16[264,256]{1,0:T(8,128)(2,1)S(1)}) custom-call(bf16[2,264,256]{2,1,0:T(8,128)(2,1)S(1)} %get-tuple-element.23.swap, bf16[2,2,256,1024]{3,2,1,0:T(8,128)(2,1)S(1)} %get-tuple-element.24.folds, bf16[2,1024,256]{2,1,0:T(8,128)(2,1)S(1)} %get-tuple-element.25.table), custom_call_target="tpu_custom_call" | custom-call | tf_op jit(solution)/shard_map/spectrum_kept/pallas_call | solution.py:488
  4.2 2.4 %collective-permute-start.1 = (bf16[264,256]{1,0:T(8,128)(2,1)S(1)}, bf16[264,256]{1,0:T(8,128)(2,1)S(1)}, u32[]{:S(2)}, u32[]{:S(2)}) collective-permute-start(bf16[264,256]{1,0:T(8,128)(2,1)S(1)} %get-tuple-element.28), channel_id=1, source_target_pairs={{0,2},{1,3},{2,0},{3,1},{4,6},{5,7},{6,4},{7,5},{8,10},{9,11},{10,... | collective-permute-start | bytes 405512 | tf_op jit(solution)/shard_map/ppermute | solution.py:547
  6.6 0.0 collective-permute-done.swap
  6.7 0.7 %collective-permute-start.2 = (bf16[264,256]{1,0:T(8,128)(2,1)S(1)}, bf16[264,256]{1,0:T(8,128)(2,1)S(1)}, u32[]{:S(2)}, u32[]{:S(2)}) collective-permute-start(bf16[264,256]{1,0:T(8,128)(2,1)S(1)} %get-tuple-element.29), channel_id=1, source_target_pairs={{0,2},{1,3},{2,0},{3,1},{4,6},{5,7},{6,4},{7,5},{8,10},{9,11},{10,... | collective-permute-start | bytes 405512 | tf_op jit(solution)/shard_map/ppermute | solution.py:547
  7.4 0.7 %collective-permute-start.4 = (bf16[2,264,256]{2,1,0:T(8,128)(2,1)S(1)}, bf16[2,264,256]{2,1,0:T(8,128)(2,1)S(1)}, u32[]{:S(2)}, u32[]{:S(2)}) collective-permute-start(bf16[2,264,256]{2,1,0:T(8,128)(2,1)S(1)} %get-tuple-element.27.near), channel_id=1, source_target_pairs={{4,8},{5,9},{6,10},{7,11},{8,4},{9,5},{10,6},{11,7},{20,24},{21,25... | collective-permute-start | bytes 811016 | tf_op jit(solution)/shard_map/ppermute | solution.py:547
  8.0 4.4 %collective-permute-start.3 = (bf16[2,264,256]{2,1,0:T(8,128)(2,1)S(1)}, bf16[2,264,256]{2,1,0:T(8,128)(2,1)S(1)}, u32[]{:S(2)}, u32[]{:S(2)}) collective-permute-start(bf16[2,264,256]{2,1,0:T(8,128)(2,1)S(1)} %get-tuple-element.27.near), channel_id=1, source_target_pairs={{0,4},{1,5},{2,6},{3,7},{4,0},{5,1},{6,2},{7,3},{8,12},{9,13},{10,... | collective-permute-start | bytes 811016 | tf_op jit(solution)/shard_map/ppermute | solution.py:547
  12.5 0.0 collective-permute-done.1.first
  12.5 1.0 %collective-permute-done.2.second = bf16[264,256]{1,0:T(8,128)(2,1)S(1)} collective-permute-done((bf16[264,256]{1,0:T(8,128)(2,1)S(1)}, bf16[264,256]{1,0:T(8,128)(2,1)S(1)}, u32[]{:S(2)}, u32[]{:S(2)}) %collective-permute-start.2) | collective-permute-done | bytes 135200 | tf_op jit(solution)/shard_map/ppermute | solution.py:547
  13.5 0.7 %collective-permute-start.6 = (bf16[2,264,256]{2,1,0:T(8,128)(2,1)S(1)}, bf16[2,264,256]{2,1,0:T(8,128)(2,1)S(1)}, u32[]{:S(2)}, u32[]{:S(2)}) collective-permute-start(bf16[2,264,256]{2,1,0:T(8,128)(2,1)S(1)} %stack.1.mates), channel_id=1, source_target_pairs={{4,8},{5,9},{6,10},{7,11},{8,4},{9,5},{10,6},{11,7},{20,24},{21,25... | collective-permute-start | bytes 811016 | tf_op jit(solution)/shard_map/ppermute | solution.py:547
  14.2 4.7 %collective-permute-start.5 = (bf16[2,264,256]{2,1,0:T(8,128)(2,1)S(1)}, bf16[2,264,256]{2,1,0:T(8,128)(2,1)S(1)}, u32[]{:S(2)}, u32[]{:S(2)}) collective-permute-start(bf16[2,264,256]{2,1,0:T(8,128)(2,1)S(1)} %stack.1.mates), channel_id=1, source_target_pairs={{0,4},{1,5},{2,6},{3,7},{4,0},{5,1},{6,2},{7,3},{8,12},{9,13},{10,... | collective-permute-start | bytes 811016 | tf_op jit(solution)/shard_map/ppermute | solution.py:547
  18.8 0.0 collective-permute-done.4.odd
  18.8 0.0 collective-permute-done.3.even
  18.8 0.0 copy-done
  18.8 0.0 copy-done.1
  18.8 5.3 %early_pairs.1 = (bf16[12,264,256]{2,1,0:T(8,128)(2,1)S(1)}, f32[8,128,384]{2,1,0:T(8,128)S(1)}, bf16[256,512]{1,0:T(8,128)(2,1)S(1)}, bf16[8,256,384]{2,1,0:T(8,128)(2,1)S(1)}) custom-call(bf16[2,264,256]{2,1,0:T(8,128)(2,1)S(1)} %get-tuple-element.27.near, bf16[2,264,256]{2,1,0:T(8,128)(2,1)S(1)} %stack.1.mates, ...), custom_call_target="tpu_custom_call" | custom-call | tf_op jit(solution)/shard_map/early_pairs/pallas_call | solution.py:503
  24.2 0.0 collective-permute-done.6.odd
  24.2 0.3 collective-permute-done.5.even
  24.5 1.9 %late_pairs.1 = (f32[6,128,128]{2,1,0:T(8,128)S(1)}, bf16[6,128,128]{2,1,0:T(8,128)(2,1)S(1)}, bf16[12,264,256]{2,1,0:T(8,128)(2,1)S(1)}, f32[8,128,384]{2,1,0:T(8,128)S(1)}) custom-call(bf16[12,264,256]{2,1,0:T(8,128)(2,1)S(1)} %get-tuple-element.30.spec_in, ...), custom_call_target="tpu_custom_call", output_to_operand_aliasing={{2}: (0, {}), {3}: (1, {})} | custom-call | tf_op jit(solution)/shard_map/late_pairs/pallas_call | solution.py:527
  26.4 0.1 collective-permute-start.7
  26.5 1.4 %collective-permute-done.7.received = bf16[6,128,128]{2,1,0:T(8,128)(2,1)S(1)} collective-permute-done((bf16[6,128,128]{2,1,0:T(8,128)(2,1)S(1)}, bf16[6,128,128]{2,1,0:T(8,128)(2,1)S(1)}, u32[]{:S(2)}, u32[]{:S(2)}) %collective-permute-start.7) | collective-permute-done | bytes 196640 | tf_op jit(solution)/shard_map/ppermute | solution.py:547
  28.0 1.6 %collective-permute-start.9 = (bf16[2,128,128]{2,1,0:T(8,128)(2,1)S(1)}, bf16[2,128,128]{2,1,0:T(8,128)(2,1)S(1)}, u32[]{:S(2)}, u32[]{:S(2)}) collective-permute-start(bf16[2,128,128]{2,1,0:T(8,128)(2,1)S(1)} %get-tuple-element.38), channel_id=1, source_target_pairs={{0,2},{1,3},{2,0},{3,1},{4,6},{5,7},{6,4},{7,5},{8,10},{9,11},{10,... | collective-permute-start | bytes 196616 | tf_op jit(solution)/shard_map/ppermute | solution.py:547
  29.5 0.7 %collective-permute-start.8 = (bf16[2,128,128]{2,1,0:T(8,128)(2,1)S(1)}, bf16[2,128,128]{2,1,0:T(8,128)(2,1)S(1)}, u32[]{:S(2)}, u32[]{:S(2)}) collective-permute-start(bf16[2,128,128]{2,1,0:T(8,128)(2,1)S(1)} %get-tuple-element.37), channel_id=1, source_target_pairs={{1,3},{3,1},{5,7},{7,5},{9,11},{11,9},{13,15},{15,13},{17,19},{19,... | collective-permute-start | bytes 196616 | tf_op jit(solution)/shard_map/ppermute | solution.py:547
  30.2 2.1 %collective-permute-done.9.received = bf16[2,128,128]{2,1,0:T(8,128)(2,1)S(1)} collective-permute-done((bf16[2,128,128]{2,1,0:T(8,128)(2,1)S(1)}, bf16[2,128,128]{2,1,0:T(8,128)(2,1)S(1)}, u32[]{:S(2)}, u32[]{:S(2)}) %collective-permute-start.9) | collective-permute-done | bytes 65568 | tf_op jit(solution)/shard_map/ppermute | solution.py:547
  32.3 3.6 %collective-permute-start.10 = (bf16[2,128,128]{2,1,0:T(8,128)(2,1)S(1)}, bf16[2,128,128]{2,1,0:T(8,128)(2,1)S(1)}, u32[]{:S(2)}, u32[]{:S(2)}) collective-permute-start(bf16[2,128,128]{2,1,0:T(8,128)(2,1)S(1)} %plane_sum.1), channel_id=1, source_target_pairs={{0,4},{1,9},{2,6},{4,8},{5,13},{6,10},{7,3},{8,12},{10,14},{11,7},... | collective-permute-start | bytes 196616 | tf_op jit(solution)/shard_map/ppermute | solution.py:547
  36.0 0.0 collective-permute-done.8.later
  36.0 1.9 %collective-permute-done.10.received = bf16[2,128,128]{2,1,0:T(8,128)(2,1)S(1)} collective-permute-done((bf16[2,128,128]{2,1,0:T(8,128)(2,1)S(1)}, bf16[2,128,128]{2,1,0:T(8,128)(2,1)S(1)}, u32[]{:S(2)}, u32[]{:S(2)}) %collective-permute-start.10) | collective-permute-done | bytes 65568 | tf_op jit(solution)/shard_map/ppermute | solution.py:547
  37.9 0.1 collective-permute-start.11
  38.0 1.2 %collective-permute-done.11.received = f32[128,128]{1,0:T(8,128)S(1)} collective-permute-done((f32[128,128]{1,0:T(8,128)S(1)}, f32[128,128]{1,0:T(8,128)S(1)}, u32[]{:S(2)}, u32[]{:S(2)}) %collective-permute-start.11) | collective-permute-done | bytes 65568 | tf_op jit(solution)/shard_map/ppermute | solution.py:547
  39.2 0.6 %image.1 = f32[128,128]{1,0:T(8,128)} custom-call(f32[128,128]{1,0:T(8,128)S(1)} %get-tuple-element.39.kept, f32[128,128]{1,0:T(8,128)S(1)} %collective-permute-done.11.received), custom_call_target="tpu_custom_call" | custom-call | tf_op jit(solution)/shard_map/image/pallas_call | solution.py:488
  (6 shorter events, 0.1 us)
Async XLA Ops:
  2.7 4.0 %collective-permute-start = (bf16[2,264,256]{2,1,0:T(8,128)(2,1)S(1)}, bf16[2,264,256]{2,1,0:T(8,128)(2,1)S(1)}, u32[]{:S(2)}, u32[]{:S(2)}) collective-permute-start(bf16[2,264,256]{2,1,0:T(8,128)(2,1)S(1)} %get-tuple-element.23.swap), channel_id=1, source_target_pairs={{0,1},{1,0},{2,3},{3,2},{4,5},{5,4},{6,7},{7,6},{8,9},{9,8},{10,11... | collective-permute-start | bytes 811016 | tf_op jit(solution)/shard_map/ppermute | solution.py:547
  3.5 15.3 %copy-start = (bf16[9,512,384]{2,1,0:T(8,128)(2,1)S(1)}, bf16[9,512,384]{2,1,0:T(8,128)(2,1)}, u32[]{:S(2)}) copy-start(bf16[9,512,384]{2,1,0:T(8,128)(2,1)} %lag_range.3) | copy-start | bytes 10616836
  3.5 15.4 %copy-start.1 = (bf16[9,128,256]{2,1,0:T(8,128)(2,1)S(1)}, bf16[9,128,256]{2,1,0:T(8,128)(2,1)}, u32[]{:S(2)}) copy-start(bf16[9,128,256]{2,1,0:T(8,128)(2,1)} %steering.3) | copy-start | bytes 1769476
  4.2 8.2 %collective-permute-start.1 = (bf16[264,256]{1,0:T(8,128)(2,1)S(1)}, bf16[264,256]{1,0:T(8,128)(2,1)S(1)}, u32[]{:S(2)}, u32[]{:S(2)}) collective-permute-start(bf16[264,256]{1,0:T(8,128)(2,1)S(1)} %get-tuple-element.28), channel_id=1, source_target_pairs={{0,2},{1,3},{2,0},{3,1},{4,6},{5,7},{6,4},{7,5},{8,10},{9,11},{10,... | collective-permute-start | bytes 405512 | tf_op jit(solution)/shard_map/ppermute | solution.py:547
  6.7 6.8 %collective-permute-start.2 = (bf16[264,256]{1,0:T(8,128)(2,1)S(1)}, bf16[264,256]{1,0:T(8,128)(2,1)S(1)}, u32[]{:S(2)}, u32[]{:S(2)}) collective-permute-start(bf16[264,256]{1,0:T(8,128)(2,1)S(1)} %get-tuple-element.29), channel_id=1, source_target_pairs={{0,2},{1,3},{2,0},{3,1},{4,6},{5,7},{6,4},{7,5},{8,10},{9,11},{10,... | collective-permute-start | bytes 405512 | tf_op jit(solution)/shard_map/ppermute | solution.py:547
  7.4 11.5 %collective-permute-start.4 = (bf16[2,264,256]{2,1,0:T(8,128)(2,1)S(1)}, bf16[2,264,256]{2,1,0:T(8,128)(2,1)S(1)}, u32[]{:S(2)}, u32[]{:S(2)}) collective-permute-start(bf16[2,264,256]{2,1,0:T(8,128)(2,1)S(1)} %get-tuple-element.27.near), channel_id=1, source_target_pairs={{4,8},{5,9},{6,10},{7,11},{8,4},{9,5},{10,6},{11,7},{20,24},{21,25... | collective-permute-start | bytes 811016 | tf_op jit(solution)/shard_map/ppermute | solution.py:547
  8.0 10.8 %collective-permute-start.3 = (bf16[2,264,256]{2,1,0:T(8,128)(2,1)S(1)}, bf16[2,264,256]{2,1,0:T(8,128)(2,1)S(1)}, u32[]{:S(2)}, u32[]{:S(2)}) collective-permute-start(bf16[2,264,256]{2,1,0:T(8,128)(2,1)S(1)} %get-tuple-element.27.near), channel_id=1, source_target_pairs={{0,4},{1,5},{2,6},{3,7},{4,0},{5,1},{6,2},{7,3},{8,12},{9,13},{10,... | collective-permute-start | bytes 811016 | tf_op jit(solution)/shard_map/ppermute | solution.py:547
  13.5 10.7 %collective-permute-start.6 = (bf16[2,264,256]{2,1,0:T(8,128)(2,1)S(1)}, bf16[2,264,256]{2,1,0:T(8,128)(2,1)S(1)}, u32[]{:S(2)}, u32[]{:S(2)}) collective-permute-start(bf16[2,264,256]{2,1,0:T(8,128)(2,1)S(1)} %stack.1.mates), channel_id=1, source_target_pairs={{4,8},{5,9},{6,10},{7,11},{8,4},{9,5},{10,6},{11,7},{20,24},{21,25... | collective-permute-start | bytes 811016 | tf_op jit(solution)/shard_map/ppermute | solution.py:547
  14.2 10.3 %collective-permute-start.5 = (bf16[2,264,256]{2,1,0:T(8,128)(2,1)S(1)}, bf16[2,264,256]{2,1,0:T(8,128)(2,1)S(1)}, u32[]{:S(2)}, u32[]{:S(2)}) collective-permute-start(bf16[2,264,256]{2,1,0:T(8,128)(2,1)S(1)} %stack.1.mates), channel_id=1, source_target_pairs={{0,4},{1,5},{2,6},{3,7},{4,0},{5,1},{6,2},{7,3},{8,12},{9,13},{10,... | collective-permute-start | bytes 811016 | tf_op jit(solution)/shard_map/ppermute | solution.py:547
  26.4 1.5 %collective-permute-start.7 = (bf16[6,128,128]{2,1,0:T(8,128)(2,1)S(1)}, bf16[6,128,128]{2,1,0:T(8,128)(2,1)S(1)}, u32[]{:S(2)}, u32[]{:S(2)}) collective-permute-start(bf16[6,128,128]{2,1,0:T(8,128)(2,1)S(1)} %get-tuple-element.35), channel_id=1, source_target_pairs={{0,1},{1,0},{2,3},{3,2},{4,5},{5,4},{6,7},{7,6},{8,9},{9,8},{10,11... | collective-permute-start | bytes 589832 | tf_op jit(solution)/shard_map/ppermute | solution.py:547
  28.0 4.3 %collective-permute-start.9 = (bf16[2,128,128]{2,1,0:T(8,128)(2,1)S(1)}, bf16[2,128,128]{2,1,0:T(8,128)(2,1)S(1)}, u32[]{:S(2)}, u32[]{:S(2)}) collective-permute-start(bf16[2,128,128]{2,1,0:T(8,128)(2,1)S(1)} %get-tuple-element.38), channel_id=1, source_target_pairs={{0,2},{1,3},{2,0},{3,1},{4,6},{5,7},{6,4},{7,5},{8,10},{9,11},{10,... | collective-permute-start | bytes 196616 | tf_op jit(solution)/shard_map/ppermute | solution.py:547
  29.5 6.5 %collective-permute-start.8 = (bf16[2,128,128]{2,1,0:T(8,128)(2,1)S(1)}, bf16[2,128,128]{2,1,0:T(8,128)(2,1)S(1)}, u32[]{:S(2)}, u32[]{:S(2)}) collective-permute-start(bf16[2,128,128]{2,1,0:T(8,128)(2,1)S(1)} %get-tuple-element.37), channel_id=1, source_target_pairs={{1,3},{3,1},{5,7},{7,5},{9,11},{11,9},{13,15},{15,13},{17,19},{19,... | collective-permute-start | bytes 196616 | tf_op jit(solution)/shard_map/ppermute | solution.py:547
  32.3 5.5 %collective-permute-start.10 = (bf16[2,128,128]{2,1,0:T(8,128)(2,1)S(1)}, bf16[2,128,128]{2,1,0:T(8,128)(2,1)S(1)}, u32[]{:S(2)}, u32[]{:S(2)}) collective-permute-start(bf16[2,128,128]{2,1,0:T(8,128)(2,1)S(1)} %plane_sum.1), channel_id=1, source_target_pairs={{0,4},{1,9},{2,6},{4,8},{5,13},{6,10},{7,3},{8,12},{10,14},{11,7},... | collective-permute-start | bytes 196616 | tf_op jit(solution)/shard_map/ppermute | solution.py:547
  37.9 1.3 %collective-permute-start.11 = (f32[128,128]{1,0:T(8,128)S(1)}, f32[128,128]{1,0:T(8,128)S(1)}, u32[]{:S(2)}, u32[]{:S(2)}) collective-permute-start(f32[128,128]{1,0:T(8,128)S(1)} %get-tuple-element.40), channel_id=1, source_target_pairs={{0,1},{1,0},{2,3},{3,2},{4,5},{5,4},{6,7},{7,6},{8,9},{9,8},{10,11... | collective-permute-start | bytes 196616 | tf_op jit(solution)/shard_map/ppermute | solution.py:547
